TPU v7x, 32 devices: a whole 2x2x4 slice. The times are simulated.
32 devices in a mesh: section: 2 (over core), expert: 4 (over y, x), seq: 4 (over z).
Axes of the slice: x: 2, y: 2, z: 4, core: 2. Of those that a mesh axis runs over, the one named last changes fastest.
Arguments:
- inputs: bfloat16 [2, 4, 1024, 768], P(None, 'expert', 'seq'), may hold values from -6 to 6
- cotangent: bfloat16 [2, 4, 1024, 768], P(None, 'expert', 'seq'), may hold values from -6 to 6
- query_key_value_weight: bfloat16 [2, 768, 2304], P('section', ('expert', 'seq')), may hold values from -0.21875 to 0.21875
- w_attn_out: bfloat16 [2, 768, 768], P('section', ('expert', 'seq')), may hold values from -0.625 to 0.625
- w_router: bfloat16 [2, 768, 16], P('section', ('expert', 'seq')), may hold values from -0.4375 to 0.4375
- norm_gains: bfloat16 [2, 2, 768], P('section', None, ('expert', 'seq')), may hold values from 0.5 to 1.5
- rel_table: bfloat16 [2, 64, 12], P('section', ('expert', 'seq')), may hold values from -4 to 324
- w_expert_in: bfloat16 [2, 16, 768, 3072], P('section', ('expert', 'seq')), may hold values from -0.21875 to 0.21875
- w_expert_out: bfloat16 [2, 16, 3072, 768], P('section', ('expert', 'seq')), may hold values from -0.109375 to 0.109375
- routes: int32 [2, 2, 4, 1024, 2], P('section', None, 'expert', 'seq'), may hold values from 0 to 15, all different within a row; in each aligned block of 256 rows (0 to 255, 256 to 511, ..., all dimensions but the last counted through in order) at most 64 rows name the same one
Outputs:
- activations: bfloat16 [2, 2, 4, 1024, 768], P('section', None, 'expert', 'seq')
- input_grads: float32 [2, 2, 4, 1024, 768], P('section', None, 'expert', 'seq')
- grad_qkv: float32 [2, 768, 2304], P('section', ('expert', 'seq'))
- grad_attn_out: float32 [2, 768, 768], P('section', ('expert', 'seq'))
- grad_router: float32 [2, 768, 16], P('section', ('expert', 'seq'))
- grad_gains: float32 [2, 2, 768], P('section', None, ('expert', 'seq'))
- grad_table: float32 [2, 64, 12], P('section', ('expert', 'seq'))
- grad_expert_in: float32 [2, 16, 768, 3072], P('section', ('expert', 'seq'))
- grad_expert_out: float32 [2, 16, 3072, 768], P('section', ('expert', 'seq'))
Inputs may be any that keep to these rules, and one draw needn't show every extreme that they name: `routes`: in each aligned block of 256 tokens (one device's piece of one sequence of one micro-batch) no expert is named by more than 64 tokens, a bound that some block reaches; a token's two experts differ.
All inputs are finite; a program needn't handle non-finite values.
Results may differ from a plain program's by a relative error of at most 0.025.
Values may be sent and summed in bfloat16 or wider, within the bound.
A program may use at most 384 MiB of HBM per device.

v0:
```python
import jax
import jax.numpy as jnp
from jax import lax
from jax.sharding import PartitionSpec as P

highest_precision = lax.Precision.HIGHEST


def from_behind(block, axis, distance):
    devices = range(lax.axis_size(axis))
    route = [(i - distance, i) for i in devices if i - distance in devices]
    return lax.ppermute(block, axis, route)


def rms_norm(values, gain):
    return values * lax.rsqrt(jnp.mean(values * values, axis=-1, keepdims=True) + 1e-06) * gain


def exact_gelu(values):
    return jax.nn.gelu(values, approximate=False)


def take_block(stacked, position):
    return lax.dynamic_index_in_dim(stacked, position, 0, keepdims=False)


def put_block(buffer, update, position, active):
    return jnp.where(active, lax.dynamic_update_index_in_dim(buffer, update, position, 0), buffer)


def prepare_weights(collected):
    return (
        collected[0][0],
        collected[1][0],
        collected[2][0],
        collected[3][0].astype(jnp.float32),
        collected[4][0].astype(jnp.float32),
    )


def bucket_onehot(query_start, key_start, row_count, buckets, spacing):
    query_pos = query_start + jnp.arange(row_count, dtype=jnp.int32)
    key_pos = key_start + jnp.arange(row_count, dtype=jnp.int32)
    distance = query_pos[:, None] - key_pos[None, :]
    causal = distance >= 0
    bucket = jnp.where(causal, distance, 0) // spacing
    onehot = (bucket[:, :, None] == jnp.arange(buckets, dtype=jnp.int32)[None, None, :]).astype(
        jnp.float32
    )
    return (causal, onehot)


def attention_scores(queries, gathered, rel_bias, query_start):
    row_count, feature_count = queries.shape
    length = gathered.shape[0]
    buckets, head_count = rel_bias.shape
    head_size = feature_count // head_count
    spacing = length // buckets
    query_heads = queries.reshape(row_count, head_count, head_size)
    key_heads = gathered[:, :feature_count].reshape(length, head_count, head_size)
    products = jnp.einsum(
        "qhd,khd->hqk", query_heads, key_heads, preferred_element_type=jnp.float32
    ) * head_size ** (-0.5)

    def block_bias(block_index):
        causal, onehot = bucket_onehot(
            query_start, block_index * row_count, row_count, buckets, spacing
        )
        return (jnp.einsum("qkr,rh->hqk", onehot, rel_bias, precision=highest_precision), causal)

    offsets, causal = lax.map(block_bias, jnp.arange(length // row_count, dtype=jnp.int32))
    offsets = jnp.transpose(offsets, (1, 2, 0, 3)).reshape(head_count, row_count, length)
    causal = jnp.transpose(causal, (1, 0, 2)).reshape(row_count, length)
    return (products + offsets, causal)


def table_gradient(score_grad, query_start, buckets):
    head_count, row_count, length = score_grad.shape
    spacing = length // buckets
    blocks = jnp.transpose(
        score_grad.reshape(head_count, row_count, length // row_count, row_count), (2, 0, 1, 3)
    )

    def add_block(carry, members):
        block_index, block = members
        causal, onehot = bucket_onehot(
            query_start, block_index * row_count, row_count, buckets, spacing
        )
        return (
            carry
            + jnp.einsum(
                "hqk,qkr->rh", block.astype(jnp.float32), onehot, precision=highest_precision
            ),
            None,
        )

    initial = jnp.zeros((buckets, head_count), jnp.float32)
    summed, unused = lax.scan(
        add_block, initial, (jnp.arange(length // row_count, dtype=jnp.int32), blocks)
    )
    return summed


def slot_targets(route_rows, experts, capacity):
    flat_routes = route_rows.reshape(-1)
    member = (flat_routes[:, None] == jnp.arange(experts, dtype=jnp.int32)[None, :]).astype(
        jnp.int32
    )
    earlier = jnp.cumsum(member, axis=0) - member
    return flat_routes * capacity + jnp.sum(earlier * member, axis=1)


def forward_layer(residual_stream, weights, w_in, w_down, route_rows):
    query_key_value_weight, output_weight, w_gate, gains_pair, rel_bias = weights
    row_count, feature_count = residual_stream.shape
    head_count = rel_bias.shape[1]
    head_size = feature_count // head_count
    normalized_input = rms_norm(residual_stream, gains_pair[0]).astype(jnp.bfloat16)
    mixed_stream = jnp.dot(
        normalized_input, query_key_value_weight, preferred_element_type=jnp.float32
    ).astype(jnp.bfloat16)
    gathered = lax.all_gather(mixed_stream[:, feature_count:], "seq", axis=0, tiled=True)
    length = gathered.shape[0]
    scores, causal = attention_scores(
        mixed_stream[:, :feature_count], gathered, rel_bias, lax.axis_index("seq") * row_count
    )
    row_max = jnp.max(jnp.where(causal[None], scores, -1e30), axis=2)
    expo_values = jnp.where(causal[None], jnp.exp(scores - row_max[:, :, None]), 0.0)
    row_sum = jnp.sum(expo_values, axis=2)
    probs_low = (expo_values / row_sum[:, :, None]).astype(jnp.bfloat16)
    value_heads = gathered[:, feature_count:].reshape(length, head_count, head_size)
    attention_result = jnp.einsum(
        "hqk,khd->qhd", probs_low, value_heads, preferred_element_type=jnp.float32
    )
    attention_result = attention_result.reshape(row_count, feature_count).astype(jnp.bfloat16)
    middle_stream = residual_stream + jnp.dot(
        attention_result, output_weight, preferred_element_type=jnp.float32
    )
    normed_two = rms_norm(middle_stream, gains_pair[1]).astype(jnp.bfloat16)
    logits = jnp.dot(normed_two, w_gate, preferred_element_type=jnp.float32)
    experts = logits.shape[1]
    chosen_mask = route_rows[:, :, None] == jnp.arange(experts, dtype=jnp.int32)[None, None, :]
    chosen = jnp.sum(jnp.where(chosen_mask, logits[:, None, :], 0.0), axis=2)
    first_gate = jax.nn.sigmoid(chosen[:, 0] - chosen[:, 1])
    gate_pair = jnp.stack([first_gate, 1.0 - first_gate], axis=1)
    capacity = max(2, 4 * row_count // experts)
    target = slot_targets(route_rows, experts, capacity)
    outgoing = (
        jnp.zeros((experts * capacity, feature_count), jnp.bfloat16)
        .at[target]
        .set(jnp.repeat(normed_two, 2, axis=0))
    )
    arrived = lax.all_to_all(
        outgoing.reshape(experts, capacity, feature_count),
        ("expert", "seq"),
        split_axis=0,
        concat_axis=0,
        tiled=True,
    )
    sources, slot_count, unused = arrived.shape
    arrived_rows = arrived.reshape(sources * slot_count, feature_count)
    hidden = jnp.dot(arrived_rows, w_in, preferred_element_type=jnp.float32)
    activation = exact_gelu(hidden).astype(jnp.bfloat16)
    produced = jnp.dot(activation, w_down, preferred_element_type=jnp.float32).astype(jnp.bfloat16)
    returned = lax.all_to_all(
        produced.reshape(sources, slot_count, feature_count),
        ("expert", "seq"),
        split_axis=0,
        concat_axis=0,
        tiled=True,
    )
    returned, arrived, hidden = (
        returned,
        arrived,
        hidden.reshape(sources, slot_count, hidden.shape[1]),
    )
    produced = returned.reshape(experts * capacity, feature_count)[target].reshape(
        row_count, 2, feature_count
    )
    result = middle_stream + jnp.sum(gate_pair[:, :, None] * produced.astype(jnp.float32), axis=1)
    state = (
        residual_stream,
        normalized_input,
        mixed_stream,
        row_max,
        row_sum,
        attention_result,
        middle_stream,
        normed_two,
        gate_pair,
        target,
        arrived.reshape(experts * capacity, feature_count),
        hidden.reshape(experts * capacity, hidden.shape[2]),
        produced,
    )
    return (result, state, gathered)


def backward_layer(upstream, state, gathered, weights, w_in, w_down, route_rows):
    query_key_value_weight, output_weight, w_gate, gains_pair, rel_bias = weights
    (
        residual_stream,
        normalized_input,
        mixed_stream,
        row_max,
        row_sum,
        attention_result,
        middle_stream,
        normed_two,
        gate_pair,
        target,
        arrived_rows,
        hidden,
        produced,
    ) = state
    row_count, feature_count = residual_stream.shape
    head_count = rel_bias.shape[1]
    head_size = feature_count // head_count
    experts = w_gate.shape[1]
    capacity = arrived_rows.shape[0] // experts
    gate_grad = jnp.sum(upstream[:, None, :] * produced.astype(jnp.float32), axis=2)
    produced_grad = (
        (gate_pair[:, :, None] * upstream[:, None, :])
        .astype(jnp.bfloat16)
        .reshape(row_count * 2, feature_count)
    )
    slots_grad = (
        jnp.zeros((experts * capacity, feature_count), jnp.bfloat16).at[target].set(produced_grad)
    )
    arrived_grad = lax.all_to_all(
        slots_grad.reshape(experts, capacity, feature_count),
        ("expert", "seq"),
        split_axis=0,
        concat_axis=0,
        tiled=True,
    )
    arrived_grad = arrived_grad.reshape(experts * capacity, feature_count)
    activation = exact_gelu(hidden).astype(jnp.bfloat16)
    grad_down = jnp.einsum(
        "rf,rd->fd", activation, arrived_grad, preferred_element_type=jnp.float32
    )
    activation_grad = jnp.einsum(
        "rd,fd->rf", arrived_grad, w_down, preferred_element_type=jnp.float32
    )
    unused, gelu_back = jax.vjp(exact_gelu, hidden)
    hidden_grad = gelu_back(activation_grad)[0].astype(jnp.bfloat16)
    grad_in = jnp.einsum("rd,rf->df", arrived_rows, hidden_grad, preferred_element_type=jnp.float32)
    rows_grad = jnp.einsum(
        "rf,df->rd", hidden_grad, w_in, preferred_element_type=jnp.float32
    ).astype(jnp.bfloat16)
    returned_grad = lax.all_to_all(
        rows_grad.reshape(experts, capacity, feature_count),
        ("expert", "seq"),
        split_axis=0,
        concat_axis=0,
        tiled=True,
    )
    returned_grad = returned_grad.reshape(experts * capacity, feature_count)
    token_grad = jnp.sum(
        returned_grad[target].astype(jnp.float32).reshape(row_count, 2, feature_count), axis=1
    )
    first_gate = gate_pair[:, 0]
    shift_grad = (gate_grad[:, 0] - gate_grad[:, 1]) * first_gate * (1.0 - first_gate)
    chosen_mask = (
        route_rows[:, :, None] == jnp.arange(experts, dtype=jnp.int32)[None, None, :]
    ).astype(jnp.float32)
    logits_grad = (shift_grad[:, None] * (chosen_mask[:, 0] - chosen_mask[:, 1])).astype(
        jnp.bfloat16
    )
    grad_gate = jnp.einsum("td,te->de", normed_two, logits_grad, preferred_element_type=jnp.float32)
    normed_two_grad = token_grad + jnp.einsum(
        "te,de->td", logits_grad, w_gate, preferred_element_type=jnp.float32
    )
    unused, second_back = jax.vjp(rms_norm, middle_stream, gains_pair[1])
    middle_norm_grad, gain_two_grad = second_back(normed_two_grad)
    middle_grad = upstream + middle_norm_grad
    branch_grad = middle_grad.astype(jnp.bfloat16)
    grad_out = jnp.einsum(
        "td,te->de", attention_result, branch_grad, preferred_element_type=jnp.float32
    )
    attended_grad = jnp.einsum(
        "te,de->td", branch_grad, output_weight, preferred_element_type=jnp.float32
    ).astype(jnp.bfloat16)
    length = gathered.shape[0]
    query_start = lax.axis_index("seq") * row_count
    scores, causal = attention_scores(
        mixed_stream[:, :feature_count], gathered, rel_bias, query_start
    )
    probs_full = (
        jnp.where(causal[None], jnp.exp(scores - row_max[:, :, None]), 0.0) / row_sum[:, :, None]
    )
    attended_heads = attended_grad.reshape(row_count, head_count, head_size)
    query_heads = mixed_stream[:, :feature_count].reshape(row_count, head_count, head_size)
    key_heads = gathered[:, :feature_count].reshape(length, head_count, head_size)
    value_heads = gathered[:, feature_count:].reshape(length, head_count, head_size)
    probs_grad = jnp.einsum(
        "qhd,khd->hqk", attended_heads, value_heads, preferred_element_type=jnp.float32
    )
    row_delta = jnp.sum(probs_full * probs_grad, axis=2)
    scores_grad = (probs_full * (probs_grad - row_delta[:, :, None])).astype(jnp.bfloat16)
    scale = head_size ** (-0.5)
    query_grad = (
        jnp.einsum("hqk,khd->qhd", scores_grad, key_heads, preferred_element_type=jnp.float32)
        * scale
    )
    probs_low = probs_full.astype(jnp.bfloat16)
    values_grad = jnp.einsum(
        "hqk,qhd->khd", probs_low, attended_heads, preferred_element_type=jnp.float32
    )
    keys_grad = (
        jnp.einsum("hqk,qhd->khd", scores_grad, query_heads, preferred_element_type=jnp.float32)
        * scale
    )
    pair_terms = jnp.concatenate(
        [keys_grad.reshape(length, feature_count), values_grad.reshape(length, feature_count)],
        axis=1,
    )
    pair_grad = lax.psum_scatter(
        pair_terms.astype(jnp.bfloat16), "seq", scatter_dimension=0, tiled=True
    ).astype(jnp.float32)
    mixed_grad = jnp.concatenate(
        [query_grad.reshape(row_count, feature_count), pair_grad], axis=1
    ).astype(jnp.bfloat16)
    grad_bias = table_gradient(scores_grad, query_start, rel_bias.shape[0])
    grad_qkv = jnp.einsum(
        "td,te->de", normalized_input, mixed_grad, preferred_element_type=jnp.float32
    )
    normed_grad = jnp.einsum(
        "te,de->td", mixed_grad, query_key_value_weight, preferred_element_type=jnp.float32
    )
    unused, first_back = jax.vjp(rms_norm, residual_stream, gains_pair[0])
    stream_norm_grad, gain_one_grad = first_back(normed_grad)
    stream_grad = middle_grad + stream_norm_grad
    gains_grad = jnp.stack([gain_one_grad, gain_two_grad])
    return (stream_grad, (grad_qkv, grad_out, grad_gate, gains_grad, grad_bias, grad_in, grad_down))


def per_device(
    inputs,
    cotangent,
    query_key_value_weight,
    w_attn_out,
    w_router,
    norm_gains,
    rel_table,
    w_expert_in,
    w_expert_out,
    routes,
):
    section_index = lax.axis_index("section")
    micro_count = inputs.shape[0]
    row_count = inputs.shape[2]
    feature_count = inputs.shape[3]
    w_in = w_expert_in[0, 0]
    w_down = w_expert_out[0, 0]
    shards = (query_key_value_weight, w_attn_out, w_router, norm_gains, rel_table)
    weights = prepare_weights(
        (
            lax.all_gather(query_key_value_weight, ("expert", "seq"), axis=1, tiled=True),
            lax.all_gather(w_attn_out, ("expert", "seq"), axis=1, tiled=True),
            lax.all_gather(w_router, ("expert", "seq"), axis=1, tiled=True),
            lax.all_gather(norm_gains, ("expert", "seq"), axis=2, tiled=True),
            lax.all_gather(rel_table, ("expert", "seq"), axis=1, tiled=True),
        )
    )
    arriving = jnp.zeros((row_count, feature_count), jnp.bfloat16)
    section_outputs = jnp.zeros((micro_count, row_count, feature_count), jnp.bfloat16)
    stored = None
    for turn_index in range(micro_count + 1):
        batch_index = turn_index - section_index
        active = (batch_index >= 0) & (batch_index < micro_count)
        position = jnp.clip(batch_index, 0, micro_count - 1)
        own_rows = take_block(inputs, position)[0]
        residual_stream = jnp.where(section_index == 0, own_rows, arriving).astype(jnp.float32)
        route_rows = take_block(routes[0], position)[0]
        result, state, gathered = forward_layer(residual_stream, weights, w_in, w_down, route_rows)
        result_low = result.astype(jnp.bfloat16)
        section_outputs = put_block(section_outputs, result_low, position, active)
        record = state
        if stored is None:
            stored = jax.tree.map(
                lambda leaf: jnp.zeros((micro_count,) + leaf.shape, leaf.dtype), record
            )
        stored = jax.tree.map(
            lambda buffer, leaf: put_block(buffer, leaf, position, active), stored, record
        )
        arriving = from_behind(result_low, "section", 1)
    back_weights = prepare_weights(
        (
            lax.all_gather(shards[0], ("expert", "seq"), axis=1, tiled=True),
            lax.all_gather(shards[1], ("expert", "seq"), axis=1, tiled=True),
            lax.all_gather(shards[2], ("expert", "seq"), axis=1, tiled=True),
            lax.all_gather(shards[3], ("expert", "seq"), axis=2, tiled=True),
            lax.all_gather(shards[4], ("expert", "seq"), axis=1, tiled=True),
        )
    )
    arriving = jnp.zeros((row_count, feature_count), jnp.bfloat16)
    section_grads = jnp.zeros((micro_count, row_count, feature_count), jnp.float32)
    totals = None
    for turn_index in range(micro_count + 1):
        batch_index = micro_count - turn_index - section_index
        active = (batch_index >= 0) & (batch_index < micro_count)
        position = jnp.clip(batch_index, 0, micro_count - 1)
        given = take_block(cotangent, position)[0].astype(jnp.float32)
        upstream = jnp.where(section_index == 1, given, arriving.astype(jnp.float32))
        record = jax.tree.map(lambda buffer: take_block(buffer, position), stored)
        state = record
        gathered = lax.all_gather(state[2][:, feature_count:], "seq", axis=0, tiled=True)
        route_rows = take_block(routes[0], position)[0]
        stream_grad, contributions = backward_layer(
            upstream, state, gathered, back_weights, w_in, w_down, route_rows
        )
        contributions = tuple((jnp.where(active, part_grad, 0.0) for part_grad in contributions))
        totals = (
            contributions
            if totals is None
            else tuple((left + right for left, right in zip(totals, contributions)))
        )
        section_grads = put_block(section_grads, stream_grad, position, active)
        arriving = from_behind(stream_grad.astype(jnp.bfloat16), "section", -1)
    owned = (
        lax.psum_scatter(totals[0], ("expert", "seq"), scatter_dimension=0, tiled=True),
        lax.psum_scatter(totals[1], ("expert", "seq"), scatter_dimension=0, tiled=True),
        lax.psum_scatter(totals[2], ("expert", "seq"), scatter_dimension=0, tiled=True),
        lax.psum_scatter(totals[3], ("expert", "seq"), scatter_dimension=1, tiled=True),
        lax.psum_scatter(totals[4], ("expert", "seq"), scatter_dimension=0, tiled=True),
    )
    return (
        section_outputs[None, :, None],
        section_grads[None, :, None],
        owned[0][None],
        owned[1][None],
        owned[2][None],
        owned[3][None],
        owned[4][None],
        totals[5][None, None],
        totals[6][None, None],
    )


def solution(mesh):
    in_specs = (
        P(None, "expert", "seq", None),
        P(None, "expert", "seq", None),
        P("section", ("expert", "seq"), None),
        P("section", ("expert", "seq"), None),
        P("section", ("expert", "seq"), None),
        P("section", None, ("expert", "seq")),
        P("section", ("expert", "seq"), None),
        P("section", ("expert", "seq"), None, None),
        P("section", ("expert", "seq"), None, None),
        P("section", None, "expert", "seq", None),
    )
    out_specs = (
        P("section", None, "expert", "seq", None),
        P("section", None, "expert", "seq", None),
        P("section", ("expert", "seq"), None),
        P("section", ("expert", "seq"), None),
        P("section", ("expert", "seq"), None),
        P("section", None, ("expert", "seq")),
        P("section", ("expert", "seq"), None),
        P("section", ("expert", "seq"), None, None),
        P("section", ("expert", "seq"), None, None),
    )
    return jax.shard_map(
        per_device, mesh=mesh, in_specs=in_specs, out_specs=out_specs, check_vma=False
    )
```

profile of v0, /device:TPU:0, one launch (start us, length us, event | category | flops | bytes accessed | tf_op | source)
XLA Modules:
  0.0 2204.8 jit_solution(6440032822520297973)
XLA Ops:
  8.8 48.2 %all_gather.38 = bf16[1,2,768]{1,0,2:T(2,128)(2,1)S(1)} all-gather(bf16[1,2,48]{1,0,2:T(2,128)(2,1)S(1)} %copy.216), channel_id=1, replica_groups=mesh['section'=2,'expert'=4,'seq'=4] {'expert','seq'}, dimensions={2}, use_global_device_ids=true | all-gather | bytes 3264 | tf_op jit(solution)/shard_map/all_gather | solution.py:362
  63.2 21.9 all-gather.9.cloned.1.call-done
  93.7 40.3 %all_gather.41 = bf16[1,64,12]{2,0,1:T(2,128)(2,1)S(1)} all-gather(bf16[1,4,12]{2,0,1:T(2,128)(2,1)S(1)} %copy.218), channel_id=1, replica_groups=mesh['section'=2,'expert'=4,'seq'=4] {'expert','seq'}, dimensions={1}, use_global_device_ids=true | all-gather | bytes 1632 | tf_op jit(solution)/shard_map/all_gather | solution.py:363
  134.2 33.9 %while.36 = (s32[]{:T(128)}, f32[4,12,256,256]{3,1,2,0:T(8,128)}, pred[4,256,256]{1,2,0:T(8,128)(4,1)S(1)}, s32[]{:T(128)}, s32[4]{0:T(128)S(1)}, /*index=5*/f32[64,12]{0,1:T(8,128)S(1)}, s32[]{:T(128)}, s32[1]{0:T(128)}) while((s32[]{:T(128)}, f32[4,12,256,256]{3,1,2,0:T(8,128)}, pred[4,256,256]{1,2,0:T(8,128)(4,1)S(1)}, s32[]{:T(128)}, ...), condition=%wide.region_2.3_spmd, body=%wide.region_1.2_spmd.sunk | while | flops 609485312 | bytes 5055621 | solution.py:71
  168.5 17.2 copy.224
  242.2 35.2 %all_to_all.60 = bf16[16,64,768]{2,1,0:T(8,128)(2,1)S(1)} all-to-all(bf16[16,64,768]{2,1,0:T(8,128)(2,1)} %bitcast.1055), channel_id=1, replica_groups=mesh['section'=2,'expert'=4,'seq'=4] {'expert','seq'}, dimensions={0} | all-to-all | bytes 3145728 | tf_op jit(solution)/shard_map/all_to_all | solution.py:153
  296.9 34.9 %fusion.254 = bf16[1024,768]{1,0:T(8,128)(2,1)} fusion(bf16[1,1,3072,768]{3,2,1,0:T(8,128)(2,1)} %param.26, f32[1024,3072]{1,0:T(8,128)S(1)} %get-tuple-element.616), kind=kOutput, calls=%fused_computation.378 | convolution fusion | flops 5037096960 | bytes 18874368 | tf_op jit(solution)/shard_map/dot_general | solution.py:164
  335.9 69.0 %all_gather.43 = bf16[1,768,16]{2,0,1:T(2,128)(2,1)} all-gather(bf16[1,48,16]{2,0,1:T(2,128)(2,1)S(1)} %copy.225), channel_id=1, replica_groups=mesh['section'=2,'expert'=4,'seq'=4] {'expert','seq'}, dimensions={1}, use_global_device_ids=true | all-gather | bytes 26112 | tf_op jit(solution)/shard_map/all_gather | solution.py:361
  432.3 56.1 %all-gather.15.cloned.1.call-done = bf16[1024,1536]{1,0:T(8,128)(2,1)} async-done(((bf16[256,1536]{1,0:T(8,128)(2,1)}), bf16[1024,1536]{1,0:T(8,128)(2,1)}) %all-gather.15.cloned.1.call-update) | async-done | bytes 3145744 | tf_op jit(solution)/shard_map/all_gather | solution.py:122
  517.7 43.0 %all_to_all.61 = bf16[16,64,768]{2,1,0:T(8,128)(2,1)S(1)} all-to-all(bf16[16,64,768]{2,1,0:T(8,128)(2,1)S(1)} %bitcast.1056), channel_id=1, replica_groups=mesh['section'=2,'expert'=4,'seq'=4] {'expert','seq'}, dimensions={0} | all-to-all | bytes 3145728 | tf_op jit(solution)/shard_map/all_to_all | solution.py:153
  576.4 35.5 %fusion.259 = bf16[1024,768]{1,0:T(8,128)(2,1)} fusion(bf16[1,1,3072,768]{3,2,1,0:T(8,128)(2,1)} %param.26, f32[1024,3072]{1,0:T(8,128)} %get-tuple-element.618), kind=kOutput, calls=%fused_computation.379 | convolution fusion | flops 5037096960 | bytes 18874368 | tf_op jit(solution)/shard_map/dot_general | solution.py:164
  617.2 36.4 %all-to-all-done.3 = bf16[16,64,768]{2,1,0:T(8,128)(2,1)S(1)} async-done(((bf16[16,64,768]{2,1,0:T(8,128)(2,1)}), bf16[16,64,768]{2,1,0:T(8,128)(2,1)S(1)}, u32[]{:S(2)}, u32[]{:S(2)}) %all-to-all-start.3) | async-done | bytes 1572896 | tf_op jit(solution)/shard_map/all_to_all | solution.py:165
  675.7 59.6 %all-gather.17.cloned.1.call-done = bf16[1024,1536]{1,0:T(8,128)(2,1)} async-done(((bf16[256,1536]{1,0:T(8,128)(2,1)}), bf16[1024,1536]{1,0:T(8,128)(2,1)}) %all-gather.17.cloned.1.call-update) | async-done | bytes 3145744 | tf_op jit(solution)/shard_map/all_gather | solution.py:122
  838.6 38.4 %all-to-all-done.6 = bf16[16,64,768]{2,1,0:T(8,128)(2,1)} async-done(((bf16[16,64,768]{2,1,0:T(8,128)(2,1)}), bf16[16,64,768]{2,1,0:T(8,128)(2,1)}, u32[]{:S(2)}, u32[]{:S(2)}) %all-to-all-start.6) | async-done | bytes 1572896 | tf_op jit(solution)/shard_map/all_to_all | solution.py:230
  877.0 35.6 %fusion.61 = bf16[1024,3072]{1,0:T(8,128)(2,1)S(1)} fusion(f32[2,1024,3072]{2,1,0:T(8,128)} %get-tuple-element.619, s32[]{:T(128)S(6)} %min.15, bf16[1024,768]{1,0:T(8,128)(2,1)} %bitcast.78, bf16[1,1,3072,768]{3,2,1,0:T(8,128)(2,1)} %param.26), kind=kOutput, calls=%fused_computation.109 | convolution fusion | flops 5058330624 | bytes 25165828 | tf_op jit(solution)/shard_map/rd,fd->rf/dot_general | solution.py:242
  922.8 35.5 %fusion.264 = bf16[1024,768]{1,0:T(8,128)(2,1)} fusion(bf16[1,1,3072,768]{3,2,1,0:T(8,128)(2,1)} %param.26, f32[1024,3072]{1,0:T(8,128)} %get-tuple-element.620), kind=kOutput, calls=%fused_computation.380 | convolution fusion | flops 5037096960 | bytes 18874368 | tf_op jit(solution)/shard_map/dot_general | solution.py:164
  1066.8 55.7 %reduce-scatter.13.cloned.1.call-done = bf16[256,1536]{0,1:T(8,128)(2,1)} async-done(((bf16[1024,1536]{0,1:T(8,128)(2,1)}), bf16[256,1536]{0,1:T(8,128)(2,1)}) %reduce-scatter.13.cloned.1.call-update) | async-done | bytes 786448 | tf_op jit(solution)/shard_map/reduce_scatter | solution.py:318
  1147.2 72.9 %all-to-all-done.8 = bf16[16,64,768]{2,1,0:T(8,128)(2,1)S(1)} async-done(((bf16[16,64,768]{2,1,0:T(8,128)(2,1)}), bf16[16,64,768]{2,1,0:T(8,128)(2,1)S(1)}, u32[]{:S(2)}, u32[]{:S(2)}) %all-to-all-start.8) | async-done | bytes 1572896 | tf_op jit(solution)/shard_map/all_to_all | solution.py:230
  1220.1 37.0 %fusion.66 = bf16[1024,3072]{1,0:T(8,128)(2,1)S(1)} fusion(f32[2,1024,3072]{2,1,0:T(8,128)} %get-tuple-element.619, s32[]{:T(128)S(6)} %min.14, bf16[1024,768]{1,0:T(8,128)(2,1)S(1)} %bitcast.1082, bf16[1,1,3072,768]{3,2,1,0:T(8,128)(2,1)} %param.26), kind=kOutput, calls=%fused_computation.114 | convolution fusion | flops 5058330624 | bytes 25165828 | tf_op jit(solution)/shard_map/rd,fd->rf/dot_general | solution.py:242
  1285.7 49.1 %all-to-all-done.9 = bf16[16,64,768]{2,1,0:T(8,128)(2,1)S(1)} async-done(((bf16[16,64,768]{2,1,0:T(8,128)(2,1)}), bf16[16,64,768]{2,1,0:T(8,128)(2,1)S(1)}, u32[]{:S(2)}, u32[]{:S(2)}) %all-to-all-start.9) | async-done | bytes 1572896 | tf_op jit(solution)/shard_map/all_to_all | solution.py:251
  1419.4 17.6 reduce-scatter.15.cloned.1.call-done
  1496.3 23.0 %while.37 = (s32[]{:T(128)}, f32[64,12]{0,1:T(8,128)S(1)}, s32[]{:T(128)}, s32[4]{0:T(128)S(1)}, bf16[4,12,256,256]{2,1,3,0:T(8,128)(2,1)}, /*index=5*/s32[]{:T(128)}, s32[1]{0:T(128)}, s32[]{:T(128)}) while((s32[]{:T(128)}, f32[64,12]{0,1:T(8,128)S(1)}, s32[]{:T(128)}, s32[4]{0:T(128)S(1)}, ...), condition=%wide.region_70.71_spmd.clone, body=%wide.region_69.70_spmd.clone.sunk | while | flops 106039296 | bytes 2631819 | solution.py:98
  1519.2 35.8 %fusion.71 = bf16[1024,3072]{1,0:T(8,128)(2,1)S(1)} fusion(f32[2,1024,3072]{2,1,0:T(8,128)} %get-tuple-element.619, s32[]{:T(128)S(6)} %min.13, bf16[1024,768]{1,0:T(8,128)(2,1)} %bitcast.152, bf16[1,1,3072,768]{3,2,1,0:T(8,128)(2,1)} %param.26), kind=kOutput, calls=%fused_computation.119 | convolution fusion | flops 5058330624 | bytes 25165828 | tf_op jit(solution)/shard_map/rd,fd->rf/dot_general | solution.py:242
  1653.7 33.4 %fusion.178 = f32[3072,768]{1,0:T(8,128)} fusion(bf16[1024,768]{1,0:T(8,128)(2,1)S(1)} %bitcast.1083, f32[2,1024,3072]{2,1,0:T(8,128)} %get-tuple-element.619, s32[]{:T(128)S(6)} %min.14), kind=kOutput, calls=%fused_computation.316 | convolution fusion | flops 5036310528 | bytes 23592964 | tf_op jit(solution)/shard_map/rf,rd->fd/dot_general | solution.py:239
  1712.6 23.2 %while.38 = (s32[]{:T(128)}, f32[64,12]{0,1:T(8,128)S(1)}, s32[]{:T(128)}, s32[4]{0:T(128)S(1)}, bf16[4,12,256,256]{2,1,3,0:T(8,128)(2,1)}, /*index=5*/s32[]{:T(128)}, s32[1]{0:T(128)}, s32[]{:T(128)}) while((s32[]{:T(128)}, f32[64,12]{0,1:T(8,128)S(1)}, s32[]{:T(128)}, s32[4]{0:T(128)S(1)}, ...), condition=%wide.region_72.73_spmd.clone, body=%wide.region_71.72_spmd.clone.sunk | while | flops 106039296 | bytes 2631819 | solution.py:98
  1754.6 23.4 %reduce-scatter.17.cloned.1.call-done = bf16[256,1536]{0,1:T(8,128)(2,1)} async-done(((bf16[1024,1536]{0,1:T(8,128)(2,1)}), bf16[256,1536]{0,1:T(8,128)(2,1)}) %reduce-scatter.17.cloned.1.call-update) | async-done | bytes 786448 | tf_op jit(solution)/shard_map/reduce_scatter | solution.py:318
  1788.7 34.0 %fusion.176 = f32[3072,768]{1,0:T(8,128)} fusion(bf16[1024,768]{1,0:T(8,128)(2,1)} %bitcast.152, f32[2,1024,3072]{2,1,0:T(8,128)} %get-tuple-element.619, s32[]{:T(128)S(6)} %min.13), kind=kOutput, calls=%fused_computation.314 | convolution fusion | flops 5036310528 | bytes 23592964 | tf_op jit(solution)/shard_map/rf,rd->fd/dot_general | solution.py:239
  1842.6 34.8 %add_bitcast_fusion = f32[1,1,3072,768]{3,2,1,0:T(8,128)} fusion(f32[3072,768]{1,0:T(8,128)} %fusion.176, f32[3072,768]{1,0:T(8,128)} %fusion.178, pred[]{:T(512)S(6)} %and.92, pred[]{:T(512)S(6)} %and.93, pred[]{:T(512)S(6)} %and.94, bf16[1024,768]{1,0:T(8,128)(2,1)} %bitcast.78, f32[2,1024,3072]{2,1,0:T(8,128)} %get-tuple-element.619, s32[]{:T(128)S(6)} %min.15), kind=kOutput, calls=%fused_computation.311 | convolution fusion | flops 5048107008 | bytes 42467336 | tf_op jit(solution)/shard_map/rf,rd->fd/dot_general | solution.py:239
  1889.5 23.3 %while.39 = (s32[]{:T(128)}, f32[64,12]{0,1:T(8,128)S(1)}, s32[]{:T(128)}, s32[4]{0:T(128)S(1)}, bf16[4,12,256,256]{2,1,3,0:T(8,128)(2,1)}, /*index=5*/s32[]{:T(128)}, s32[1]{0:T(128)}, s32[]{:T(128)}) while((s32[]{:T(128)}, f32[64,12]{0,1:T(8,128)S(1)}, s32[]{:T(128)}, s32[4]{0:T(128)S(1)}, ...), condition=%wide.region_74.75_spmd.clone, body=%wide.region_73.74_spmd.clone.sunk | while | flops 106039296 | bytes 2631819 | solution.py:98
  1912.8 41.9 %all-reduce = f32[64,12]{0,1:T(8,128)S(1)} all-reduce(f32[64,12]{0,1:T(8,128)S(1)} %select_add_fusion.2), channel_id=9, replica_groups=mesh['section'=2,'expert'=4,'seq'=4] {'expert','seq'}, use_global_device_ids=true, to_apply=%region_75.76.clone | all-reduce | flops 768 | bytes 6144
  1958.7 82.4 %reduce-scatter.21.cloned.1.call-done = f32[48,768]{1,0:T(8,128)} async-done(((f32[768,768]{1,0:T(8,128)}), f32[48,768]{1,0:T(8,128)}) %reduce-scatter.21.cloned.1.call-update) | async-done | bytes 147472 | tf_op jit(solution)/shard_map/reduce_scatter | solution.py:423
  2041.1 156.9 %reduce-scatter.19.cloned.1.call-done = f32[48,2304]{1,0:T(8,128)} async-done(((f32[768,2304]{1,0:T(8,128)}), f32[48,2304]{1,0:T(8,128)}) %reduce-scatter.19.cloned.1.call-update) | async-done | bytes 442384 | tf_op jit(solution)/shard_map/reduce_scatter | solution.py:422
  (865 shorter events, 894.2 us)
Async XLA Ops:
  7.2 77.9 %all-gather.9.cloned.1.call-start = ((), (), s32[]{:S(2)}) async-start(), calls=%async_computation.19 | async-start | bytes 3760128 | tf_op jit(solution)/shard_map/all_gather | solution.py:359
  7.9 195.6 %all-gather.11.cloned.1.call-start = ((), (), s32[]{:S(2)}) async-start(), calls=%async_computation.20 | async-start | bytes 3932160 | tf_op jit(solution)/shard_map/all_gather | solution.py:122
  63.2 693.9 %copy-start.89 = (f32[768]{0:T(1024)}, f32[768]{0:T(1024)S(1)}, u32[]{:S(2)}) copy-start(f32[768]{0:T(1024)S(1)} %get-tuple-element.484) | copy-start | bytes 9220
  91.9 141.0 %all-gather.13.cloned.1.call-start = ((), (), s32[]{:S(2)}) async-start(), calls=%async_computation.21 | async-start | bytes 1253376 | tf_op jit(solution)/shard_map/all_gather | solution.py:360
  168.5 583.8 %copy-start.17 = (pred[256,1024]{1,0:T(8,128)(4,1)}, pred[256,1024]{1,0:T(8,128)(4,1)S(1)}, u32[]{:S(2)}) copy-start(pred[256,1024]{1,0:T(8,128)(4,1)S(1)} %copy.221) | copy-start | bytes 786436
  331.8 75.1 %all-to-all-start.1 = ((bf16[16,64,768]{2,1,0:T(8,128)(2,1)}), bf16[16,64,768]{2,1,0:T(8,128)(2,1)S(1)}, u32[]{:S(2)}, u32[]{:S(2)}) async-start(bf16[16,64,768]{2,1,0:T(8,128)(2,1)} %bitcast.1088), calls=%async_computation.1 | async-start | bytes 3145728 | tf_op jit(solution)/shard_map/all_to_all | solution.py:165
  335.7 152.7 %all-gather.15.cloned.1.call-start = ((), (), s32[]{:S(2)}) async-start(), calls=%async_computation.22 | async-start | bytes 3932160 | tf_op jit(solution)/shard_map/all_gather | solution.py:122
  414.9 4.5 collective-permute-start
  612.0 41.7 %all-to-all-start.3 = ((bf16[16,64,768]{2,1,0:T(8,128)(2,1)}), bf16[16,64,768]{2,1,0:T(8,128)(2,1)S(1)}, u32[]{:S(2)}, u32[]{:S(2)}) async-start(bf16[16,64,768]{2,1,0:T(8,128)(2,1)} %bitcast.1089), calls=%async_computation.3 | async-start | bytes 3145728 | tf_op jit(solution)/shard_map/all_to_all | solution.py:165
  615.7 119.6 %all-gather.17.cloned.1.call-start = ((), (), s32[]{:S(2)}) async-start(), calls=%async_computation.23 | async-start | bytes 3932160 | tf_op jit(solution)/shard_map/all_gather | solution.py:122
  662.7 2.6 collective-permute-start.1
  764.7 43.0 %all-to-all-start.4 = ((bf16[16,64,768]{2,1,0:T(8,128)(2,1)}), bf16[16,64,768]{2,1,0:T(8,128)(2,1)S(1)}, u32[]{:S(2)}, u32[]{:S(2)}) async-start(bf16[16,64,768]{2,1,0:T(8,128)(2,1)} %bitcast.1046), calls=%async_computation.4 | async-start | bytes 3145728 | tf_op jit(solution)/shard_map/all_to_all | solution.py:153
  807.7 69.3 %all-to-all-start.6 = ((bf16[16,64,768]{2,1,0:T(8,128)(2,1)}), bf16[16,64,768]{2,1,0:T(8,128)(2,1)}, u32[]{:S(2)}, u32[]{:S(2)}) async-start(bf16[16,64,768]{2,1,0:T(8,128)(2,1)} %bitcast.1048), calls=%async_computation.6 | async-start | bytes 3145728 | tf_op jit(solution)/shard_map/all_to_all | solution.py:230
  812.1 174.8 %all-gather.19.cloned.1.call-start = ((), (), s32[]{:S(2)}) async-start(), calls=%async_computation.24 | async-start | bytes 3932160 | tf_op jit(solution)/shard_map/all_gather | solution.py:408
  918.9 40.9 %all-to-all-start.7 = ((bf16[16,64,768]{2,1,0:T(8,128)(2,1)}), bf16[16,64,768]{2,1,0:T(8,128)(2,1)S(1)}, u32[]{:S(2)}, u32[]{:S(2)}) async-start(bf16[16,64,768]{2,1,0:T(8,128)(2,1)} %bitcast.80), calls=%async_computation.7 | async-start | bytes 3145728 | tf_op jit(solution)/shard_map/all_to_all | solution.py:251
  959.8 48.9 %all-to-all-start.5 = ((bf16[16,64,768]{2,1,0:T(8,128)(2,1)}), bf16[16,64,768]{2,1,0:T(8,128)(2,1)S(1)}, u32[]{:S(2)}, u32[]{:S(2)}) async-start(bf16[16,64,768]{2,1,0:T(8,128)(2,1)} %bitcast.1085), calls=%async_computation.5 | async-start | bytes 3145728 | tf_op jit(solution)/shard_map/all_to_all | solution.py:165
  965.3 157.1 %reduce-scatter.13.cloned.1.call-start = ((), (), s32[]{:S(2)}) async-start(), calls=%async_computation.25 | async-start | bytes 3932160 | tf_op jit(solution)/shard_map/reduce_scatter | solution.py:318
  1129.3 3.6 collective-permute-start.2
  1139.5 80.6 %all-to-all-start.8 = ((bf16[16,64,768]{2,1,0:T(8,128)(2,1)}), bf16[16,64,768]{2,1,0:T(8,128)(2,1)S(1)}, u32[]{:S(2)}, u32[]{:S(2)}) async-start(bf16[16,64,768]{2,1,0:T(8,128)(2,1)} %bitcast.121), calls=%async_computation.9 | async-start | bytes 3145728 | tf_op jit(solution)/shard_map/all_to_all | solution.py:230
  1145.1 128.3 %all-gather.21.cloned.1.call-start = ((), (), s32[]{:S(2)}) async-start(), calls=%async_computation.26 | async-start | bytes 3932160 | tf_op jit(solution)/shard_map/all_gather | solution.py:408
  1263.5 71.3 %all-to-all-start.9 = ((bf16[16,64,768]{2,1,0:T(8,128)(2,1)}), bf16[16,64,768]{2,1,0:T(8,128)(2,1)S(1)}, u32[]{:S(2)}, u32[]{:S(2)}) async-start(bf16[16,64,768]{2,1,0:T(8,128)(2,1)} %bitcast.1087), calls=%async_computation.10 | async-start | bytes 3145728 | tf_op jit(solution)/shard_map/all_to_all | solution.py:251
  1267.3 141.6 %all-gather.23.cloned.1.call-start = ((), (), s32[]{:S(2)}) async-start(), calls=%async_computation.28 | async-start | bytes 3932160 | tf_op jit(solution)/shard_map/all_gather | solution.py:408
  1273.3 163.6 %reduce-scatter.15.cloned.1.call-start = ((), (), s32[]{:S(2)}) async-start(), calls=%async_computation.27 | async-start | bytes 3932160 | tf_op jit(solution)/shard_map/reduce_scatter | solution.py:318
  1444.6 10.5 collective-permute-start.3
  1464.3 54.9 %all-to-all-start.10 = ((bf16[16,64,768]{2,1,0:T(8,128)(2,1)}), bf16[16,64,768]{2,1,0:T(8,128)(2,1)}, u32[]{:S(2)}, u32[]{:S(2)}) async-start(bf16[16,64,768]{2,1,0:T(8,128)(2,1)} %bitcast.151), calls=%async_computation.12 | async-start | bytes 3145728 | tf_op jit(solution)/shard_map/all_to_all | solution.py:230
  1561.3 46.8 %all-to-all-start.11 = ((bf16[16,64,768]{2,1,0:T(8,128)(2,1)}), bf16[16,64,768]{2,1,0:T(8,128)(2,1)S(1)}, u32[]{:S(2)}, u32[]{:S(2)}) async-start(bf16[16,64,768]{2,1,0:T(8,128)(2,1)} %bitcast.1086), calls=%async_computation.13 | async-start | bytes 3145728 | tf_op jit(solution)/shard_map/all_to_all | solution.py:251
  1568.5 178.8 %reduce-scatter.23.cloned.1.call-start = ((), (), s32[]{:S(2)}) async-start(), calls=%async_computation.32 | async-start | bytes 417792
  1591.0 186.9 %reduce-scatter.17.cloned.1.call-start = ((), (), s32[]{:S(2)}) async-start(), calls=%async_computation.29 | async-start | bytes 3932160 | tf_op jit(solution)/shard_map/reduce_scatter | solution.py:318
  1653.7 303.6 %reduce-scatter.25.cloned.1.call-start = ((), (), s32[]{:S(2)}) async-start(), calls=%async_computation.33 | async-start | bytes 417792
  1784.8 256.3 %reduce-scatter.21.cloned.1.call-start = ((), (), s32[]{:S(2)}) async-start(), calls=%async_computation.31 | async-start | bytes 2506752 | tf_op jit(solution)/shard_map/reduce_scatter | solution.py:423
  1788.7 409.4 %reduce-scatter.19.cloned.1.call-start = ((), (), s32[]{:S(2)}) async-start(), calls=%async_computation.30 | async-start | bytes 7520256 | tf_op jit(solution)/shard_map/reduce_scatter | solution.py:422
  1957.3 240.8 %copy-start.75 = (f32[1,2,1,256,768]{4,3,1,2,0:T(8,128)}, f32[1,2,1,256,768]{4,3,1,2,0:T(8,128)S(1)}, u32[]{:S(2)}) copy-start(f32[1,2,1,256,768]{4,3,1,2,0:T(8,128)S(1)} %fusion.314) | copy-start | bytes 4718596
  (178 other events, 4803.5 us)
Sparse Core Ops, SparseCore 0:
  10.8 74.2 all-gather.8
  92.0 62.3 all-gather.10
  157.2 54.6 all-gather.12
  428.0 60.3 all-gather.14
  673.9 61.3 all-gather.16
  823.3 75.9 all-gather.18
  1060.8 61.6 reduce-scatter.12
  1147.5 85.6 all-gather.20
  1273.4 79.4 all-gather.22
  1380.2 56.7 reduce-scatter.14
  1591.2 125.0 reduce-scatter.22
  1718.4 59.4 reduce-scatter.16
  1784.9 122.9 reduce-scatter.24
  1913.2 127.8 reduce-scatter.20
  2046.9 151.0 reduce-scatter.18
where the time goes:
time: 2220 us; the launch traced here: 2200 us
  waiting for transfers between devices  710 us (32%)
  matrix products  673 us (30%)
  local copies, waits for them, and re-layouts  299 us (13%)
  blocking collectives  278 us (13%)
  other arithmetic  163 us (7%)
  starting transfers between devices  54 us (2%)
    reduce_scatter x1, waiting for transfers between devices, per_device(): lax.psum_scatter(totals[0], ('expert', 'seq'), scatter_dimension=0, tiled...  157 us
    all_gather x3, waiting for transfers between devices, forward_layer(): lax.all_gather(mixed_stream[:, feature_count:], 'seq', axis=0, tiled=True)  116 us
    all_to_all x3, waiting for transfers between devices, backward_layer(): lax.all_to_all(slots_grad.reshape(experts, capacity, feature_count), ('ex...  111 us
    dot_general x3, matrix products, backward_layer(): jnp.einsum('rd,fd->rf', arrived_grad, w_down, preferred_element_type=jnp....  108 us
    dot_general x3, matrix products, forward_layer(): jnp.dot(activation, w_down, preferred_element_type=jnp.float32)  106 us
    dot_general x3, matrix products, backward_layer(): jnp.einsum('rf,rd->fd', activation, arrived_grad, preferred_element_type=...  102 us
    reduce_scatter x3, waiting for transfers between devices, backward_layer(): lax.psum_scatter(pair_terms.astype(jnp.bfloat16), 'seq', scatter_dimensio...  96.6 us
    reduce_scatter x1, waiting for transfers between devices, per_device(): lax.psum_scatter(totals[1], ('expert', 'seq'), scatter_dimension=0, tiled...  82.4 us
  transfers between devices with their start and end apart: 29, of which 17 were waited for; matrix products, arithmetic and copies ran while one was open for 35% of the time, Pallas kernels for 0%

commit v1 on v0

v1 whole, which is shorter than its diff:
```python
import functools

import jax
import jax.numpy as jnp
from jax import lax
from jax.experimental import pallas as pl
from jax.experimental.pallas import tpu as pltpu
from jax.sharding import Mesh
from jax.sharding import PartitionSpec as P

F32 = jnp.float32
BF16 = jnp.bfloat16
EPS = 1e-06
MASKED = -1e30
GROUP = 4
RANKS = ("expert", "zhi", "zlo")
VMEM_LIMIT = 60 << 20

NN = (((1,), (0,)), ((), ()))
NT = (((1,), (1,)), ((), ()))
TN = (((0,), (0,)), ((), ()))


def mm(left, right, dims=NN):
    return lax.dot_general(left, right, dims, preferred_element_type=F32)


def inverse_rms(values):
    return lax.rsqrt(jnp.mean(values * values, axis=-1, keepdims=True) + EPS)


def whole(array):
    rank = len(array.shape)
    return pl.BlockSpec(array.shape, lambda *unused: (0,) * rank)


def call(body, name, outs, args, scalars=None, scratch=(), flops=0):
    specs = [pl.BlockSpec(memory_space=pltpu.SMEM)] if scalars is not None else []
    specs += [pl.BlockSpec(memory_space=pltpu.VMEM)] * len(args)
    operands = ([scalars] if scalars is not None else []) + list(args)
    moved = sum(a.size * a.dtype.itemsize for a in list(args) + list(outs))
    return pl.pallas_call(
        body,
        name=name,
        in_specs=specs,
        out_specs=[pl.BlockSpec(memory_space=pltpu.VMEM)] * len(outs),
        out_shape=list(outs),
        scratch_shapes=list(scratch),
        compiler_params=pltpu.CompilerParams(vmem_limit_bytes=VMEM_LIMIT),
        cost_estimate=pl.CostEstimate(flops=flops, bytes_accessed=moved, transcendentals=0),
    )(*operands)


def shape(dims, dtype):
    return jax.ShapeDtypeStruct(tuple(dims), dtype)


def bucket_onehot(buckets, span, spacing):
    width = 2 * span * GROUP
    column = lax.broadcasted_iota(jnp.int32, (buckets, width), 1)
    delta = column // (2 * span)
    distance = column - delta * (2 * span) - span + span * delta
    bucket = jnp.where(distance >= 0, distance // spacing, -1)
    row = lax.broadcasted_iota(jnp.int32, (buckets, width), 0)
    return (bucket == row).astype(BF16)


def fill_bias(first_head, heads, table, vectors, bias, span, spacing):
    buckets, head_count = table.shape
    hot = bucket_onehot(buckets, span, spacing)
    rows = mm(table[...], hot, TN)
    column = lax.broadcasted_iota(jnp.int32, (1, 2 * span * GROUP), 1)
    rows = jnp.where(column < span, MASKED, rows)
    vectors[0:head_count, :] = rows
    for head in range(heads):
        picked = vectors[pl.ds(first_head + head, 1), :]
        for delta in range(GROUP):
            piece = picked[:, delta * 2 * span : (delta + 1) * 2 * span]
            spread = jnp.broadcast_to(piece, (span, 2 * span))
            rolled = pltpu.roll(spread, span, 1, stride=1, stride_axis=0)
            bias[head * GROUP + delta] = rolled[:, :span]


def attention_forward(sizes, ids, own, flip, side, side_flip, gain, weight, table,
                      out, mixed, gathered, stats, vectors, bias, turned):
    span, heads, size, spacing = sizes
    width = heads * size
    fill_bias(ids[4] * heads, heads, table, vectors, bias, span, spacing)
    for slot, piece in enumerate((own, flip, side, side_flip)):
        gathered[pl.ds(pl.multiple_of(ids[slot] * span, span), span), :] = piece[...]
    for part in range(GROUP):
        rows = slice(part * span, (part + 1) * span)
        values = gathered[rows, :].astype(F32)
        normed = (values * inverse_rms(values) * gain[...].astype(F32)).astype(BF16)
        mixed[rows, :] = mm(normed, weight[...]).astype(BF16)
    for head in range(heads):
        columns = slice(head * size, (head + 1) * size)
        query_t = (mixed[:, columns].astype(F32) * size ** (-0.5)).T.astype(BF16)
        key = mixed[:, width + head * size : width + (head + 1) * size]
        value_t = mixed[:, 2 * width + head * size : 2 * width + (head + 1) * size].astype(F32).T.astype(BF16)
        for part in range(GROUP):
            mine = slice(part * span, (part + 1) * span)
            blocks = []
            for other in range(part + 1):
                raw = mm(key[other * span : (other + 1) * span], query_t[:, mine])
                blocks.append(raw + bias[head * GROUP + part - other])
            top = functools.reduce(jnp.maximum, [jnp.max(b, axis=0, keepdims=True) for b in blocks])
            total = jnp.zeros_like(top)
            gained = jnp.zeros((size, span), F32)
            for other, block in enumerate(blocks):
                raised = jnp.exp(block - top)
                total = total + jnp.sum(raised, axis=0, keepdims=True)
                gained = gained + mm(value_t[:, other * span : (other + 1) * span], raised.astype(BF16))
            turned[columns, mine] = gained / total
            stats[head : head + 1, mine] = top + jnp.log(total)
    for part in range(GROUP):
        mine = slice(part * span, (part + 1) * span)
        out[part] = turned[:, mine].T.astype(BF16)


def route_masks(routes, experts):
    lane = lax.broadcasted_iota(jnp.int32, (routes.shape[0], experts), 1)
    return [(routes[:, k : k + 1] == lane).astype(F32) for k in range(2)]


def pick_rows(slot, slots):
    lane = lax.broadcasted_iota(jnp.int32, (slot.shape[0], slots), 1).astype(F32)
    return (lane == slot).astype(BF16)


def fill_slots(aux_t, slots, k):
    row = lax.broadcasted_iota(jnp.int32, (slots, aux_t.shape[1]), 0).astype(F32)
    return (row == aux_t[k : k + 1, :]).astype(BF16)


def after_attention(capacity, attended, own, w_out, gain, router, routes,
                    outgoing, middle, normed_two, aux):
    tokens = own.shape[0]
    experts = router.shape[1]
    slots = experts * capacity
    width = attended.shape[2]
    total = own[...].astype(F32)
    for group in range(GROUP):
        total = total + mm(attended[group], w_out[group * width : (group + 1) * width, :])
    middle[...] = total
    normed = (total * inverse_rms(total) * gain[...].astype(F32)).astype(BF16)
    normed_two[...] = normed
    logits = mm(normed, router[...])
    masks = route_masks(routes, experts)
    members = (masks[0] + masks[1]).astype(BF16)
    row = lax.broadcasted_iota(jnp.int32, (tokens, tokens), 0)
    column = lax.broadcasted_iota(jnp.int32, (tokens, tokens), 1)
    earlier = mm((row > column).astype(BF16), members)
    chosen = [jnp.sum(logits * mask, axis=1, keepdims=True) for mask in masks]
    first = jax.nn.sigmoid(chosen[0] - chosen[1])
    places = [
        routes[:, k : k + 1].astype(F32) * capacity + jnp.sum(earlier * masks[k], axis=1, keepdims=True)
        for k in range(2)
    ]
    lane = lax.broadcasted_iota(jnp.int32, (tokens, 128), 1)
    packed = jnp.zeros((tokens, 128), F32)
    for index, entry in enumerate((places[0], places[1], first, 1.0 - first)):
        packed = jnp.where(lane == index, entry, packed)
    aux[...] = packed
    packed_t = packed.T
    hot = fill_slots(packed_t, slots, 0) + fill_slots(packed_t, slots, 1)
    outgoing[...] = mm(hot, normed).astype(BF16)


def expert_forward(rows, w_in, w_down, activation, slope, produced, total):
    step = pl.program_id(0)

    @pl.when(step == 0)
    def clear():
        total[...] = jnp.zeros_like(total)

    chunk = rows.shape[0] // 4
    for part in range(4):
        mine = slice(part * chunk, (part + 1) * chunk)
        hidden = mm(rows[mine, :], w_in[...])
        half = 0.5 * (1.0 + lax.erf(hidden * 0.7071067811865476))
        bell = jnp.exp(-0.5 * hidden * hidden) * 0.3989422804014327
        raised = (hidden * half).astype(BF16)
        activation[mine, :] = raised
        slope[mine, :] = (half + hidden * bell).astype(BF16)
        total[mine, :] += mm(raised, w_down[...])

    @pl.when(step == pl.num_programs(0) - 1)
    def finish():
        produced[...] = total[...].astype(BF16)


def expert_backward(arrived_grad, w_in, w_down, slope, hidden_grad, rows_grad, total):
    step = pl.program_id(0)

    @pl.when(step == 0)
    def clear():
        total[...] = jnp.zeros_like(total)

    chunk = arrived_grad.shape[0] // 4
    for part in range(4):
        mine = slice(part * chunk, (part + 1) * chunk)
        lifted = mm(arrived_grad[mine, :], w_down[...], NT) * slope[mine, :].astype(F32)
        lowered = lifted.astype(BF16)
        hidden_grad[mine, :] = lowered
        total[mine, :] += mm(lowered, w_in[...], NT)

    @pl.when(step == pl.num_programs(0) - 1)
    def finish():
        rows_grad[...] = total[...].astype(BF16)


def tile_of(hidden):
    return 768 if hidden % 768 == 0 else hidden


def run_expert_forward(rows, w_in, w_down):
    count, features = rows.shape
    hidden = w_in.shape[1]
    tile = tile_of(hidden)
    return pl.pallas_call(
        expert_forward,
        name="expert_forward",
        grid=(hidden // tile,),
        in_specs=[
            whole(rows),
            pl.BlockSpec((features, tile), lambda j: (0, j)),
            pl.BlockSpec((tile, features), lambda j: (j, 0)),
        ],
        out_specs=[
            pl.BlockSpec((count, tile), lambda j: (0, j)),
            pl.BlockSpec((count, tile), lambda j: (0, j)),
            pl.BlockSpec((count, features), lambda j: (0, 0)),
        ],
        out_shape=[shape((count, hidden), BF16), shape((count, hidden), BF16), shape((count, features), BF16)],
        scratch_shapes=[pltpu.VMEM((count, features), F32)],
        compiler_params=pltpu.CompilerParams(vmem_limit_bytes=VMEM_LIMIT),
        cost_estimate=pl.CostEstimate(
            flops=4 * count * features * hidden, bytes_accessed=30 << 20, transcendentals=2 * count * hidden
        ),
    )(rows, w_in, w_down)


def run_expert_backward(arrived_grad, w_in, w_down, slope):
    count, features = arrived_grad.shape
    hidden = w_in.shape[1]
    tile = tile_of(hidden)
    return pl.pallas_call(
        expert_backward,
        name="expert_backward",
        grid=(hidden // tile,),
        in_specs=[
            whole(arrived_grad),
            pl.BlockSpec((features, tile), lambda j: (0, j)),
            pl.BlockSpec((tile, features), lambda j: (j, 0)),
            pl.BlockSpec((count, tile), lambda j: (0, j)),
        ],
        out_specs=[
            pl.BlockSpec((count, tile), lambda j: (0, j)),
            pl.BlockSpec((count, features), lambda j: (0, 0)),
        ],
        out_shape=[shape((count, hidden), BF16), shape((count, features), BF16)],
        scratch_shapes=[pltpu.VMEM((count, features), F32)],
        compiler_params=pltpu.CompilerParams(vmem_limit_bytes=VMEM_LIMIT),
        cost_estimate=pl.CostEstimate(
            flops=4 * count * features * hidden, bytes_accessed=30 << 20, transcendentals=0
        ),
    )(arrived_grad, w_in, w_down, slope)


def weight_partials(scalars, rows, hidden_grad, activation, arrived_grad, grad_in, grad_down):
    @pl.when(scalars[0] == 1)
    def wanted():
        grad_in[...] = mm(rows[...], hidden_grad[...], TN).astype(BF16)
        grad_down[...] = mm(activation[...], arrived_grad[...], TN).astype(BF16)


def run_weight_partials(wanted, rows, hidden_grad, activation, arrived_grad):
    count, features = rows.shape
    hidden = hidden_grad.shape[1]
    tile = tile_of(hidden)
    return pl.pallas_call(
        weight_partials,
        name="weight_partials",
        grid_spec=pltpu.PrefetchScalarGridSpec(
            num_scalar_prefetch=1,
            grid=(hidden // tile,),
            in_specs=[
                pl.BlockSpec((count, features), lambda j, s: (0, 0)),
                pl.BlockSpec((count, tile), lambda j, s: (0, j * s[0])),
                pl.BlockSpec((count, tile), lambda j, s: (0, j * s[0])),
                pl.BlockSpec((count, features), lambda j, s: (0, 0)),
            ],
            out_specs=[
                pl.BlockSpec((features, tile), lambda j, s: (0, j * s[0])),
                pl.BlockSpec((tile, features), lambda j, s: (j * s[0], 0)),
            ],
        ),
        out_shape=[shape((features, hidden), BF16), shape((hidden, features), BF16)],
        compiler_params=pltpu.CompilerParams(vmem_limit_bytes=VMEM_LIMIT),
        cost_estimate=pl.CostEstimate(
            flops=4 * count * features * hidden, bytes_accessed=30 << 20, transcendentals=0
        ),
    )(wanted, rows, hidden_grad, activation, arrived_grad)


def weight_totals(scalars, rows, hidden_grad, activation, arrived_grad,
                  rows_1, hidden_grad_1, activation_1, arrived_grad_1,
                  sent_in, sent_down, grad_in, grad_down):
    def build(left, right, left_down, right_down):
        grad_in[...] = mm(left[...], right[...], TN) + sent_in[...].astype(F32)
        grad_down[...] = mm(left_down[...], right_down[...], TN) + sent_down[...].astype(F32)

    @pl.when(scalars[0] == 0)
    def first():
        build(rows, hidden_grad, activation, arrived_grad)

    @pl.when(scalars[0] == 1)
    def second():
        build(rows_1, hidden_grad_1, activation_1, arrived_grad_1)


def run_weight_totals(core, first, second, sent_in, sent_down):
    count, features = first[0].shape
    hidden = first[1].shape[1]
    tile = tile_of(hidden) // 2

    def operand_specs(which):
        def column(j, s):
            return (0, jnp.where(s[0] == which, j, 0))

        return [
            pl.BlockSpec((count, features), lambda j, s: (0, 0)),
            pl.BlockSpec((count, tile), column),
            pl.BlockSpec((count, tile), column),
            pl.BlockSpec((count, features), lambda j, s: (0, 0)),
        ]

    across = pl.BlockSpec((features, tile), lambda j, s: (0, j))
    down = pl.BlockSpec((tile, features), lambda j, s: (j, 0))
    return pl.pallas_call(
        weight_totals,
        name="weight_totals",
        grid_spec=pltpu.PrefetchScalarGridSpec(
            num_scalar_prefetch=1,
            grid=(hidden // tile,),
            in_specs=operand_specs(0) + operand_specs(1) + [across, down],
            out_specs=[across, down],
        ),
        out_shape=[shape((features, hidden), F32), shape((hidden, features), F32)],
        compiler_params=pltpu.CompilerParams(vmem_limit_bytes=VMEM_LIMIT),
        cost_estimate=pl.CostEstimate(
            flops=4 * count * features * hidden, bytes_accessed=60 << 20, transcendentals=0
        ),
    )(core, *first, *second, sent_in, sent_down)


def combine(returned, aux, middle, result, difference):
    slots = returned.shape[0]
    packed = aux[...]
    outs = [mm(pick_rows(packed[:, k : k + 1], slots), returned[...]) for k in range(2)]
    total = middle[...] + packed[:, 2:3] * outs[0] + packed[:, 3:4] * outs[1]
    result[...] = total.astype(BF16)
    difference[...] = outs[0] - outs[1]


def spread_grads(upstream, aux, outgoing):
    slots = outgoing.shape[0]
    packed = aux[...]
    packed_t = packed.T
    values = upstream[...].astype(F32)
    total = jnp.zeros(outgoing.shape, F32)
    for k in range(2):
        total = total + mm(fill_slots(packed_t, slots, k), (values * packed[:, 2 + k : 3 + k]).astype(BF16))
    outgoing[...] = total.astype(BF16)


def bucket_sums(block_sums, buckets):
    heads, deltas, sides, count, unused = block_sums.shape
    dims = (deltas, sides, count, count, buckets)
    delta, side, key, query, bucket = [lax.broadcasted_iota(jnp.int32, dims, axis) for axis in range(5)]
    hot = (delta * count + query - key - side == bucket).astype(F32)
    return jnp.einsum("hdskq,dskqb->hb", block_sums, hot, precision=lax.Precision.HIGHEST)


def norm_backward(values, gain, grad):
    scale = inverse_rms(values)
    unit = values * scale
    lifted = grad * gain
    back = scale * (lifted - unit * jnp.mean(lifted * unit, axis=-1, keepdims=True))
    return back, jnp.sum(grad * unit, axis=0, keepdims=True)


def before_attention(returned, aux, upstream, difference, middle, normed_two, attended, gain,
                     router, w_out, routes, middle_grad, attended_grad, out_grad, router_grad, gain_grad):
    slots = returned.shape[0]
    experts = router.shape[1]
    width = attended.shape[2]
    packed = aux[...]
    hot = pick_rows(packed[:, 0:1], slots) + pick_rows(packed[:, 1:2], slots)
    token_grad = mm(hot, returned[...])
    flow = upstream[...].astype(F32)
    shift = jnp.sum(flow * difference[...], axis=1, keepdims=True) * packed[:, 2:3] * packed[:, 3:4]
    masks = route_masks(routes, experts)
    logits_grad = (shift * (masks[0] - masks[1])).astype(BF16)
    router_grad[...] = mm(normed_two[...], logits_grad, TN)
    token_grad = token_grad + mm(logits_grad, router[...], NT)
    back, gain_part = norm_backward(middle[...], gain[...].astype(F32), token_grad)
    gain_grad[...] = gain_part
    total = flow + back
    middle_grad[...] = total
    branch = total.astype(BF16)
    for group in range(GROUP):
        mine = slice(group * width, (group + 1) * width)
        out_grad[mine, :] = mm(attended[group], branch, TN)
        attended_grad[group] = mm(branch, w_out[mine, :], NT).astype(BF16)


def attention_backward(sizes, ids, mixed, stats, attended, grads, gathered, gain, weight, table,
                       kept, sent, qkv_grad, gain_grad, table_grad,
                       vectors, bias, mixed_grad, sums, key_total, value_total, turned, strips):
    span, heads, size, spacing = sizes
    width = heads * size
    count = span // spacing
    row = lax.broadcasted_iota(jnp.int32, (span, span), 0)
    column = lax.broadcasted_iota(jnp.int32, (span, span), 1)
    later = (column % spacing) >= (row % spacing)
    fill_bias(ids[4] * heads, heads, table, vectors, bias, span, spacing)
    for head in range(heads):
        columns = slice(head * size, (head + 1) * size)
        key_columns = slice(width + head * size, width + (head + 1) * size)
        value_columns = slice(2 * width + head * size, 2 * width + (head + 1) * size)
        query = (mixed[:, columns].astype(F32) * size ** (-0.5)).astype(BF16)
        query_t = query.astype(F32).T.astype(BF16)
        key = mixed[:, key_columns]
        key_t = key.astype(F32).T.astype(BF16)
        value = mixed[:, value_columns]
        key_total[...] = jnp.zeros_like(key_total)
        value_total[...] = jnp.zeros_like(value_total)
        sums[...] = jnp.zeros_like(sums)
        for part in range(GROUP):
            mine = slice(part * span, (part + 1) * span)
            grad = grads[part, :, columns]
            grad_wide = grad.astype(F32)
            grad_t = grad_wide.T
            outcome_t = attended[part, :, columns].astype(F32).T
            delta_row = jnp.sum(grad_t * outcome_t, axis=0, keepdims=True)
            grad_t = grad_t.astype(BF16)
            level = stats[head : head + 1, mine]
            query_total = jnp.zeros((size, span), F32)
            for other in range(part + 1):
                theirs = slice(other * span, (other + 1) * span)
                raw = mm(key[theirs], query_t[:, mine])
                prob = jnp.exp(raw + (bias[head * GROUP + part - other] - level))
                prob_grad = mm(value[theirs], grad_t)
                low = (prob * (prob_grad - delta_row)).astype(BF16)
                sums[part - other] += low.astype(F32)
                query_total = query_total + mm(key_t[:, theirs], low)
                key_total[theirs, :] += mm(low, query[mine])
                value_total[theirs, :] += mm(prob.astype(BF16), grad)
            turned[:, mine] = query_total * size ** (-0.5)
        mixed_grad[:, columns] = turned[...].T.astype(BF16)
        mixed_grad[:, key_columns] = key_total[...].astype(BF16)
        mixed_grad[:, value_columns] = value_total[...].astype(BF16)
        for delta in range(GROUP):
            upper = jnp.where(later, sums[delta], 0.0)
            for side, block in enumerate((upper, sums[delta] - upper)):
                start = ((head * GROUP + delta) * 2 + side) * count
                strips[start : start + count, :] = jnp.sum(block.reshape(count, spacing, span), axis=1)
    lane = lax.broadcasted_iota(jnp.int32, (span, count), 0) // spacing
    hot = (lane == lax.broadcasted_iota(jnp.int32, (span, count), 1)).astype(F32)
    table_grad[...] = lax.dot_general(
        strips[...], hot, NN, precision=lax.Precision.HIGHEST, preferred_element_type=F32
    )
    gain_total = jnp.zeros(gain_grad.shape, F32)
    weight_total = jnp.zeros(qkv_grad.shape, F32)
    for part in range(GROUP):
        place = ids[5 + part]
        rows = pl.ds(pl.multiple_of(place * span, span), span)
        values = gathered[rows, :].astype(F32)
        unit = values * inverse_rms(values)
        normed = (unit * gain[...].astype(F32)).astype(BF16)
        lowered = mixed_grad[rows, :]
        weight_total = weight_total + mm(normed, lowered, TN)
        back = mm(lowered, weight[...], NT)
        gain_total = gain_total + jnp.sum(back * unit, axis=0, keepdims=True)
        target = kept if part < 2 else sent
        target[part % 2] = back.astype(BF16)
    qkv_grad[...] = weight_total
    gain_grad[...] = gain_total


def first_norm_grad(kept, arrived, own, gain, middle_grad, wide, low):
    grad = kept[...].astype(F32) + arrived[...].astype(F32)
    back, unused = norm_backward(own[...].astype(F32), gain[...].astype(F32), grad)
    total = middle_grad[...] + back
    wide[...] = total
    low[...] = total.astype(BF16)


FLIP = [(0, 1), (1, 0)]


def flip(block):
    return lax.ppermute(block, "section", FLIP)


def beside(block):
    return lax.ppermute(block, "zlo", FLIP)


def scatter_pairs(turn):
    return [
        (core * 4 + a * 2 + b, b * 4 + (core ^ turn) * 2 + a)
        for core in range(2)
        for a in range(2)
        for b in range(2)
    ]


def to_working(block, turn):
    return lax.ppermute(block, ("section", "zhi", "zlo"), scatter_pairs(turn))


def to_home(block, turn):
    pairs = [(after, before) for before, after in scatter_pairs(turn)]
    return lax.ppermute(block, ("section", "zhi", "zlo"), pairs)


def exchange(block, experts, capacity):
    features = block.shape[-1]
    moved = lax.all_to_all(
        block.reshape(experts, capacity, features), RANKS, split_axis=0, concat_axis=0, tiled=True
    )
    return moved.reshape(experts * capacity, features)


def regroup(block):
    return lax.all_to_all(block, ("zlo", "section"), split_axis=0, concat_axis=0, tiled=True)


def per_device(inputs, cotangent, qkv_shard, out_shard, router_shard, gain_shard, table_shard,
               w_expert_in, w_expert_out, routes):
    core = lax.axis_index("section")
    zhi = lax.axis_index("zhi")
    zlo = lax.axis_index("zlo")
    span, features = inputs.shape[2:]
    ranks = lax.axis_size(RANKS)
    shard_rows = qkv_shard.shape[1]
    experts = router_shard.shape[2]
    table_rows, head_count = table_shard.shape[1:]
    buckets = table_rows * ranks
    heads = head_count // GROUP
    size = features // head_count
    width = heads * size
    spacing = GROUP * span // buckets
    capacity = max(2, 4 * span // experts)
    slots = experts * capacity
    group = 2 * zlo + core
    sizes = (span, heads, size, spacing)
    ids = jnp.stack([
        group, 2 * zlo + 1 - core, 2 * (1 - zlo) + core, 2 * (1 - zlo) + 1 - core, group,
        core, 2 + core, 1 - core, 3 - core,
    ]).astype(jnp.int32)
    core_id = core.astype(jnp.int32).reshape(1)

    own = to_working(lax.dynamic_index_in_dim(inputs, core, 0, keepdims=False)[0], 0)
    given = to_working(lax.dynamic_index_in_dim(cotangent, core, 0, keepdims=False)[0], 0)
    route_parts = [
        to_working(lax.dynamic_index_in_dim(routes[0], core ^ turn, 0, keepdims=False)[0], turn)
        for turn in range(2)
    ]
    section_routes = [
        jnp.where(zhi == section, route_parts[0], route_parts[1]) for section in range(2)
    ]

    small = jnp.concatenate([
        router_shard[0],
        gain_shard[0].T,
        jnp.pad(table_shard[0], ((0, shard_rows - table_rows), (0, 0))),
    ], axis=1)
    small = jnp.pad(small, ((0, 0), (0, -small.shape[1] % 128)))
    packed = jnp.concatenate([qkv_shard[0], out_shard[0], small], axis=1)
    full = lax.all_gather(packed, RANKS, axis=0, tiled=True)
    qkv_full = full[:, : 3 * features].reshape(features, 3, GROUP, width)

    def columns_of(which):
        return lax.dynamic_index_in_dim(qkv_full, which, 2, keepdims=False).reshape(features, 3 * width)

    rest = full[:, 3 * features :]
    mine = (columns_of(group), rest)
    theirs = (flip(columns_of(2 * zlo + 1 - core)), flip(rest))
    w_in = w_expert_in[0, 0]
    w_down = w_expert_out[0, 0]
    w_in_other = flip(w_in)
    w_down_other = flip(w_down)

    weights = []
    for section in range(2):
        is_own = core == section
        qkv = jnp.where(is_own, mine[0], theirs[0])
        others = jnp.where(is_own, mine[1], theirs[1])
        w_out = others[:, :features]
        router = others[:, features : features + experts]
        gains = others[:, features + experts : features + experts + 2].T
        table = others[:, features + experts + 2 : features + experts + 2 + head_count]
        table = table.reshape(ranks, shard_rows, head_count)[:, :table_rows].reshape(buckets, head_count)
        weights.append((
            qkv, w_out, router, gains[0:1], gains[1:2], table,
            jnp.where(is_own, w_in, w_in_other), jnp.where(is_own, w_down, w_down_other),
        ))

    bias_scratch = [
        pltpu.VMEM((-(-head_count // 8) * 8, 2 * span * GROUP), F32),
        pltpu.VMEM((heads * GROUP, span, span), F32),
    ]
    length = GROUP * span
    blocks = span // spacing
    states = []
    results = []
    stream = own
    for section in range(2):
        qkv, w_out, router, gain_one, gain_two, table, expert_in, expert_down = weights[section]
        route_rows = section_routes[section]
        side = beside(stream)
        pieces = (stream, flip(stream), side, flip(side))
        outcome, mixed, gathered, stats = call(
            functools.partial(attention_forward, sizes), "attention_forward",
            [shape((GROUP, span, width), BF16), shape((length, 3 * width), BF16),
             shape((length, features), BF16), shape((8, length), F32)],
            [*pieces, gain_one, qkv, table], scalars=ids,
            scratch=[*bias_scratch, pltpu.VMEM((width, length), F32)], flops=4 << 30,
        )
        attended = regroup(outcome)
        outgoing, middle, normed_two, aux = call(
            functools.partial(after_attention, capacity), "after_attention",
            [shape((slots, features), BF16), shape((span, features), F32),
             shape((span, features), BF16), shape((span, 128), F32)],
            [attended, stream, w_out, gain_two, router, route_rows], flops=1 << 30,
        )
        arrived = exchange(outgoing, experts, capacity)
        activation, slope, produced = run_expert_forward(arrived, expert_in, expert_down)
        returned = exchange(produced, experts, capacity)
        result, difference = call(
            combine, "combine", [shape((span, features), BF16), shape((span, features), F32)],
            [returned, aux, middle], flops=1 << 30,
        )
        states.append((stream, outcome, mixed, gathered, stats, attended, middle, normed_two, aux,
                       arrived, activation, slope, difference))
        results.append(result)
        stream = result

    home = [
        to_home(jnp.where((zhi ^ turn) == 0, results[0], results[1]), turn) for turn in range(2)
    ]
    section_outputs = jnp.stack([
        jnp.where(core == 0, home[0], home[1]), jnp.where(core == 0, home[1], home[0])
    ])

    upstream = given
    small_grads = [None, None]
    qkv_grads = [None, None]
    expert_states = [None, None]
    partials = [None, None]
    stream_grads = [None, None]
    for section in (1, 0):
        qkv, w_out, router, gain_one, gain_two, table, expert_in, expert_down = weights[section]
        (stream, outcome, mixed, gathered, stats, attended, middle, normed_two, aux,
         arrived, activation, slope, difference) = states[section]
        route_rows = section_routes[section]
        (spread,) = call(spread_grads, "spread_grads", [shape((slots, features), BF16)],
                         [upstream, aux], flops=1 << 30)
        arrived_grad = exchange(spread, experts, capacity)
        hidden_grad, rows_grad = run_expert_backward(arrived_grad, expert_in, expert_down, slope)
        returned = exchange(rows_grad, experts, capacity)
        expert_states[section] = (arrived, hidden_grad, activation, arrived_grad)
        wanted = (core != section).astype(jnp.int32).reshape(1)
        partials[section] = [
            lax.ppermute(part, "section", [(1 - section, section)])
            for part in run_weight_partials(wanted, *expert_states[section])
        ]
        middle_grad, attended_grad, out_grad, router_grad, gain_two_grad = call(
            before_attention, "before_attention",
            [shape((span, features), F32), shape((GROUP, span, width), BF16),
             shape((features, features), F32), shape((features, experts), F32), shape((1, features), F32)],
            [returned, aux, upstream, difference, middle, normed_two, attended, gain_two, router, w_out,
             route_rows], flops=2 << 30,
        )
        small_grads[section] = jnp.concatenate([out_grad, router_grad, gain_two_grad.T], axis=1)
        grads = regroup(attended_grad)
        kept, sent, qkv_grad, gain_one_grad, table_grad = call(
            functools.partial(attention_backward, sizes), "attention_backward",
            [shape((2, span, features), BF16), shape((2, span, features), BF16),
             shape((features, 3 * width), F32), shape((1, features), F32), shape((heads * GROUP * 2 * blocks, blocks), F32)],
            [mixed, stats, outcome, grads, gathered, gain_one, qkv, table], scalars=ids,
            scratch=[*bias_scratch, pltpu.VMEM((length, 3 * width), BF16),
                     pltpu.VMEM((GROUP, span, span), F32), pltpu.VMEM((length, size), F32),
                     pltpu.VMEM((length, size), F32), pltpu.VMEM((size, length), F32),
                     pltpu.VMEM((heads * GROUP * 2 * blocks, span), F32)],
            flops=8 << 30,
        )
        pair = kept.astype(F32) + flip(sent).astype(F32)
        stay = lax.dynamic_index_in_dim(pair, zlo, 0, keepdims=False)
        leave = lax.dynamic_index_in_dim(pair, 1 - zlo, 0, keepdims=False).astype(BF16)
        wide, low = call(
            first_norm_grad, "first_norm_grad", [shape((span, features), F32), shape((span, features), BF16)],
            [stay, beside(leave), stream, gain_one, middle_grad],
        )
        table_total = bucket_sums(table_grad.reshape(heads, GROUP, 2, blocks, blocks), buckets)
        per_block = buckets // (ranks // 2)
        block_rows = features // (ranks // 2)
        table_column = jnp.pad(
            table_total.T.reshape(ranks // 2, per_block, heads),
            ((0, 0), (0, block_rows - per_block), (0, 0)),
        ).reshape(features, heads)
        packed_grad = jnp.concatenate([qkv_grad, gain_one_grad.T, table_column], axis=1)
        packed_grad = jnp.pad(packed_grad, ((0, 0), (0, -packed_grad.shape[1] % 128)))
        qkv_grads[section] = packed_grad.astype(BF16)
        stream_grads[section] = low
        upstream = low

    def spread_sum(block, axes, parts):
        rows, columns = block.shape
        moved = lax.all_to_all(
            block.reshape(parts, rows // parts, columns), axes, split_axis=0, concat_axis=0, tiled=True
        )
        return jnp.sum(moved.astype(F32), axis=0)

    def of_core(pair, which):
        return jnp.where(which == 0, pair[0], pair[1])

    shared = of_core(small_grads, core) + flip(of_core(small_grads, 1 - core).astype(BF16)).astype(F32)
    shared = jnp.pad(shared, ((0, 0), (0, -shared.shape[1] % 128))).astype(BF16)
    shared = spread_sum(shared, RANKS, ranks)
    grad_out = shared[:, :features]
    grad_router = shared[:, features : features + experts]
    grad_gain_two = shared[:, features + experts]

    reduced = jnp.stack([spread_sum(block, ("expert", "zhi"), ranks // 2) for block in qkv_grads])
    half = reduced.shape[1] // 2
    columns = reduced.shape[2]
    heads_of = reduced.reshape(2, 2, half, columns)
    gains_part = reduced[:, :, 3 * width].reshape(2, 2, half)
    per_row = buckets // ranks
    table_part = reduced[:, : 2 * per_row, 3 * width + 1 : 3 * width + 1 + heads].reshape(2, 2, per_row, heads)
    heads_of = heads_of.at[:, :, :, 3 * width + 1 :].set(0.0)
    heads_of = heads_of.at[:, :, :per_row, 3 * width + 1 : 3 * width + 1 + heads].set(table_part)
    sending = jnp.transpose(heads_of, (1, 0, 2, 3)).reshape(GROUP, half, columns)
    gathered_grad = regroup(sending)
    split = gathered_grad[:, :, : 3 * width].reshape(GROUP, half, 3, width)
    grad_qkv = jnp.transpose(split, (1, 2, 0, 3)).reshape(half, 3 * features)
    grad_gain_one = jnp.sum(gathered_grad[:, :, 3 * width], axis=0)
    grad_table = jnp.transpose(
        gathered_grad[:, :per_row, 3 * width + 1 : 3 * width + 1 + heads], (1, 0, 2)
    ).reshape(per_row, head_count)
    grad_gains = jnp.stack([grad_gain_one, grad_gain_two])

    home = [
        to_home(jnp.where((zhi ^ turn) == 0, stream_grads[0], stream_grads[1]), turn) for turn in range(2)
    ]
    section_grads = jnp.stack([
        jnp.where(core == 0, home[0], home[1]), jnp.where(core == 0, home[1], home[0])
    ]).astype(F32)

    sent_in = jnp.where(core == 0, partials[0][0], partials[1][0])
    sent_down = jnp.where(core == 0, partials[0][1], partials[1][1])
    grad_in, grad_down = run_weight_totals(core_id, expert_states[0], expert_states[1], sent_in, sent_down)
    return (
        section_outputs[None, :, None],
        section_grads[None, :, None],
        grad_qkv[None],
        grad_out[None],
        grad_router[None],
        grad_gains[None],
        grad_table[None],
        grad_in[None, None],
        grad_down[None, None],
    )


def solution(mesh):
    sections, ranks, pieces = mesh.devices.shape
    work = Mesh(
        mesh.devices.reshape(sections, ranks, pieces // 2, 2), ("section", "expert", "zhi", "zlo")
    )
    piece = ("zhi", "zlo")
    in_specs = (
        P(None, "expert", piece, None),
        P(None, "expert", piece, None),
        P("section", RANKS, None),
        P("section", RANKS, None),
        P("section", RANKS, None),
        P("section", None, RANKS),
        P("section", RANKS, None),
        P("section", RANKS, None, None),
        P("section", RANKS, None, None),
        P("section", None, "expert", piece, None),
    )
    out_specs = (
        P("section", None, "expert", piece, None),
        P("section", None, "expert", piece, None),
        P("section", RANKS, None),
        P("section", RANKS, None),
        P("section", RANKS, None),
        P("section", None, RANKS),
        P("section", RANKS, None),
        P("section", RANKS, None, None),
        P("section", RANKS, None, None),
    )
    return jax.shard_map(per_device, mesh=work, in_specs=in_specs, out_specs=out_specs, check_vma=False)
```

time: 2220 us -> 888 us (0.40)
  matrix products: 673 us -> 29.1 us
  waiting for transfers between devices: 710 us -> 290 us
  local copies, waits for them, and re-layouts: 299 us -> 71.6 us
  Pallas kernels: 0 us -> 206 us
  blocking collectives: 278 us -> 95.8 us
  other arithmetic: 163 us -> 59.3 us
  starting transfers between devices: 54 us -> 112 us
    dot_general x82 -> x2, matrix products: 673 us -> 29.1 us  [bucket_sums(): jnp.einsum('hdskq,dskqb->hb', block_sums, hot, precision=lax.Precision.HI...]
    reduce_scatter x5 -> x0, waiting for transfers between devices: 336 us -> none  [the longest x1 157 us: per_device(): lax.psum_scatter(totals[0], ('expert', 'seq'), scatter_dimension=0, tiled...]
    pallas_call x0 -> x21, Pallas kernels: none -> 206 us  [the longest x14 95.8 us: call(): pl.pallas_call(body, name=name, in_specs=specs, out_specs=[pl.BlockSpec(m...]
    all_gather x3 -> x0, blocking collectives: 158 us -> none  [the longest x1 69 us: per_device(): lax.all_gather(w_router, ('expert', 'seq'), axis=1, tiled=True)]
    all_to_all x10 -> x13, waiting for transfers between devices: 231 us -> 159 us  [the longest x6 147 us: exchange(): lax.all_to_all(block.reshape(experts, capacity, features), RANKS, split_a...]
    slice x41 -> x18, local copies, waits for them, and re-layouts: 68.5 us -> 13.1 us  [the longest x1 4.02 us: per_device(): qkv_full = full[:, :3 * features].reshape(features, 3, GROUP, width)]
    reshape x13 -> x4, local copies, waits for them, and re-layouts: 57.1 us -> 2.08 us  [the longest x1 1.53 us: columns_of(): lax.dynamic_index_in_dim(qkv_full, which, 2, keepdims=False)]
    all_gather x8 -> x1, waiting for transfers between devices: 138 us -> 83.7 us  [per_device(): full = lax.all_gather(packed, RANKS, axis=0, tiled=True)]
  transfers between devices with their start and end apart: 29 -> 41, of which waited for: 17 -> 16; matrix products, arithmetic and copies ran while one was open for 35% -> 16% of each run, Pallas kernels for 0% -> 14%
where the time goes in v1:
time: 888 us; the launch traced here: 878 us
  waiting for transfers between devices  290 us (33%)
  Pallas kernels  206 us (23%)
  starting transfers between devices  112 us (13%)
  blocking collectives  95.8 us (11%)
  local copies, waits for them, and re-layouts  71.6 us (8%)
  other arithmetic  59.3 us (7%)
  matrix products  29.1 us (3%)
  between operations  15 us (2%)
    all_to_all x6, waiting for transfers between devices, exchange(): lax.all_to_all(block.reshape(experts, capacity, features), RANKS, split_a...  147 us
    pallas_call x14, Pallas kernels, call(): pl.pallas_call(body, name=name, in_specs=specs, out_specs=[pl.BlockSpec(m...  95.8 us
    all_to_all x2, blocking collectives, exchange(): lax.all_to_all(block.reshape(experts, capacity, features), RANKS, split_a...  86 us
    all_gather x1, waiting for transfers between devices, per_device(): full = lax.all_gather(packed, RANKS, axis=0, tiled=True)  83.7 us
    ppermute x4, waiting for transfers between devices, beside(): return lax.ppermute(block, 'zlo', FLIP)  41.4 us
    pallas_call x2, Pallas kernels, run_expert_forward(): pl.pallas_call(expert_forward, name='expert_forward', grid=(hidden // til...  34.5 us
    pallas_call x2, Pallas kernels, run_expert_backward(): pl.pallas_call(expert_backward, name='expert_backward', grid=(hidden // t...  33.3 us
    all_to_all x6, starting transfers between devices, exchange(): lax.all_to_all(block.reshape(experts, capacity, features), RANKS, split_a...  32.6 us
  transfers between devices with their start and end apart: 41, of which 16 were waited for; matrix products, arithmetic and copies ran while one was open for 16% of the time, Pallas kernels for 14%

profile of v1, /device:TPU:0, one launch (start us, length us, event | category | flops | bytes accessed | tf_op | source)
XLA Modules:
  0.0 877.8 jit_solution(3638942262416961710)
XLA Ops:
  11.9 83.7 %all-gather.2.cloned.1.call-done = bf16[768,3200]{1,0:T(8,128)(2,1)} async-done(((bf16[48,3200]{1,0:T(8,128)(2,1)}), bf16[768,3200]{1,0:T(8,128)(2,1)}) %all-gather.2.cloned.1.call-update) | async-done | bytes 4915216 | tf_op jit(solution)/shard_map/all_gather | solution.py:584
  115.0 11.3 %collective-permute-start.2 = (bf16[256,768]{1,0:T(8,128)(2,1)S(1)}, bf16[256,768]{1,0:T(8,128)(2,1)}, u32[]{:S(2)}, u32[]{:S(2)}) collective-permute-start(bf16[256,768]{1,0:T(8,128)(2,1)S(1)} %collective-permute-done.own), channel_id=1, source_target_pairs={{0,1},{1,0},{2,3},{3,2},{4,5},{5,4},{6,7},{7,6},{8,9},{9,8},{10,11... | collective-permute-start | bytes 1179656 | tf_op jit(solution)/shard_map/ppermute | solution.py:509
  143.7 8.8 %attention_forward.2 = (bf16[4,256,192]{2,1,0:T(8,128)(2,1)}, bf16[1024,576]{1,0:T(8,128)(2,1)}, bf16[1024,768]{1,0:T(8,128)(2,1)}, f32[8,1024]{1,0:T(8,128)}) custom-call(s32[9]{0:T(128)} %stack.75.ids, bf16[256,768]{1,0:T(8,128)(2,1)} %copy-done.17, bf16[256,768]{1,0:T(8,128)(2,1)} %collective-permute-done.1.flip, ...), custom_call_target="tpu_custom_call" | custom-call | flops 4294967296 | bytes 5639168 | tf_op jit(solution)/shard_map/attention_forward/pallas_call | solution.py:42
  175.8 7.2 all-to-all-start.1
  183.0 8.0 broadcast_select_fusion.1
  191.0 8.0 broadcast_select_fusion
  199.0 23.1 %all-to-all-done.1 = bf16[16,64,768]{2,1,0:T(8,128)(2,1)S(1)} async-done(((bf16[16,64,768]{2,1,0:T(8,128)(2,1)}), bf16[16,64,768]{2,1,0:T(8,128)(2,1)S(1)}, u32[]{:S(2)}, u32[]{:S(2)}) %all-to-all-start.1) | async-done | bytes 1572896 | tf_op jit(solution)/shard_map/all_to_all | solution.py:532
  223.3 17.2 %expert_forward.2 = (bf16[1024,3072]{1,0:T(8,128)(2,1)}, bf16[1024,3072]{1,0:T(8,128)(2,1)}, bf16[1024,768]{1,0:T(8,128)(2,1)}) custom-call(bf16[1024,768]{1,0:T(8,128)(2,1)} %bitcast.133, bf16[768,3072]{1,0:T(8,128)(2,1)} %get-tuple-element.206.w_in, bf16[3072,768]{1,0:T(8,128)(2,1)} %get-tuple-element.204.w_down), custom_call_target="tpu_custom_call" | custom-call | flops 9663676416 | bytes 31457280 | tf_op jit(solution)/shard_map/expert_forward/pallas_call | solution.py:221
  240.5 43.2 %all_to_all.80 = bf16[16,64,768]{2,1,0:T(8,128)(2,1)} all-to-all(bf16[16,64,768]{2,1,0:T(8,128)(2,1)} %bitcast.163), channel_id=1, replica_groups=mesh['section'=2,'expert'=4,'zhi'=2,'zlo'=2] {'expert','zhi','zlo'}, dimensions={0} | all-to-all | bytes 3145728 | tf_op jit(solution)/shard_map/all_to_all | solution.py:532
  287.6 10.0 %collective-permute-done.11.side = bf16[256,768]{1,0:T(8,128)(2,1)S(1)} collective-permute-done((bf16[256,768]{1,0:T(8,128)(2,1)}, bf16[256,768]{1,0:T(8,128)(2,1)S(1)}, u32[]{:S(2)}, u32[]{:S(2)}) %collective-permute-start.11) | collective-permute-done | bytes 393248 | tf_op jit(solution)/shard_map/ppermute | solution.py:509
  300.1 8.8 %attention_forward.3 = (bf16[4,256,192]{2,1,0:T(8,128)(2,1)}, bf16[1024,576]{1,0:T(8,128)(2,1)}, bf16[1024,768]{1,0:T(8,128)(2,1)}, f32[8,1024]{1,0:T(8,128)}) custom-call(s32[9]{0:T(128)} %stack.75.ids, bf16[256,768]{1,0:T(8,128)(2,1)} %get-tuple-element.96.own, bf16[256,768]{1,0:T(8,128)(2,1)} %copy-done.31, bf16[256,768]{1,0:T(8,128)(2,1)} %copy-done.30, ...), custom_call_target="tpu_custom_call" | custom-call | flops 4294967296 | bytes 5639168 | tf_op jit(solution)/shard_map/attention_forward/pallas_call | solution.py:42
  336.2 38.1 %all-to-all-done.4 = bf16[16,64,768]{2,1,0:T(8,128)(2,1)S(1)} async-done(((bf16[16,64,768]{2,1,0:T(8,128)(2,1)}), bf16[16,64,768]{2,1,0:T(8,128)(2,1)S(1)}, u32[]{:S(2)}, u32[]{:S(2)}) %all-to-all-start.4) | async-done | bytes 1572896 | tf_op jit(solution)/shard_map/all_to_all | solution.py:532
  374.2 10.4 %all-to-all-start.6 = ((bf16[16,64,768]{2,1,0:T(8,128)(2,1)}), bf16[16,64,768]{2,1,0:T(8,128)(2,1)}, u32[]{:S(2)}, u32[]{:S(2)}) async-start(bf16[16,64,768]{2,1,0:T(8,128)(2,1)} %bitcast.162), calls=%async_computation.6 | async-start | bytes 3145728 | tf_op jit(solution)/shard_map/all_to_all | solution.py:532
  384.7 17.3 %expert_forward.3 = (bf16[1024,3072]{1,0:T(8,128)(2,1)}, bf16[1024,3072]{1,0:T(8,128)(2,1)}, bf16[1024,768]{1,0:T(8,128)(2,1)}) custom-call(bf16[1024,768]{1,0:T(8,128)(2,1)} %bitcast.136, bf16[768,3072]{1,0:T(8,128)(2,1)} %get-tuple-element.205.w_in, bf16[3072,768]{1,0:T(8,128)(2,1)} %get-tuple-element.203.w_down), custom_call_target="tpu_custom_call" | custom-call | flops 9663676416 | bytes 31457280 | tf_op jit(solution)/shard_map/expert_forward/pallas_call | solution.py:221
  402.0 21.4 %all-to-all-done.6 = bf16[16,64,768]{2,1,0:T(8,128)(2,1)} async-done(((bf16[16,64,768]{2,1,0:T(8,128)(2,1)}), bf16[16,64,768]{2,1,0:T(8,128)(2,1)}, u32[]{:S(2)}, u32[]{:S(2)}) %all-to-all-start.6) | async-done | bytes 1572896 | tf_op jit(solution)/shard_map/all_to_all | solution.py:532
  427.1 16.8 %expert_backward.2 = (bf16[1024,3072]{1,0:T(8,128)(2,1)}, bf16[1024,768]{1,0:T(8,128)(2,1)}) custom-call(bf16[1024,768]{1,0:T(8,128)(2,1)} %bitcast.40.arrived_grad.arrived_grad_1, bf16[768,3072]{1,0:T(8,128)(2,1)} %get-tuple-element.205.w_in, bf16[3072,768]{1,0:T(8,128)(2,1)} %get-tuple-element.203.w_down, bf16[1024,3072]{1,0:T(8,128)(2,1)} %get-tuple-element.107.slope), custom_call_target="tpu_custom_call" | custom-call | flops 9663676416 | bytes 31457280 | tf_op jit(solution)/shard_map/expert_backward/pallas_call | solution.py:248
  443.8 21.4 %all-to-all-done.5 = bf16[16,64,768]{2,1,0:T(8,128)(2,1)S(1)} async-done(((bf16[16,64,768]{2,1,0:T(8,128)(2,1)}), bf16[16,64,768]{2,1,0:T(8,128)(2,1)S(1)}, u32[]{:S(2)}, u32[]{:S(2)}) %all-to-all-start.5) | async-done | bytes 1572896 | tf_op jit(solution)/shard_map/all_to_all | solution.py:532
  473.9 34.5 %all-to-all-done.7 = bf16[16,64,768]{2,1,0:T(8,128)(2,1)S(1)} async-done(((bf16[16,64,768]{2,1,0:T(8,128)(2,1)}), bf16[16,64,768]{2,1,0:T(8,128)(2,1)S(1)}, u32[]{:S(2)}, u32[]{:S(2)}) %all-to-all-start.7) | async-done | bytes 1572896 | tf_op jit(solution)/shard_map/all_to_all | solution.py:532
  509.5 7.7 before_attention.2
  518.5 9.8 %all_to_all.81 = bf16[4,256,192]{1,2,0:T(8,128)(2,1)S(1)} all-to-all(bf16[4,256,192]{1,2,0:T(8,128)(2,1)S(1)} %copy.227), channel_id=1, replica_groups=mesh['section'=2,'expert'=4,'zhi'=2,'zlo'=2] {'zlo','section'}, dimensions={0} | all-to-all | bytes 786432 | tf_op jit(solution)/shard_map/all_to_all | solution.py:539
  529.3 16.5 %attention_backward.2 = (bf16[2,256,768]{2,1,0:T(8,128)(2,1)}, bf16[2,256,768]{2,1,0:T(8,128)(2,1)}, f32[768,576]{1,0:T(8,128)}, f32[1,768]{1,0:T(1,128)}, f32[384,16]{1,0:T(8,128)}) custom-call(s32[9]{0:T(128)} %stack.75.ids, bf16[1024,576]{1,0:T(8,128)(2,1)} %get-tuple-element.105.mixed, f32[8,1024]{1,0:T(8,128)} %get-tuple-element.106.stats, ...), custom_call_target="tpu_custom_call" | custom-call | flops 8589934592 | bytes 7829504 | tf_op jit(solution)/shard_map/attention_backward/pallas_call | solution.py:42
  551.5 9.8 %collective-permute-done.17.arrived = bf16[256,768]{1,0:T(8,128)(2,1)S(1)} collective-permute-done((bf16[256,768]{1,0:T(8,128)(2,1)S(1)}, bf16[256,768]{1,0:T(8,128)(2,1)S(1)}, u32[]{:S(2)}, u32[]{:S(2)}) %collective-permute-start.17) | collective-permute-done | bytes 393248 | tf_op jit(solution)/shard_map/ppermute | solution.py:509
  568.4 42.8 %all_to_all.82 = bf16[16,64,768]{2,1,0:T(8,128)(2,1)} all-to-all(bf16[16,64,768]{2,1,0:T(8,128)(2,1)} %bitcast.165), channel_id=1, replica_groups=mesh['section'=2,'expert'=4,'zhi'=2,'zlo'=2] {'expert','zhi','zlo'}, dimensions={0} | all-to-all | bytes 3145728 | tf_op jit(solution)/shard_map/all_to_all | solution.py:532
  611.2 16.6 %expert_backward.3 = (bf16[1024,3072]{1,0:T(8,128)(2,1)}, bf16[1024,768]{1,0:T(8,128)(2,1)}) custom-call(bf16[1024,768]{1,0:T(8,128)(2,1)} %bitcast.139, bf16[768,3072]{1,0:T(8,128)(2,1)} %get-tuple-element.206.w_in, bf16[3072,768]{1,0:T(8,128)(2,1)} %get-tuple-element.204.w_down, bf16[1024,3072]{1,0:T(8,128)(2,1)} %get-tuple-element.117.slope), custom_call_target="tpu_custom_call" | custom-call | flops 9663676416 | bytes 31457280 | tf_op jit(solution)/shard_map/expert_backward/pallas_call | solution.py:248
  631.6 15.2 %weight_partials.3 = (bf16[768,3072]{1,0:T(8,128)(2,1)}, bf16[3072,768]{1,0:T(8,128)(2,1)}) custom-call(s32[1]{0:T(128)} %bitcast.86.scalars, bf16[1024,768]{1,0:T(8,128)(2,1)} %bitcast.137, bf16[1024,3072]{1,0:T(8,128)(2,1)} %get-tuple-element.141.hidden_grad.hidden_grad_1, bf16[1024,3072]{1,0:T(8,128)(2,1)} %get-tuple-element.142.activation.activation_1, ...), custom_call_target="tpu_custom_call" | custom-call | flops 9663676416 | bytes 31457280 | tf_op jit(solution)/shard_map/weight_partials/pallas_call | solution.py:282
  661.6 8.8 %all-to-all-done.10 = bf16[16,64,768]{2,1,0:T(8,128)(2,1)S(1)} async-done(((bf16[16,64,768]{2,1,0:T(8,128)(2,1)}), bf16[16,64,768]{2,1,0:T(8,128)(2,1)S(1)}, u32[]{:S(2)}, u32[]{:S(2)}) %all-to-all-start.10) | async-done | bytes 1572896 | tf_op jit(solution)/shard_map/all_to_all | solution.py:532
  671.7 7.7 before_attention.3
  688.2 13.9 %fusion.14 = bf16[8,8,3]{1,2,0:T(4,128)(2,1)S(1)} fusion(s32[8,8]{1,0:T(8,128)S(1)} %multiply_add_fusion, s32[4]{0:T(128)S(1)} %iota_multiply_fusion.1, f32[3,4,2,16,16,1]{4,3,2,1,0,5:T(8,128)S(1)} %bitcast.188), kind=kOutput, calls=%fused_computation.33 | convolution fusion | flops 5243072 | bytes 25232 | tf_op jit(solution)/shard_map/hdskq,dskqb->hb/dot_general | solution.py:383
  725.9 16.5 %attention_backward.3 = (bf16[2,256,768]{2,1,0:T(8,128)(2,1)}, bf16[2,256,768]{2,1,0:T(8,128)(2,1)}, f32[768,576]{1,0:T(8,128)}, f32[1,768]{1,0:T(1,128)}, f32[384,16]{1,0:T(8,128)}) custom-call(s32[9]{0:T(128)} %stack.75.ids, bf16[1024,576]{1,0:T(8,128)(2,1)} %get-tuple-element.103.mixed, f32[8,1024]{1,0:T(8,128)} %get-tuple-element.104.stats, ...), custom_call_target="tpu_custom_call" | custom-call | flops 8589934592 | bytes 7829504 | tf_op jit(solution)/shard_map/attention_backward/pallas_call | solution.py:42
  742.4 15.2 %fusion.15 = bf16[8,8,3]{1,2,0:T(4,128)(2,1)S(1)} fusion(s32[8,8]{1,0:T(8,128)S(1)} %multiply_add_fusion, s32[4]{0:T(128)S(1)} %iota_multiply_fusion.1, f32[3,4,2,16,16,1]{4,3,2,1,0,5:T(8,128)} %bitcast.189), kind=kOutput, calls=%fused_computation.34 | convolution fusion | flops 5243072 | bytes 25232 | tf_op jit(solution)/shard_map/hdskq,dskqb->hb/dot_general | solution.py:383
  782.2 16.6 %collective-permute-done.19.arrived = bf16[256,768]{1,0:T(8,128)(2,1)S(1)} collective-permute-done((bf16[256,768]{1,0:T(8,128)(2,1)S(1)}, bf16[256,768]{1,0:T(8,128)(2,1)S(1)}, u32[]{:S(2)}, u32[]{:S(2)}) %collective-permute-start.19) | collective-permute-done | bytes 393248 | tf_op jit(solution)/shard_map/ppermute | solution.py:509
  839.1 22.4 %weight_totals.1 = (f32[768,3072]{1,0:T(8,128)}, f32[3072,768]{1,0:T(8,128)}) custom-call(s32[1]{0:T(128)} %bitcast.4.scalars, bf16[1024,768]{1,0:T(8,128)(2,1)} %bitcast.135, bf16[1024,3072]{1,0:T(8,128)(2,1)} %get-tuple-element.139.hidden_grad, bf16[1024,3072]{1,0:T(8,128)(2,1)} %get-tuple-element.140.activation, bf16[1024,768]{1,0:T(8,128)(2,1)} %bitcast.141, ...), custom_call_target="tpu_custom_call" | custom-call | flops 9663676416 | bytes 62914560 | tf_op jit(solution)/shard_map/weight_totals/pallas_call | solution.py:341
  (253 shorter events, 254.0 us)
Async XLA Ops:
  7.2 88.4 %all-gather.2.cloned.1.call-start = ((), (), s32[]{:S(2)}) async-start(), calls=%async_computation.16 | async-start | bytes 5222400 | tf_op jit(solution)/shard_map/all_gather | solution.py:584
  11.3 171.6 %collective-permute-start.8 = (bf16[768,3072]{1,0:T(8,128)(2,1)}, bf16[768,3072]{1,0:T(8,128)(2,1)}, u32[]{:S(2)}, u32[]{:S(2)}) collective-permute-start(bf16[768,3072]{1,0:T(8,128)(2,1)} %bitcast.142), channel_id=1, source_target_pairs={{0,16},{16,0},{1,17},{17,1},{2,18},{18,2},{3,19},{19,3},{4,20},{20... | collective-permute-start | bytes 14155784 | tf_op jit(solution)/shard_map/ppermute | solution.py:505
  97.8 41.1 %collective-permute-start.4 = (bf16[768,896]{0,1:T(8,128)(2,1)S(1)}, bf16[768,896]{0,1:T(8,128)(2,1)}, u32[]{:S(2)}, u32[]{:S(2)}) collective-permute-start(bf16[768,896]{0,1:T(8,128)(2,1)S(1)} %copy.260), channel_id=1, source_target_pairs={{0,16},{16,0},{1,17},{17,1},{2,18},{18,2},{3,19},{19,3},{4,20},{20... | collective-permute-start | bytes 4128776 | tf_op jit(solution)/shard_map/ppermute | solution.py:505
  110.4 23.1 %collective-permute-start.5 = (bf16[768,576]{0,1:T(8,128)(2,1)}, bf16[768,576]{0,1:T(8,128)(2,1)}, u32[]{:S(2)}, u32[]{:S(2)}) collective-permute-start(bf16[768,576]{0,1:T(8,128)(2,1)} %bitcast.18), channel_id=1, source_target_pairs={{0,16},{16,0},{1,17},{17,1},{2,18},{18,2},{3,19},{19,3},{4,20},{20... | collective-permute-start | bytes 2654216 | tf_op jit(solution)/shard_map/ppermute | solution.py:505
  111.6 79.4 %collective-permute-start.9 = (bf16[3072,768]{1,0:T(8,128)(2,1)}, bf16[3072,768]{1,0:T(8,128)(2,1)}, u32[]{:S(2)}, u32[]{:S(2)}) collective-permute-start(bf16[3072,768]{1,0:T(8,128)(2,1)} %bitcast.143), channel_id=1, source_target_pairs={{0,16},{16,0},{1,17},{17,1},{2,18},{18,2},{3,19},{19,3},{4,20},{20... | collective-permute-start | bytes 14155784 | tf_op jit(solution)/shard_map/ppermute | solution.py:505
  115.0 18.4 %collective-permute-start.2 = (bf16[256,768]{1,0:T(8,128)(2,1)S(1)}, bf16[256,768]{1,0:T(8,128)(2,1)}, u32[]{:S(2)}, u32[]{:S(2)}) collective-permute-start(bf16[256,768]{1,0:T(8,128)(2,1)S(1)} %collective-permute-done.own), channel_id=1, source_target_pairs={{0,1},{1,0},{2,3},{3,2},{4,5},{5,4},{6,7},{7,6},{8,9},{9,8},{10,11... | collective-permute-start | bytes 1179656 | tf_op jit(solution)/shard_map/ppermute | solution.py:509
  154.7 15.4 %all-to-all-start = ((bf16[4,256,192]{1,2,0:T(8,128)(2,1)}), bf16[4,256,192]{1,2,0:T(8,128)(2,1)S(1)}, u32[]{:S(2)}, u32[]{:S(2)}) async-start(bf16[4,256,192]{1,2,0:T(8,128)(2,1)} %copy.211), calls=%async_computation | async-start | bytes 786432 | tf_op jit(solution)/shard_map/all_to_all | solution.py:539
  175.8 46.3 %all-to-all-start.1 = ((bf16[16,64,768]{2,1,0:T(8,128)(2,1)}), bf16[16,64,768]{2,1,0:T(8,128)(2,1)S(1)}, u32[]{:S(2)}, u32[]{:S(2)}) async-start(bf16[16,64,768]{2,1,0:T(8,128)(2,1)} %bitcast.157), calls=%async_computation.1 | async-start | bytes 3145728 | tf_op jit(solution)/shard_map/all_to_all | solution.py:532
  287.6 11.6 %collective-permute-start.10 = (bf16[256,768]{1,0:T(8,128)(2,1)}, bf16[256,768]{1,0:T(8,128)(2,1)S(1)}, u32[]{:S(2)}, u32[]{:S(2)}) collective-permute-start(bf16[256,768]{1,0:T(8,128)(2,1)} %get-tuple-element.96.own), channel_id=1, source_target_pairs={{0,16},{16,0},{1,17},{17,1},{2,18},{18,2},{3,19},{19,3},{4,20},{20... | collective-permute-start | bytes 1179656 | tf_op jit(solution)/shard_map/ppermute | solution.py:505
  310.9 10.8 %all-to-all-start.3 = ((bf16[4,256,192]{1,2,0:T(8,128)(2,1)}), bf16[4,256,192]{1,2,0:T(8,128)(2,1)S(1)}, u32[]{:S(2)}, u32[]{:S(2)}) async-start(bf16[4,256,192]{1,2,0:T(8,128)(2,1)} %copy.220), calls=%async_computation.3 | async-start | bytes 786432 | tf_op jit(solution)/shard_map/all_to_all | solution.py:539
  327.5 46.7 %all-to-all-start.4 = ((bf16[16,64,768]{2,1,0:T(8,128)(2,1)}), bf16[16,64,768]{2,1,0:T(8,128)(2,1)S(1)}, u32[]{:S(2)}, u32[]{:S(2)}) async-start(bf16[16,64,768]{2,1,0:T(8,128)(2,1)} %bitcast.159), calls=%async_computation.4 | async-start | bytes 3145728 | tf_op jit(solution)/shard_map/all_to_all | solution.py:532
  374.2 49.1 %all-to-all-start.6 = ((bf16[16,64,768]{2,1,0:T(8,128)(2,1)}), bf16[16,64,768]{2,1,0:T(8,128)(2,1)}, u32[]{:S(2)}, u32[]{:S(2)}) async-start(bf16[16,64,768]{2,1,0:T(8,128)(2,1)} %bitcast.162), calls=%async_computation.6 | async-start | bytes 3145728 | tf_op jit(solution)/shard_map/all_to_all | solution.py:532
  423.4 41.9 %all-to-all-start.5 = ((bf16[16,64,768]{2,1,0:T(8,128)(2,1)}), bf16[16,64,768]{2,1,0:T(8,128)(2,1)S(1)}, u32[]{:S(2)}, u32[]{:S(2)}) async-start(bf16[16,64,768]{2,1,0:T(8,128)(2,1)} %bitcast.161), calls=%async_computation.5 | async-start | bytes 3145728 | tf_op jit(solution)/shard_map/all_to_all | solution.py:532
  466.4 41.9 %all-to-all-start.7 = ((bf16[16,64,768]{2,1,0:T(8,128)(2,1)}), bf16[16,64,768]{2,1,0:T(8,128)(2,1)S(1)}, u32[]{:S(2)}, u32[]{:S(2)}) async-start(bf16[16,64,768]{2,1,0:T(8,128)(2,1)} %bitcast.160), calls=%async_computation.7 | async-start | bytes 3145728 | tf_op jit(solution)/shard_map/all_to_all | solution.py:532
  550.1 11.2 %collective-permute-start.17 = (bf16[256,768]{1,0:T(8,128)(2,1)S(1)}, bf16[256,768]{1,0:T(8,128)(2,1)S(1)}, u32[]{:S(2)}, u32[]{:S(2)}) collective-permute-start(bf16[256,768]{1,0:T(8,128)(2,1)S(1)} %fusion.21), channel_id=1, source_target_pairs={{0,1},{1,0},{2,3},{3,2},{4,5},{5,4},{6,7},{7,6},{8,9},{9,8},{10,11... | collective-permute-start | bytes 1179656 | tf_op jit(solution)/shard_map/ppermute | solution.py:509
  627.8 42.7 %all-to-all-start.10 = ((bf16[16,64,768]{2,1,0:T(8,128)(2,1)}), bf16[16,64,768]{2,1,0:T(8,128)(2,1)S(1)}, u32[]{:S(2)}, u32[]{:S(2)}) async-start(bf16[16,64,768]{2,1,0:T(8,128)(2,1)} %bitcast.155), calls=%async_computation.10 | async-start | bytes 3145728 | tf_op jit(solution)/shard_map/all_to_all | solution.py:532
  646.8 170.8 %collective-permute-start.24 = (bf16[768,3072]{1,0:T(8,128)(2,1)}, bf16[768,3072]{1,0:T(8,128)(2,1)}, u32[]{:S(2)}, u32[]{:S(2)}) collective-permute-start(bf16[768,3072]{1,0:T(8,128)(2,1)} %get-tuple-element.144), channel_id=1, source_target_pairs={{0,16},{1,17},{2,18},{3,19},{4,20},{5,21},{6,22},{7,23},{8,24},{9,... | collective-permute-start | bytes 14155784 | tf_op jit(solution)/shard_map/ppermute | solution.py:679
  651.2 69.2 %collective-permute-start.13 = (bf16[256,768]{1,0:T(8,128)(2,1)}, bf16[256,768]{1,0:T(8,128)(2,1)}, u32[]{:S(2)}, u32[]{:S(2)}) collective-permute-start(bf16[256,768]{1,0:T(8,128)(2,1)} %get-tuple-element.219), channel_id=1, source_target_pairs={{0,0},{16,1},{1,2},{17,3},{2,16},{18,17},{3,18},{19,19},{4,4},{20,... | collective-permute-start | bytes 1179656 | tf_op jit(solution)/shard_map/ppermute | solution.py:527
  655.7 68.7 %collective-permute-start.14 = (bf16[256,768]{1,0:T(8,128)(2,1)}, bf16[256,768]{1,0:T(8,128)(2,1)}, u32[]{:S(2)}, u32[]{:S(2)}) collective-permute-start(bf16[256,768]{1,0:T(8,128)(2,1)} %get-tuple-element.220), channel_id=1, source_target_pairs={{2,0},{18,1},{3,2},{19,3},{0,16},{16,17},{1,18},{17,19},{6,4},{22,... | collective-permute-start | bytes 1179656 | tf_op jit(solution)/shard_map/ppermute | solution.py:527
  660.2 157.9 %collective-permute-start.23 = (bf16[768,3072]{1,0:T(8,128)(2,1)}, bf16[768,3072]{1,0:T(8,128)(2,1)}, u32[]{:S(2)}, u32[]{:S(2)}) collective-permute-start(bf16[768,3072]{1,0:T(8,128)(2,1)} %get-tuple-element.143), channel_id=1, source_target_pairs={{16,0},{17,1},{18,2},{19,3},{20,4},{21,5},{22,6},{23,7},{24,8},{25... | collective-permute-start | bytes 14155784 | tf_op jit(solution)/shard_map/ppermute | solution.py:679
  681.4 22.6 %all-to-all-start.11 = ((bf16[4,256,192]{1,2,0:T(8,128)(2,1)}), bf16[4,256,192]{1,2,0:T(8,128)(2,1)}, u32[]{:S(2)}, u32[]{:S(2)}) async-start(bf16[4,256,192]{1,2,0:T(8,128)(2,1)} %copy.232), calls=%async_computation.11 | async-start | bytes 786432 | tf_op jit(solution)/shard_map/all_to_all | solution.py:539
  704.0 60.2 %all-to-all-start.13 = ((bf16[8,96,640]{2,1,0:T(8,128)(2,1)}), bf16[8,96,640]{2,1,0:T(8,128)(2,1)}, u32[]{:S(2)}, u32[]{:S(2)}) async-start(bf16[8,96,640]{2,1,0:T(8,128)(2,1)} %bitcast.144), calls=%async_computation.13 | async-start | bytes 1966080 | tf_op jit(solution)/shard_map/all_to_all | solution.py:724
  714.2 43.4 %collective-permute-start.22 = (bf16[768,785]{0,1:T(8,128)(2,1)}, bf16[768,785]{0,1:T(8,128)(2,1)}, u32[]{:S(2)}, u32[]{:S(2)}) collective-permute-start(bf16[768,785]{0,1:T(8,128)(2,1)} %copy.246), channel_id=1, source_target_pairs={{0,16},{16,0},{1,17},{17,1},{2,18},{18,2},{3,19},{19,3},{4,20},{20... | collective-permute-start | bytes 3617288 | tf_op jit(solution)/shard_map/ppermute | solution.py:505
  720.4 113.7 %collective-permute-start.26 = (bf16[3072,768]{1,0:T(8,128)(2,1)}, bf16[3072,768]{1,0:T(8,128)(2,1)}, u32[]{:S(2)}, u32[]{:S(2)}) collective-permute-start(bf16[3072,768]{1,0:T(8,128)(2,1)} %get-tuple-element.146), channel_id=1, source_target_pairs={{0,16},{1,17},{2,18},{3,19},{4,20},{5,21},{6,22},{7,23},{8,24},{9,... | collective-permute-start | bytes 14155784 | tf_op jit(solution)/shard_map/ppermute | solution.py:679
  724.4 109.7 %collective-permute-start.25 = (bf16[3072,768]{1,0:T(8,128)(2,1)}, bf16[3072,768]{1,0:T(8,128)(2,1)}, u32[]{:S(2)}, u32[]{:S(2)}) collective-permute-start(bf16[3072,768]{1,0:T(8,128)(2,1)} %get-tuple-element.145), channel_id=1, source_target_pairs={{16,0},{17,1},{18,2},{19,3},{20,4},{21,5},{22,6},{23,7},{24,8},{25... | collective-permute-start | bytes 14155784 | tf_op jit(solution)/shard_map/ppermute | solution.py:679
  757.6 18.2 %collective-permute-start.18 = (bf16[2,256,768]{2,1,0:T(8,128)(2,1)}, bf16[2,256,768]{2,1,0:T(8,128)(2,1)}, u32[]{:S(2)}, u32[]{:S(2)}) collective-permute-start(bf16[2,256,768]{2,1,0:T(8,128)(2,1)} %get-tuple-element.124), channel_id=1, source_target_pairs={{0,16},{16,0},{1,17},{17,1},{2,18},{18,2},{3,19},{19,3},{4,20},{20... | collective-permute-start | bytes 2359304 | tf_op jit(solution)/shard_map/ppermute | solution.py:505
  764.2 41.9 %all-to-all-start.12 = ((bf16[8,96,640]{2,1,0:T(8,128)(2,1)}), bf16[8,96,640]{2,1,0:T(8,128)(2,1)}, u32[]{:S(2)}, u32[]{:S(2)}) async-start(bf16[8,96,640]{2,1,0:T(8,128)(2,1)} %bitcast.145), calls=%async_computation.12 | async-start | bytes 1966080 | tf_op jit(solution)/shard_map/all_to_all | solution.py:724
  777.5 21.3 %collective-permute-start.19 = (bf16[256,768]{1,0:T(8,128)(2,1)S(1)}, bf16[256,768]{1,0:T(8,128)(2,1)S(1)}, u32[]{:S(2)}, u32[]{:S(2)}) collective-permute-start(bf16[256,768]{1,0:T(8,128)(2,1)S(1)} %fusion.22), channel_id=1, source_target_pairs={{0,1},{1,0},{2,3},{3,2},{4,5},{5,4},{6,7},{7,6},{8,9},{9,8},{10,11... | collective-permute-start | bytes 1179656 | tf_op jit(solution)/shard_map/ppermute | solution.py:509
  804.4 57.0 %collective-permute-start.20 = (bf16[256,768]{1,0:T(8,128)(2,1)}, bf16[256,768]{1,0:T(8,128)(2,1)S(1)}, u32[]{:S(2)}, u32[]{:S(2)}) collective-permute-start(bf16[256,768]{1,0:T(8,128)(2,1)} %get-tuple-element.215), channel_id=1, source_target_pairs={{0,0},{16,1},{1,2},{17,3},{2,16},{18,17},{3,18},{19,19},{4,4},{20,... | collective-permute-start | bytes 1179656 | tf_op jit(solution)/shard_map/ppermute | solution.py:527
  814.1 15.8 %all-to-all-start.14 = ((f32[4,48,640]{2,1,0:T(8,128)}), f32[4,48,640]{2,1,0:T(8,128)S(1)}, u32[]{:S(2)}, u32[]{:S(2)}) async-start(f32[4,48,640]{2,1,0:T(8,128)} %bitcast.75), calls=%async_computation.14 | async-start | bytes 983040 | tf_op jit(solution)/shard_map/all_to_all | solution.py:539
  817.6 43.9 %collective-permute-start.21 = (bf16[256,768]{1,0:T(8,128)(2,1)S(1)}, bf16[256,768]{1,0:T(8,128)(2,1)}, u32[]{:S(2)}, u32[]{:S(2)}) collective-permute-start(bf16[256,768]{1,0:T(8,128)(2,1)S(1)} %get-tuple-element.216), channel_id=1, source_target_pairs={{2,0},{18,1},{3,2},{19,3},{0,16},{16,17},{1,18},{17,19},{6,4},{22,... | collective-permute-start | bytes 1179656 | tf_op jit(solution)/shard_map/ppermute | solution.py:527
  829.9 38.6 %all-to-all-start.15 = ((bf16[16,48,896]{2,1,0:T(8,128)(2,1)}), bf16[16,48,896]{2,1,0:T(8,128)(2,1)S(1)}, u32[]{:S(2)}, u32[]{:S(2)}) async-start(bf16[16,48,896]{2,1,0:T(8,128)(2,1)} %bitcast.79), calls=%async_computation.15 | async-start | bytes 2752512 | tf_op jit(solution)/shard_map/all_to_all | solution.py:724
  (44 other events, 440.5 us)
Sparse Core Ops, SparseCore 0:
  11.5 84.0 all-gather.1

commit v2 on v1

--- a/solution.py
+++ b/solution.py
@@ -34,11 +34,20 @@
     return pl.BlockSpec(array.shape, lambda *unused: (0,) * rank)
 
 
-def call(body, name, outs, args, scalars=None, scratch=(), flops=0):
-    specs = [pl.BlockSpec(memory_space=pltpu.SMEM)] if scalars is not None else []
+def ordered(body, skipped):
+    def inner(*refs):
+        return body(*refs[skipped:])
+
+    return inner if skipped else body
+
+
+def call(body, name, outs, args, scalars=None, scratch=(), flops=0, after=()):
+    specs = [pl.BlockSpec(memory_space=pl.ANY)] * len(after)
+    specs += [pl.BlockSpec(memory_space=pltpu.SMEM)] if scalars is not None else []
     specs += [pl.BlockSpec(memory_space=pltpu.VMEM)] * len(args)
-    operands = ([scalars] if scalars is not None else []) + list(args)
+    operands = list(after) + ([scalars] if scalars is not None else []) + list(args)
     moved = sum(a.size * a.dtype.itemsize for a in list(args) + list(outs))
+    body = ordered(body, len(after))
     return pl.pallas_call(
         body,
         name=name,
@@ -82,8 +91,8 @@
 
 
 def attention_forward(sizes, ids, own, flip, side, side_flip, gain, weight, table,
-                      out, mixed, gathered, stats, vectors, bias, turned):
-    span, heads, size, spacing = sizes
+                      out, mixed, gathered, stats, vectors, bias):
+    span, heads, size, spacing, unused = sizes
     width = heads * size
     fill_bias(ids[4] * heads, heads, table, vectors, bias, span, spacing)
     for slot, piece in enumerate((own, flip, side, side_flip)):
@@ -92,7 +101,7 @@
         rows = slice(part * span, (part + 1) * span)
         values = gathered[rows, :].astype(F32)
         normed = (values * inverse_rms(values) * gain[...].astype(F32)).astype(BF16)
-        mixed[rows, :] = mm(normed, weight[...]).astype(BF16)
+        mixed[rows, :] = mm(normed, weight[:, : 3 * width]).astype(BF16)
     for head in range(heads):
         columns = slice(head * size, (head + 1) * size)
         query_t = (mixed[:, columns].astype(F32) * size ** (-0.5)).T.astype(BF16)
@@ -111,11 +120,8 @@
                 raised = jnp.exp(block - top)
                 total = total + jnp.sum(raised, axis=0, keepdims=True)
                 gained = gained + mm(value_t[:, other * span : (other + 1) * span], raised.astype(BF16))
-            turned[columns, mine] = gained / total
+            out[part, columns, :] = (gained / total).astype(BF16)
             stats[head : head + 1, mine] = top + jnp.log(total)
-    for part in range(GROUP):
-        mine = slice(part * span, (part + 1) * span)
-        out[part] = turned[:, mine].T.astype(BF16)
 
 
 def route_masks(routes, experts):
@@ -138,10 +144,10 @@
     tokens = own.shape[0]
     experts = router.shape[1]
     slots = experts * capacity
-    width = attended.shape[2]
+    width = attended.shape[1]
     total = own[...].astype(F32)
     for group in range(GROUP):
-        total = total + mm(attended[group], w_out[group * width : (group + 1) * width, :])
+        total = total + mm(attended[group], w_out[group * width : (group + 1) * width, :], TN)
     middle[...] = total
     normed = (total * inverse_rms(total) * gain[...].astype(F32)).astype(BF16)
     normed_two[...] = normed
@@ -304,55 +310,50 @@
     )(wanted, rows, hidden_grad, activation, arrived_grad)
 
 
-def weight_totals(scalars, rows, hidden_grad, activation, arrived_grad,
-                  rows_1, hidden_grad_1, activation_1, arrived_grad_1,
-                  sent_in, sent_down, grad_in, grad_down):
-    def build(left, right, left_down, right_down):
-        grad_in[...] = mm(left[...], right[...], TN) + sent_in[...].astype(F32)
-        grad_down[...] = mm(left_down[...], right_down[...], TN) + sent_down[...].astype(F32)
-
+def weight_totals(scalars, left, right, sent, left_1, right_1, sent_1, after, total):
     @pl.when(scalars[0] == 0)
     def first():
-        build(rows, hidden_grad, activation, arrived_grad)
+        total[...] = mm(left[...], right[...], TN) + sent[...].astype(F32)
 
     @pl.when(scalars[0] == 1)
     def second():
-        build(rows_1, hidden_grad_1, activation_1, arrived_grad_1)
-
-
-def run_weight_totals(core, first, second, sent_in, sent_down):
-    count, features = first[0].shape
-    hidden = first[1].shape[1]
-    tile = tile_of(hidden) // 2
-
-    def operand_specs(which):
-        def column(j, s):
-            return (0, jnp.where(s[0] == which, j, 0))
-
-        return [
-            pl.BlockSpec((count, features), lambda j, s: (0, 0)),
-            pl.BlockSpec((count, tile), column),
-            pl.BlockSpec((count, tile), column),
-            pl.BlockSpec((count, features), lambda j, s: (0, 0)),
-        ]
-
-    across = pl.BlockSpec((features, tile), lambda j, s: (0, j))
-    down = pl.BlockSpec((tile, features), lambda j, s: (j, 0))
+        total[...] = mm(left_1[...], right_1[...], TN) + sent_1[...].astype(F32)
+
+
+def run_weight_totals(core, first, second, tiled_left, after):
+    count, features = first[1 if tiled_left else 0].shape
+    hidden = first[0 if tiled_left else 1].shape[1]
+    tile = tile_of(hidden)
+
+    def specs(which):
+        def step(j, s):
+            return jnp.where(s[0] == which, j, 0)
+
+        full = pl.BlockSpec((count, features), lambda j, s: (0, 0))
+        part = pl.BlockSpec((count, tile), lambda j, s: (0, step(j, s)))
+        if tiled_left:
+            return [part, full, pl.BlockSpec((tile, features), lambda j, s: (step(j, s), 0))]
+        return [full, part, pl.BlockSpec((features, tile), lambda j, s: (0, step(j, s)))]
+
+    if tiled_left:
+        out_spec = pl.BlockSpec((tile, features), lambda j, s: (j, 0))
+        dims = (hidden, features)
+    else:
+        out_spec = pl.BlockSpec((features, tile), lambda j, s: (0, j))
+        dims = (features, hidden)
     return pl.pallas_call(
         weight_totals,
         name="weight_totals",
         grid_spec=pltpu.PrefetchScalarGridSpec(
-            num_scalar_prefetch=1,
-            grid=(hidden // tile,),
-            in_specs=operand_specs(0) + operand_specs(1) + [across, down],
-            out_specs=[across, down],
+            num_scalar_prefetch=1, grid=(hidden // tile,),
+            in_specs=specs(0) + specs(1) + [pl.BlockSpec(memory_space=pl.ANY)], out_specs=out_spec,
         ),
-        out_shape=[shape((features, hidden), F32), shape((hidden, features), F32)],
+        out_shape=shape(dims, F32),
         compiler_params=pltpu.CompilerParams(vmem_limit_bytes=VMEM_LIMIT),
         cost_estimate=pl.CostEstimate(
-            flops=4 * count * features * hidden, bytes_accessed=60 << 20, transcendentals=0
+            flops=2 * count * features * hidden, bytes_accessed=30 << 20, transcendentals=0
         ),
-    )(core, *first, *second, sent_in, sent_down)
+    )(core, *first, *second, after)
 
 
 def combine(returned, aux, middle, result, difference):
@@ -375,14 +376,6 @@
     outgoing[...] = total.astype(BF16)
 
 
-def bucket_sums(block_sums, buckets):
-    heads, deltas, sides, count, unused = block_sums.shape
-    dims = (deltas, sides, count, count, buckets)
-    delta, side, key, query, bucket = [lax.broadcasted_iota(jnp.int32, dims, axis) for axis in range(5)]
-    hot = (delta * count + query - key - side == bucket).astype(F32)
-    return jnp.einsum("hdskq,dskqb->hb", block_sums, hot, precision=lax.Precision.HIGHEST)
-
-
 def norm_backward(values, gain, grad):
     scale = inverse_rms(values)
     unit = values * scale
@@ -392,10 +385,11 @@
 
 
 def before_attention(returned, aux, upstream, difference, middle, normed_two, attended, gain,
-                     router, w_out, routes, middle_grad, attended_grad, out_grad, router_grad, gain_grad):
+                     router, w_out, routes, middle_grad, attended_grad, shared_grad):
     slots = returned.shape[0]
     experts = router.shape[1]
-    width = attended.shape[2]
+    width = attended.shape[1]
+    features = w_out.shape[1]
     packed = aux[...]
     hot = pick_rows(packed[:, 0:1], slots) + pick_rows(packed[:, 1:2], slots)
     token_grad = mm(hot, returned[...])
@@ -403,28 +397,36 @@
     shift = jnp.sum(flow * difference[...], axis=1, keepdims=True) * packed[:, 2:3] * packed[:, 3:4]
     masks = route_masks(routes, experts)
     logits_grad = (shift * (masks[0] - masks[1])).astype(BF16)
-    router_grad[...] = mm(normed_two[...], logits_grad, TN)
     token_grad = token_grad + mm(logits_grad, router[...], NT)
     back, gain_part = norm_backward(middle[...], gain[...].astype(F32), token_grad)
-    gain_grad[...] = gain_part
     total = flow + back
     middle_grad[...] = total
     branch = total.astype(BF16)
     for group in range(GROUP):
         mine = slice(group * width, (group + 1) * width)
-        out_grad[mine, :] = mm(attended[group], branch, TN)
-        attended_grad[group] = mm(branch, w_out[mine, :], NT).astype(BF16)
+        shared_grad[mine, :features] = mm(attended[group], branch).astype(BF16)
+        attended_grad[group] = mm(w_out[mine, :], branch, NT).astype(BF16)
+    tail = shared_grad.shape[1] - features
+    gain_column = jnp.broadcast_to(gain_part, (8, features)).T
+    lane = lax.broadcasted_iota(jnp.int32, (features, tail), 1)
+    shared_grad[:, features:] = jnp.where(lane == experts, gain_column[:, 0:1], 0.0).astype(BF16)
+    shared_grad[:, features : features + experts] = mm(normed_two[...], logits_grad, TN).astype(BF16)
 
 
 def attention_backward(sizes, ids, mixed, stats, attended, grads, gathered, gain, weight, table,
-                       kept, sent, qkv_grad, gain_grad, table_grad,
+                       stay, leave, sent, shared_grad,
                        vectors, bias, mixed_grad, sums, key_total, value_total, turned, strips):
-    span, heads, size, spacing = sizes
+    span, heads, size, spacing, ranks = sizes
     width = heads * size
     count = span // spacing
+    buckets = table.shape[0]
+    features = weight.shape[0]
     row = lax.broadcasted_iota(jnp.int32, (span, span), 0)
     column = lax.broadcasted_iota(jnp.int32, (span, span), 1)
     later = (column % spacing) >= (row % spacing)
+    lane = lax.broadcasted_iota(jnp.int32, (span, 128), 0) // spacing
+    backwards = (count - 1 - lane == lax.broadcasted_iota(jnp.int32, (span, 128), 1)).astype(F32)
+    strips[...] = jnp.zeros_like(strips)
     fill_bias(ids[4] * heads, heads, table, vectors, bias, span, spacing)
     for head in range(heads):
         columns = slice(head * size, (head + 1) * size)
@@ -440,12 +442,10 @@
         sums[...] = jnp.zeros_like(sums)
         for part in range(GROUP):
             mine = slice(part * span, (part + 1) * span)
-            grad = grads[part, :, columns]
-            grad_wide = grad.astype(F32)
-            grad_t = grad_wide.T
-            outcome_t = attended[part, :, columns].astype(F32).T
-            delta_row = jnp.sum(grad_t * outcome_t, axis=0, keepdims=True)
-            grad_t = grad_t.astype(BF16)
+            grad_t = grads[part, columns, :]
+            delta_row = jnp.sum(
+                grad_t.astype(F32) * attended[part, columns, :].astype(F32), axis=0, keepdims=True
+            )
             level = stats[head : head + 1, mine]
             query_total = jnp.zeros((size, span), F32)
             for other in range(part + 1):
@@ -457,7 +457,7 @@
                 sums[part - other] += low.astype(F32)
                 query_total = query_total + mm(key_t[:, theirs], low)
                 key_total[theirs, :] += mm(low, query[mine])
-                value_total[theirs, :] += mm(prob.astype(BF16), grad)
+                value_total[theirs, :] += mm(prob.astype(BF16), grad_t, NT)
             turned[:, mine] = query_total * size ** (-0.5)
         mixed_grad[:, columns] = turned[...].T.astype(BF16)
         mixed_grad[:, key_columns] = key_total[...].astype(BF16)
@@ -465,15 +465,21 @@
         for delta in range(GROUP):
             upper = jnp.where(later, sums[delta], 0.0)
             for side, block in enumerate((upper, sums[delta] - upper)):
-                start = ((head * GROUP + delta) * 2 + side) * count
-                strips[start : start + count, :] = jnp.sum(block.reshape(count, spacing, span), axis=1)
-    lane = lax.broadcasted_iota(jnp.int32, (span, count), 0) // spacing
-    hot = (lane == lax.broadcasted_iota(jnp.int32, (span, count), 1)).astype(F32)
-    table_grad[...] = lax.dot_general(
-        strips[...], hot, NN, precision=lax.Precision.HIGHEST, preferred_element_type=F32
+                tiles = lax.dot_general(
+                    jnp.sum(block.reshape(count, spacing, span), axis=1), backwards, NN,
+                    precision=lax.Precision.HIGHEST, preferred_element_type=F32,
+                )
+                turned_tiles = pltpu.roll(tiles, 0, 1, stride=1, stride_axis=0)
+                place = (delta * 2 + side) * 128
+                strips[head : head + 1, place : place + 128] = jnp.sum(turned_tiles, axis=0, keepdims=True)
+    entry = lax.broadcasted_iota(jnp.int32, (GROUP * 2 * 128, 128), 0)
+    bucket = (entry // 256) * count + count - 1 - entry % 128 - (entry // 128) % 2
+    hot = (bucket == lax.broadcasted_iota(jnp.int32, (GROUP * 2 * 128, 128), 1)) & (entry % 128 < 2 * count)
+    table_rows = lax.dot_general(
+        strips[...], hot.astype(F32), NN, precision=lax.Precision.HIGHEST, preferred_element_type=F32
     )
-    gain_total = jnp.zeros(gain_grad.shape, F32)
-    weight_total = jnp.zeros(qkv_grad.shape, F32)
+    gain_total = jnp.zeros((1, features), F32)
+    weight_total = jnp.zeros((features, 3 * width), F32)
     for part in range(GROUP):
         place = ids[5 + part]
         rows = pl.ds(pl.multiple_of(place * span, span), span)
@@ -482,20 +488,31 @@
         normed = (unit * gain[...].astype(F32)).astype(BF16)
         lowered = mixed_grad[rows, :]
         weight_total = weight_total + mm(normed, lowered, TN)
-        back = mm(lowered, weight[...], NT)
+        back = mm(lowered, weight[:, : 3 * width], NT)
         gain_total = gain_total + jnp.sum(back * unit, axis=0, keepdims=True)
-        target = kept if part < 2 else sent
-        target[part % 2] = back.astype(BF16)
-    qkv_grad[...] = weight_total
-    gain_grad[...] = gain_total
-
-
-def first_norm_grad(kept, arrived, own, gain, middle_grad, wide, low):
-    grad = kept[...].astype(F32) + arrived[...].astype(F32)
+        if part == 0:
+            stay[...] = back.astype(BF16)
+        elif part == 1:
+            leave[...] = back.astype(BF16)
+        else:
+            sent[part - 2] = back.astype(BF16)
+    owned = buckets // ranks
+    bucket = lax.broadcasted_iota(jnp.int32, (128, features), 0)
+    target = (bucket // owned) * (features // ranks) + bucket % owned
+    spot = (target == lax.broadcasted_iota(jnp.int32, (128, features), 1)) & (bucket < buckets)
+    placed = lax.dot_general(
+        table_rows, spot.astype(F32), NN, precision=lax.Precision.HIGHEST, preferred_element_type=F32
+    )
+    extra = jnp.concatenate([placed, jnp.broadcast_to(gain_total, (8, features))], axis=0)
+    shared_grad[...] = jnp.zeros_like(shared_grad)
+    shared_grad[:, : 3 * width] = weight_total.astype(BF16)
+    shared_grad[:, 3 * width : 3 * width + 16] = extra.T.astype(BF16)
+
+
+def first_norm_grad(stay, partner, arrived, own, gain, middle_grad, low):
+    grad = stay[...].astype(F32) + partner[0].astype(F32) + arrived[...].astype(F32)
     back, unused = norm_backward(own[...].astype(F32), gain[...].astype(F32), grad)
-    total = middle_grad[...] + back
-    wide[...] = total
-    low[...] = total.astype(BF16)
+    low[...] = (middle_grad[...] + back).astype(BF16)
 
 
 FLIP = [(0, 1), (1, 0)]
@@ -522,9 +539,17 @@
     return lax.ppermute(block, ("section", "zhi", "zlo"), scatter_pairs(turn))
 
 
-def to_home(block, turn):
-    pairs = [(after, before) for before, after in scatter_pairs(turn)]
+def to_home(block, section, batch):
+    turn = section ^ batch
+    pairs = [(after, before) for before, after in scatter_pairs(turn) if before // 4 == section]
     return lax.ppermute(block, ("section", "zhi", "zlo"), pairs)
+
+
+def home_pair(blocks, core):
+    return jnp.stack([
+        jnp.where(core == 0, to_home(blocks[0], 0, batch), to_home(blocks[1], 1, batch))
+        for batch in range(2)
+    ])
 
 
 def exchange(block, experts, capacity):
@@ -535,8 +560,132 @@
     return moved.reshape(experts * capacity, features)
 
 
+def spread_sum(block, axes, parts):
+    rows, columns = block.shape
+    moved = lax.all_to_all(
+        block.reshape(parts, rows // parts, columns), axes, split_axis=0, concat_axis=0, tiled=True
+    )
+    return jnp.sum(moved.astype(F32), axis=0)
+
+
 def regroup(block):
     return lax.all_to_all(block, ("zlo", "section"), split_axis=0, concat_axis=0, tiled=True)
+
+
+def gather_columns(blocks, out, staged, local_sem, send_sem, recv_sem, stage_send, stage_recv):
+    core = lax.axis_index("section")
+    expert = lax.axis_index("expert")
+    zhi = lax.axis_index("zhi")
+    zlo = lax.axis_index("zlo")
+    place = 2 * zhi + zlo
+    other = 1 - core
+    beside_x = expert + 1 - 2 * (expert % 2)
+    beside_y = (expert + 2) % 4
+    places = [place, place + 1 - 2 * zlo, (place + 2) % 4, 3 - place]
+
+    def at(section, rank_expert, rank_place):
+        return out.at[section, rank_expert * 4 + rank_place]
+
+    barrier = pltpu.get_barrier_semaphore()
+    peers = [{"section": other}, {"expert": beside_x}, {"expert": beside_y}]
+    peers += [{"zhi": spot // 2, "zlo": spot % 2} for spot in places[1:]]
+    for peer in peers:
+        pl.semaphore_signal(barrier, inc=1, device_id=peer, device_id_type=pl.DeviceIdType.MESH)
+    pl.semaphore_wait(barrier, len(peers))
+
+    started = []
+
+    def send(source, target, index, section, owner, spot, peer):
+        copy = pltpu.make_async_remote_copy(
+            src_ref=source, dst_ref=target, send_sem=send_sem.at[index],
+            recv_sem=recv_sem.at[section, owner * 4 + spot], device_id=peer,
+            device_id_type=pl.DeviceIdType.MESH,
+        )
+        copy.start()
+        started.append(copy)
+
+    def arrived(section, owner, spot):
+        pltpu.make_async_remote_copy(
+            src_ref=at(section, owner, spot), dst_ref=at(section, owner, spot), send_sem=send_sem.at[0],
+            recv_sem=recv_sem.at[section, owner * 4 + spot], device_id={"section": other},
+            device_id_type=pl.DeviceIdType.MESH,
+        ).wait_recv()
+
+    trades = []
+    for parity in range(2):
+        trade = pltpu.make_async_remote_copy(
+            src_ref=blocks.at[2 * parity + other], dst_ref=staged.at[parity], send_sem=stage_send.at[parity],
+            recv_sem=stage_recv.at[parity], device_id={"section": other},
+            device_id_type=pl.DeviceIdType.MESH,
+        )
+        trade.start()
+        trades.append(trade)
+
+    index = 0
+    for which in range(2):
+        section = core if which == 0 else other
+        if which == 1:
+            for trade in trades:
+                trade.wait()
+
+        def block_for(parity):
+            return blocks.at[2 * parity + core] if which == 0 else staged.at[parity]
+
+        for step, spot in enumerate(places[1:]):
+            send(block_for(spot % 2), at(section, expert, place), index, section, expert, place,
+                 {"zhi": spot // 2, "zlo": spot % 2})
+            index += 1
+        for peer in (beside_x, beside_y):
+            send(block_for(zlo), at(section, expert, place), index, section, expert, place, {"expert": peer})
+            index += 1
+        local = pltpu.make_async_copy(block_for(zlo), at(section, expert, place), local_sem)
+        local.start()
+        local.wait()
+    sections = (core, other)
+    for spot in places[1:]:
+        for section in sections:
+            arrived(section, expert, spot)
+            for peer in (beside_x, beside_y):
+                send(at(section, expert, spot), at(section, expert, spot), index, section, expert, spot,
+                     {"expert": peer})
+                index += 1
+    for section in sections:
+        for step, spot in enumerate(places):
+            arrived(section, beside_x, spot)
+            arrived(section, beside_y, spot)
+            source, peer = ((beside_x, beside_y), (beside_y, beside_x))[step % 2]
+            send(at(section, source, spot), at(section, source, spot), index, section, source, spot,
+                 {"expert": peer})
+            index += 1
+    diagonal = 3 - expert
+    for section in sections:
+        for spot in places:
+            arrived(section, diagonal, spot)
+    for copy in started:
+        copy.wait_send()
+
+
+def run_gather_columns(blocks, ranks):
+    groups, rows, columns = blocks.shape
+    return pl.pallas_call(
+        gather_columns,
+        name="gather_columns",
+        in_specs=[pl.BlockSpec(memory_space=pltpu.VMEM)],
+        out_specs=pl.BlockSpec(memory_space=pltpu.VMEM),
+        out_shape=shape((2, ranks, rows, columns), blocks.dtype),
+        scratch_shapes=[
+            pltpu.VMEM((2, rows, columns), blocks.dtype),
+            pltpu.SemaphoreType.DMA,
+            pltpu.SemaphoreType.DMA((30,)),
+            pltpu.SemaphoreType.DMA((2, ranks)),
+            pltpu.SemaphoreType.DMA((2,)),
+            pltpu.SemaphoreType.DMA((2,)),
+        ],
+        compiler_params=pltpu.CompilerParams(
+            collective_id=0, has_side_effects=True, vmem_limit_bytes=16 << 20
+        ),
+        cost_estimate=pl.CostEstimate(flops=0, bytes_accessed=40 << 20, transcendentals=0),
+    )(blocks)
 
 
 def per_device(inputs, cotangent, qkv_shard, out_shard, router_shard, gain_shard, table_shard,
@@ -557,10 +706,10 @@
     capacity = max(2, 4 * span // experts)
     slots = experts * capacity
     group = 2 * zlo + core
-    sizes = (span, heads, size, spacing)
+    sizes = (span, heads, size, spacing, ranks)
     ids = jnp.stack([
         group, 2 * zlo + 1 - core, 2 * (1 - zlo) + core, 2 * (1 - zlo) + 1 - core, group,
-        core, 2 + core, 1 - core, 3 - core,
+        group, 2 * (1 - zlo) + core, 2 * zlo + 1 - core, 2 * (1 - zlo) + 1 - core,
     ]).astype(jnp.int32)
     core_id = core.astype(jnp.int32).reshape(1)
 
@@ -579,17 +728,25 @@
         gain_shard[0].T,
         jnp.pad(table_shard[0], ((0, shard_rows - table_rows), (0, 0))),
     ], axis=1)
-    small = jnp.pad(small, ((0, 0), (0, -small.shape[1] % 128)))
-    packed = jnp.concatenate([qkv_shard[0], out_shard[0], small], axis=1)
-    full = lax.all_gather(packed, RANKS, axis=0, tiled=True)
-    qkv_full = full[:, : 3 * features].reshape(features, 3, GROUP, width)
-
-    def columns_of(which):
-        return lax.dynamic_index_in_dim(qkv_full, which, 2, keepdims=False).reshape(features, 3 * width)
-
-    rest = full[:, 3 * features :]
-    mine = (columns_of(group), rest)
-    theirs = (flip(columns_of(2 * zlo + 1 - core)), flip(rest))
+    by_group = jnp.transpose(
+        qkv_shard[0].reshape(shard_rows, 3, GROUP, width), (2, 0, 1, 3)
+    ).reshape(GROUP, shard_rows, 3 * width)
+    by_group = jnp.concatenate(
+        [by_group, jnp.broadcast_to(small[None], (GROUP, *small.shape))], axis=2
+    )
+    by_group = jnp.pad(by_group, ((0, 0), (0, 0), (0, -by_group.shape[2] % 128)))
+    columns = by_group.shape[2]
+    if lax.axis_size("expert") == 4:
+        early = run_gather_columns(by_group, ranks).reshape(2, features, columns)
+        early = [early[0], early[1]]
+    else:
+        whole_early = lax.all_gather(by_group, RANKS, axis=1, tiled=True)
+        kept = lax.dynamic_index_in_dim(whole_early, group, 0, keepdims=False)
+        traded = flip(lax.dynamic_index_in_dim(whole_early, 2 * zlo + 1 - core, 0, keepdims=False))
+        early = [
+            jnp.where(core == section, kept, traded).reshape(features, columns) for section in range(2)
+        ]
+    w_out_own = lax.all_gather(out_shard[0], RANKS, axis=0, tiled=True)
     w_in = w_expert_in[0, 0]
     w_down = w_expert_out[0, 0]
     w_in_other = flip(w_in)
@@ -598,15 +755,13 @@
     weights = []
     for section in range(2):
         is_own = core == section
-        qkv = jnp.where(is_own, mine[0], theirs[0])
-        others = jnp.where(is_own, mine[1], theirs[1])
-        w_out = others[:, :features]
-        router = others[:, features : features + experts]
-        gains = others[:, features + experts : features + experts + 2].T
-        table = others[:, features + experts + 2 : features + experts + 2 + head_count]
+        others = early[section][:, 3 * width :]
+        router = others[:, :experts]
+        gains = others[:, experts : experts + 2].T
+        table = others[:, experts + 2 : experts + 2 + head_count]
         table = table.reshape(ranks, shard_rows, head_count)[:, :table_rows].reshape(buckets, head_count)
         weights.append((
-            qkv, w_out, router, gains[0:1], gains[1:2], table,
+            early[section], router, gains[0:1], gains[1:2], table,
             jnp.where(is_own, w_in, w_in_other), jnp.where(is_own, w_down, w_down_other),
         ))
 
@@ -620,18 +775,22 @@
     results = []
     stream = own
     for section in range(2):
-        qkv, w_out, router, gain_one, gain_two, table, expert_in, expert_down = weights[section]
+        qkv, router, gain_one, gain_two, table, expert_in, expert_down = weights[section]
         route_rows = section_routes[section]
         side = beside(stream)
         pieces = (stream, flip(stream), side, flip(side))
         outcome, mixed, gathered, stats = call(
             functools.partial(attention_forward, sizes), "attention_forward",
-            [shape((GROUP, span, width), BF16), shape((length, 3 * width), BF16),
+            [shape((GROUP, width, span), BF16), shape((length, 3 * width), BF16),
              shape((length, features), BF16), shape((8, length), F32)],
-            [*pieces, gain_one, qkv, table], scalars=ids,
-            scratch=[*bias_scratch, pltpu.VMEM((width, length), F32)], flops=4 << 30,
+            [*pieces, gain_one, qkv, table], scalars=ids, scratch=bias_scratch, flops=4 << 30,
         )
         attended = regroup(outcome)
+        if section == 0:
+            attended, w_out_own = lax.optimization_barrier((attended, w_out_own))
+            w_out_other = flip(w_out_own)
+            w_outs = [jnp.where(core == which, w_out_own, w_out_other) for which in range(2)]
+        w_out = w_outs[section]
         outgoing, middle, normed_two, aux = call(
             functools.partial(after_attention, capacity), "after_attention",
             [shape((slots, features), BF16), shape((span, features), F32),
@@ -650,121 +809,99 @@
         results.append(result)
         stream = result
 
-    home = [
-        to_home(jnp.where((zhi ^ turn) == 0, results[0], results[1]), turn) for turn in range(2)
-    ]
-    section_outputs = jnp.stack([
-        jnp.where(core == 0, home[0], home[1]), jnp.where(core == 0, home[1], home[0])
-    ])
+    section_outputs = home_pair(results, core)
 
     upstream = given
-    small_grads = [None, None]
+    shared_grads = [None, None]
+    shared_partner = [None, None]
+    shared_qkv = [None, None]
     qkv_grads = [None, None]
     expert_states = [None, None]
     partials = [None, None]
     stream_grads = [None, None]
     for section in (1, 0):
-        qkv, w_out, router, gain_one, gain_two, table, expert_in, expert_down = weights[section]
+        qkv, router, gain_one, gain_two, table, expert_in, expert_down = weights[section]
+        w_out = w_outs[section]
         (stream, outcome, mixed, gathered, stats, attended, middle, normed_two, aux,
          arrived, activation, slope, difference) = states[section]
         route_rows = section_routes[section]
         (spread,) = call(spread_grads, "spread_grads", [shape((slots, features), BF16)],
                          [upstream, aux], flops=1 << 30)
         arrived_grad = exchange(spread, experts, capacity)
+        if section == 0:
+            waiting, arrived_grad = lax.optimization_barrier((shared_qkv[1], arrived_grad))
+            qkv_grads[1] = spread_sum(waiting, ("expert", "zhi"), ranks // 2)
         hidden_grad, rows_grad = run_expert_backward(arrived_grad, expert_in, expert_down, slope)
         returned = exchange(rows_grad, experts, capacity)
         expert_states[section] = (arrived, hidden_grad, activation, arrived_grad)
         wanted = (core != section).astype(jnp.int32).reshape(1)
-        partials[section] = [
-            lax.ppermute(part, "section", [(1 - section, section)])
-            for part in run_weight_partials(wanted, *expert_states[section])
-        ]
-        middle_grad, attended_grad, out_grad, router_grad, gain_two_grad = call(
+        shares = run_weight_partials(wanted, *expert_states[section])
+        partials[section] = [lax.ppermute(part, "section", [(1 - section, section)]) for part in shares]
+        middle_grad, attended_grad, shared_grads[section] = call(
             before_attention, "before_attention",
-            [shape((span, features), F32), shape((GROUP, span, width), BF16),
-             shape((features, features), F32), shape((features, experts), F32), shape((1, features), F32)],
+            [shape((span, features), F32), shape((GROUP, width, span), BF16),
+             shape((features, features + -(-(experts + 1) // 128) * 128), BF16)],
             [returned, aux, upstream, difference, middle, normed_two, attended, gain_two, router, w_out,
-             route_rows], flops=2 << 30,
+             route_rows], flops=2 << 30, after=shares[:1],
         )
-        small_grads[section] = jnp.concatenate([out_grad, router_grad, gain_two_grad.T], axis=1)
+        shared_partner[section] = lax.ppermute(shared_grads[section], "section", [(1 - section, section)])
         grads = regroup(attended_grad)
-        kept, sent, qkv_grad, gain_one_grad, table_grad = call(
+        stay, leave, sent, shared_qkv[section] = call(
             functools.partial(attention_backward, sizes), "attention_backward",
-            [shape((2, span, features), BF16), shape((2, span, features), BF16),
-             shape((features, 3 * width), F32), shape((1, features), F32), shape((heads * GROUP * 2 * blocks, blocks), F32)],
+            [shape((span, features), BF16), shape((span, features), BF16), shape((2, span, features), BF16),
+             shape((features, -(-(3 * width + 16) // 128) * 128), BF16)],
             [mixed, stats, outcome, grads, gathered, gain_one, qkv, table], scalars=ids,
             scratch=[*bias_scratch, pltpu.VMEM((length, 3 * width), BF16),
                      pltpu.VMEM((GROUP, span, span), F32), pltpu.VMEM((length, size), F32),
                      pltpu.VMEM((length, size), F32), pltpu.VMEM((size, length), F32),
-                     pltpu.VMEM((heads * GROUP * 2 * blocks, span), F32)],
+                     pltpu.VMEM((8, GROUP * 2 * 128), F32)],
             flops=8 << 30,
         )
-        pair = kept.astype(F32) + flip(sent).astype(F32)
-        stay = lax.dynamic_index_in_dim(pair, zlo, 0, keepdims=False)
-        leave = lax.dynamic_index_in_dim(pair, 1 - zlo, 0, keepdims=False).astype(BF16)
-        wide, low = call(
-            first_norm_grad, "first_norm_grad", [shape((span, features), F32), shape((span, features), BF16)],
-            [stay, beside(leave), stream, gain_one, middle_grad],
+        partner = flip(sent)
+        leave = leave + partner[1]
+        filler = ()
+        if section == 0:
+            leave, waiting = lax.optimization_barrier((leave, shared_qkv[0]))
+            qkv_grads[0] = spread_sum(waiting, ("expert", "zhi"), ranks // 2)
+            grad_in = run_weight_totals(
+                core_id, *[(expert_states[which][0], expert_states[which][1], partials[which][0])
+                           for which in range(2)], False, sent)
+            filler = (grad_in,)
+        arrived_share = beside(leave)
+        (low,) = call(
+            first_norm_grad, "first_norm_grad", [shape((span, features), BF16)],
+            [stay, partner, arrived_share, stream, gain_one, middle_grad], after=filler,
         )
-        table_total = bucket_sums(table_grad.reshape(heads, GROUP, 2, blocks, blocks), buckets)
-        per_block = buckets // (ranks // 2)
-        block_rows = features // (ranks // 2)
-        table_column = jnp.pad(
-            table_total.T.reshape(ranks // 2, per_block, heads),
-            ((0, 0), (0, block_rows - per_block), (0, 0)),
-        ).reshape(features, heads)
-        packed_grad = jnp.concatenate([qkv_grad, gain_one_grad.T, table_column], axis=1)
-        packed_grad = jnp.pad(packed_grad, ((0, 0), (0, -packed_grad.shape[1] % 128)))
-        qkv_grads[section] = packed_grad.astype(BF16)
         stream_grads[section] = low
         upstream = low
 
-    def spread_sum(block, axes, parts):
-        rows, columns = block.shape
-        moved = lax.all_to_all(
-            block.reshape(parts, rows // parts, columns), axes, split_axis=0, concat_axis=0, tiled=True
-        )
-        return jnp.sum(moved.astype(F32), axis=0)
-
-    def of_core(pair, which):
-        return jnp.where(which == 0, pair[0], pair[1])
-
-    shared = of_core(small_grads, core) + flip(of_core(small_grads, 1 - core).astype(BF16)).astype(F32)
-    shared = jnp.pad(shared, ((0, 0), (0, -shared.shape[1] % 128))).astype(BF16)
+    shared = jnp.where(
+        core == 0,
+        shared_grads[0].astype(F32) + shared_partner[0].astype(F32),
+        shared_grads[1].astype(F32) + shared_partner[1].astype(F32),
+    ).astype(BF16)
     shared = spread_sum(shared, RANKS, ranks)
     grad_out = shared[:, :features]
     grad_router = shared[:, features : features + experts]
     grad_gain_two = shared[:, features + experts]
 
-    reduced = jnp.stack([spread_sum(block, ("expert", "zhi"), ranks // 2) for block in qkv_grads])
-    half = reduced.shape[1] // 2
-    columns = reduced.shape[2]
-    heads_of = reduced.reshape(2, 2, half, columns)
-    gains_part = reduced[:, :, 3 * width].reshape(2, 2, half)
-    per_row = buckets // ranks
-    table_part = reduced[:, : 2 * per_row, 3 * width + 1 : 3 * width + 1 + heads].reshape(2, 2, per_row, heads)
-    heads_of = heads_of.at[:, :, :, 3 * width + 1 :].set(0.0)
-    heads_of = heads_of.at[:, :, :per_row, 3 * width + 1 : 3 * width + 1 + heads].set(table_part)
-    sending = jnp.transpose(heads_of, (1, 0, 2, 3)).reshape(GROUP, half, columns)
-    gathered_grad = regroup(sending)
-    split = gathered_grad[:, :, : 3 * width].reshape(GROUP, half, 3, width)
-    grad_qkv = jnp.transpose(split, (1, 2, 0, 3)).reshape(half, 3 * features)
-    grad_gain_one = jnp.sum(gathered_grad[:, :, 3 * width], axis=0)
+    columns = qkv_grads[0].shape[1]
+    halves = [block.reshape(2, shard_rows, columns) for block in qkv_grads]
+    sending = jnp.stack([halves[0][0], halves[1][0], halves[0][1], halves[1][1]])
+    owned = regroup(sending)
+    split = owned[:, :, : 3 * width].reshape(GROUP, shard_rows, 3, width)
+    grad_qkv = jnp.transpose(split, (1, 2, 0, 3)).reshape(shard_rows, 3 * features)
     grad_table = jnp.transpose(
-        gathered_grad[:, :per_row, 3 * width + 1 : 3 * width + 1 + heads], (1, 0, 2)
-    ).reshape(per_row, head_count)
+        owned[:, :table_rows, 3 * width : 3 * width + heads], (1, 0, 2)
+    ).reshape(table_rows, head_count)
+    grad_gain_one = jnp.sum(owned[:, :, 3 * width + 8], axis=0)
     grad_gains = jnp.stack([grad_gain_one, grad_gain_two])
 
-    home = [
-        to_home(jnp.where((zhi ^ turn) == 0, stream_grads[0], stream_grads[1]), turn) for turn in range(2)
-    ]
-    section_grads = jnp.stack([
-        jnp.where(core == 0, home[0], home[1]), jnp.where(core == 0, home[1], home[0])
-    ]).astype(F32)
-
-    sent_in = jnp.where(core == 0, partials[0][0], partials[1][0])
-    sent_down = jnp.where(core == 0, partials[0][1], partials[1][1])
-    grad_in, grad_down = run_weight_totals(core_id, expert_states[0], expert_states[1], sent_in, sent_down)
+    section_grads = home_pair(stream_grads, core).astype(F32)
+
+    grad_down = run_weight_totals(
+        core_id, *[(expert_states[which][2], expert_states[which][3], partials[which][1])
+                   for which in range(2)], True, stream_grads[0])
     return (
         section_outputs[None, :, None],
         section_grads[None, :, None],

time: 888 us -> 797 us (0.90)
  waiting for transfers between devices: 290 us -> 237 us
  local copies, waits for them, and re-layouts: 71.6 us -> 24.5 us
  Pallas kernels: 206 us -> 236 us
  matrix products: 29.1 us -> 0 us
  other arithmetic: 59.3 us -> 32.4 us
  starting transfers between devices: 112 us -> 129 us
  blocking collectives: 95.8 us -> 110 us
    all_gather x1, waiting for transfers between devices: 83.7 us -> 0.01 us  [per_device(): w_out_own = lax.all_gather(out_shard[0], RANKS, axis=0, tiled=True)]
    dot_general x2 -> x0, matrix products: 29.1 us -> none  [bucket_sums(): jnp.einsum('hdskq,dskqb->hb', block_sums, hot, precision=lax.Precision.HI...]
    pallas_call x0 -> x1, Pallas kernels: none -> 28.3 us  [run_gather_columns(): pl.pallas_call(gather_columns, name='gather_columns', in_specs=[pl.BlockS...]
    all_to_all x3, waiting for transfers between devices: 0.01 us -> 22 us  [spread_sum(): lax.all_to_all(block.reshape(parts, rows // parts, columns), axes, split_...]
    select_n x6 -> x1, other arithmetic: 16.9 us -> 2.83 us  [per_device(): jnp.where(core == which, w_out_own, w_out_other)]
    all_to_all x1 -> x2, blocking collectives: 9.8 us -> 23.4 us  [regroup(): lax.all_to_all(block, ('zlo', 'section'), split_axis=0, concat_axis=0, ti...]
    all_to_all x6, waiting for transfers between devices: 147 us -> 158 us  [exchange(): lax.all_to_all(block.reshape(experts, capacity, features), RANKS, split_a...]
    ppermute x4 -> x8, waiting for transfers between devices: 0.01 us -> 10.4 us  [to_home(): return lax.ppermute(block, ('section', 'zhi', 'zlo'), pairs)]
  transfers between devices with their start and end apart: 41 -> 44, of which waited for: 16 -> 16; matrix products, arithmetic and copies ran while one was open for 16% -> 6% of each run, Pallas kernels for 14% -> 19%
where the time goes in v2:
time: 797 us; the launch traced here: 785 us
  waiting for transfers between devices  237 us (30%)
  Pallas kernels  236 us (30%)
  starting transfers between devices  129 us (16%)
  blocking collectives  110 us (14%)
  other arithmetic  32.4 us (4%)
  local copies, waits for them, and re-layouts  24.5 us (3%)
  between operations  15.3 us (2%)
    all_to_all x6, waiting for transfers between devices, exchange(): lax.all_to_all(block.reshape(experts, capacity, features), RANKS, split_a...  158 us
    pallas_call x14, Pallas kernels, call(): pl.pallas_call(body, name=name, in_specs=specs, out_specs=[pl.BlockSpec(m...  94.9 us
    all_to_all x2, blocking collectives, exchange(): lax.all_to_all(block.reshape(experts, capacity, features), RANKS, split_a...  86.5 us
    pallas_call x2, Pallas kernels, run_expert_forward(): pl.pallas_call(expert_forward, name='expert_forward', grid=(hidden // til...  34.5 us
    pallas_call x2, Pallas kernels, run_expert_backward(): pl.pallas_call(expert_backward, name='expert_backward', grid=(hidden // t...  33.5 us
    ppermute x4, waiting for transfers between devices, beside(): return lax.ppermute(block, 'zlo', FLIP)  32.6 us
    all_to_all x6, starting transfers between devices, exchange(): lax.all_to_all(block.reshape(experts, capacity, features), RANKS, split_a...  31.2 us
    pallas_call x1, Pallas kernels, run_gather_columns(): pl.pallas_call(gather_columns, name='gather_columns', in_specs=[pl.BlockS...  28.3 us
  transfers between devices with their start and end apart: 44, of which 16 were waited for; matrix products, arithmetic and copies ran while one was open for 6% of the time, Pallas kernels for 19%

profile of v2, /device:TPU:0, one launch (start us, length us, event | category | flops | bytes accessed | tf_op | source)
XLA Modules:
  0.0 784.9 jit_solution(13524889527792067036)
XLA Ops:
  9.1 16.2 %collective-permute-start.2 = (bf16[256,768]{1,0:T(8,128)(2,1)S(1)}, bf16[256,768]{1,0:T(8,128)(2,1)S(1)}, u32[]{:S(2)}, u32[]{:S(2)}) collective-permute-start(bf16[256,768]{1,0:T(8,128)(2,1)S(1)} %collective-permute-done.own.refs_4_), channel_id=1, source_target_pairs={{0,1},{1,0},{2,3},{3,2},{4,5},{5,4},{6,7},{7,6},{8,9},{9,8},{10,11... | collective-permute-start | bytes 1179656 | tf_op jit(solution)/shard_map/ppermute | solution.py:526
  27.3 28.3 %gather_columns.1 = bf16[2,16,48,640]{3,2,1,0:T(8,128)(2,1)S(1)} custom-call(bf16[4,48,640]{2,1,0:T(8,128)(2,1)S(1)} %fusion.4.blocks), custom_call_target="tpu_custom_call" | custom-call | bytes 41943040 | tf_op jit(solution)/shard_map/gather_columns/pallas_call | solution.py:670
  59.6 8.7 %attention_forward.2 = (bf16[4,192,256]{2,1,0:T(8,128)(2,1)}, bf16[1024,576]{1,0:T(8,128)(2,1)}, bf16[1024,768]{1,0:T(8,128)(2,1)}, f32[8,1024]{1,0:T(8,128)}) custom-call(s32[9]{0:T(128)} %stack.51.ids, bf16[256,768]{1,0:T(8,128)(2,1)} %copy-done.15, bf16[256,768]{1,0:T(8,128)(2,1)} %copy-done.33, bf16[256,768]{1,0:T(8,128)(2,1)} %copy-done.32, ...), custom_call_target="tpu_custom_call" | custom-call | flops 4294967296 | bytes 5737472 | tf_op jit(solution)/shard_map/attention_forward/pallas_call | solution.py:51
  68.3 11.8 %all_to_all.80.attended.refs_7_ = bf16[4,192,256]{2,1,0:T(8,128)(2,1)} all-to-all(bf16[4,192,256]{2,1,0:T(8,128)(2,1)} %get-tuple-element.63.attended), channel_id=1, replica_groups=mesh['section'=2,'expert'=4,'zhi'=2,'zlo'=2] {'zlo','section'}, dimensions={0} | all-to-all | bytes 786432 | tf_op jit(solution)/shard_map/all_to_all | solution.py:572
  103.5 7.9 %broadcast_select_fusion = (bf16[3072,768]{1,0:T(8,128)(2,1)}, bf16[3072,768]{1,0:T(8,128)(2,1)}) fusion(bf16[3072,768]{1,0:T(8,128)(2,1)} %collective-permute-done.8, pred[]{:T(512)S(6)} %eq.10, bf16[1,1,3072,768]{3,2,1,0:T(8,128)(2,1)} %param.18, pred[]{:T(512)S(6)} %eq.8), kind=kLoop, calls=%fused_computation | loop fusion | flops 4718592 | bytes 18874370 | tf_op jit(solution)/shard_map/jit(_where)/select_n | solution.py:765
  111.5 7.9 %broadcast_select_fusion.1 = (bf16[768,3072]{1,0:T(8,128)(2,1)}, bf16[768,3072]{1,0:T(8,128)(2,1)}) fusion(bf16[768,3072]{1,0:T(8,128)(2,1)} %collective-permute-done.7, pred[]{:T(512)S(6)} %eq.10, bf16[1,1,768,3072]{3,2,1,0:T(8,128)(2,1)} %param.17, pred[]{:T(512)S(6)} %eq.8), kind=kLoop, calls=%fused_computation.1 | loop fusion | flops 4718592 | bytes 18874370 | tf_op jit(solution)/shard_map/jit(_where)/select_n | solution.py:765
  119.4 24.2 %all-to-all-done.1 = bf16[16,64,768]{2,1,0:T(8,128)(2,1)S(1)} async-done(((bf16[16,64,768]{2,1,0:T(8,128)(2,1)}), bf16[16,64,768]{2,1,0:T(8,128)(2,1)S(1)}, u32[]{:S(2)}, u32[]{:S(2)}) %all-to-all-start.1) | async-done | bytes 1572896 | tf_op jit(solution)/shard_map/all_to_all | solution.py:557
  144.8 17.2 %expert_forward.2 = (bf16[1024,3072]{1,0:T(8,128)(2,1)}, bf16[1024,3072]{1,0:T(8,128)(2,1)}, bf16[1024,768]{1,0:T(8,128)(2,1)}) custom-call(bf16[1024,768]{1,0:T(8,128)(2,1)} %bitcast.99, bf16[768,3072]{1,0:T(8,128)(2,1)} %get-tuple-element.156.w_in, bf16[3072,768]{1,0:T(8,128)(2,1)} %get-tuple-element.154.w_down), custom_call_target="tpu_custom_call" | custom-call | flops 9663676416 | bytes 31457280 | tf_op jit(solution)/shard_map/expert_forward/pallas_call | solution.py:227
  162.0 43.7 %all_to_all.81 = bf16[16,64,768]{2,1,0:T(8,128)(2,1)} all-to-all(bf16[16,64,768]{2,1,0:T(8,128)(2,1)} %bitcast.134), channel_id=1, replica_groups=mesh['section'=2,'expert'=4,'zhi'=2,'zlo'=2] {'expert','zhi','zlo'}, dimensions={0} | all-to-all | bytes 3145728 | tf_op jit(solution)/shard_map/all_to_all | solution.py:557
  209.6 10.2 %collective-permute-done.11.side = bf16[256,768]{1,0:T(8,128)(2,1)S(1)} collective-permute-done((bf16[256,768]{1,0:T(8,128)(2,1)}, bf16[256,768]{1,0:T(8,128)(2,1)S(1)}, u32[]{:S(2)}, u32[]{:S(2)}) %collective-permute-start.11) | collective-permute-done | bytes 393248 | tf_op jit(solution)/shard_map/ppermute | solution.py:526
  222.3 8.7 %attention_forward.3 = (bf16[4,192,256]{2,1,0:T(8,128)(2,1)}, bf16[1024,576]{1,0:T(8,128)(2,1)}, bf16[1024,768]{1,0:T(8,128)(2,1)}, f32[8,1024]{1,0:T(8,128)}) custom-call(s32[9]{0:T(128)} %stack.51.ids, bf16[256,768]{1,0:T(8,128)(2,1)} %get-tuple-element.70.own, bf16[256,768]{1,0:T(8,128)(2,1)} %copy-done.35, bf16[256,768]{1,0:T(8,128)(2,1)} %copy-done.34, ...), custom_call_target="tpu_custom_call" | custom-call | flops 4294967296 | bytes 5737472 | tf_op jit(solution)/shard_map/attention_forward/pallas_call | solution.py:51
  231.0 14.2 %all-to-all-start.3 = ((bf16[4,192,256]{2,1,0:T(8,128)(2,1)}), bf16[4,192,256]{2,1,0:T(8,128)(2,1)S(1)}, u32[]{:S(2)}, u32[]{:S(2)}) async-start(bf16[4,192,256]{2,1,0:T(8,128)(2,1)} %get-tuple-element.71.attended), calls=%async_computation.3 | async-start | bytes 786432 | tf_op jit(solution)/shard_map/all_to_all | solution.py:572
  266.7 38.1 %all-to-all-done.4 = bf16[16,64,768]{2,1,0:T(8,128)(2,1)S(1)} async-done(((bf16[16,64,768]{2,1,0:T(8,128)(2,1)}), bf16[16,64,768]{2,1,0:T(8,128)(2,1)S(1)}, u32[]{:S(2)}, u32[]{:S(2)}) %all-to-all-start.4) | async-done | bytes 1572896 | tf_op jit(solution)/shard_map/all_to_all | solution.py:557
  304.7 10.2 %all-to-all-start.6 = ((bf16[16,64,768]{2,1,0:T(8,128)(2,1)}), bf16[16,64,768]{2,1,0:T(8,128)(2,1)S(1)}, u32[]{:S(2)}, u32[]{:S(2)}) async-start(bf16[16,64,768]{2,1,0:T(8,128)(2,1)} %bitcast.133), calls=%async_computation.6 | async-start | bytes 3145728 | tf_op jit(solution)/shard_map/all_to_all | solution.py:557
  314.9 17.3 %expert_forward.3 = (bf16[1024,3072]{1,0:T(8,128)(2,1)}, bf16[1024,3072]{1,0:T(8,128)(2,1)}, bf16[1024,768]{1,0:T(8,128)(2,1)}) custom-call(bf16[1024,768]{1,0:T(8,128)(2,1)} %bitcast.105, bf16[768,3072]{1,0:T(8,128)(2,1)} %get-tuple-element.155.w_in, bf16[3072,768]{1,0:T(8,128)(2,1)} %get-tuple-element.153.w_down), custom_call_target="tpu_custom_call" | custom-call | flops 9663676416 | bytes 31457280 | tf_op jit(solution)/shard_map/expert_forward/pallas_call | solution.py:227
  332.2 21.4 %all-to-all-done.6 = bf16[16,64,768]{2,1,0:T(8,128)(2,1)S(1)} async-done(((bf16[16,64,768]{2,1,0:T(8,128)(2,1)}), bf16[16,64,768]{2,1,0:T(8,128)(2,1)S(1)}, u32[]{:S(2)}, u32[]{:S(2)}) %all-to-all-start.6) | async-done | bytes 1572896 | tf_op jit(solution)/shard_map/all_to_all | solution.py:557
  357.3 16.8 %expert_backward.2 = (bf16[1024,3072]{1,0:T(8,128)(2,1)}, bf16[1024,768]{1,0:T(8,128)(2,1)}) custom-call(bf16[1024,768]{1,0:T(8,128)(2,1)} %bitcast.102, bf16[768,3072]{1,0:T(8,128)(2,1)} %get-tuple-element.155.w_in, bf16[3072,768]{1,0:T(8,128)(2,1)} %get-tuple-element.153.w_down, bf16[1024,3072]{1,0:T(8,128)(2,1)} %get-tuple-element.79.slope), custom_call_target="tpu_custom_call" | custom-call | flops 9663676416 | bytes 31457280 | tf_op jit(solution)/shard_map/expert_backward/pallas_call | solution.py:254
  374.1 21.4 %all-to-all-done.5 = bf16[16,64,768]{2,1,0:T(8,128)(2,1)S(1)} async-done(((bf16[16,64,768]{2,1,0:T(8,128)(2,1)}), bf16[16,64,768]{2,1,0:T(8,128)(2,1)S(1)}, u32[]{:S(2)}, u32[]{:S(2)}) %all-to-all-start.5) | async-done | bytes 1572896 | tf_op jit(solution)/shard_map/all_to_all | solution.py:557
  399.2 15.0 %weight_partials.2 = (bf16[768,3072]{1,0:T(8,128)(2,1)}, bf16[3072,768]{1,0:T(8,128)(2,1)}) custom-call(s32[1]{0:T(128)} %bitcast.36.scalars, bf16[1024,768]{1,0:T(8,128)(2,1)} %bitcast.106, bf16[1024,3072]{1,0:T(8,128)(2,1)} %get-tuple-element.80.hidden_grad.right_1, bf16[1024,3072]{1,0:T(8,128)(2,1)} %get-tuple-element.81.activation.left_1, ...), custom_call_target="tpu_custom_call" | custom-call | flops 9663676416 | bytes 31457280 | tf_op jit(solution)/shard_map/weight_partials/pallas_call | solution.py:288
  418.0 19.5 %all-to-all-done.7 = bf16[16,64,768]{2,1,0:T(8,128)(2,1)S(1)} async-done(((bf16[16,64,768]{2,1,0:T(8,128)(2,1)}), bf16[16,64,768]{2,1,0:T(8,128)(2,1)S(1)}, u32[]{:S(2)}, u32[]{:S(2)}) %all-to-all-start.7) | async-done | bytes 1572896 | tf_op jit(solution)/shard_map/all_to_all | solution.py:557
  445.3 11.6 %all_to_all.82.grads = bf16[4,192,256]{2,1,0:T(8,128)(2,1)} all-to-all(bf16[4,192,256]{2,1,0:T(8,128)(2,1)} %get-tuple-element.86), channel_id=1, replica_groups=mesh['section'=2,'expert'=4,'zhi'=2,'zlo'=2] {'zlo','section'}, dimensions={0} | all-to-all | bytes 786432 | tf_op jit(solution)/shard_map/all_to_all | solution.py:572
  456.9 17.3 %attention_backward.2 = (bf16[256,768]{1,0:T(8,128)(2,1)}, bf16[256,768]{1,0:T(8,128)(2,1)}, bf16[2,256,768]{2,1,0:T(8,128)(2,1)}, bf16[768,640]{1,0:T(8,128)(2,1)}) custom-call(s32[9]{0:T(128)} %stack.51.ids, bf16[1024,576]{1,0:T(8,128)(2,1)} %get-tuple-element.77.mixed, f32[8,1024]{1,0:T(8,128)} %get-tuple-element.78.stats, ...), custom_call_target="tpu_custom_call" | custom-call | flops 8589934592 | bytes 7113728 | tf_op jit(solution)/shard_map/attention_backward/pallas_call | solution.py:51
  478.5 10.8 %collective-permute-done.18.arrived = bf16[256,768]{1,0:T(8,128)(2,1)S(1)} collective-permute-done((bf16[256,768]{1,0:T(8,128)(2,1)S(1)}, bf16[256,768]{1,0:T(8,128)(2,1)S(1)}, u32[]{:S(2)}, u32[]{:S(2)}) %collective-permute-start.18) | collective-permute-done | bytes 393248 | tf_op jit(solution)/shard_map/ppermute | solution.py:526
  496.2 42.8 %all_to_all.83 = bf16[16,64,768]{2,1,0:T(8,128)(2,1)} all-to-all(bf16[16,64,768]{2,1,0:T(8,128)(2,1)} %bitcast.136), channel_id=1, replica_groups=mesh['section'=2,'expert'=4,'zhi'=2,'zlo'=2] {'expert','zhi','zlo'}, dimensions={0} | all-to-all | bytes 3145728 | tf_op jit(solution)/shard_map/all_to_all | solution.py:557
  539.0 16.7 %expert_backward.3 = (bf16[1024,3072]{1,0:T(8,128)(2,1)}, bf16[1024,768]{1,0:T(8,128)(2,1)}) custom-call(bf16[1024,768]{1,0:T(8,128)(2,1)} %bitcast.108, bf16[768,3072]{1,0:T(8,128)(2,1)} %get-tuple-element.156.w_in, bf16[3072,768]{1,0:T(8,128)(2,1)} %get-tuple-element.154.w_down, bf16[1024,3072]{1,0:T(8,128)(2,1)} %get-tuple-element.94.slope), custom_call_target="tpu_custom_call" | custom-call | flops 9663676416 | bytes 31457280 | tf_op jit(solution)/shard_map/expert_backward/pallas_call | solution.py:254
  563.7 33.6 %all-to-all-done.10 = bf16[16,64,768]{2,1,0:T(8,128)(2,1)S(1)} async-done(((bf16[16,64,768]{2,1,0:T(8,128)(2,1)}), bf16[16,64,768]{2,1,0:T(8,128)(2,1)S(1)}, u32[]{:S(2)}, u32[]{:S(2)}) %all-to-all-start.10) | async-done | bytes 1572896 | tf_op jit(solution)/shard_map/all_to_all | solution.py:557
  621.9 17.4 %attention_backward.3 = (bf16[256,768]{1,0:T(8,128)(2,1)}, bf16[256,768]{1,0:T(8,128)(2,1)}, bf16[2,256,768]{2,1,0:T(8,128)(2,1)}, bf16[768,640]{1,0:T(8,128)(2,1)}) custom-call(s32[9]{0:T(128)} %stack.51.ids, bf16[1024,576]{1,0:T(8,128)(2,1)} %get-tuple-element.98.mixed, f32[8,1024]{1,0:T(8,128)} %get-tuple-element.99.stats, ...), custom_call_target="tpu_custom_call" | custom-call | flops 8589934592 | bytes 7113728 | tf_op jit(solution)/shard_map/attention_backward/pallas_call | solution.py:51
  645.2 10.4 %collective-permute-done.14 = bf16[256,768]{1,0:T(8,128)(2,1)S(1)} collective-permute-done((bf16[256,768]{1,0:T(8,128)(2,1)S(1)}, bf16[256,768]{1,0:T(8,128)(2,1)S(1)}, u32[]{:S(2)}, u32[]{:S(2)}) %collective-permute-start.14) | collective-permute-done | bytes 393248 | tf_op jit(solution)/shard_map/ppermute | solution.py:545
  673.6 22.0 %all-to-all-done.12 = bf16[8,96,640]{2,1,0:T(8,128)(2,1)S(1)} async-done(((bf16[8,96,640]{2,1,0:T(8,128)(2,1)}), bf16[8,96,640]{2,1,0:T(8,128)(2,1)S(1)}, u32[]{:S(2)}, u32[]{:S(2)}) %all-to-all-start.12) | async-done | bytes 983072 | tf_op jit(solution)/shard_map/all_to_all | solution.py:565
  721.5 12.9 %weight_totals.2.refs_0_ = f32[768,3072]{1,0:T(8,128)} custom-call(s32[1]{0:T(128)} %bitcast.35.scalars, bf16[1024,768]{1,0:T(8,128)(2,1)} %bitcast.101, bf16[1024,3072]{1,0:T(8,128)(2,1)} %get-tuple-element.95.hidden_grad.right, bf16[768,3072]{1,0:T(8,128)(2,1)} %collective-permute-done.19.sent, bf16[1024,768]{1,0:T(8,128)(2,1)} %bitcast.107, ...), custom_call_target="tpu_custom_call" | custom-call | flops 4831838208 | bytes 31457280 | tf_op jit(solution)/shard_map/weight_totals/pallas_call | solution.py:344
  734.4 11.6 %collective-permute-done.22.refs_3_ = bf16[256,768]{1,0:T(8,128)(2,1)S(1)} collective-permute-done((bf16[256,768]{1,0:T(8,128)(2,1)S(1)}, bf16[256,768]{1,0:T(8,128)(2,1)S(1)}, u32[]{:S(2)}, u32[]{:S(2)}) %collective-permute-start.22) | collective-permute-done | bytes 393248 | tf_op jit(solution)/shard_map/ppermute | solution.py:526
  755.4 12.8 %weight_totals.3 = f32[3072,768]{1,0:T(8,128)} custom-call(s32[1]{0:T(128)} %bitcast.35.scalars, bf16[1024,3072]{1,0:T(8,128)(2,1)} %get-tuple-element.96.activation.left, bf16[1024,768]{1,0:T(8,128)(2,1)} %bitcast.110, bf16[3072,768]{1,0:T(8,128)(2,1)} %collective-permute-done.29.sent, bf16[1024,3072]{1,0:T(8,128)(2,1)} %get-tuple-element.81.activation.left_1, ...), custom_call_target="tpu_custom_call" | custom-call | flops 4831838208 | bytes 31457280 | tf_op jit(solution)/shard_map/weight_totals/pallas_call | solution.py:344
  (216 shorter events, 191.1 us)
Async XLA Ops:
  7.2 72.8 %all-gather.3.cloned.1.call-start = ((), (), s32[]{:S(2)}) async-start(), calls=%async_computation.16 | async-start | bytes 1253376 | tf_op jit(solution)/shard_map/all_gather | solution.py:749
  7.3 96.3 %collective-permute-start.8 = (bf16[3072,768]{1,0:T(8,128)(2,1)}, bf16[3072,768]{1,0:T(8,128)(2,1)}, u32[]{:S(2)}, u32[]{:S(2)}) collective-permute-start(bf16[3072,768]{1,0:T(8,128)(2,1)} %bitcast.113), channel_id=1, source_target_pairs={{0,16},{16,0},{1,17},{17,1},{2,18},{18,2},{3,19},{19,3},{4,20},{20... | collective-permute-start | bytes 14155784 | tf_op jit(solution)/shard_map/ppermute | solution.py:522
  9.1 46.6 %collective-permute-start.2 = (bf16[256,768]{1,0:T(8,128)(2,1)S(1)}, bf16[256,768]{1,0:T(8,128)(2,1)S(1)}, u32[]{:S(2)}, u32[]{:S(2)}) collective-permute-start(bf16[256,768]{1,0:T(8,128)(2,1)S(1)} %collective-permute-done.own.refs_4_), channel_id=1, source_target_pairs={{0,1},{1,0},{2,3},{3,2},{4,5},{5,4},{6,7},{7,6},{8,9},{9,8},{10,11... | collective-permute-start | bytes 1179656 | tf_op jit(solution)/shard_map/ppermute | solution.py:526
  25.3 86.2 %collective-permute-start.7 = (bf16[768,3072]{1,0:T(8,128)(2,1)}, bf16[768,3072]{1,0:T(8,128)(2,1)}, u32[]{:S(2)}, u32[]{:S(2)}) collective-permute-start(bf16[768,3072]{1,0:T(8,128)(2,1)} %bitcast.114), channel_id=1, source_target_pairs={{0,16},{16,0},{1,17},{17,1},{2,18},{18,2},{3,19},{19,3},{4,20},{20... | collective-permute-start | bytes 14155784 | tf_op jit(solution)/shard_map/ppermute | solution.py:522
  97.5 46.1 %all-to-all-start.1 = ((bf16[16,64,768]{2,1,0:T(8,128)(2,1)}), bf16[16,64,768]{2,1,0:T(8,128)(2,1)S(1)}, u32[]{:S(2)}, u32[]{:S(2)}) async-start(bf16[16,64,768]{2,1,0:T(8,128)(2,1)} %bitcast.129), calls=%async_computation.1 | async-start | bytes 3145728 | tf_op jit(solution)/shard_map/all_to_all | solution.py:557
  209.6 11.9 %collective-permute-start.10 = (bf16[256,768]{1,0:T(8,128)(2,1)}, bf16[256,768]{1,0:T(8,128)(2,1)S(1)}, u32[]{:S(2)}, u32[]{:S(2)}) collective-permute-start(bf16[256,768]{1,0:T(8,128)(2,1)} %get-tuple-element.70.own), channel_id=1, source_target_pairs={{0,16},{16,0},{1,17},{17,1},{2,18},{18,2},{3,19},{19,3},{4,20},{20... | collective-permute-start | bytes 1179656 | tf_op jit(solution)/shard_map/ppermute | solution.py:522
  231.0 21.6 %all-to-all-start.3 = ((bf16[4,192,256]{2,1,0:T(8,128)(2,1)}), bf16[4,192,256]{2,1,0:T(8,128)(2,1)S(1)}, u32[]{:S(2)}, u32[]{:S(2)}) async-start(bf16[4,192,256]{2,1,0:T(8,128)(2,1)} %get-tuple-element.71.attended), calls=%async_computation.3 | async-start | bytes 786432 | tf_op jit(solution)/shard_map/all_to_all | solution.py:572
  258.0 46.7 %all-to-all-start.4 = ((bf16[16,64,768]{2,1,0:T(8,128)(2,1)}), bf16[16,64,768]{2,1,0:T(8,128)(2,1)S(1)}, u32[]{:S(2)}, u32[]{:S(2)}) async-start(bf16[16,64,768]{2,1,0:T(8,128)(2,1)} %bitcast.130), calls=%async_computation.4 | async-start | bytes 3145728 | tf_op jit(solution)/shard_map/all_to_all | solution.py:557
  304.7 48.8 %all-to-all-start.6 = ((bf16[16,64,768]{2,1,0:T(8,128)(2,1)}), bf16[16,64,768]{2,1,0:T(8,128)(2,1)S(1)}, u32[]{:S(2)}, u32[]{:S(2)}) async-start(bf16[16,64,768]{2,1,0:T(8,128)(2,1)} %bitcast.133), calls=%async_computation.6 | async-start | bytes 3145728 | tf_op jit(solution)/shard_map/all_to_all | solution.py:557
  353.6 41.9 %all-to-all-start.5 = ((bf16[16,64,768]{2,1,0:T(8,128)(2,1)}), bf16[16,64,768]{2,1,0:T(8,128)(2,1)S(1)}, u32[]{:S(2)}, u32[]{:S(2)}) async-start(bf16[16,64,768]{2,1,0:T(8,128)(2,1)} %bitcast.132), calls=%async_computation.5 | async-start | bytes 3145728 | tf_op jit(solution)/shard_map/all_to_all | solution.py:557
  395.5 41.9 %all-to-all-start.7 = ((bf16[16,64,768]{2,1,0:T(8,128)(2,1)}), bf16[16,64,768]{2,1,0:T(8,128)(2,1)S(1)}, u32[]{:S(2)}, u32[]{:S(2)}) async-start(bf16[16,64,768]{2,1,0:T(8,128)(2,1)} %bitcast.128), calls=%async_computation.7 | async-start | bytes 3145728 | tf_op jit(solution)/shard_map/all_to_all | solution.py:557
  555.6 41.6 %all-to-all-start.10 = ((bf16[16,64,768]{2,1,0:T(8,128)(2,1)}), bf16[16,64,768]{2,1,0:T(8,128)(2,1)S(1)}, u32[]{:S(2)}, u32[]{:S(2)}) async-start(bf16[16,64,768]{2,1,0:T(8,128)(2,1)} %bitcast.131), calls=%async_computation.10 | async-start | bytes 3145728 | tf_op jit(solution)/shard_map/all_to_all | solution.py:557
  605.3 12.8 %all-to-all-start.11 = ((bf16[4,192,256]{2,1,0:T(8,128)(2,1)}), bf16[4,192,256]{2,1,0:T(8,128)(2,1)S(1)}, u32[]{:S(2)}, u32[]{:S(2)}) async-start(bf16[4,192,256]{2,1,0:T(8,128)(2,1)} %get-tuple-element.103), calls=%async_computation.11 | async-start | bytes 786432 | tf_op jit(solution)/shard_map/all_to_all | solution.py:572
  608.7 35.1 %collective-permute-start.9 = (bf16[256,768]{1,0:T(8,128)(2,1)S(1)}, bf16[256,768]{1,0:T(8,128)(2,1)S(1)}, u32[]{:S(2)}, u32[]{:S(2)}) collective-permute-start(bf16[256,768]{1,0:T(8,128)(2,1)S(1)} %copy-done.18), channel_id=1, source_target_pairs={{0,0},{16,1},{1,2},{17,3},{4,4},{20,5},{5,6},{21,7},{8,8},{24,9},{... | collective-permute-start | bytes 1179656 | tf_op jit(solution)/shard_map/ppermute | solution.py:545
  609.4 109.1 %collective-permute-start.20 = (bf16[768,3072]{1,0:T(8,128)(2,1)}, bf16[768,3072]{1,0:T(8,128)(2,1)}, u32[]{:S(2)}, u32[]{:S(2)}) collective-permute-start(bf16[768,3072]{1,0:T(8,128)(2,1)} %get-tuple-element.82.refs_0_), channel_id=1, source_target_pairs={{0,16},{1,17},{2,18},{3,19},{4,20},{5,21},{6,22},{7,23},{8,24},{9,... | collective-permute-start | bytes 14155784 | tf_op jit(solution)/shard_map/ppermute | solution.py:839
  616.8 102.4 %collective-permute-start.19 = (bf16[768,3072]{1,0:T(8,128)(2,1)}, bf16[768,3072]{1,0:T(8,128)(2,1)}, u32[]{:S(2)}, u32[]{:S(2)}) collective-permute-start(bf16[768,3072]{1,0:T(8,128)(2,1)} %get-tuple-element.97.refs_0_), channel_id=1, source_target_pairs={{16,0},{17,1},{18,2},{19,3},{20,4},{21,5},{22,6},{23,7},{24,8},{25... | collective-permute-start | bytes 14155784 | tf_op jit(solution)/shard_map/ppermute | solution.py:839
  618.1 50.3 %all-to-all-start.13 = ((bf16[8,96,640]{2,1,0:T(8,128)(2,1)}), bf16[8,96,640]{2,1,0:T(8,128)(2,1)S(1)}, u32[]{:S(2)}, u32[]{:S(2)}) async-start(bf16[8,96,640]{2,1,0:T(8,128)(2,1)} %bitcast.53), calls=%async_computation.13 | async-start | bytes 1966080 | tf_op jit(solution)/shard_map/all_to_all | solution.py:565
  639.3 21.0 %collective-permute-start.21 = (bf16[2,256,768]{2,1,0:T(8,128)(2,1)}, bf16[2,256,768]{2,1,0:T(8,128)(2,1)S(1)}, u32[]{:S(2)}, u32[]{:S(2)}) collective-permute-start(bf16[2,256,768]{2,1,0:T(8,128)(2,1)} %get-tuple-element.105.after), channel_id=1, source_target_pairs={{0,16},{16,0},{1,17},{17,1},{2,18},{18,2},{3,19},{19,3},{4,20},{20... | collective-permute-start | bytes 2359304 | tf_op jit(solution)/shard_map/ppermute | solution.py:522
  642.5 13.1 %collective-permute-start.14 = (bf16[256,768]{1,0:T(8,128)(2,1)S(1)}, bf16[256,768]{1,0:T(8,128)(2,1)S(1)}, u32[]{:S(2)}, u32[]{:S(2)}) collective-permute-start(bf16[256,768]{1,0:T(8,128)(2,1)S(1)} %copy-done.18), channel_id=1, source_target_pairs={{2,0},{18,1},{3,2},{19,3},{6,4},{22,5},{7,6},{23,7},{10,8},{26,9},... | collective-permute-start | bytes 1179656 | tf_op jit(solution)/shard_map/ppermute | solution.py:545
  643.8 15.1 %collective-permute-start.13 = (bf16[256,768]{1,0:T(8,128)(2,1)}, bf16[256,768]{1,0:T(8,128)(2,1)S(1)}, u32[]{:S(2)}, u32[]{:S(2)}) collective-permute-start(bf16[256,768]{1,0:T(8,128)(2,1)} %get-tuple-element.76), channel_id=1, source_target_pairs={{0,16},{16,17},{1,18},{17,19},{4,20},{20,21},{5,22},{21,23},{8,24}... | collective-permute-start | bytes 1179656 | tf_op jit(solution)/shard_map/ppermute | solution.py:545
  655.6 98.5 %collective-permute-start.30 = (bf16[3072,768]{1,0:T(8,128)(2,1)}, bf16[3072,768]{1,0:T(8,128)(2,1)}, u32[]{:S(2)}, u32[]{:S(2)}) collective-permute-start(bf16[3072,768]{1,0:T(8,128)(2,1)} %get-tuple-element.116), channel_id=1, source_target_pairs={{0,16},{1,17},{2,18},{3,19},{4,20},{5,21},{6,22},{7,23},{8,24},{9,... | collective-permute-start | bytes 14155784 | tf_op jit(solution)/shard_map/ppermute | solution.py:839
  659.0 96.4 %collective-permute-start.29 = (bf16[3072,768]{1,0:T(8,128)(2,1)}, bf16[3072,768]{1,0:T(8,128)(2,1)}, u32[]{:S(2)}, u32[]{:S(2)}) collective-permute-start(bf16[3072,768]{1,0:T(8,128)(2,1)} %get-tuple-element.115), channel_id=1, source_target_pairs={{16,0},{17,1},{18,2},{19,3},{20,4},{21,5},{22,6},{23,7},{24,8},{25... | collective-permute-start | bytes 14155784 | tf_op jit(solution)/shard_map/ppermute | solution.py:839
  668.4 27.1 %all-to-all-start.12 = ((bf16[8,96,640]{2,1,0:T(8,128)(2,1)}), bf16[8,96,640]{2,1,0:T(8,128)(2,1)S(1)}, u32[]{:S(2)}, u32[]{:S(2)}) async-start(bf16[8,96,640]{2,1,0:T(8,128)(2,1)} %bitcast.140), calls=%async_computation.12 | async-start | bytes 1966080 | tf_op jit(solution)/shard_map/all_to_all | solution.py:565
  672.1 27.9 %collective-permute-start.27 = (bf16[768,896]{1,0:T(8,128)(2,1)}, bf16[768,896]{1,0:T(8,128)(2,1)}, u32[]{:S(2)}, u32[]{:S(2)}) collective-permute-start(bf16[768,896]{1,0:T(8,128)(2,1)} %get-tuple-element.113), channel_id=1, source_target_pairs={{16,0},{17,1},{18,2},{19,3},{20,4},{21,5},{22,6},{23,7},{24,8},{25... | collective-permute-start | bytes 4128776 | tf_op jit(solution)/shard_map/ppermute | solution.py:847
  696.5 13.7 %all-to-all-start.14 = ((f32[4,48,640]{2,1,0:T(8,128)}), f32[4,48,640]{2,1,0:T(8,128)S(1)}, u32[]{:S(2)}, u32[]{:S(2)}) async-start(f32[4,48,640]{2,1,0:T(8,128)} %pad_maximum_fusion), calls=%async_computation.14 | async-start | bytes 983040 | tf_op jit(solution)/shard_map/all_to_all | solution.py:572
  700.0 14.1 %collective-permute-start.15 = (bf16[256,768]{1,0:T(8,128)(2,1)}, bf16[256,768]{1,0:T(8,128)(2,1)}, u32[]{:S(2)}, u32[]{:S(2)}) collective-permute-start(bf16[256,768]{1,0:T(8,128)(2,1)} %get-tuple-element.76), channel_id=1, source_target_pairs={{2,16},{18,17},{3,18},{19,19},{6,20},{22,21},{7,22},{23,23},{10,24... | collective-permute-start | bytes 1179656 | tf_op jit(solution)/shard_map/ppermute | solution.py:545
  710.2 65.1 %all-to-all-start.15 = ((bf16[16,48,896]{2,1,0:T(8,128)(2,1)}), bf16[16,48,896]{2,1,0:T(8,128)(2,1)S(1)}, u32[]{:S(2)}, u32[]{:S(2)}) async-start(bf16[16,48,896]{2,1,0:T(8,128)(2,1)} %bitcast.58), calls=%async_computation.15 | async-start | bytes 2752512 | tf_op jit(solution)/shard_map/all_to_all | solution.py:565
  715.2 53.0 %collective-permute-start.24 = (bf16[256,768]{1,0:T(8,128)(2,1)S(1)}, bf16[256,768]{1,0:T(8,128)(2,1)S(1)}, u32[]{:S(2)}, u32[]{:S(2)}) collective-permute-start(bf16[256,768]{1,0:T(8,128)(2,1)S(1)} %copy-done.11), channel_id=1, source_target_pairs={{0,16},{16,17},{1,18},{17,19},{4,20},{20,21},{5,22},{21,23},{8,24}... | collective-permute-start | bytes 1179656 | tf_op jit(solution)/shard_map/ppermute | solution.py:545
  718.5 50.8 %collective-permute-start.26 = (bf16[256,768]{1,0:T(8,128)(2,1)S(1)}, bf16[256,768]{1,0:T(8,128)(2,1)S(1)}, u32[]{:S(2)}, u32[]{:S(2)}) collective-permute-start(bf16[256,768]{1,0:T(8,128)(2,1)S(1)} %copy-done.11), channel_id=1, source_target_pairs={{2,16},{18,17},{3,18},{19,19},{6,20},{22,21},{7,22},{23,23},{10,24... | collective-permute-start | bytes 1179656 | tf_op jit(solution)/shard_map/ppermute | solution.py:545
  719.2 26.7 %collective-permute-start.22 = (bf16[256,768]{1,0:T(8,128)(2,1)S(1)}, bf16[256,768]{1,0:T(8,128)(2,1)S(1)}, u32[]{:S(2)}, u32[]{:S(2)}) collective-permute-start(bf16[256,768]{1,0:T(8,128)(2,1)S(1)} %copy-done.25), channel_id=1, source_target_pairs={{0,1},{1,0},{2,3},{3,2},{4,5},{5,4},{6,7},{7,6},{8,9},{9,8},{10,11... | collective-permute-start | bytes 1179656 | tf_op jit(solution)/shard_map/ppermute | solution.py:526
  749.6 18.6 %collective-permute-start.23 = (bf16[256,768]{1,0:T(8,128)(2,1)}, bf16[256,768]{1,0:T(8,128)(2,1)}, u32[]{:S(2)}, u32[]{:S(2)}) collective-permute-start(bf16[256,768]{1,0:T(8,128)(2,1)} %first_norm_grad.3.after), channel_id=1, source_target_pairs={{0,0},{16,1},{1,2},{17,3},{4,4},{20,5},{5,6},{21,7},{8,8},{24,9},{... | collective-permute-start | bytes 1179656 | tf_op jit(solution)/shard_map/ppermute | solution.py:545
  754.1 15.2 %collective-permute-start.25 = (bf16[256,768]{1,0:T(8,128)(2,1)}, bf16[256,768]{1,0:T(8,128)(2,1)S(1)}, u32[]{:S(2)}, u32[]{:S(2)}) collective-permute-start(bf16[256,768]{1,0:T(8,128)(2,1)} %first_norm_grad.3.after), channel_id=1, source_target_pairs={{2,0},{18,1},{3,2},{19,3},{6,4},{22,5},{7,6},{23,7},{10,8},{26,9},... | collective-permute-start | bytes 1179656 | tf_op jit(solution)/shard_map/ppermute | solution.py:545
  (49 other events, 531.2 us)
Sparse Core Ops, SparseCore 0:
  10.8 60.1 all-gather.2

commit v3 on v2

--- a/solution.py
+++ b/solution.py
@@ -688,6 +688,274 @@
     )(blocks)
 
 
+OFFSETS = [(step, place) for place in (0, 3, 1, 2) for step in range(4)]
+SENDS = (4, 5, 6, 7, 12, 13, 14, 15, 8, 9, 10, 11, 1, 2, 3)
+BATCH = 4
+REMOTE = pl.DeviceIdType.MESH
+
+
+def across(index, step):
+    return (index, index + 1 - 2 * (index % 2), (index + 2) % 4, 3 - index)[step]
+
+
+def expert_layer(mode, section, *refs):
+    forward = mode != "backward"
+    backward = mode != "forward"
+    refs = list(refs)
+
+    def take(count):
+        taken = refs[:count]
+        del refs[:count]
+        return taken
+
+    weights = take(4)
+    outgoing = take(2 if mode == "both" else 1)
+    if mode == "backward":
+        saved_rows, saved_activation, saved_slope, unused, unused_1 = take(5)
+    returned = take(len(outgoing))
+    if mode == "forward":
+        kept_rows, kept_activation, kept_slope = take(3)
+    else:
+        grad_in, grad_down = take(2)
+    arrived = take(len(outgoing))
+    finished = take(len(outgoing))
+    w_in, w_down, activation, slope, totals = take(5)
+    send_sem, recv_sem, back_send, back_recv, load_sem = take(5)
+    if backward:
+        parts, staged, part_send, part_recv, out_sem = take(5)
+
+    core = lax.axis_index("section")
+    expert = lax.axis_index("expert")
+    place = 2 * lax.axis_index("zhi") + lax.axis_index("zlo")
+    me = expert * 4 + place
+    hidden = w_in.shape[1]
+    slot_rows, features = arrived[0].shape[1:]
+    rows_in_batch = BATCH * slot_rows
+    tile = tile_of(hidden)
+    tiles = hidden // tile
+    peers = []
+    ranks = []
+    for step, move in OFFSETS:
+        to_expert, to_place = across(expert, step), across(place, move)
+        ranks.append(to_expert * 4 + to_place)
+        peers.append({"expert": to_expert, "zhi": to_place // 2, "zlo": to_place % 2})
+
+    loads = []
+
+    def load(source, target, index):
+        copy = pltpu.make_async_copy(source, target, load_sem.at[index])
+        copy.start()
+        loads.append(copy)
+
+    @pl.when(core == section)
+    def own_weights():
+        pltpu.make_async_copy(weights[0], w_in, load_sem.at[0]).start()
+        pltpu.make_async_copy(weights[1], w_down, load_sem.at[1]).start()
+
+    @pl.when(core != section)
+    def other_weights():
+        pltpu.make_async_copy(weights[2], w_in, load_sem.at[0]).start()
+        pltpu.make_async_copy(weights[3], w_down, load_sem.at[1]).start()
+
+    if mode == "backward":
+        load(saved_activation, activation, 2)
+        load(saved_slope, slope, 3)
+
+    barrier = pltpu.get_barrier_semaphore()
+    for peer in peers[1:] + ([{"section": 1 - core}] if backward else []):
+        pl.semaphore_signal(barrier, inc=1, device_id=peer, device_id_type=REMOTE)
+    pl.semaphore_wait(barrier, 16 if backward else 15)
+
+    def remote(source, target, send, recv, peer):
+        return pltpu.make_async_remote_copy(
+            src_ref=source, dst_ref=target, send_sem=send, recv_sem=recv, device_id=peer, device_id_type=REMOTE
+        )
+
+    sent = []
+    for slot in SENDS:
+        for kind, block in enumerate(outgoing):
+            copy = remote(block.at[ranks[slot]], arrived[kind].at[slot], send_sem.at[kind, slot],
+                          recv_sem.at[kind, slot], peers[slot])
+            copy.start()
+            sent.append(copy)
+    for kind, block in enumerate(outgoing):
+        arrived[kind][0] = block[me]
+
+    pltpu.make_async_copy(weights[0], w_in, load_sem.at[0]).wait()
+    pltpu.make_async_copy(weights[1], w_down, load_sem.at[1]).wait()
+    for copy in loads:
+        copy.wait()
+
+    saves = []
+    for batch in range(len(OFFSETS) // BATCH):
+        slots = range(batch * BATCH, (batch + 1) * BATCH)
+        mine = slice(batch * rows_in_batch, (batch + 1) * rows_in_batch)
+        for slot in slots:
+            for kind in range(len(outgoing)):
+                if slot:
+                    remote(arrived[kind].at[slot], arrived[kind].at[slot], send_sem.at[kind, slot],
+                           recv_sem.at[kind, slot], peers[slot]).wait_recv()
+
+        def block_of(kind):
+            return arrived[kind][slots[0] : slots[-1] + 1].reshape(rows_in_batch, features)
+
+        def one_tile(index, unused):
+            spot = pl.ds(pl.multiple_of(index * tile, tile), tile)
+            if forward:
+                values = mm(block_of(0), w_in[:, spot])
+                half = 0.5 * (1.0 + lax.erf(values * 0.7071067811865476))
+                bell = jnp.exp(-0.5 * values * values) * 0.3989422804014327
+                raised = (values * half).astype(BF16)
+                steep = half + values * bell
+                activation[mine, spot] = raised
+                if mode == "forward":
+                    slope[mine, spot] = steep.astype(BF16)
+                totals[0] += mm(raised, w_down[spot, :])
+            else:
+                steep = slope[mine, spot].astype(F32)
+            if backward:
+                lowered = (mm(block_of(len(outgoing) - 1), w_down[spot, :], NT) * steep).astype(BF16)
+                slope[mine, spot] = lowered
+                totals[len(outgoing) - 1] += mm(lowered, w_in[:, spot], NT)
+            return unused
+
+        totals[...] = jnp.zeros_like(totals)
+        lax.fori_loop(0, tiles, one_tile, 0)
+        for kind in range(len(outgoing)):
+            finished[kind][slots[0] : slots[-1] + 1] = (
+                totals[kind].astype(BF16).reshape(BATCH, slot_rows, features)
+            )
+        for slot in slots:
+            for kind in range(len(outgoing)):
+                if slot:
+                    copy = remote(finished[kind].at[slot], returned[kind].at[me], back_send.at[kind, slot],
+                                  back_recv.at[kind, slot], peers[slot])
+                    copy.start()
+                    sent.append(copy)
+                else:
+                    returned[kind][me] = finished[kind][0]
+        if mode == "forward":
+            for index, (source, target) in enumerate(((activation, kept_activation), (slope, kept_slope))):
+                copy = pltpu.make_async_copy(
+                    source.at[mine, :], target.at[mine, :], load_sem.at[2 + 2 * batch + index]
+                )
+                copy.start()
+                saves.append(copy)
+    if mode == "forward":
+        kept_rows[...] = arrived[0][...]
+
+    if backward:
+        count = slot_rows * len(OFFSETS)
+        grads = arrived[len(outgoing) - 1]
+        inputs = arrived[0] if forward else saved_rows
+        partner = {"section": 1 - core}
+
+        def share_copy(index):
+            return remote(parts.at[index], parts.at[index], part_send.at[index], part_recv.at[index], partner)
+
+        def out_copy(index):
+            spot = pl.ds(index // 2 * tile, tile)
+            target = grad_down.at[spot, :] if index % 2 else grad_in.at[:, spot]
+            return pltpu.make_async_copy(staged.at[index % 2], target, out_sem.at[index])
+
+        for index in range(2 * tiles):
+            spot = pl.ds(index // 2 * tile, tile)
+            if index % 2:
+                value = mm(activation[:, spot], grads[...].reshape(count, features), TN)
+            else:
+                value = mm(inputs[...].reshape(count, features), slope[:, spot], TN)
+
+            @pl.when(core != section)
+            def give():
+                parts[index] = value.astype(BF16)
+                share_copy(index).start()
+
+            @pl.when(core == section)
+            def keep():
+                share_copy(index).wait_recv()
+                if index >= 2:
+                    out_copy(index - 2).wait()
+                staged[index % 2] = value + parts[index].astype(F32)
+                out_copy(index).start()
+
+    for slot in range(1, len(OFFSETS)):
+        for kind in range(len(outgoing)):
+            remote(finished[kind].at[slot], returned[kind].at[ranks[slot]], back_send.at[kind, slot],
+                   back_recv.at[kind, slot], peers[slot]).wait_recv()
+    for copy in sent:
+        copy.wait_send()
+    for copy in saves:
+        copy.wait()
+    if backward:
+        @pl.when(core != section)
+        def given():
+            for index in range(2 * tiles):
+                share_copy(index).wait_send()
+
+        @pl.when(core == section)
+        def stored():
+            for index in range(2 * tiles - 2, 2 * tiles):
+                out_copy(index).wait()
+
+
+def run_expert_layer(mode, section, weights, outgoing, saved=(), grads=()):
+    ranks, slot_rows, features = outgoing[0].shape
+    hidden = weights[0].shape[1]
+    count = ranks * slot_rows
+    tile = tile_of(hidden)
+    kinds = len(outgoing)
+    anywhere = pl.BlockSpec(memory_space=pl.ANY)
+    local = pl.BlockSpec(memory_space=pltpu.VMEM)
+    block = shape((ranks, slot_rows, features), BF16)
+    wide = shape((count, hidden), BF16)
+    in_specs = [anywhere] * 4 + [local] * kinds
+    operands = [*weights, *outgoing]
+    out_shape = [block] * kinds
+    out_specs = [local] * kinds
+    aliases = {}
+    if mode == "forward":
+        out_shape += [block, wide, wide]
+        out_specs += [local, anywhere, anywhere]
+    else:
+        out_shape += [shape((features, hidden), F32), shape((hidden, features), F32)]
+        out_specs += [anywhere, anywhere]
+    if mode == "backward":
+        aliases = {len(operands) + 3: kinds, len(operands) + 4: kinds + 1}
+        operands += [*saved, *grads]
+        in_specs += [local, anywhere, anywhere, anywhere, anywhere]
+    scratch = [pltpu.VMEM(block.shape, BF16)] * (2 * kinds) + [
+        pltpu.VMEM((features, hidden), BF16), pltpu.VMEM((hidden, features), BF16),
+        pltpu.VMEM((count, hidden), BF16), pltpu.VMEM((count, hidden), BF16),
+        pltpu.VMEM((kinds, BATCH * slot_rows, features), F32),
+        pltpu.SemaphoreType.DMA((kinds, ranks)), pltpu.SemaphoreType.DMA((kinds, ranks)),
+        pltpu.SemaphoreType.DMA((kinds, ranks)), pltpu.SemaphoreType.DMA((kinds, ranks)),
+        pltpu.SemaphoreType.DMA((10,)),
+    ]
+    if mode != "forward":
+        pieces = 2 * hidden // tile
+        scratch += [
+            pltpu.VMEM((pieces, features, tile), BF16), pltpu.VMEM((2, features, tile), F32),
+            pltpu.SemaphoreType.DMA((pieces,)), pltpu.SemaphoreType.DMA((pieces,)),
+            pltpu.SemaphoreType.DMA((pieces,)),
+        ]
+    return pl.pallas_call(
+        functools.partial(expert_layer, mode, section),
+        name="expert_layer_" + mode,
+        in_specs=in_specs,
+        out_specs=out_specs,
+        out_shape=out_shape,
+        scratch_shapes=scratch,
+        input_output_aliases=aliases,
+        compiler_params=pltpu.CompilerParams(
+            collective_id={"forward": 1, "both": 2, "backward": 3}[mode], has_side_effects=True,
+            vmem_limit_bytes=VMEM_LIMIT,
+        ),
+        cost_estimate=pl.CostEstimate(
+            flops=8 * kinds * count * features * hidden, bytes_accessed=160 << 20, transcendentals=0
+        ),
+    )(*operands)
+
+
 def per_device(inputs, cotangent, qkv_shard, out_shard, router_shard, gain_shard, table_shard,
                w_expert_in, w_expert_out, routes):
     core = lax.axis_index("section")
@@ -752,6 +1020,15 @@
     w_in_other = flip(w_in)
     w_down_other = flip(w_down)
 
+    fused = lax.axis_size("expert") == 4 and features == tile_of(w_in.shape[1])
+    expert_weights = (w_in, w_down, w_in_other, w_down_other)
+
+    def by_rank(block):
+        return block.reshape(ranks, capacity, features)
+
+    def by_slot(block):
+        return block.reshape(slots, features)
+
     weights = []
     for section in range(2):
         is_own = core == section
@@ -762,7 +1039,8 @@
         table = table.reshape(ranks, shard_rows, head_count)[:, :table_rows].reshape(buckets, head_count)
         weights.append((
             early[section], router, gains[0:1], gains[1:2], table,
-            jnp.where(is_own, w_in, w_in_other), jnp.where(is_own, w_down, w_down_other),
+            None if fused else jnp.where(is_own, w_in, w_in_other),
+            None if fused else jnp.where(is_own, w_down, w_down_other),
         ))
 
     bias_scratch = [
@@ -797,9 +1075,21 @@
              shape((span, features), BF16), shape((span, 128), F32)],
             [attended, stream, w_out, gain_two, router, route_rows], flops=1 << 30,
         )
-        arrived = exchange(outgoing, experts, capacity)
-        activation, slope, produced = run_expert_forward(arrived, expert_in, expert_down)
-        returned = exchange(produced, experts, capacity)
+        if fused and section == 0:
+            returned, arrived, activation, slope = run_expert_layer(
+                "forward", section, expert_weights, [by_rank(outgoing)])
+            returned = by_slot(returned)
+        elif fused:
+            (spread,) = call(spread_grads, "spread_grads", [shape((slots, features), BF16)],
+                             [given, aux], flops=1 << 30)
+            returned, returned_grad, grad_in, grad_down = run_expert_layer(
+                "both", section, expert_weights, [by_rank(outgoing), by_rank(spread)])
+            returned = by_slot(returned)
+            arrived = activation = slope = None
+        else:
+            arrived = exchange(outgoing, experts, capacity)
+            activation, slope, produced = run_expert_forward(arrived, expert_in, expert_down)
+            returned = exchange(produced, experts, capacity)
         result, difference = call(
             combine, "combine", [shape((span, features), BF16), shape((span, features), F32)],
             [returned, aux, middle], flops=1 << 30,
@@ -825,18 +1115,28 @@
         (stream, outcome, mixed, gathered, stats, attended, middle, normed_two, aux,
          arrived, activation, slope, difference) = states[section]
         route_rows = section_routes[section]
-        (spread,) = call(spread_grads, "spread_grads", [shape((slots, features), BF16)],
-                         [upstream, aux], flops=1 << 30)
-        arrived_grad = exchange(spread, experts, capacity)
+        shares = ()
+        if fused and section == 1:
+            returned = by_slot(returned_grad)
+        else:
+            (spread,) = call(spread_grads, "spread_grads", [shape((slots, features), BF16)],
+                             [upstream, aux], flops=1 << 30)
+        if fused and section == 0:
+            returned, grad_in, grad_down = run_expert_layer(
+                "backward", section, expert_weights, [by_rank(spread)], [arrived, activation, slope],
+                [grad_in, grad_down])
+            returned = by_slot(returned)
+        elif not fused:
+            arrived_grad = exchange(spread, experts, capacity)
+            hidden_grad, rows_grad = run_expert_backward(arrived_grad, expert_in, expert_down, slope)
+            returned = exchange(rows_grad, experts, capacity)
+            expert_states[section] = (arrived, hidden_grad, activation, arrived_grad)
+            wanted = (core != section).astype(jnp.int32).reshape(1)
+            shares = run_weight_partials(wanted, *expert_states[section])
+            partials[section] = [lax.ppermute(part, "section", [(1 - section, section)]) for part in shares]
         if section == 0:
-            waiting, arrived_grad = lax.optimization_barrier((shared_qkv[1], arrived_grad))
+            waiting, returned = lax.optimization_barrier((shared_qkv[1], returned))
             qkv_grads[1] = spread_sum(waiting, ("expert", "zhi"), ranks // 2)
-        hidden_grad, rows_grad = run_expert_backward(arrived_grad, expert_in, expert_down, slope)
-        returned = exchange(rows_grad, experts, capacity)
-        expert_states[section] = (arrived, hidden_grad, activation, arrived_grad)
-        wanted = (core != section).astype(jnp.int32).reshape(1)
-        shares = run_weight_partials(wanted, *expert_states[section])
-        partials[section] = [lax.ppermute(part, "section", [(1 - section, section)]) for part in shares]
         middle_grad, attended_grad, shared_grads[section] = call(
             before_attention, "before_attention",
             [shape((span, features), F32), shape((GROUP, width, span), BF16),
@@ -863,10 +1163,11 @@
         if section == 0:
             leave, waiting = lax.optimization_barrier((leave, shared_qkv[0]))
             qkv_grads[0] = spread_sum(waiting, ("expert", "zhi"), ranks // 2)
-            grad_in = run_weight_totals(
-                core_id, *[(expert_states[which][0], expert_states[which][1], partials[which][0])
-                           for which in range(2)], False, sent)
-            filler = (grad_in,)
+            if not fused:
+                grad_in = run_weight_totals(
+                    core_id, *[(expert_states[which][0], expert_states[which][1], partials[which][0])
+                               for which in range(2)], False, sent)
+                filler = (grad_in,)
         arrived_share = beside(leave)
         (low,) = call(
             first_norm_grad, "first_norm_grad", [shape((span, features), BF16)],
@@ -899,9 +1200,10 @@
 
     section_grads = home_pair(stream_grads, core).astype(F32)
 
-    grad_down = run_weight_totals(
-        core_id, *[(expert_states[which][2], expert_states[which][3], partials[which][1])
-                   for which in range(2)], True, stream_grads[0])
+    if not fused:
+        grad_down = run_weight_totals(
+            core_id, *[(expert_states[which][2], expert_states[which][3], partials[which][1])
+                       for which in range(2)], True, stream_grads[0])
     return (
         section_outputs[None, :, None],
         section_grads[None, :, None],

time: 797 us -> 707 us (0.89)
  Pallas kernels: 236 us -> 429 us
  waiting for transfers between devices: 237 us -> 98.7 us
  blocking collectives: 110 us -> 34.7 us
  starting transfers between devices: 129 us -> 70.4 us
  other arithmetic: 32.4 us -> 17.7 us
    pallas_call x8 -> x3, Pallas kernels: 113 us -> 307 us  [run_expert_layer(): pl.pallas_call(functools.partial(expert_layer, mode, section), name='expe...]
    all_to_all x6 -> x0, waiting for transfers between devices: 158 us -> none  [exchange(): lax.all_to_all(block.reshape(experts, capacity, features), RANKS, split_a...]
    all_to_all x2 -> x0, blocking collectives: 86.5 us -> none  [exchange(): lax.all_to_all(block.reshape(experts, capacity, features), RANKS, split_a...]
    all_to_all x6 -> x0, starting transfers between devices: 31.2 us -> none  [exchange(): lax.all_to_all(block.reshape(experts, capacity, features), RANKS, split_a...]
    select_n x2 -> x0, other arithmetic: 15.9 us -> none  [the longest x1 7.95 us: per_device(): jnp.where(is_own, w_down, w_down_other)]
    all_to_all x3 -> x2, starting transfers between devices: 21.1 us -> 6.93 us  [regroup(): lax.all_to_all(block, ('zlo', 'section'), split_axis=0, concat_axis=0, ti...]
    ppermute x4 -> x0, starting transfers between devices: 13.3 us -> none  [per_device(): lax.ppermute(part, 'section', [(1 - section, section)])]
    all_to_all x2 -> x3, blocking collectives: 23.4 us -> 34.7 us  [regroup(): lax.all_to_all(block, ('zlo', 'section'), split_axis=0, concat_axis=0, ti...]
  transfers between devices with their start and end apart: 44 -> 33, of which waited for: 16 -> 13; matrix products, arithmetic and copies ran while one was open for 6% -> 4% of each run, Pallas kernels for 19% -> 9%
where the time goes in v3:
time: 707 us; the launch traced here: 697 us
  Pallas kernels  429 us (61%)
  waiting for transfers between devices  98.7 us (14%)
  starting transfers between devices  70.4 us (10%)
  blocking collectives  34.7 us (5%)
  local copies, waits for them, and re-layouts  31.5 us (4%)
  other arithmetic  17.7 us (3%)
  between operations  14.8 us (2%)
    pallas_call x3, Pallas kernels, run_expert_layer(): pl.pallas_call(functools.partial(expert_layer, mode, section), name='expe...  307 us
    pallas_call x14, Pallas kernels, call(): pl.pallas_call(body, name=name, in_specs=specs, out_specs=[pl.BlockSpec(m...  94.8 us
    ppermute x4, waiting for transfers between devices, beside(): return lax.ppermute(block, 'zlo', FLIP)  43.4 us
    all_to_all x3, blocking collectives, regroup(): lax.all_to_all(block, ('zlo', 'section'), split_axis=0, concat_axis=0, ti...  34.7 us
    pallas_call x1, Pallas kernels, run_gather_columns(): pl.pallas_call(gather_columns, name='gather_columns', in_specs=[pl.BlockS...  26.8 us
    all_to_all x3, waiting for transfers between devices, spread_sum(): lax.all_to_all(block.reshape(parts, rows // parts, columns), axes, split_...  24.4 us
    ppermute x8, starting transfers between devices, to_home(): return lax.ppermute(block, ('section', 'zhi', 'zlo'), pairs)  20.9 us
    unnamed x52, local copies, waits for them, and re-layouts  18.5 us
  transfers between devices with their start and end apart: 33, of which 13 were waited for; matrix products, arithmetic and copies ran while one was open for 4% of the time, Pallas kernels for 9%

profile of v3, /device:TPU:0, one launch (start us, length us, event | category | flops | bytes accessed | tf_op | source)
XLA Modules:
  0.0 696.8 jit_solution(9725732958824991980)
XLA Ops:
  9.1 16.2 %collective-permute-start.4 = (bf16[256,768]{1,0:T(8,128)(2,1)S(1)}, bf16[256,768]{1,0:T(8,128)(2,1)}, u32[]{:S(2)}, u32[]{:S(2)}) collective-permute-start(bf16[256,768]{1,0:T(8,128)(2,1)S(1)} %collective-permute-done.2.own), channel_id=1, source_target_pairs={{0,1},{1,0},{2,3},{3,2},{4,5},{5,4},{6,7},{7,6},{8,9},{9,8},{10,11... | collective-permute-start | bytes 1179656 | tf_op jit(solution)/shard_map/ppermute | solution.py:526
  28.7 26.8 %gather_columns.1 = bf16[2,16,48,640]{3,2,1,0:T(8,128)(2,1)S(1)} custom-call(bf16[4,48,640]{2,1,0:T(8,128)(2,1)S(1)} %fusion.4.blocks), custom_call_target="tpu_custom_call" | custom-call | bytes 41943040 | tf_op jit(solution)/shard_map/gather_columns/pallas_call | solution.py:670
  59.5 8.7 %attention_forward.2 = (bf16[4,192,256]{2,1,0:T(8,128)(2,1)}, bf16[1024,576]{1,0:T(8,128)(2,1)}, bf16[1024,768]{1,0:T(8,128)(2,1)}, f32[8,1024]{1,0:T(8,128)}) custom-call(s32[9]{0:T(128)} %stack.51.ids, bf16[256,768]{1,0:T(8,128)(2,1)} %copy-done.7, bf16[256,768]{1,0:T(8,128)(2,1)} %copy-done.15, bf16[256,768]{1,0:T(8,128)(2,1)} %collective-permute-done.4.side, ...), custom_call_target="tpu_custom_call" | custom-call | flops 4294967296 | bytes 5737472 | tf_op jit(solution)/shard_map/attention_forward/pallas_call | solution.py:51
  68.2 11.6 %all_to_all.40.attended = bf16[4,192,256]{2,1,0:T(8,128)(2,1)} all-to-all(bf16[4,192,256]{2,1,0:T(8,128)(2,1)} %get-tuple-element.60.attended), channel_id=1, replica_groups=mesh['section'=2,'expert'=4,'zhi'=2,'zlo'=2] {'zlo','section'}, dimensions={0} | all-to-all | bytes 786432 | tf_op jit(solution)/shard_map/all_to_all | solution.py:572
  80.9 5.0 collective-permute-start.8
  92.6 4.7 after_attention.2
  97.3 83.1 %expert_layer_forward.1 = (bf16[16,64,768]{2,1,0:T(8,128)(2,1)}, bf16[16,64,768]{2,1,0:T(8,128)(2,1)}, bf16[1024,3072]{1,0:T(8,128)(2,1)}, bf16[1024,3072]{1,0:T(8,128)(2,1)}) custom-call(bf16[768,3072]{1,0:T(8,128)(2,1)} %bitcast.118, bf16[3072,768]{1,0:T(8,128)(2,1)} %bitcast.122, bf16[768,3072]{1,0:T(8,128)(2,1)} %collective-permute-done.refs_2_, ...), custom_call_target="tpu_custom_call" | custom-call | flops 19327352832 | bytes 167772160 | tf_op jit(solution)/shard_map/expert_layer_forward/pallas_call | solution.py:941
  184.1 11.0 %collective-permute-done.11.side = bf16[256,768]{1,0:T(8,128)(2,1)S(1)} collective-permute-done((bf16[256,768]{1,0:T(8,128)(2,1)}, bf16[256,768]{1,0:T(8,128)(2,1)S(1)}, u32[]{:S(2)}, u32[]{:S(2)}) %collective-permute-start.11) | collective-permute-done | bytes 393248 | tf_op jit(solution)/shard_map/ppermute | solution.py:526
  197.6 8.7 %attention_forward.3 = (bf16[4,192,256]{2,1,0:T(8,128)(2,1)}, bf16[1024,576]{1,0:T(8,128)(2,1)}, bf16[1024,768]{1,0:T(8,128)(2,1)}, f32[8,1024]{1,0:T(8,128)}) custom-call(s32[9]{0:T(128)} %stack.51.ids, bf16[256,768]{1,0:T(8,128)(2,1)} %get-tuple-element.67.own, bf16[256,768]{1,0:T(8,128)(2,1)} %copy-done.18, bf16[256,768]{1,0:T(8,128)(2,1)} %copy-done.17, ...), custom_call_target="tpu_custom_call" | custom-call | flops 4294967296 | bytes 5737472 | tf_op jit(solution)/shard_map/attention_forward/pallas_call | solution.py:51
  212.7 4.5 all-to-all-done.1.attended
  217.9 4.7 after_attention.3
  226.7 148.3 %expert_layer_both.1 = (bf16[16,64,768]{2,1,0:T(8,128)(2,1)}, bf16[16,64,768]{2,1,0:T(8,128)(2,1)}, f32[768,3072]{1,0:T(8,128)}, f32[3072,768]{1,0:T(8,128)}) custom-call(bf16[768,3072]{1,0:T(8,128)(2,1)} %bitcast.119, bf16[3072,768]{1,0:T(8,128)(2,1)} %bitcast.123, bf16[768,3072]{1,0:T(8,128)(2,1)} %collective-permute-done.refs_2_, ...), custom_call_target="tpu_custom_call" | custom-call | flops 38654705664 | bytes 167772160 | tf_op jit(solution)/shard_map/expert_layer_both/pallas_call | solution.py:941
  375.0 3.8 combine.3
  378.8 6.7 before_attention.2
  385.5 11.6 %all_to_all.41.grads = bf16[4,192,256]{2,1,0:T(8,128)(2,1)} all-to-all(bf16[4,192,256]{2,1,0:T(8,128)(2,1)} %get-tuple-element.81), channel_id=1, replica_groups=mesh['section'=2,'expert'=4,'zhi'=2,'zlo'=2] {'zlo','section'}, dimensions={0} | all-to-all | bytes 786432 | tf_op jit(solution)/shard_map/all_to_all | solution.py:572
  397.0 17.3 %attention_backward.2 = (bf16[256,768]{1,0:T(8,128)(2,1)}, bf16[256,768]{1,0:T(8,128)(2,1)}, bf16[2,256,768]{2,1,0:T(8,128)(2,1)}, bf16[768,640]{1,0:T(8,128)(2,1)}) custom-call(s32[9]{0:T(128)} %stack.51.ids, bf16[1024,576]{1,0:T(8,128)(2,1)} %get-tuple-element.76.mixed, f32[8,1024]{1,0:T(8,128)} %get-tuple-element.77.stats, ...), custom_call_target="tpu_custom_call" | custom-call | flops 8589934592 | bytes 7113728 | tf_op jit(solution)/shard_map/attention_backward/pallas_call | solution.py:51
  418.6 10.8 %collective-permute-done.18.arrived = bf16[256,768]{1,0:T(8,128)(2,1)S(1)} collective-permute-done((bf16[256,768]{1,0:T(8,128)(2,1)S(1)}, bf16[256,768]{1,0:T(8,128)(2,1)S(1)}, u32[]{:S(2)}, u32[]{:S(2)}) %collective-permute-start.18) | collective-permute-done | bytes 393248 | tf_op jit(solution)/shard_map/ppermute | solution.py:526
  436.3 76.0 %expert_layer_backward.1 = (bf16[16,64,768]{2,1,0:T(8,128)(2,1)}, f32[768,3072]{1,0:T(8,128)}, f32[3072,768]{1,0:T(8,128)}) custom-call(bf16[768,3072]{1,0:T(8,128)(2,1)} %bitcast.120, bf16[3072,768]{1,0:T(8,128)(2,1)} %bitcast.124, bf16[768,3072]{1,0:T(8,128)(2,1)} %collective-permute-done.refs_2_, ...), custom_call_target="tpu_custom_call", output_to_operand_aliasing={{1}: (8, {}), {2}: (9, {})} | custom-call | flops 19327352832 | bytes 167772160 | tf_op jit(solution)/shard_map/expert_layer_backward/pallas_call | solution.py:941
  512.3 6.7 before_attention.3
  519.0 11.6 %all_to_all.42.grads = bf16[4,192,256]{2,1,0:T(8,128)(2,1)} all-to-all(bf16[4,192,256]{2,1,0:T(8,128)(2,1)} %get-tuple-element.97), channel_id=1, replica_groups=mesh['section'=2,'expert'=4,'zhi'=2,'zlo'=2] {'zlo','section'}, dimensions={0} | all-to-all | bytes 786432 | tf_op jit(solution)/shard_map/all_to_all | solution.py:572
  530.6 4.0 all-to-all-start.5
  534.6 17.3 %attention_backward.3 = (bf16[256,768]{1,0:T(8,128)(2,1)}, bf16[256,768]{1,0:T(8,128)(2,1)}, bf16[2,256,768]{2,1,0:T(8,128)(2,1)}, bf16[768,640]{1,0:T(8,128)(2,1)}) custom-call(s32[9]{0:T(128)} %stack.51.ids, bf16[1024,576]{1,0:T(8,128)(2,1)} %get-tuple-element.74.mixed, f32[8,1024]{1,0:T(8,128)} %get-tuple-element.75.stats, ...), custom_call_target="tpu_custom_call" | custom-call | flops 8589934592 | bytes 7113728 | tf_op jit(solution)/shard_map/attention_backward/pallas_call | solution.py:51
  555.7 4.4 all-to-all-done.5
  567.9 20.0 %all-to-all-done.4 = bf16[8,96,640]{2,1,0:T(8,128)(2,1)S(1)} async-done(((bf16[8,96,640]{2,1,0:T(8,128)(2,1)}), bf16[8,96,640]{2,1,0:T(8,128)(2,1)S(1)}, u32[]{:S(2)}, u32[]{:S(2)}) %all-to-all-start.4) | async-done | bytes 983072 | tf_op jit(solution)/shard_map/all_to_all | solution.py:565
  592.4 4.3 select_convert_fusion
  596.7 4.1 all-to-all-done.6
  610.5 4.3 collective-permute-start.14
  614.8 21.6 %collective-permute-done.20.arrived = bf16[256,768]{1,0:T(8,128)(2,1)S(1)} collective-permute-done((bf16[256,768]{1,0:T(8,128)(2,1)S(1)}, bf16[256,768]{1,0:T(8,128)(2,1)S(1)}, u32[]{:S(2)}, u32[]{:S(2)}) %collective-permute-start.20) | collective-permute-done | bytes 393248 | tf_op jit(solution)/shard_map/ppermute | solution.py:526
  640.1 6.5 collective-permute-done.15
  649.0 8.9 %collective-permute-start.22 = (bf16[256,768]{1,0:T(8,128)(2,1)S(1)}, bf16[256,768]{1,0:T(8,128)(2,1)S(1)}, u32[]{:S(2)}, u32[]{:S(2)}) collective-permute-start(bf16[256,768]{1,0:T(8,128)(2,1)S(1)} %copy-done.9), channel_id=1, source_target_pairs={{0,16},{16,17},{1,18},{17,19},{4,20},{20,21},{5,22},{21,23},{8,24}... | collective-permute-start | bytes 1179656 | tf_op jit(solution)/shard_map/ppermute | solution.py:545
  661.5 9.3 %collective-permute-done.23 = bf16[256,768]{1,0:T(8,128)(2,1)S(1)} collective-permute-done((bf16[256,768]{1,0:T(8,128)(2,1)}, bf16[256,768]{1,0:T(8,128)(2,1)S(1)}, u32[]{:S(2)}, u32[]{:S(2)}) %collective-permute-start.23) | collective-permute-done | bytes 393248 | tf_op jit(solution)/shard_map/ppermute | solution.py:545
  677.2 8.8 %copy.87 = f32[1,1,768,3072]{3,2,1,0:T(8,128)} copy(f32[1,1,768,3072]{3,2,1,0:T(8,128)} %bitcast.82) | data formatting | bytes 18874368
  (161 shorter events, 91.0 us)
Async XLA Ops:
  7.2 72.6 %all-gather.3.cloned.1.call-start = ((), (), s32[]{:S(2)}) async-start(), calls=%async_computation.8 | async-start | bytes 1253376 | tf_op jit(solution)/shard_map/all_gather | solution.py:1017
  7.2 90.0 %collective-permute-start = (bf16[768,3072]{1,0:T(8,128)(2,1)}, bf16[768,3072]{1,0:T(8,128)(2,1)}, u32[]{:S(2)}, u32[]{:S(2)}) collective-permute-start(bf16[768,3072]{1,0:T(8,128)(2,1)} %bitcast.117), channel_id=1, source_target_pairs={{0,16},{16,0},{1,17},{17,1},{2,18},{18,2},{3,19},{19,3},{4,20},{20... | collective-permute-start | bytes 14155784 | tf_op jit(solution)/shard_map/ppermute | solution.py:522
  7.8 89.5 %collective-permute-start.1 = (bf16[3072,768]{1,0:T(8,128)(2,1)}, bf16[3072,768]{1,0:T(8,128)(2,1)}, u32[]{:S(2)}, u32[]{:S(2)}) collective-permute-start(bf16[3072,768]{1,0:T(8,128)(2,1)} %bitcast.121), channel_id=1, source_target_pairs={{0,16},{16,0},{1,17},{17,1},{2,18},{18,2},{3,19},{19,3},{4,20},{20... | collective-permute-start | bytes 14155784 | tf_op jit(solution)/shard_map/ppermute | solution.py:522
  9.1 46.5 %collective-permute-start.4 = (bf16[256,768]{1,0:T(8,128)(2,1)S(1)}, bf16[256,768]{1,0:T(8,128)(2,1)}, u32[]{:S(2)}, u32[]{:S(2)}) collective-permute-start(bf16[256,768]{1,0:T(8,128)(2,1)S(1)} %collective-permute-done.2.own), channel_id=1, source_target_pairs={{0,1},{1,0},{2,3},{3,2},{4,5},{5,4},{6,7},{7,6},{8,9},{9,8},{10,11... | collective-permute-start | bytes 1179656 | tf_op jit(solution)/shard_map/ppermute | solution.py:526
  55.5 3.3 collective-permute-start.3
  55.5 3.2 collective-permute-start.5
  79.8 10.0 %collective-permute-start.6 = (bf16[768,768]{1,0:T(8,128)(2,1)}, bf16[768,768]{1,0:T(8,128)(2,1)}, u32[]{:S(2)}, u32[]{:S(2)}) collective-permute-start(bf16[768,768]{1,0:T(8,128)(2,1)} %bitcast.99), channel_id=1, source_target_pairs={{0,16},{16,0},{1,17},{17,1},{2,18},{18,2},{3,19},{19,3},{4,20},{20... | collective-permute-start | bytes 3538952 | tf_op jit(solution)/shard_map/ppermute | solution.py:522
  79.9 7.7 %collective-permute-start.7 = (s32[256,2]{1,0:T(8,128)S(1)}, s32[256,2]{1,0:T(8,128)S(1)}, u32[]{:S(2)}, u32[]{:S(2)}) collective-permute-start(s32[256,2]{1,0:T(8,128)S(1)} %bitcast.104), channel_id=1, source_target_pairs={{0,0},{1,16},{2,1},{3,17},{16,2},{17,18},{18,3},{19,19},{4,4},{5,2... | collective-permute-start | bytes 6152 | tf_op jit(solution)/shard_map/ppermute | solution.py:539
  80.9 8.1 %collective-permute-start.8 = (s32[256,2]{1,0:T(8,128)S(1)}, s32[256,2]{1,0:T(8,128)S(1)}, u32[]{:S(2)}, u32[]{:S(2)}) collective-permute-start(s32[256,2]{1,0:T(8,128)S(1)} %bitcast.105), channel_id=1, source_target_pairs={{0,2},{1,18},{2,3},{3,19},{16,0},{17,16},{18,1},{19,17},{4,6},{5,2... | collective-permute-start | bytes 6152 | tf_op jit(solution)/shard_map/ppermute | solution.py:539
  184.1 11.0 %collective-permute-start.11 = (bf16[256,768]{1,0:T(8,128)(2,1)}, bf16[256,768]{1,0:T(8,128)(2,1)S(1)}, u32[]{:S(2)}, u32[]{:S(2)}) collective-permute-start(bf16[256,768]{1,0:T(8,128)(2,1)} %get-tuple-element.67.own), channel_id=1, source_target_pairs={{0,1},{1,0},{2,3},{3,2},{4,5},{5,4},{6,7},{7,6},{8,9},{9,8},{10,11... | collective-permute-start | bytes 1179656 | tf_op jit(solution)/shard_map/ppermute | solution.py:526
  184.1 12.6 %collective-permute-start.10 = (bf16[256,768]{1,0:T(8,128)(2,1)}, bf16[256,768]{1,0:T(8,128)(2,1)S(1)}, u32[]{:S(2)}, u32[]{:S(2)}) collective-permute-start(bf16[256,768]{1,0:T(8,128)(2,1)} %get-tuple-element.67.own), channel_id=1, source_target_pairs={{0,16},{16,0},{1,17},{17,1},{2,18},{18,2},{3,19},{19,3},{4,20},{20... | collective-permute-start | bytes 1179656 | tf_op jit(solution)/shard_map/ppermute | solution.py:522
  195.1 1.7 collective-permute-start.12
  206.3 10.8 %all-to-all-start.1 = ((bf16[4,192,256]{2,1,0:T(8,128)(2,1)}), bf16[4,192,256]{2,1,0:T(8,128)(2,1)S(1)}, u32[]{:S(2)}, u32[]{:S(2)}) async-start(bf16[4,192,256]{2,1,0:T(8,128)(2,1)} %get-tuple-element.68.attended), calls=%async_computation.1 | async-start | bytes 786432 | tf_op jit(solution)/shard_map/all_to_all | solution.py:572
  209.9 12.8 %collective-permute-start.13 = (bf16[256,768]{1,0:T(8,128)(2,1)S(1)}, bf16[256,768]{1,0:T(8,128)(2,1)S(1)}, u32[]{:S(2)}, u32[]{:S(2)}) collective-permute-start(bf16[256,768]{1,0:T(8,128)(2,1)S(1)} %dynamic-slice_bitcast_fusion), channel_id=1, source_target_pairs={{0,0},{1,16},{2,1},{3,17},{16,2},{17,18},{18,3},{19,19},{4,4},{5,2... | collective-permute-start | bytes 1179656 | tf_op jit(solution)/shard_map/ppermute | solution.py:539
  414.3 2.5 collective-permute-start.17
  418.1 11.2 %collective-permute-start.18 = (bf16[256,768]{1,0:T(8,128)(2,1)S(1)}, bf16[256,768]{1,0:T(8,128)(2,1)S(1)}, u32[]{:S(2)}, u32[]{:S(2)}) collective-permute-start(bf16[256,768]{1,0:T(8,128)(2,1)S(1)} %fusion.3), channel_id=1, source_target_pairs={{0,1},{1,0},{2,3},{3,2},{4,5},{5,4},{6,7},{7,6},{8,9},{9,8},{10,11... | collective-permute-start | bytes 1179656 | tf_op jit(solution)/shard_map/ppermute | solution.py:526
  530.6 29.5 %all-to-all-start.5 = ((bf16[8,96,640]{2,1,0:T(8,128)(2,1)}), bf16[8,96,640]{2,1,0:T(8,128)(2,1)S(1)}, u32[]{:S(2)}, u32[]{:S(2)}) async-start(bf16[8,96,640]{2,1,0:T(8,128)(2,1)} %bitcast.42), calls=%async_computation.5 | async-start | bytes 1966080 | tf_op jit(solution)/shard_map/all_to_all | solution.py:565
  551.9 2.5 collective-permute-start.19
  560.1 27.8 %all-to-all-start.4 = ((bf16[8,96,640]{2,1,0:T(8,128)(2,1)}), bf16[8,96,640]{2,1,0:T(8,128)(2,1)S(1)}, u32[]{:S(2)}, u32[]{:S(2)}) async-start(bf16[8,96,640]{2,1,0:T(8,128)(2,1)} %bitcast.101), calls=%async_computation.4 | async-start | bytes 1966080 | tf_op jit(solution)/shard_map/all_to_all | solution.py:565
  563.7 28.7 %collective-permute-start.26 = (bf16[768,896]{1,0:T(8,128)(2,1)}, bf16[768,896]{1,0:T(8,128)(2,1)}, u32[]{:S(2)}, u32[]{:S(2)}) collective-permute-start(bf16[768,896]{1,0:T(8,128)(2,1)} %get-tuple-element.108), channel_id=1, source_target_pairs={{0,16},{1,17},{2,18},{3,19},{4,20},{5,21},{6,22},{7,23},{8,24},{9,... | collective-permute-start | bytes 4128776 | tf_op jit(solution)/shard_map/ppermute | solution.py:1147
  566.5 25.9 %collective-permute-start.25 = (bf16[768,896]{1,0:T(8,128)(2,1)}, bf16[768,896]{1,0:T(8,128)(2,1)}, u32[]{:S(2)}, u32[]{:S(2)}) collective-permute-start(bf16[768,896]{1,0:T(8,128)(2,1)} %get-tuple-element.107), channel_id=1, source_target_pairs={{16,0},{17,1},{18,2},{19,3},{20,4},{21,5},{22,6},{23,7},{24,8},{25... | collective-permute-start | bytes 4128776 | tf_op jit(solution)/shard_map/ppermute | solution.py:1147
  588.9 11.9 %all-to-all-start.6 = ((f32[4,48,640]{2,1,0:T(8,128)}), f32[4,48,640]{2,1,0:T(8,128)S(1)}, u32[]{:S(2)}, u32[]{:S(2)}) async-start(f32[4,48,640]{2,1,0:T(8,128)} %pad_maximum_fusion), calls=%async_computation.6 | async-start | bytes 983040 | tf_op jit(solution)/shard_map/all_to_all | solution.py:572
  600.8 74.1 %all-to-all-start.7 = ((bf16[16,48,896]{2,1,0:T(8,128)(2,1)}), bf16[16,48,896]{2,1,0:T(8,128)(2,1)S(1)}, u32[]{:S(2)}, u32[]{:S(2)}) async-start(bf16[16,48,896]{2,1,0:T(8,128)(2,1)} %bitcast.47), calls=%async_computation.7 | async-start | bytes 2752512 | tf_op jit(solution)/shard_map/all_to_all | solution.py:565
  604.5 31.9 %collective-permute-start.20 = (bf16[256,768]{1,0:T(8,128)(2,1)S(1)}, bf16[256,768]{1,0:T(8,128)(2,1)S(1)}, u32[]{:S(2)}, u32[]{:S(2)}) collective-permute-start(bf16[256,768]{1,0:T(8,128)(2,1)S(1)} %fusion.2), channel_id=1, source_target_pairs={{0,1},{1,0},{2,3},{3,2},{4,5},{5,4},{6,7},{7,6},{8,9},{9,8},{10,11... | collective-permute-start | bytes 1179656 | tf_op jit(solution)/shard_map/ppermute | solution.py:526
  606.3 40.3 %collective-permute-start.15 = (bf16[256,768]{1,0:T(8,128)(2,1)S(1)}, bf16[256,768]{1,0:T(8,128)(2,1)}, u32[]{:S(2)}, u32[]{:S(2)}) collective-permute-start(bf16[256,768]{1,0:T(8,128)(2,1)S(1)} %copy-done.8), channel_id=1, source_target_pairs={{2,0},{18,1},{3,2},{19,3},{6,4},{22,5},{7,6},{23,7},{10,8},{26,9},... | collective-permute-start | bytes 1179656 | tf_op jit(solution)/shard_map/ppermute | solution.py:545
  607.6 40.3 %collective-permute-start.16 = (bf16[256,768]{1,0:T(8,128)(2,1)}, bf16[256,768]{1,0:T(8,128)(2,1)}, u32[]{:S(2)}, u32[]{:S(2)}) collective-permute-start(bf16[256,768]{1,0:T(8,128)(2,1)} %get-tuple-element.73), channel_id=1, source_target_pairs={{2,16},{18,17},{3,18},{19,19},{6,20},{22,21},{7,22},{23,23},{10,24... | collective-permute-start | bytes 1179656 | tf_op jit(solution)/shard_map/ppermute | solution.py:545
  609.1 48.8 %collective-permute-start.9 = (bf16[256,768]{1,0:T(8,128)(2,1)S(1)}, bf16[256,768]{1,0:T(8,128)(2,1)}, u32[]{:S(2)}, u32[]{:S(2)}) collective-permute-start(bf16[256,768]{1,0:T(8,128)(2,1)S(1)} %copy-done.8), channel_id=1, source_target_pairs={{0,0},{16,1},{1,2},{17,3},{4,4},{20,5},{5,6},{21,7},{8,8},{24,9},{... | collective-permute-start | bytes 1179656 | tf_op jit(solution)/shard_map/ppermute | solution.py:545
  610.5 49.0 %collective-permute-start.14 = (bf16[256,768]{1,0:T(8,128)(2,1)}, bf16[256,768]{1,0:T(8,128)(2,1)}, u32[]{:S(2)}, u32[]{:S(2)}) collective-permute-start(bf16[256,768]{1,0:T(8,128)(2,1)} %get-tuple-element.73), channel_id=1, source_target_pairs={{0,16},{16,17},{1,18},{17,19},{4,20},{20,21},{5,22},{21,23},{8,24}... | collective-permute-start | bytes 1179656 | tf_op jit(solution)/shard_map/ppermute | solution.py:545
  636.4 25.1 %collective-permute-start.24 = (bf16[256,768]{1,0:T(8,128)(2,1)S(1)}, bf16[256,768]{1,0:T(8,128)(2,1)S(1)}, u32[]{:S(2)}, u32[]{:S(2)}) collective-permute-start(bf16[256,768]{1,0:T(8,128)(2,1)S(1)} %copy-done.9), channel_id=1, source_target_pairs={{2,16},{18,17},{3,18},{19,19},{6,20},{22,21},{7,22},{23,23},{10,24... | collective-permute-start | bytes 1179656 | tf_op jit(solution)/shard_map/ppermute | solution.py:545
  646.6 24.2 %collective-permute-start.23 = (bf16[256,768]{1,0:T(8,128)(2,1)}, bf16[256,768]{1,0:T(8,128)(2,1)S(1)}, u32[]{:S(2)}, u32[]{:S(2)}) collective-permute-start(bf16[256,768]{1,0:T(8,128)(2,1)} %first_norm_grad.3), channel_id=1, source_target_pairs={{2,0},{18,1},{3,2},{19,3},{6,4},{22,5},{7,6},{23,7},{10,8},{26,9},... | collective-permute-start | bytes 1179656 | tf_op jit(solution)/shard_map/ppermute | solution.py:545
  649.0 21.9 %collective-permute-start.22 = (bf16[256,768]{1,0:T(8,128)(2,1)S(1)}, bf16[256,768]{1,0:T(8,128)(2,1)S(1)}, u32[]{:S(2)}, u32[]{:S(2)}) collective-permute-start(bf16[256,768]{1,0:T(8,128)(2,1)S(1)} %copy-done.9), channel_id=1, source_target_pairs={{0,16},{16,17},{1,18},{17,19},{4,20},{20,21},{5,22},{21,23},{8,24}... | collective-permute-start | bytes 1179656 | tf_op jit(solution)/shard_map/ppermute | solution.py:545
  657.8 13.0 %collective-permute-start.21 = (bf16[256,768]{1,0:T(8,128)(2,1)}, bf16[256,768]{1,0:T(8,128)(2,1)S(1)}, u32[]{:S(2)}, u32[]{:S(2)}) collective-permute-start(bf16[256,768]{1,0:T(8,128)(2,1)} %first_norm_grad.3), channel_id=1, source_target_pairs={{0,0},{16,1},{1,2},{17,3},{4,4},{20,5},{5,6},{21,7},{8,8},{24,9},{... | collective-permute-start | bytes 1179656 | tf_op jit(solution)/shard_map/ppermute | solution.py:545
  (24 other events, 339.1 us)
Sparse Core Ops, SparseCore 0:
  10.8 60.6 all-gather.2

commit v4 on v3

--- a/solution.py
+++ b/solution.py
@@ -41,10 +41,33 @@
     return inner if skipped else body
 
 
-def call(body, name, outs, args, scalars=None, scratch=(), flops=0, after=()):
+REMOTE = pl.DeviceIdType.MESH
+
+
+def remote(source, target, send, recv, peer):
+    return pltpu.make_async_remote_copy(
+        src_ref=source, dst_ref=target, send_sem=send, recv_sem=recv, device_id=peer, device_id_type=REMOTE
+    )
+
+
+def across(index, step):
+    return (index, index + 1 - 2 * (index % 2), (index + 2) % 4, 3 - index)[step]
+
+
+def greet(peers):
+    barrier = pltpu.get_barrier_semaphore()
+    for peer in peers:
+        pl.semaphore_signal(barrier, inc=1, device_id=peer, device_id_type=REMOTE)
+    pl.semaphore_wait(barrier, len(peers))
+
+
+def call(body, name, outs, args, scalars=None, scratch=(), flops=0, after=(), collective=None, anywhere=(),
+         out_anywhere=()):
     specs = [pl.BlockSpec(memory_space=pl.ANY)] * len(after)
     specs += [pl.BlockSpec(memory_space=pltpu.SMEM)] if scalars is not None else []
-    specs += [pl.BlockSpec(memory_space=pltpu.VMEM)] * len(args)
+    specs += [
+        pl.BlockSpec(memory_space=pl.ANY if index in anywhere else pltpu.VMEM) for index in range(len(args))
+    ]
     operands = list(after) + ([scalars] if scalars is not None else []) + list(args)
     moved = sum(a.size * a.dtype.itemsize for a in list(args) + list(outs))
     body = ordered(body, len(after))
@@ -52,10 +75,15 @@
         body,
         name=name,
         in_specs=specs,
-        out_specs=[pl.BlockSpec(memory_space=pltpu.VMEM)] * len(outs),
+        out_specs=[
+            pl.BlockSpec(memory_space=pl.ANY if index in out_anywhere else pltpu.VMEM)
+            for index in range(len(outs))
+        ],
         out_shape=list(outs),
         scratch_shapes=list(scratch),
-        compiler_params=pltpu.CompilerParams(vmem_limit_bytes=VMEM_LIMIT),
+        compiler_params=pltpu.CompilerParams(
+            vmem_limit_bytes=VMEM_LIMIT, collective_id=collective, has_side_effects=collective is not None
+        ),
         cost_estimate=pl.CostEstimate(flops=flops, bytes_accessed=moved, transcendentals=0),
     )(*operands)
 
@@ -385,7 +413,27 @@
 
 
 def before_attention(returned, aux, upstream, difference, middle, normed_two, attended, gain,
-                     router, w_out, routes, middle_grad, attended_grad, shared_grad):
+                     router, w_out, routes, *refs):
+    if len(refs) > 3:
+        grad_in, grad_down, middle_grad, attended_grad, shared_grad, out_in, out_down, held, in_sem, out_sem = refs
+        tile = held.shape[2]
+        tiles = held.shape[0] // 2
+        places = [(slice(None), pl.ds(index * tile, tile)) for index in range(tiles)]
+        places = [(grad_in.at[p], out_in.at[p]) for p in places] + [
+            (grad_down.at[pl.ds(index * tile, tile)], out_down.at[pl.ds(index * tile, tile)])
+            for index in range(tiles)
+        ]
+        fetches = [
+            pltpu.make_async_copy(pair[0], held.at[index], in_sem.at[index]) for index, pair in enumerate(places)
+        ]
+        stores = [
+            pltpu.make_async_copy(held.at[index], pair[1], out_sem.at[index]) for index, pair in enumerate(places)
+        ]
+        for fetch in fetches:
+            fetch.start()
+    else:
+        middle_grad, attended_grad, shared_grad = refs
+        fetches = stores = ()
     slots = returned.shape[0]
     experts = router.shape[1]
     width = attended.shape[1]
@@ -402,6 +450,9 @@
     total = flow + back
     middle_grad[...] = total
     branch = total.astype(BF16)
+    for fetch, store in zip(fetches, stores):
+        fetch.wait()
+        store.start()
     for group in range(GROUP):
         mine = slice(group * width, (group + 1) * width)
         shared_grad[mine, :features] = mm(attended[group], branch).astype(BF16)
@@ -411,6 +462,8 @@
     lane = lax.broadcasted_iota(jnp.int32, (features, tail), 1)
     shared_grad[:, features:] = jnp.where(lane == experts, gain_column[:, 0:1], 0.0).astype(BF16)
     shared_grad[:, features : features + experts] = mm(normed_two[...], logits_grad, TN).astype(BF16)
+    for store in stores:
+        store.wait()
 
 
 def attention_backward(sizes, ids, mixed, stats, attended, grads, gathered, gain, weight, table,
@@ -515,6 +568,116 @@
     low[...] = (middle_grad[...] + back).astype(BF16)
 
 
+def settle(home_sections, final, stay, leave, sent, own, gain, middle_grad, *refs):
+    refs = list(refs)
+
+    def take(count):
+        taken = refs[:count]
+        del refs[:count]
+        return taken
+
+    going = take(len(home_sections))
+    qkv = take(2 if final else 0)
+    low, home = take(2)
+    owned = take(1 if final else 0)
+    partner_share, side_share, leaving, pair_send, pair_recv, home_send, home_recv = take(7)
+    core = lax.axis_index("section")
+    expert = lax.axis_index("expert")
+    zhi = lax.axis_index("zhi")
+    zlo = lax.axis_index("zlo")
+    place = 2 * zhi + zlo
+    line = []
+    for move in range(4):
+        spot = across(place, move)
+        for turn in range(2):
+            if move or turn:
+                line.append({"section": 1 - core if turn else core, "zhi": spot // 2, "zlo": spot % 2})
+    plane = [across(expert, step) for step in range(1, 4)]
+    greet(line + ([{"expert": spot} for spot in plane] if final else []))
+
+    partner_copy = remote(sent, partner_share, pair_send.at[0], pair_recv.at[0], {"section": 1 - core})
+    partner_copy.start()
+    aligned = (zlo == zhi) & (zlo == core)
+
+    def home_copy(block, section, index):
+        return remote(block, home.at[zhi], home_send.at[index], home_recv.at[zhi],
+                      {"section": section, "zhi": zlo, "zlo": core})
+
+    def send_home(block, section, index):
+        here = aligned & (core == section)
+
+        @pl.when(here)
+        def keep():
+            home[zhi] = block[...]
+
+        @pl.when(jnp.logical_not(here))
+        def give():
+            home_copy(block, section, index).start()
+
+    for index, (block, section) in enumerate(zip(going, home_sections)):
+        send_home(block, section, index)
+    if final:
+        shares, totals, pieces, plane_send, plane_recv, line_send, line_recv = take(7)
+        copies = []
+        for section in range(2):
+            for step, spot in enumerate(plane):
+                copy = remote(qkv[section].at[pl.ds(4 * spot, 4)], shares.at[section, step],
+                              plane_send.at[section, step], plane_recv.at[section, step], {"expert": spot})
+                copy.start()
+                copies.append(copy)
+    partner_copy.wait()
+    leaving[...] = leave[...] + partner_share[1]
+    side_copy = remote(leaving, side_share, pair_send.at[1], pair_recv.at[1], {"zlo": 1 - zlo})
+    side_copy.start()
+    grad = stay[...].astype(F32) + partner_share[0].astype(F32)
+    side_copy.wait()
+    grad = grad + side_share[...].astype(F32)
+    back, unused = norm_backward(own[...].astype(F32), gain[...].astype(F32), grad)
+    low[...] = (middle_grad[...] + back).astype(BF16)
+    sent_home = list(zip(going, home_sections))
+    if final:
+        send_home(low, 0, len(going))
+        sent_home.append((low, 0))
+        for copy in copies:
+            copy.wait()
+        for section in range(2):
+            total = qkv[section][pl.ds(4 * expert, 4)].astype(F32)
+            for step in range(3):
+                total = total + shares[section, step].astype(F32)
+            totals[section] = total.astype(BF16)
+        line_copies = []
+        for turn in range(2):
+            section = 1 - core if turn else core
+            for move in range(4):
+                spot = across(place, move)
+                if move or turn:
+                    copy = remote(totals.at[section, spot], pieces.at[2 * place + core],
+                                  line_send.at[turn, move], line_recv.at[turn, move],
+                                  {"section": section, "zhi": spot // 2, "zlo": spot % 2})
+                    copy.start()
+                    line_copies.append((copy, turn, spot))
+        pieces[2 * place + core] = totals[core, place]
+        for turn in range(2):
+            for move in range(4):
+                if move or turn:
+                    source = pieces.at[2 * across(place, move) + (1 - core if turn else core)]
+                    remote(source, source, line_send.at[turn, move], line_recv.at[turn, move],
+                           {"section": 1 - core}).wait_recv()
+        for group in range(GROUP):
+            owned[0][group] = pieces[group].astype(F32) + pieces[GROUP + group].astype(F32)
+        for copy, unused, unused_1 in line_copies:
+            copy.wait_send()
+    for batch in range(2):
+        @pl.when(jnp.logical_not(aligned & (zhi == batch)))
+        def landed():
+            remote(home.at[batch], home.at[batch], home_send.at[0], home_recv.at[batch],
+                   {"section": 1 - core}).wait_recv()
+    for index, (block, section) in enumerate(sent_home):
+        @pl.when(jnp.logical_not(aligned & (core == section)))
+        def left():
+            home_copy(block, section, index).wait_send()
+
+
 FLIP = [(0, 1), (1, 0)]
 
 
@@ -691,11 +854,6 @@
 OFFSETS = [(step, place) for place in (0, 3, 1, 2) for step in range(4)]
 SENDS = (4, 5, 6, 7, 12, 13, 14, 15, 8, 9, 10, 11, 1, 2, 3)
 BATCH = 4
-REMOTE = pl.DeviceIdType.MESH
-
-
-def across(index, step):
-    return (index, index + 1 - 2 * (index % 2), (index + 2) % 4, 3 - index)[step]
 
 
 def expert_layer(mode, section, *refs):
@@ -761,15 +919,7 @@
         load(saved_activation, activation, 2)
         load(saved_slope, slope, 3)
 
-    barrier = pltpu.get_barrier_semaphore()
-    for peer in peers[1:] + ([{"section": 1 - core}] if backward else []):
-        pl.semaphore_signal(barrier, inc=1, device_id=peer, device_id_type=REMOTE)
-    pl.semaphore_wait(barrier, 16 if backward else 15)
-
-    def remote(source, target, send, recv, peer):
-        return pltpu.make_async_remote_copy(
-            src_ref=source, dst_ref=target, send_sem=send, recv_sem=recv, device_id=peer, device_id_type=REMOTE
-        )
+    greet(peers[1:] + ([{"section": 1 - core}] if backward else []))
 
     sent = []
     for slot in SENDS:
@@ -956,6 +1106,27 @@
     )(*operands)
 
 
+def run_settle(final, main, going, home_sections, qkv, collective):
+    span, features = main[0].shape
+    dma = pltpu.SemaphoreType.DMA
+    block = pltpu.VMEM((span, features), BF16)
+    outs = [shape((span, features), BF16), shape((2, span, features), BF16)]
+    scratch = [
+        pltpu.VMEM((2, span, features), BF16), block, block, dma((2,)), dma((2,)), dma((2,)), dma((2,)),
+    ]
+    if final:
+        ranks, rows, columns = qkv[0].shape
+        outs.append(shape((GROUP, rows, columns), F32))
+        scratch += [
+            pltpu.VMEM((2, 3, 4, rows, columns), BF16), pltpu.VMEM((2, 4, rows, columns), BF16),
+            pltpu.VMEM((2 * GROUP, rows, columns), BF16), dma((2, 3)), dma((2, 3)), dma((2, 4)), dma((2, 4)),
+        ]
+    return call(
+        functools.partial(settle, tuple(home_sections), final), "settle_last" if final else "settle",
+        outs, [*main, *going, *qkv], scratch=scratch, collective=collective,
+    )
+
+
 def per_device(inputs, cotangent, qkv_shard, out_shard, router_shard, gain_shard, table_shard,
                w_expert_in, w_expert_out, routes):
     core = lax.axis_index("section")
@@ -1099,7 +1270,8 @@
         results.append(result)
         stream = result
 
-    section_outputs = home_pair(results, core)
+    if not fused:
+        section_outputs = home_pair(results, core)
 
     upstream = given
     shared_grads = [None, None]
@@ -1134,16 +1306,26 @@
             wanted = (core != section).astype(jnp.int32).reshape(1)
             shares = run_weight_partials(wanted, *expert_states[section])
             partials[section] = [lax.ppermute(part, "section", [(1 - section, section)]) for part in shares]
-        if section == 0:
+        if section == 0 and not fused:
             waiting, returned = lax.optimization_barrier((shared_qkv[1], returned))
             qkv_grads[1] = spread_sum(waiting, ("expert", "zhi"), ranks // 2)
-        middle_grad, attended_grad, shared_grads[section] = call(
-            before_attention, "before_attention",
-            [shape((span, features), F32), shape((GROUP, width, span), BF16),
-             shape((features, features + -(-(experts + 1) // 128) * 128), BF16)],
-            [returned, aux, upstream, difference, middle, normed_two, attended, gain_two, router, w_out,
-             route_rows], flops=2 << 30, after=shares[:1],
+        outs = [shape((span, features), F32), shape((GROUP, width, span), BF16),
+                shape((features, features + -(-(experts + 1) // 128) * 128), BF16)]
+        operands = [returned, aux, upstream, difference, middle, normed_two, attended, gain_two, router, w_out,
+                    route_rows]
+        scratch = []
+        if fused and section == 0:
+            outs += [shape(grad_in.shape, F32), shape(grad_down.shape, F32)]
+            operands += [grad_in, grad_down]
+            pieces = 2 * grad_in.shape[1] // features
+            scratch = [pltpu.VMEM((pieces, features, features), F32),
+                       pltpu.SemaphoreType.DMA((pieces,)), pltpu.SemaphoreType.DMA((pieces,))]
+        middle_grad, attended_grad, shared_grads[section], *published = call(
+            before_attention, "before_attention", outs, operands, scratch=scratch, flops=2 << 30,
+            after=shares[:1], anywhere=(11, 12), out_anywhere=(3, 4),
         )
+        if published:
+            grad_in, grad_down = published
         shared_partner[section] = lax.ppermute(shared_grads[section], "section", [(1 - section, section)])
         grads = regroup(attended_grad)
         stay, leave, sent, shared_qkv[section] = call(
@@ -1157,22 +1339,33 @@
                      pltpu.VMEM((8, GROUP * 2 * 128), F32)],
             flops=8 << 30,
         )
-        partner = flip(sent)
-        leave = leave + partner[1]
-        filler = ()
-        if section == 0:
-            leave, waiting = lax.optimization_barrier((leave, shared_qkv[0]))
-            qkv_grads[0] = spread_sum(waiting, ("expert", "zhi"), ranks // 2)
-            if not fused:
+        if fused:
+            low, *settled = run_settle(
+                section == 0, [stay, leave, sent, stream, gain_one, middle_grad],
+                [stream_grads[1]] if section == 0 else results, [1] if section == 0 else [0, 1],
+                [block.reshape(ranks, shard_rows, -1) for block in shared_qkv] if section == 0 else [],
+                10 if section == 0 else 11,
+            )
+            if section == 1:
+                section_outputs = settled[0]
+            else:
+                section_grads, owned = settled
+        else:
+            partner = flip(sent)
+            leave = leave + partner[1]
+            filler = ()
+            if section == 0:
+                leave, waiting = lax.optimization_barrier((leave, shared_qkv[0]))
+                qkv_grads[0] = spread_sum(waiting, ("expert", "zhi"), ranks // 2)
                 grad_in = run_weight_totals(
                     core_id, *[(expert_states[which][0], expert_states[which][1], partials[which][0])
                                for which in range(2)], False, sent)
                 filler = (grad_in,)
-        arrived_share = beside(leave)
-        (low,) = call(
-            first_norm_grad, "first_norm_grad", [shape((span, features), BF16)],
-            [stay, partner, arrived_share, stream, gain_one, middle_grad], after=filler,
-        )
+            arrived_share = beside(leave)
+            (low,) = call(
+                first_norm_grad, "first_norm_grad", [shape((span, features), BF16)],
+                [stay, partner, arrived_share, stream, gain_one, middle_grad], after=filler,
+            )
         stream_grads[section] = low
         upstream = low
 
@@ -1186,10 +1379,11 @@
     grad_router = shared[:, features : features + experts]
     grad_gain_two = shared[:, features + experts]
 
-    columns = qkv_grads[0].shape[1]
-    halves = [block.reshape(2, shard_rows, columns) for block in qkv_grads]
-    sending = jnp.stack([halves[0][0], halves[1][0], halves[0][1], halves[1][1]])
-    owned = regroup(sending)
+    if not fused:
+        columns = qkv_grads[0].shape[1]
+        halves = [block.reshape(2, shard_rows, columns) for block in qkv_grads]
+        owned = regroup(jnp.stack([halves[0][0], halves[1][0], halves[0][1], halves[1][1]]))
+        section_grads = home_pair(stream_grads, core)
     split = owned[:, :, : 3 * width].reshape(GROUP, shard_rows, 3, width)
     grad_qkv = jnp.transpose(split, (1, 2, 0, 3)).reshape(shard_rows, 3 * features)
     grad_table = jnp.transpose(
@@ -1198,7 +1392,7 @@
     grad_gain_one = jnp.sum(owned[:, :, 3 * width + 8], axis=0)
     grad_gains = jnp.stack([grad_gain_one, grad_gain_two])
 
-    section_grads = home_pair(stream_grads, core).astype(F32)
+    section_grads = section_grads.astype(F32)
 
     if not fused:
         grad_down = run_weight_totals(

time: 707 us -> 644 us (0.911)
  Pallas kernels: 429 us -> 504 us
  waiting for transfers between devices: 98.7 us -> 25.4 us
  starting transfers between devices: 70.4 us -> 44.6 us
  blocking collectives: 34.7 us -> 11.6 us
  local copies, waits for them, and re-layouts: 31.5 us -> 21.5 us
    pallas_call x14, Pallas kernels: 94.8 us -> 170 us  [call(): pl.pallas_call(body, name=name, in_specs=specs, out_specs=[pl.BlockSpec(m...]
    ppermute x4 -> x2, waiting for transfers between devices: 43.4 us -> 11 us  [beside(): return lax.ppermute(block, 'zlo', FLIP)]
    all_to_all x3 -> x1, waiting for transfers between devices: 24.4 us -> 0.01 us  [spread_sum(): lax.all_to_all(block.reshape(parts, rows // parts, columns), axes, split_...]
    all_to_all x3 -> x1, blocking collectives: 34.7 us -> 11.6 us  [regroup(): lax.all_to_all(block, ('zlo', 'section'), split_axis=0, concat_axis=0, ti...]
    ppermute x8 -> x0, starting transfers between devices: 20.9 us -> none  [to_home(): return lax.ppermute(block, ('section', 'zhi', 'zlo'), pairs)]
    ppermute x8 -> x0, waiting for transfers between devices: 15.8 us -> none  [to_home(): return lax.ppermute(block, ('section', 'zhi', 'zlo'), pairs)]
    unnamed x52 -> x41, local copies, waits for them, and re-layouts: 18.5 us -> 6.8 us
    ppermute x4 -> x2, starting transfers between devices: 18.5 us -> 16.2 us  [beside(): return lax.ppermute(block, 'zlo', FLIP)]
  transfers between devices with their start and end apart: 33 -> 20, of which waited for: 13 -> 7; matrix products, arithmetic and copies ran while one was open for 4% -> 4% of each run, Pallas kernels for 9% -> 39%
where the time goes in v4:
time: 644 us; the launch traced here: 634 us
  Pallas kernels  504 us (78%)
  starting transfers between devices  44.6 us (7%)
  waiting for transfers between devices  25.4 us (4%)
  local copies, waits for them, and re-layouts  21.5 us (3%)
  between operations  14.7 us (2%)
  other arithmetic  12.2 us (2%)
  blocking collectives  11.6 us (2%)
    pallas_call x3, Pallas kernels, run_expert_layer(): pl.pallas_call(functools.partial(expert_layer, mode, section), name='expe...  308 us
    pallas_call x14, Pallas kernels, call(): pl.pallas_call(body, name=name, in_specs=specs, out_specs=[pl.BlockSpec(m...  170 us
    pallas_call x1, Pallas kernels, run_gather_columns(): pl.pallas_call(gather_columns, name='gather_columns', in_specs=[pl.BlockS...  26.8 us
    ppermute x2, starting transfers between devices, beside(): return lax.ppermute(block, 'zlo', FLIP)  16.2 us
  transfers between devices with their start and end apart: 20, of which 7 were waited for; matrix products, arithmetic and copies ran while one was open for 4% of the time, Pallas kernels for 39%

profile of v4, /device:TPU:0, one launch (start us, length us, event | category | flops | bytes accessed | tf_op | source)
XLA Modules:
  0.0 634.5 jit_solution(17663134382685396813)
XLA Ops:
  9.1 16.2 %collective-permute-start.4 = (bf16[256,768]{1,0:T(8,128)(2,1)S(1)}, bf16[256,768]{1,0:T(8,128)(2,1)}, u32[]{:S(2)}, u32[]{:S(2)}) collective-permute-start(bf16[256,768]{1,0:T(8,128)(2,1)S(1)} %collective-permute-done.2.own), channel_id=1, source_target_pairs={{0,1},{1,0},{2,3},{3,2},{4,5},{5,4},{6,7},{7,6},{8,9},{9,8},{10,11... | collective-permute-start | bytes 1179656 | tf_op jit(solution)/shard_map/ppermute | solution.py:689
  28.7 26.8 %gather_columns.1 = bf16[2,16,48,640]{3,2,1,0:T(8,128)(2,1)S(1)} custom-call(bf16[4,48,640]{2,1,0:T(8,128)(2,1)S(1)} %fusion.2.blocks), custom_call_target="tpu_custom_call" | custom-call | bytes 41943040 | tf_op jit(solution)/shard_map/gather_columns/pallas_call | solution.py:833
  59.4 8.7 %attention_forward.2 = (bf16[4,192,256]{2,1,0:T(8,128)(2,1)}, bf16[1024,576]{1,0:T(8,128)(2,1)}, bf16[1024,768]{1,0:T(8,128)(2,1)}, f32[8,1024]{1,0:T(8,128)}) custom-call(s32[9]{0:T(128)} %stack.30.ids, bf16[256,768]{1,0:T(8,128)(2,1)} %copy-done.10, bf16[256,768]{1,0:T(8,128)(2,1)} %copy-done.13, bf16[256,768]{1,0:T(8,128)(2,1)} %collective-permute-done.4.side, ...), custom_call_target="tpu_custom_call" | custom-call | flops 4294967296 | bytes 5737472 | tf_op jit(solution)/shard_map/attention_forward/pallas_call | solution.py:74
  68.1 11.6 %all_to_all.25.attended = bf16[4,192,256]{2,1,0:T(8,128)(2,1)} all-to-all(bf16[4,192,256]{2,1,0:T(8,128)(2,1)} %get-tuple-element.62.attended), channel_id=1, replica_groups=mesh['section'=2,'expert'=4,'zhi'=2,'zlo'=2] {'zlo','section'}, dimensions={0} | all-to-all | bytes 786432 | tf_op jit(solution)/shard_map/all_to_all | solution.py:735
  80.8 5.0 collective-permute-start.8
  89.7 2.8 broadcast_select_fusion
  92.5 4.7 after_attention.2
  97.2 83.0 %expert_layer_forward.1 = (bf16[16,64,768]{2,1,0:T(8,128)(2,1)}, bf16[16,64,768]{2,1,0:T(8,128)(2,1)}, bf16[1024,3072]{1,0:T(8,128)(2,1)}, bf16[1024,3072]{1,0:T(8,128)(2,1)}) custom-call(bf16[768,3072]{1,0:T(8,128)(2,1)} %bitcast.100, bf16[3072,768]{1,0:T(8,128)(2,1)} %bitcast.104, bf16[768,3072]{1,0:T(8,128)(2,1)} %collective-permute-done.refs_2_, ...), custom_call_target="tpu_custom_call" | custom-call | flops 19327352832 | bytes 167772160 | tf_op jit(solution)/shard_map/expert_layer_forward/pallas_call | solution.py:1091
  180.2 3.8 combine.2
  184.0 11.0 %collective-permute-done.10.side = bf16[256,768]{1,0:T(8,128)(2,1)S(1)} collective-permute-done((bf16[256,768]{1,0:T(8,128)(2,1)}, bf16[256,768]{1,0:T(8,128)(2,1)S(1)}, u32[]{:S(2)}, u32[]{:S(2)}) %collective-permute-start.10) | collective-permute-done | bytes 393248 | tf_op jit(solution)/shard_map/ppermute | solution.py:689
  197.4 8.7 %attention_forward.3 = (bf16[4,192,256]{2,1,0:T(8,128)(2,1)}, bf16[1024,576]{1,0:T(8,128)(2,1)}, bf16[1024,768]{1,0:T(8,128)(2,1)}, f32[8,1024]{1,0:T(8,128)}) custom-call(s32[9]{0:T(128)} %stack.30.ids, bf16[256,768]{1,0:T(8,128)(2,1)} %get-tuple-element.69.own.refs_0_, bf16[256,768]{1,0:T(8,128)(2,1)} %copy-done.16, bf16[256,768]{1,0:T(8,128)(2,1)} %copy-done.15, ...), custom_call_target="tpu_custom_call" | custom-call | flops 4294967296 | bytes 5737472 | tf_op jit(solution)/shard_map/attention_forward/pallas_call | solution.py:74
  206.2 3.5 all-to-all-start.1
  212.6 4.5 all-to-all-done.1.attended
  217.8 4.7 after_attention.3
  223.3 3.3 spread_grads.2
  226.6 148.3 %expert_layer_both.1 = (bf16[16,64,768]{2,1,0:T(8,128)(2,1)}, bf16[16,64,768]{2,1,0:T(8,128)(2,1)}, f32[768,3072]{1,0:T(8,128)}, f32[3072,768]{1,0:T(8,128)}) custom-call(bf16[768,3072]{1,0:T(8,128)(2,1)} %bitcast.101, bf16[3072,768]{1,0:T(8,128)(2,1)} %bitcast.105, bf16[768,3072]{1,0:T(8,128)(2,1)} %collective-permute-done.refs_2_, ...), custom_call_target="tpu_custom_call" | custom-call | flops 38654705664 | bytes 167772160 | tf_op jit(solution)/shard_map/expert_layer_both/pallas_call | solution.py:1091
  374.8 3.7 combine.3
  378.6 6.7 %before_attention.2 = (f32[256,768]{1,0:T(8,128)}, bf16[4,192,256]{2,1,0:T(8,128)(2,1)}, bf16[768,896]{1,0:T(8,128)(2,1)}) custom-call(bf16[1024,768]{1,0:T(8,128)(2,1)} %bitcast.107, f32[256,128]{1,0:T(8,128)} %get-tuple-element.74.aux, bf16[256,768]{1,0:T(8,128)(2,1)} %copy-done.14, f32[256,768]{1,0:T(8,128)} %get-tuple-element.78.difference, ...), custom_call_target="tpu_custom_call" | custom-call | flops 2147483648 | bytes 8220160 | tf_op jit(solution)/shard_map/before_attention/pallas_call | solution.py:74
  385.3 3.5 all-to-all-start.2
  388.8 2.9 collective-permute-start.14
  391.6 4.5 all-to-all-done.2.grads
  396.9 17.3 %attention_backward.2 = (bf16[256,768]{1,0:T(8,128)(2,1)}, bf16[256,768]{1,0:T(8,128)(2,1)}, bf16[2,256,768]{2,1,0:T(8,128)(2,1)}, bf16[768,640]{1,0:T(8,128)(2,1)}) custom-call(s32[9]{0:T(128)} %stack.30.ids, bf16[1024,576]{1,0:T(8,128)(2,1)} %get-tuple-element.70.mixed, f32[8,1024]{1,0:T(8,128)} %get-tuple-element.71.stats, ...), custom_call_target="tpu_custom_call" | custom-call | flops 8589934592 | bytes 7113728 | tf_op jit(solution)/shard_map/attention_backward/pallas_call | solution.py:74
  414.2 25.1 %settle.1 = (bf16[256,768]{1,0:T(8,128)(2,1)}, bf16[2,256,768]{2,1,0:T(8,128)(2,1)}) custom-call(bf16[256,768]{1,0:T(8,128)(2,1)} %get-tuple-element.82.stay, bf16[256,768]{1,0:T(8,128)(2,1)} %get-tuple-element.83.leave, bf16[2,256,768]{2,1,0:T(8,128)(2,1)} %get-tuple-element.84.sent, bf16[256,768]{1,0:T(8,128)(2,1)} %get-tuple-element.69.own.refs_0_, ...), custom_call_target="tpu_custom_call" | custom-call | bytes 4720128 | tf_op jit(solution)/shard_map/settle/pallas_call | solution.py:74
  439.3 3.3 spread_grads.3
  442.6 77.0 %expert_layer_backward.1 = (bf16[16,64,768]{2,1,0:T(8,128)(2,1)}, f32[768,3072]{1,0:T(8,128)}, f32[3072,768]{1,0:T(8,128)}) custom-call(bf16[768,3072]{1,0:T(8,128)(2,1)} %bitcast.102, bf16[3072,768]{1,0:T(8,128)(2,1)} %bitcast.106, bf16[768,3072]{1,0:T(8,128)(2,1)} %collective-permute-done.refs_2_, ...), custom_call_target="tpu_custom_call", output_to_operand_aliasing={{1}: (8, {}), {2}: (9, {})} | custom-call | flops 19327352832 | bytes 167772160 | tf_op jit(solution)/shard_map/expert_layer_backward/pallas_call | solution.py:1091
  519.6 17.4 %before_attention.3 = (f32[256,768]{1,0:T(8,128)}, bf16[4,192,256]{2,1,0:T(8,128)(2,1)}, bf16[768,896]{1,0:T(8,128)(2,1)}, f32[768,3072]{1,0:T(8,128)}, f32[3072,768]{1,0:T(8,128)}) custom-call(bf16[1024,768]{1,0:T(8,128)(2,1)} %bitcast.74, f32[256,128]{1,0:T(8,128)} %get-tuple-element.67.aux, bf16[256,768]{1,0:T(8,128)(2,1)} %get-tuple-element.90.upstream.refs_0_, ...), custom_call_target="tpu_custom_call" | custom-call | flops 2147483648 | bytes 45968896 | tf_op jit(solution)/shard_map/before_attention/pallas_call | solution.py:74
  538.3 3.5 all-to-all-start.3
  542.3 3.5 select_convert_fusion
  545.9 3.3 all-to-all-done.3.grads
  549.1 5.0 all-to-all-start.4
  554.2 17.3 %attention_backward.3 = (bf16[256,768]{1,0:T(8,128)(2,1)}, bf16[256,768]{1,0:T(8,128)(2,1)}, bf16[2,256,768]{2,1,0:T(8,128)(2,1)}, bf16[768,640]{1,0:T(8,128)(2,1)}) custom-call(s32[9]{0:T(128)} %stack.30.ids, bf16[1024,576]{1,0:T(8,128)(2,1)} %get-tuple-element.88.mixed, f32[8,1024]{1,0:T(8,128)} %get-tuple-element.89.stats, ...), custom_call_target="tpu_custom_call" | custom-call | flops 8589934592 | bytes 7113728 | tf_op jit(solution)/shard_map/attention_backward/pallas_call | solution.py:74
  571.5 44.8 %settle_last.1 = (bf16[256,768]{1,0:T(8,128)(2,1)}, bf16[2,256,768]{2,1,0:T(8,128)(2,1)}, f32[4,48,640]{2,1,0:T(8,128)}) custom-call(bf16[256,768]{1,0:T(8,128)(2,1)} %get-tuple-element.103.stay, bf16[256,768]{1,0:T(8,128)(2,1)} %get-tuple-element.104.leave, bf16[2,256,768]{2,1,0:T(8,128)(2,1)} %get-tuple-element.105.sent, bf16[256,768]{1,0:T(8,128)(2,1)} %copy-done.10, ...), custom_call_target="tpu_custom_call" | custom-call | bytes 6784512 | tf_op jit(solution)/shard_map/settle_last/pallas_call | solution.py:74
  (109 shorter events, 34.6 us)
Async XLA Ops:
  7.2 1.1 copy-start
  7.2 72.5 %all-gather.3.cloned.1.call-start = ((), (), s32[]{:S(2)}) async-start(), calls=%async_computation.5 | async-start | bytes 1253376 | tf_op jit(solution)/shard_map/all_gather | solution.py:1188
  7.2 89.9 %collective-permute-start = (bf16[768,3072]{1,0:T(8,128)(2,1)}, bf16[768,3072]{1,0:T(8,128)(2,1)}, u32[]{:S(2)}, u32[]{:S(2)}) collective-permute-start(bf16[768,3072]{1,0:T(8,128)(2,1)} %bitcast.99), channel_id=1, source_target_pairs={{0,16},{16,0},{1,17},{17,1},{2,18},{18,2},{3,19},{19,3},{4,20},{20... | collective-permute-start | bytes 14155784 | tf_op jit(solution)/shard_map/ppermute | solution.py:685
  7.8 89.4 %collective-permute-start.1 = (bf16[3072,768]{1,0:T(8,128)(2,1)}, bf16[3072,768]{1,0:T(8,128)(2,1)}, u32[]{:S(2)}, u32[]{:S(2)}) collective-permute-start(bf16[3072,768]{1,0:T(8,128)(2,1)} %bitcast.103), channel_id=1, source_target_pairs={{0,16},{16,0},{1,17},{17,1},{2,18},{18,2},{3,19},{19,3},{4,20},{20... | collective-permute-start | bytes 14155784 | tf_op jit(solution)/shard_map/ppermute | solution.py:685
  8.3 0.7 collective-permute-start.2
  9.1 46.4 %copy-start.10 = (bf16[256,768]{1,0:T(8,128)(2,1)}, bf16[256,768]{1,0:T(8,128)(2,1)S(1)}, u32[]{:S(2)}) copy-start(bf16[256,768]{1,0:T(8,128)(2,1)S(1)} %collective-permute-done.2.own) | copy-start | bytes 1179652
  9.1 46.5 %collective-permute-start.4 = (bf16[256,768]{1,0:T(8,128)(2,1)S(1)}, bf16[256,768]{1,0:T(8,128)(2,1)}, u32[]{:S(2)}, u32[]{:S(2)}) collective-permute-start(bf16[256,768]{1,0:T(8,128)(2,1)S(1)} %collective-permute-done.2.own), channel_id=1, source_target_pairs={{0,1},{1,0},{2,3},{3,2},{4,5},{5,4},{6,7},{7,6},{8,9},{9,8},{10,11... | collective-permute-start | bytes 1179656 | tf_op jit(solution)/shard_map/ppermute | solution.py:689
  55.5 3.2 collective-permute-start.3
  55.5 3.1 collective-permute-start.5
  56.2 2.5 copy-start.2
  56.2 138.9 %copy-start.3 = (bf16[1,16,48,640]{3,2,1,0:T(8,128)(2,1)}, bf16[1,16,48,640]{3,2,1,0:T(8,128)(2,1)S(1)}, u32[]{:S(2)}) copy-start(bf16[1,16,48,640]{3,2,1,0:T(8,128)(2,1)S(1)} %get-tuple-element.144) | copy-start | bytes 2949124
  59.4 20.3 %copy-start.12 = (s32[1,2,1,256,2]{3,4,2,1,0:T(2,128)S(1)}, s32[1,2,1,256,2]{3,4,2,1,0:T(2,128)}, u32[]{:S(2)}) copy-start(s32[1,2,1,256,2]{3,4,2,1,0:T(2,128)} %param.19) | copy-start | bytes 12292
  79.7 10.0 %copy-start.5 = (bf16[1,768,768]{2,1,0:T(8,128)(2,1)S(1)}, bf16[1,768,768]{2,1,0:T(8,128)(2,1)}, u32[]{:S(2)}) copy-start(bf16[1,768,768]{2,1,0:T(8,128)(2,1)} %all-gather.3.cloned.1.call-done) | copy-start | bytes 3538948
  79.7 9.9 %collective-permute-start.6 = (bf16[768,768]{1,0:T(8,128)(2,1)}, bf16[768,768]{1,0:T(8,128)(2,1)}, u32[]{:S(2)}, u32[]{:S(2)}) collective-permute-start(bf16[768,768]{1,0:T(8,128)(2,1)} %bitcast.76), channel_id=1, source_target_pairs={{0,16},{16,0},{1,17},{17,1},{2,18},{18,2},{3,19},{19,3},{4,20},{20... | collective-permute-start | bytes 3538952 | tf_op jit(solution)/shard_map/ppermute | solution.py:685
  79.9 7.7 %collective-permute-start.7 = (s32[256,2]{1,0:T(8,128)S(1)}, s32[256,2]{1,0:T(8,128)S(1)}, u32[]{:S(2)}, u32[]{:S(2)}) collective-permute-start(s32[256,2]{1,0:T(8,128)S(1)} %bitcast.84), channel_id=1, source_target_pairs={{0,0},{1,16},{2,1},{3,17},{16,2},{17,18},{18,3},{19,19},{4,4},{5,2... | collective-permute-start | bytes 6152 | tf_op jit(solution)/shard_map/ppermute | solution.py:702
  80.8 8.1 %collective-permute-start.8 = (s32[256,2]{1,0:T(8,128)S(1)}, s32[256,2]{1,0:T(8,128)S(1)}, u32[]{:S(2)}, u32[]{:S(2)}) collective-permute-start(s32[256,2]{1,0:T(8,128)S(1)} %bitcast.85), channel_id=1, source_target_pairs={{0,2},{1,18},{2,3},{3,19},{16,0},{17,16},{18,1},{19,17},{4,6},{5,2... | collective-permute-start | bytes 6152 | tf_op jit(solution)/shard_map/ppermute | solution.py:702
  184.0 11.0 %collective-permute-start.10 = (bf16[256,768]{1,0:T(8,128)(2,1)}, bf16[256,768]{1,0:T(8,128)(2,1)S(1)}, u32[]{:S(2)}, u32[]{:S(2)}) collective-permute-start(bf16[256,768]{1,0:T(8,128)(2,1)} %get-tuple-element.69.own.refs_0_), channel_id=1, source_target_pairs={{0,1},{1,0},{2,3},{3,2},{4,5},{5,4},{6,7},{7,6},{8,9},{9,8},{10,11... | collective-permute-start | bytes 1179656 | tf_op jit(solution)/shard_map/ppermute | solution.py:689
  184.0 12.6 %collective-permute-start.9 = (bf16[256,768]{1,0:T(8,128)(2,1)}, bf16[256,768]{1,0:T(8,128)(2,1)S(1)}, u32[]{:S(2)}, u32[]{:S(2)}) collective-permute-start(bf16[256,768]{1,0:T(8,128)(2,1)} %get-tuple-element.69.own.refs_0_), channel_id=1, source_target_pairs={{0,16},{16,0},{1,17},{17,1},{2,18},{18,2},{3,19},{19,3},{4,20},{20... | collective-permute-start | bytes 1179656 | tf_op jit(solution)/shard_map/ppermute | solution.py:685
  195.0 1.7 copy-start.15
  195.0 1.7 collective-permute-start.11
  197.4 12.2 %copy-start.11 = (bf16[2,1,256,768]{3,2,1,0:T(8,128)(2,1)S(1)}, bf16[2,1,256,768]{3,2,1,0:T(8,128)(2,1)}, u32[]{:S(2)}) copy-start(bf16[2,1,256,768]{3,2,1,0:T(8,128)(2,1)} %param.11) | copy-start | bytes 2359300
  206.2 10.8 %all-to-all-start.1 = ((bf16[4,192,256]{2,1,0:T(8,128)(2,1)}), bf16[4,192,256]{2,1,0:T(8,128)(2,1)S(1)}, u32[]{:S(2)}, u32[]{:S(2)}) async-start(bf16[4,192,256]{2,1,0:T(8,128)(2,1)} %get-tuple-element.72.attended), calls=%async_computation.1 | async-start | bytes 786432 | tf_op jit(solution)/shard_map/all_to_all | solution.py:735
  209.7 12.8 %collective-permute-start.12 = (bf16[256,768]{1,0:T(8,128)(2,1)S(1)}, bf16[256,768]{1,0:T(8,128)(2,1)S(1)}, u32[]{:S(2)}, u32[]{:S(2)}) collective-permute-start(bf16[256,768]{1,0:T(8,128)(2,1)S(1)} %dynamic-slice_bitcast_fusion), channel_id=1, source_target_pairs={{0,0},{1,16},{2,1},{3,17},{16,2},{17,18},{18,3},{19,19},{4,4},{5,2... | collective-permute-start | bytes 1179656 | tf_op jit(solution)/shard_map/ppermute | solution.py:702
  385.3 10.8 %all-to-all-start.2 = ((bf16[4,192,256]{2,1,0:T(8,128)(2,1)}), bf16[4,192,256]{2,1,0:T(8,128)(2,1)S(1)}, u32[]{:S(2)}, u32[]{:S(2)}) async-start(bf16[4,192,256]{2,1,0:T(8,128)(2,1)} %get-tuple-element.80), calls=%async_computation.2 | async-start | bytes 786432 | tf_op jit(solution)/shard_map/all_to_all | solution.py:735
  388.8 153.0 %collective-permute-start.14 = (bf16[768,896]{1,0:T(8,128)(2,1)}, bf16[768,896]{1,0:T(8,128)(2,1)S(1)}, u32[]{:S(2)}, u32[]{:S(2)}) collective-permute-start(bf16[768,896]{1,0:T(8,128)(2,1)} %get-tuple-element.112), channel_id=1, source_target_pairs={{0,16},{1,17},{2,18},{3,19},{4,20},{5,21},{6,22},{7,23},{8,24},{9,... | collective-permute-start | bytes 4128776 | tf_op jit(solution)/shard_map/ppermute | solution.py:1329
  519.6 22.8 %copy-start.4 = (bf16[768,896]{1,0:T(8,128)(2,1)S(1)}, bf16[768,896]{1,0:T(8,128)(2,1)}, u32[]{:S(2)}) copy-start(bf16[768,896]{1,0:T(8,128)(2,1)} %get-tuple-element.112) | copy-start | bytes 4128772
  537.0 5.4 collective-permute-start.13
  538.3 10.9 %all-to-all-start.3 = ((bf16[4,192,256]{2,1,0:T(8,128)(2,1)}), bf16[4,192,256]{2,1,0:T(8,128)(2,1)S(1)}, u32[]{:S(2)}, u32[]{:S(2)}) async-start(bf16[4,192,256]{2,1,0:T(8,128)(2,1)} %get-tuple-element.101), calls=%async_computation.3 | async-start | bytes 786432 | tf_op jit(solution)/shard_map/all_to_all | solution.py:735
  549.1 5.1 copy-start.8
  549.1 75.1 %all-to-all-start.4 = ((bf16[16,48,896]{2,1,0:T(8,128)(2,1)}), bf16[16,48,896]{2,1,0:T(8,128)(2,1)S(1)}, u32[]{:S(2)}, u32[]{:S(2)}) async-start(bf16[16,48,896]{2,1,0:T(8,128)(2,1)} %bitcast.39), calls=%async_computation.4 | async-start | bytes 2752512 | tf_op jit(solution)/shard_map/all_to_all | solution.py:728
  621.7 4.8 copy-start.6
  621.7 5.7 copy-start.1
  (6 other events, 4.5 us)
Sparse Core Ops, SparseCore 0:
  10.8 60.6 all-gather.2

commit v5 on v3

v5 whole, which is shorter than its diff:
```python
import functools

import jax
import jax.numpy as jnp
from jax import lax
from jax.experimental import pallas as pl
from jax.experimental.pallas import tpu as pltpu
from jax.sharding import Mesh
from jax.sharding import PartitionSpec as P

F32 = jnp.float32
BF16 = jnp.bfloat16
EPS = 1e-06
SECTION, EXPERT, ZHI, ZLO = "section", "expert", "zhi", "zlo"
FORWARD, BACKWARD, BOTH = "forward", "backward", "both"
MASKED = -1e30
GROUP = 4
RANKS = (EXPERT, ZHI, ZLO)
VMEM_LIMIT = 60 << 20

NN = (((1,), (0,)), ((), ()))
NT = (((1,), (1,)), ((), ()))
TN = (((0,), (0,)), ((), ()))


def mm(left, right, dims=NN):
    return lax.dot_general(left, right, dims, preferred_element_type=F32)


def inverse_rms(values):
    return lax.rsqrt(jnp.mean(values * values, axis=-1, keepdims=True) + EPS)


def whole(array):
    rank = len(array.shape)
    return pl.BlockSpec(array.shape, lambda *unused: (0,) * rank)


def ordered(body, skipped):
    def inner(*refs):
        return body(*refs[skipped:])

    return inner if skipped else body


def fetched(body, picked, skipped):
    def inner(*refs):
        refs = list(refs)
        semaphores = refs.pop()
        blocks = refs[-len(picked) :]
        del refs[-len(picked) :]
        copies = []
        for place, index in enumerate(sorted(picked)):
            source = refs[skipped + index].at[pl.ds(picked[index], 1)]
            copy = pltpu.make_async_copy(source, blocks[place], semaphores.at[place])
            copy.start()
            copies.append(copy)
            refs[skipped + index] = blocks[place]
        for copy in copies:
            copy.wait()
        return body(*refs)

    return inner


REMOTE = pl.DeviceIdType.MESH


def remote(source, target, send, recv, peer):
    return pltpu.make_async_remote_copy(
        src_ref=source, dst_ref=target, send_sem=send, recv_sem=recv, device_id=peer, device_id_type=REMOTE
    )


def across(index, step):
    return (index, index + 1 - 2 * (index % 2), (index + 2) % 4, 3 - index)[step]


def greet(peers):
    barrier = pltpu.get_barrier_semaphore()
    for peer in peers:
        pl.semaphore_signal(barrier, inc=1, device_id=peer, device_id_type=REMOTE)
    pl.semaphore_wait(barrier, len(peers))


def call(body, name, outs, args, scalars=None, scratch=(), flops=0, after=(), collective=None, anywhere=(),
         out_anywhere=(), picks=()):
    specs = [pl.BlockSpec(memory_space=pl.ANY)] * len(after)
    specs += [pl.BlockSpec(memory_space=pltpu.SMEM)] if scalars is not None else []
    picked = dict(picks)
    specs += [
        pl.BlockSpec(memory_space=pl.ANY if index in anywhere or index in picked else pltpu.VMEM)
        for index in range(len(args))
    ]
    operands = list(after) + ([scalars] if scalars is not None else []) + list(args)
    moved = sum(a.size * a.dtype.itemsize for a in list(args) + list(outs))
    body = ordered(body, len(after))
    if picked:
        body = fetched(body, picked, int(scalars is not None))
        scratch = list(scratch) + [
            pltpu.VMEM((1, *args[index].shape[1:]), args[index].dtype) for index in sorted(picked)
        ] + [pltpu.SemaphoreType.DMA((len(picked),))]
    return pl.pallas_call(
        body,
        name=name,
        in_specs=specs,
        out_specs=[
            pl.BlockSpec(memory_space=pl.ANY if index in out_anywhere else pltpu.VMEM)
            for index in range(len(outs))
        ],
        out_shape=list(outs),
        scratch_shapes=list(scratch),
        compiler_params=pltpu.CompilerParams(
            vmem_limit_bytes=VMEM_LIMIT, collective_id=collective, has_side_effects=collective is not None
        ),
        cost_estimate=pl.CostEstimate(flops=flops, bytes_accessed=moved, transcendentals=0),
    )(*operands)


def shape(dims, dtype):
    return jax.ShapeDtypeStruct(tuple(dims), dtype)


def bucket_onehot(buckets, span, spacing):
    width = 2 * span * GROUP
    column = lax.broadcasted_iota(jnp.int32, (buckets, width), 1)
    delta = column // (2 * span)
    distance = column - delta * (2 * span) - span + span * delta
    bucket = jnp.where(distance >= 0, distance // spacing, -1)
    row = lax.broadcasted_iota(jnp.int32, (buckets, width), 0)
    return (bucket == row).astype(BF16)


def fill_bias(first_head, heads, table, vectors, bias, span, spacing):
    buckets, head_count = table.shape
    hot = bucket_onehot(buckets, span, spacing)
    rows = mm(table, hot, TN)
    column = lax.broadcasted_iota(jnp.int32, (1, 2 * span * GROUP), 1)
    rows = jnp.where(column < span, MASKED, rows)
    vectors[0:head_count, :] = rows
    for head in range(heads):
        picked = vectors[pl.ds(first_head + head, 1), :]
        for delta in range(GROUP):
            piece = picked[:, delta * 2 * span : (delta + 1) * 2 * span]
            spread = jnp.broadcast_to(piece, (span, 2 * span))
            rolled = pltpu.roll(spread, span, 1, stride=1, stride_axis=0)
            bias[head * GROUP + delta] = rolled[:, :span]


def attention_forward(sizes, ids, own, flip, side, side_flip, gain, weight, table,
                      out, mixed, gathered, stats, vectors, bias):
    span, heads, size, spacing, unused = sizes
    width = heads * size
    fill_bias(ids[4] * heads, heads, table[...], vectors, bias, span, spacing)
    for slot, piece in enumerate((own, flip, side, side_flip)):
        gathered[pl.ds(pl.multiple_of(ids[slot] * span, span), span), :] = piece[...]
    for part in range(GROUP):
        project(gathered, slice(part * span, (part + 1) * span), gain[...], weight[:, : 3 * width], mixed)
    for head in range(heads):
        attend_head(sizes, head, mixed, bias, out, stats)


def project(gathered, rows, gain, weight, mixed):
    values = gathered[rows, :].astype(F32)
    normed = (values * inverse_rms(values) * gain.astype(F32)).astype(BF16)
    mixed[rows, :] = mm(normed, weight).astype(BF16)


def attend_head(sizes, head, mixed, bias, out, stats):
    span, heads, size = sizes[:3]
    width = heads * size
    columns = slice(head * size, (head + 1) * size)
    query_t = (mixed[:, columns].astype(F32) * size ** (-0.5)).T.astype(BF16)
    key = mixed[:, width + head * size : width + (head + 1) * size]
    value_t = mixed[:, 2 * width + head * size : 2 * width + (head + 1) * size].astype(F32).T.astype(BF16)
    for part in range(GROUP):
        mine = slice(part * span, (part + 1) * span)
        blocks = []
        for other in range(part + 1):
            raw = mm(key[other * span : (other + 1) * span], query_t[:, mine])
            blocks.append(raw + bias[head * GROUP + part - other])
        top = functools.reduce(jnp.maximum, [jnp.max(b, axis=0, keepdims=True) for b in blocks])
        total = jnp.zeros_like(top)
        gained = jnp.zeros((size, span), F32)
        for other, block in enumerate(blocks):
            raised = jnp.exp(block - top)
            total = total + jnp.sum(raised, axis=0, keepdims=True)
            gained = gained + mm(value_t[:, other * span : (other + 1) * span], raised.astype(BF16))
        out[part, columns, :] = (gained / total).astype(BF16)
        stats[head : head + 1, mine] = top + jnp.log(total)


def route_masks(columns, experts):
    lane = lax.broadcasted_iota(jnp.int32, (columns[0].shape[0], experts), 1).astype(F32)
    return [(column == lane).astype(F32) for column in columns]


def route_columns(routes):
    return [routes[:, k : k + 1].astype(F32) for k in range(2)]


def slot_places(columns, masks, capacity):
    tokens = columns[0].shape[0]
    members = (masks[0] + masks[1]).astype(BF16)
    row = lax.broadcasted_iota(jnp.int32, (tokens, tokens), 0)
    column = lax.broadcasted_iota(jnp.int32, (tokens, tokens), 1)
    earlier = mm((row > column).astype(BF16), members)
    return [
        columns[k] * capacity + jnp.sum(earlier * masks[k], axis=1, keepdims=True) for k in range(2)
    ]


def dispatch(total, gain, router, masks, places, slots, outgoing, normed_two, aux):
    tokens = total.shape[0]
    normed = (total * inverse_rms(total) * gain.astype(F32)).astype(BF16)
    normed_two[...] = normed
    logits = mm(normed, router)
    chosen = [jnp.sum(logits * mask, axis=1, keepdims=True) for mask in masks]
    first = jax.nn.sigmoid(chosen[0] - chosen[1])
    lane = lax.broadcasted_iota(jnp.int32, (tokens, 128), 1)
    packed = jnp.zeros((tokens, 128), F32)
    for index, entry in enumerate((places[0], places[1], first, 1.0 - first)):
        packed = jnp.where(lane == index, entry, packed)
    aux[...] = packed
    packed_t = packed.T
    hot = fill_slots(packed_t, slots, 0) + fill_slots(packed_t, slots, 1)
    outgoing[...] = mm(hot, normed).astype(BF16)
    return packed


def pick_rows(slot, slots):
    lane = lax.broadcasted_iota(jnp.int32, (slot.shape[0], slots), 1).astype(F32)
    return (lane == slot).astype(BF16)


def fill_slots(aux_t, slots, k):
    row = lax.broadcasted_iota(jnp.int32, (slots, aux_t.shape[1]), 0).astype(F32)
    return (row == aux_t[k : k + 1, :]).astype(BF16)


def after_attention(capacity, attended, own, w_out, gain, router, routes,
                    outgoing, middle, normed_two, aux):
    experts = router.shape[1]
    width = attended.shape[1]
    total = own[...].astype(F32)
    for group in range(GROUP):
        total = total + mm(attended[group], w_out[group * width : (group + 1) * width, :], TN)
    middle[...] = total
    columns = route_columns(routes)
    masks = route_masks(columns, experts)
    places = slot_places(columns, masks, capacity)
    dispatch(total, gain[...], router[...], masks, places, experts * capacity, outgoing, normed_two, aux)


def expert_forward(rows, w_in, w_down, activation, slope, produced, total):
    step = pl.program_id(0)

    @pl.when(step == 0)
    def clear():
        total[...] = jnp.zeros_like(total)

    chunk = rows.shape[0] // 4
    for part in range(4):
        mine = slice(part * chunk, (part + 1) * chunk)
        hidden = mm(rows[mine, :], w_in[...])
        half = 0.5 * (1.0 + lax.erf(hidden * 0.7071067811865476))
        bell = jnp.exp(-0.5 * hidden * hidden) * 0.3989422804014327
        raised = (hidden * half).astype(BF16)
        activation[mine, :] = raised
        slope[mine, :] = (half + hidden * bell).astype(BF16)
        total[mine, :] += mm(raised, w_down[...])

    @pl.when(step == pl.num_programs(0) - 1)
    def finish():
        produced[...] = total[...].astype(BF16)


def expert_backward(arrived_grad, w_in, w_down, slope, hidden_grad, rows_grad, total):
    step = pl.program_id(0)

    @pl.when(step == 0)
    def clear():
        total[...] = jnp.zeros_like(total)

    chunk = arrived_grad.shape[0] // 4
    for part in range(4):
        mine = slice(part * chunk, (part + 1) * chunk)
        lifted = mm(arrived_grad[mine, :], w_down[...], NT) * slope[mine, :].astype(F32)
        lowered = lifted.astype(BF16)
        hidden_grad[mine, :] = lowered
        total[mine, :] += mm(lowered, w_in[...], NT)

    @pl.when(step == pl.num_programs(0) - 1)
    def finish():
        rows_grad[...] = total[...].astype(BF16)


def tile_of(hidden):
    return 768 if hidden % 768 == 0 else hidden


def run_expert_forward(rows, w_in, w_down):
    count, features = rows.shape
    hidden = w_in.shape[1]
    tile = tile_of(hidden)
    return pl.pallas_call(
        expert_forward,
        name="expert_forward",
        grid=(hidden // tile,),
        in_specs=[
            whole(rows),
            pl.BlockSpec((features, tile), lambda j: (0, j)),
            pl.BlockSpec((tile, features), lambda j: (j, 0)),
        ],
        out_specs=[
            pl.BlockSpec((count, tile), lambda j: (0, j)),
            pl.BlockSpec((count, tile), lambda j: (0, j)),
            pl.BlockSpec((count, features), lambda j: (0, 0)),
        ],
        out_shape=[shape((count, hidden), BF16), shape((count, hidden), BF16), shape((count, features), BF16)],
        scratch_shapes=[pltpu.VMEM((count, features), F32)],
        compiler_params=pltpu.CompilerParams(vmem_limit_bytes=VMEM_LIMIT),
        cost_estimate=pl.CostEstimate(
            flops=4 * count * features * hidden, bytes_accessed=30 << 20, transcendentals=2 * count * hidden
        ),
    )(rows, w_in, w_down)


def run_expert_backward(arrived_grad, w_in, w_down, slope):
    count, features = arrived_grad.shape
    hidden = w_in.shape[1]
    tile = tile_of(hidden)
    return pl.pallas_call(
        expert_backward,
        name="expert_backward",
        grid=(hidden // tile,),
        in_specs=[
            whole(arrived_grad),
            pl.BlockSpec((features, tile), lambda j: (0, j)),
            pl.BlockSpec((tile, features), lambda j: (j, 0)),
            pl.BlockSpec((count, tile), lambda j: (0, j)),
        ],
        out_specs=[
            pl.BlockSpec((count, tile), lambda j: (0, j)),
            pl.BlockSpec((count, features), lambda j: (0, 0)),
        ],
        out_shape=[shape((count, hidden), BF16), shape((count, features), BF16)],
        scratch_shapes=[pltpu.VMEM((count, features), F32)],
        compiler_params=pltpu.CompilerParams(vmem_limit_bytes=VMEM_LIMIT),
        cost_estimate=pl.CostEstimate(
            flops=4 * count * features * hidden, bytes_accessed=30 << 20, transcendentals=0
        ),
    )(arrived_grad, w_in, w_down, slope)


def weight_partials(scalars, rows, hidden_grad, activation, arrived_grad, grad_in, grad_down):
    @pl.when(scalars[0] == 1)
    def wanted():
        grad_in[...] = mm(rows[...], hidden_grad[...], TN).astype(BF16)
        grad_down[...] = mm(activation[...], arrived_grad[...], TN).astype(BF16)


def run_weight_partials(wanted, rows, hidden_grad, activation, arrived_grad):
    count, features = rows.shape
    hidden = hidden_grad.shape[1]
    tile = tile_of(hidden)
    return pl.pallas_call(
        weight_partials,
        name="weight_partials",
        grid_spec=pltpu.PrefetchScalarGridSpec(
            num_scalar_prefetch=1,
            grid=(hidden // tile,),
            in_specs=[
                pl.BlockSpec((count, features), lambda j, s: (0, 0)),
                pl.BlockSpec((count, tile), lambda j, s: (0, j * s[0])),
                pl.BlockSpec((count, tile), lambda j, s: (0, j * s[0])),
                pl.BlockSpec((count, features), lambda j, s: (0, 0)),
            ],
            out_specs=[
                pl.BlockSpec((features, tile), lambda j, s: (0, j * s[0])),
                pl.BlockSpec((tile, features), lambda j, s: (j * s[0], 0)),
            ],
        ),
        out_shape=[shape((features, hidden), BF16), shape((hidden, features), BF16)],
        compiler_params=pltpu.CompilerParams(vmem_limit_bytes=VMEM_LIMIT),
        cost_estimate=pl.CostEstimate(
            flops=4 * count * features * hidden, bytes_accessed=30 << 20, transcendentals=0
        ),
    )(wanted, rows, hidden_grad, activation, arrived_grad)


def weight_totals(scalars, left, right, sent, left_1, right_1, sent_1, after, total):
    @pl.when(scalars[0] == 0)
    def first():
        total[...] = mm(left[...], right[...], TN) + sent[...].astype(F32)

    @pl.when(scalars[0] == 1)
    def second():
        total[...] = mm(left_1[...], right_1[...], TN) + sent_1[...].astype(F32)


def run_weight_totals(core, first, second, tiled_left, after):
    count, features = first[1 if tiled_left else 0].shape
    hidden = first[0 if tiled_left else 1].shape[1]
    tile = tile_of(hidden)

    def specs(which):
        def step(j, s):
            return jnp.where(s[0] == which, j, 0)

        full = pl.BlockSpec((count, features), lambda j, s: (0, 0))
        part = pl.BlockSpec((count, tile), lambda j, s: (0, step(j, s)))
        if tiled_left:
            return [part, full, pl.BlockSpec((tile, features), lambda j, s: (step(j, s), 0))]
        return [full, part, pl.BlockSpec((features, tile), lambda j, s: (0, step(j, s)))]

    if tiled_left:
        out_spec = pl.BlockSpec((tile, features), lambda j, s: (j, 0))
        dims = (hidden, features)
    else:
        out_spec = pl.BlockSpec((features, tile), lambda j, s: (0, j))
        dims = (features, hidden)
    return pl.pallas_call(
        weight_totals,
        name="weight_totals",
        grid_spec=pltpu.PrefetchScalarGridSpec(
            num_scalar_prefetch=1, grid=(hidden // tile,),
            in_specs=specs(0) + specs(1) + [pl.BlockSpec(memory_space=pl.ANY)], out_specs=out_spec,
        ),
        out_shape=shape(dims, F32),
        compiler_params=pltpu.CompilerParams(vmem_limit_bytes=VMEM_LIMIT),
        cost_estimate=pl.CostEstimate(
            flops=2 * count * features * hidden, bytes_accessed=30 << 20, transcendentals=0
        ),
    )(core, *first, *second, after)


def combined(returned, packed, middle):
    slots = returned.shape[0]
    outs = [mm(pick_rows(packed[:, k : k + 1], slots), returned) for k in range(2)]
    return middle + packed[:, 2:3] * outs[0] + packed[:, 3:4] * outs[1], outs[0] - outs[1]


def combine(returned, aux, middle, result, difference):
    total, gap = combined(returned[...], aux[...], middle[...])
    result[...] = total.astype(BF16)
    difference[...] = gap


def spread_values(values, packed, slots):
    packed_t = packed.T
    total = jnp.zeros((slots, values.shape[1]), F32)
    for k in range(2):
        total = total + mm(fill_slots(packed_t, slots, k), (values * packed[:, 2 + k : 3 + k]).astype(BF16))
    return total.astype(BF16)


def spread_grads(upstream, aux, outgoing):
    outgoing[...] = spread_values(upstream[...].astype(F32), aux[...], outgoing.shape[0])


def norm_backward(values, gain, grad):
    scale = inverse_rms(values)
    unit = values * scale
    lifted = grad * gain
    back = scale * (lifted - unit * jnp.mean(lifted * unit, axis=-1, keepdims=True))
    return back, jnp.sum(grad * unit, axis=0, keepdims=True)


def publisher(grad_in, grad_down, out_in, out_down, held, in_sem, out_sem):
    tile = held.shape[2]
    tiles = held.shape[0] // 2
    across_tiles = [(slice(None), pl.ds(index * tile, tile)) for index in range(tiles)]
    down_tiles = [pl.ds(index * tile, tile) for index in range(tiles)]
    places = [(grad_in.at[p], out_in.at[p]) for p in across_tiles]
    places += [(grad_down.at[p], out_down.at[p]) for p in down_tiles]
    fetches = [
        pltpu.make_async_copy(pair[0], held.at[index], in_sem.at[index]) for index, pair in enumerate(places)
    ]
    stores = [
        pltpu.make_async_copy(held.at[index], pair[1], out_sem.at[index]) for index, pair in enumerate(places)
    ]
    for fetch in fetches:
        fetch.start()
    return fetches, stores


def token_backward(returned, packed, flow, difference, middle, normed_two, attended, gain, router, out_block,
                   columns, middle_grad, attended_grad, shared_grad, fetches=(), stores=()):
    slots, features = returned.shape
    experts = router.shape[1]
    width = attended.shape[1]

    def publish(quarter):
        share = len(fetches) // 4
        for index in range(quarter * share, (quarter + 1) * share):
            fetches[index].wait()
            stores[index].start()

    hot = pick_rows(packed[:, 0:1], slots) + pick_rows(packed[:, 1:2], slots)
    token_grad = mm(hot, returned)
    publish(0)
    shift = jnp.sum(flow * difference, axis=1, keepdims=True) * packed[:, 2:3] * packed[:, 3:4]
    masks = route_masks(columns, experts)
    logits_grad = (shift * (masks[0] - masks[1])).astype(BF16)
    token_grad = token_grad + mm(logits_grad, router, NT)
    back, gain_part = norm_backward(middle, gain.astype(F32), token_grad)
    total = flow + back
    middle_grad[...] = total
    branch = total.astype(BF16)
    publish(1)
    for group in range(GROUP):
        mine = slice(group * width, (group + 1) * width)
        attended_grad[group] = mm(out_block(group), branch, NT).astype(BF16)
        shared_grad[mine, :features] = mm(attended[group], branch).astype(BF16)
        if group == 1:
            publish(2)
    publish(3)
    tail = shared_grad.shape[1] - features
    gain_column = jnp.broadcast_to(gain_part, (8, features)).T
    lane = lax.broadcasted_iota(jnp.int32, (features, tail), 1)
    shared_grad[:, features:] = jnp.where(lane == experts, gain_column[:, 0:1], 0.0).astype(BF16)
    shared_grad[:, features : features + experts] = mm(normed_two, logits_grad, TN).astype(BF16)
    for store in stores:
        store.wait()


def before_attention(returned, aux, upstream, difference, middle, normed_two, attended, gain,
                     router, w_out, routes, middle_grad, attended_grad, shared_grad):
    width = attended.shape[1]
    token_backward(
        returned[...], aux[...], upstream[...].astype(F32), difference[...], middle[...], normed_two[...],
        attended, gain[...], router[...], lambda group: w_out[group * width : (group + 1) * width, :],
        route_columns(routes), middle_grad, attended_grad, shared_grad,
    )


def before_attention_fused(sizes, returned, aux, upstream, difference, middle, normed_two, attended,
                           early, w_outs, routes, grad_in, grad_down,
                           middle_grad, attended_grad, shared_grad, out_in, out_down, held, in_sem, out_sem):
    fetches, stores = publisher(grad_in, grad_down, out_in, out_down, held, in_sem, out_sem)
    router, unused, gain_two, unused_1 = unpack_small(sizes, early, 0)
    token_backward(
        returned[...], aux[...], upstream[...].astype(F32), difference[...], middle[...], normed_two[...],
        attended, gain_two, router, lambda group: out_rows(sizes, w_outs, 0, group),
        route_columns(routes[0].T), middle_grad, attended_grad, shared_grad, fetches, stores,
    )


def back_head(sizes, head, mixed, stats, attended, grads, bias, work):
    mixed_grad, sums, key_total, value_total, turned, strips = work
    span, heads, size, spacing = sizes[:4]
    width = heads * size
    count = span // spacing
    row = lax.broadcasted_iota(jnp.int32, (span, span), 0)
    column = lax.broadcasted_iota(jnp.int32, (span, span), 1)
    later = (column % spacing) >= (row % spacing)
    lane = lax.broadcasted_iota(jnp.int32, (span, 128), 0) // spacing
    backwards = (count - 1 - lane == lax.broadcasted_iota(jnp.int32, (span, 128), 1)).astype(F32)
    columns = slice(head * size, (head + 1) * size)
    key_columns = slice(width + head * size, width + (head + 1) * size)
    value_columns = slice(2 * width + head * size, 2 * width + (head + 1) * size)
    query = (mixed[:, columns].astype(F32) * size ** (-0.5)).astype(BF16)
    query_t = query.astype(F32).T.astype(BF16)
    key = mixed[:, key_columns]
    key_t = key.astype(F32).T.astype(BF16)
    value = mixed[:, value_columns]
    key_total[...] = jnp.zeros_like(key_total)
    value_total[...] = jnp.zeros_like(value_total)
    sums[...] = jnp.zeros_like(sums)
    for part in range(GROUP):
        mine = slice(part * span, (part + 1) * span)
        grad_t = grads[part, columns, :]
        delta_row = jnp.sum(
            grad_t.astype(F32) * attended[part, columns, :].astype(F32), axis=0, keepdims=True
        )
        level = stats[head : head + 1, mine]
        query_total = jnp.zeros((size, span), F32)
        for other in range(part + 1):
            theirs = slice(other * span, (other + 1) * span)
            raw = mm(key[theirs], query_t[:, mine])
            prob = jnp.exp(raw + (bias[head * GROUP + part - other] - level))
            prob_grad = mm(value[theirs], grad_t)
            low = (prob * (prob_grad - delta_row)).astype(BF16)
            sums[part - other] += low.astype(F32)
            query_total = query_total + mm(key_t[:, theirs], low)
            key_total[theirs, :] += mm(low, query[mine])
            value_total[theirs, :] += mm(prob.astype(BF16), grad_t, NT)
        turned[:, mine] = query_total * size ** (-0.5)
    mixed_grad[:, columns] = turned[...].T.astype(BF16)
    mixed_grad[:, key_columns] = key_total[...].astype(BF16)
    mixed_grad[:, value_columns] = value_total[...].astype(BF16)
    for delta in range(GROUP):
        upper = jnp.where(later, sums[delta], 0.0)
        for side, block in enumerate((upper, sums[delta] - upper)):
            tiles = lax.dot_general(
                jnp.sum(block.reshape(count, spacing, span), axis=1), backwards, NN,
                precision=lax.Precision.HIGHEST, preferred_element_type=F32,
            )
            turned_tiles = pltpu.roll(tiles, 0, 1, stride=1, stride_axis=0)
            place = (delta * 2 + side) * 128
            strips[head : head + 1, place : place + 128] = jnp.sum(turned_tiles, axis=0, keepdims=True)


def back_piece(sizes, gathered, rows, gain, weight, mixed_grad):
    values = gathered[rows, :].astype(F32)
    back = mm(mixed_grad[rows, :], weight, NT)
    return back, jnp.sum(back * values * inverse_rms(values), axis=0, keepdims=True)


def weight_share(sizes, gathered, gain, mixed_grad):
    span, heads, size = sizes[:3]
    total = jnp.zeros((gathered.shape[1], 3 * heads * size), F32)
    for part in range(GROUP):
        rows = slice(part * span, (part + 1) * span)
        values = gathered[rows, :].astype(F32)
        normed = (values * inverse_rms(values) * gain.astype(F32)).astype(BF16)
        total = total + mm(normed, mixed_grad[rows, :], TN)
    return total


def extra_columns(sizes, buckets, features, strips, gain_total):
    span, heads, size, spacing, ranks = sizes
    count = span // spacing
    entry = lax.broadcasted_iota(jnp.int32, (GROUP * 2 * 128, 128), 0)
    bucket = (entry // 256) * count + count - 1 - entry % 128 - (entry // 128) % 2
    hot = (bucket == lax.broadcasted_iota(jnp.int32, (GROUP * 2 * 128, 128), 1)) & (entry % 128 < 2 * count)
    table_rows = lax.dot_general(
        strips[...], hot.astype(F32), NN, precision=lax.Precision.HIGHEST, preferred_element_type=F32
    )
    owned = buckets // ranks
    bucket = lax.broadcasted_iota(jnp.int32, (128, features), 0)
    target = (bucket // owned) * (features // ranks) + bucket % owned
    spot = (target == lax.broadcasted_iota(jnp.int32, (128, features), 1)) & (bucket < buckets)
    placed = lax.dot_general(
        table_rows, spot.astype(F32), NN, precision=lax.Precision.HIGHEST, preferred_element_type=F32
    )
    extra = jnp.concatenate([placed, jnp.broadcast_to(gain_total, (8, features))], axis=0)
    return extra.T.astype(BF16)


def attention_backward(sizes, ids, mixed, stats, attended, grads, gathered, gain, weight, table,
                       stay, leave, sent, shared_grad, vectors, bias, *work):
    span, heads, size, spacing, ranks = sizes
    width = heads * size
    mixed_grad, strips = work[0], work[5]
    strips[...] = jnp.zeros_like(strips)
    fill_bias(ids[4] * heads, heads, table[...], vectors, bias, span, spacing)
    for head in range(heads):
        back_head(sizes, head, mixed, stats, attended, grads, bias, work)
    gain_total = 0.0
    for part in range(GROUP):
        rows = pl.ds(pl.multiple_of(ids[5 + part] * span, span), span)
        back, gain_part = back_piece(sizes, gathered, rows, gain[...], weight[:, : 3 * width], mixed_grad)
        gain_total = gain_total + gain_part
        if part == 0:
            stay[...] = back.astype(BF16)
        elif part == 1:
            leave[...] = back.astype(BF16)
        else:
            sent[part - 2] = back.astype(BF16)
    shared_grad[...] = jnp.zeros_like(shared_grad)
    shared_grad[:, : 3 * width] = weight_share(sizes, gathered, gain[...], mixed_grad).astype(BF16)
    shared_grad[:, 3 * width : 3 * width + 16] = extra_columns(
        sizes, table.shape[0], weight.shape[0], strips, gain_total
    )


def first_norm_grad(stay, partner, arrived, own, gain, middle_grad, low):
    grad = stay[...].astype(F32) + partner[0].astype(F32) + arrived[...].astype(F32)
    back, unused = norm_backward(own[...].astype(F32), gain[...].astype(F32), grad)
    low[...] = (middle_grad[...] + back).astype(BF16)


FLIP = [(0, 1), (1, 0)]


def flip(block):
    return lax.ppermute(block, SECTION, FLIP)


def beside(block):
    return lax.ppermute(block, ZLO, FLIP)


def scatter_pairs(turn):
    return [
        (core * 4 + a * 2 + b, b * 4 + (core ^ turn) * 2 + a)
        for core in range(2)
        for a in range(2)
        for b in range(2)
    ]


def to_working(block, turn):
    return lax.ppermute(block, (SECTION, ZHI, ZLO), scatter_pairs(turn))


def to_home(block, section, batch):
    turn = section ^ batch
    pairs = [(after, before) for before, after in scatter_pairs(turn) if before // 4 == section]
    return lax.ppermute(block, (SECTION, ZHI, ZLO), pairs)


def home_pair(blocks, core):
    return jnp.stack([
        jnp.where(core == 0, to_home(blocks[0], 0, batch), to_home(blocks[1], 1, batch))
        for batch in range(2)
    ])


def exchange(block, experts, capacity):
    features = block.shape[-1]
    moved = lax.all_to_all(
        block.reshape(experts, capacity, features), RANKS, split_axis=0, concat_axis=0, tiled=True
    )
    return moved.reshape(experts * capacity, features)


def spread_sum(block, axes, parts):
    rows, columns = block.shape
    moved = lax.all_to_all(
        block.reshape(parts, rows // parts, columns), axes, split_axis=0, concat_axis=0, tiled=True
    )
    return jnp.sum(moved.astype(F32), axis=0)


def regroup(block):
    return lax.all_to_all(block, (ZLO, SECTION), split_axis=0, concat_axis=0, tiled=True)


OFFSETS = [(step, place) for place in (0, 3, 1, 2) for step in range(4)]
SENDS = (12, 13, 14, 15, 4, 5, 6, 7, 8, 9, 10, 11, 1, 2, 3)
BATCH = 4
BATCH_ORDER = (0, 3, 2, 1)


def expert_layer(mode, section, *refs):
    forward = mode != BACKWARD
    backward = mode != FORWARD
    refs = list(refs)

    def take(count):
        taken = refs[:count]
        del refs[:count]
        return taken

    weights = take(4)
    outgoing = take(2 if mode == BOTH else 1)
    if mode == BACKWARD:
        saved_rows, saved_activation, saved_slope, unused, unused_1 = take(5)
    returned = take(len(outgoing))
    if mode == FORWARD:
        kept_rows, kept_activation, kept_slope = take(3)
    else:
        grad_in, grad_down = take(2)
    arrived = take(len(outgoing))
    finished = take(len(outgoing))
    w_in, w_down, activation, slope, totals = take(5)
    send_sem, recv_sem, back_send, back_recv, load_sem = take(5)
    if backward:
        parts, staged, part_send, part_recv, out_sem = take(5)

    core = lax.axis_index(SECTION)
    expert = lax.axis_index(EXPERT)
    place = 2 * lax.axis_index(ZHI) + lax.axis_index(ZLO)
    me = expert * 4 + place
    hidden = w_in.shape[1]
    slot_rows, features = arrived[0].shape[1:]
    rows_in_batch = BATCH * slot_rows
    tile = tile_of(hidden)
    tiles = hidden // tile
    peers = []
    ranks = []
    for step, move in OFFSETS:
        to_expert, to_place = across(expert, step), across(place, move)
        ranks.append(to_expert * 4 + to_place)
        peers.append(dict(expert=to_expert, zhi=to_place // 2, zlo=to_place % 2))

    loads = []

    def load(source, target, index):
        copy = pltpu.make_async_copy(source, target, load_sem.at[index])
        copy.start()
        loads.append(copy)

    @pl.when(core == section)
    def own_weights():
        pltpu.make_async_copy(weights[0], w_in, load_sem.at[0]).start()
        pltpu.make_async_copy(weights[1], w_down, load_sem.at[1]).start()

    @pl.when(core != section)
    def other_weights():
        pltpu.make_async_copy(weights[2], w_in, load_sem.at[0]).start()
        pltpu.make_async_copy(weights[3], w_down, load_sem.at[1]).start()

    if mode == BACKWARD:
        load(saved_activation, activation, 2)
        load(saved_slope, slope, 3)

    greet(peers[1:] + ([dict(section=1 - core)] if backward else []))

    sent = []
    for slot in SENDS:
        for kind, block in enumerate(outgoing):
            copy = remote(block.at[ranks[slot]], arrived[kind].at[slot], send_sem.at[kind, slot],
                          recv_sem.at[kind, slot], peers[slot])
            copy.start()
            sent.append(copy)
    for kind, block in enumerate(outgoing):
        arrived[kind][0] = block[me]

    pltpu.make_async_copy(weights[0], w_in, load_sem.at[0]).wait()
    pltpu.make_async_copy(weights[1], w_down, load_sem.at[1]).wait()
    for copy in loads:
        copy.wait()

    saves = []
    for batch in BATCH_ORDER:
        slots = range(batch * BATCH, (batch + 1) * BATCH)
        mine = slice(batch * rows_in_batch, (batch + 1) * rows_in_batch)
        for slot in slots:
            for kind in range(len(outgoing)):
                if slot:
                    remote(arrived[kind].at[slot], arrived[kind].at[slot], send_sem.at[kind, slot],
                           recv_sem.at[kind, slot], peers[slot]).wait_recv()

        def block_of(kind):
            return arrived[kind][slots[0] : slots[-1] + 1].reshape(rows_in_batch, features)

        def one_tile(index, unused):
            spot = pl.ds(pl.multiple_of(index * tile, tile), tile)
            if forward:
                values = mm(block_of(0), w_in[:, spot])
                half = 0.5 * (1.0 + lax.erf(values * 0.7071067811865476))
                bell = jnp.exp(-0.5 * values * values) * 0.3989422804014327
                raised = (values * half).astype(BF16)
                steep = half + values * bell
                activation[mine, spot] = raised
                if mode == FORWARD:
                    slope[mine, spot] = steep.astype(BF16)
                totals[0] += mm(raised, w_down[spot, :])
            else:
                steep = slope[mine, spot].astype(F32)
            if backward:
                lowered = (mm(block_of(len(outgoing) - 1), w_down[spot, :], NT) * steep).astype(BF16)
                slope[mine, spot] = lowered
                totals[len(outgoing) - 1] += mm(lowered, w_in[:, spot], NT)
            return unused

        totals[...] = jnp.zeros_like(totals)
        lax.fori_loop(0, tiles, one_tile, 0)
        for kind in range(len(outgoing)):
            finished[kind][slots[0] : slots[-1] + 1] = (
                totals[kind].astype(BF16).reshape(BATCH, slot_rows, features)
            )
        for slot in slots:
            for kind in range(len(outgoing)):
                if slot:
                    copy = remote(finished[kind].at[slot], returned[kind].at[me], back_send.at[kind, slot],
                                  back_recv.at[kind, slot], peers[slot])
                    copy.start()
                    sent.append(copy)
                else:
                    returned[kind][me] = finished[kind][0]
        if mode == FORWARD:
            for index, (source, target) in enumerate(((activation, kept_activation), (slope, kept_slope))):
                copy = pltpu.make_async_copy(
                    source.at[mine, :], target.at[mine, :], load_sem.at[2 + 2 * batch + index]
                )
                copy.start()
                saves.append(copy)
    if mode == FORWARD:
        kept_rows[...] = arrived[0][...]

    if backward:
        count = slot_rows * len(OFFSETS)
        grads = arrived[len(outgoing) - 1]
        inputs = arrived[0] if forward else saved_rows
        partner = dict(section=1 - core)

        def share_copy(index):
            return remote(parts.at[index], parts.at[index], part_send.at[index], part_recv.at[index], partner)

        def out_copy(index):
            spot = pl.ds(index // 2 * tile, tile)
            target = grad_down.at[spot, :] if index % 2 else grad_in.at[:, spot]
            return pltpu.make_async_copy(staged.at[index % 2], target, out_sem.at[index])

        for index in range(2 * tiles):
            spot = pl.ds(index // 2 * tile, tile)
            if index % 2:
                value = mm(activation[:, spot], grads[...].reshape(count, features), TN)
            else:
                value = mm(inputs[...].reshape(count, features), slope[:, spot], TN)

            @pl.when(core != section)
            def give():
                parts[index] = value.astype(BF16)
                share_copy(index).start()

            @pl.when(core == section)
            def keep():
                share_copy(index).wait_recv()
                if index >= 2:
                    out_copy(index - 2).wait()
                staged[index % 2] = value + parts[index].astype(F32)
                out_copy(index).start()

    for slot in range(1, len(OFFSETS)):
        for kind in range(len(outgoing)):
            remote(finished[kind].at[slot], returned[kind].at[ranks[slot]], back_send.at[kind, slot],
                   back_recv.at[kind, slot], peers[slot]).wait_recv()
    for copy in sent:
        copy.wait_send()
    for copy in saves:
        copy.wait()
    if backward:
        @pl.when(core != section)
        def given():
            for index in range(2 * tiles):
                share_copy(index).wait_send()

        @pl.when(core == section)
        def stored():
            for index in range(2 * tiles - 2, 2 * tiles):
                out_copy(index).wait()


def run_expert_layer(mode, section, weights, outgoing, saved=(), grads=()):
    ranks, slot_rows, features = outgoing[0].shape
    hidden = weights[0].shape[1]
    count = ranks * slot_rows
    tile = tile_of(hidden)
    kinds = len(outgoing)
    anywhere = pl.BlockSpec(memory_space=pl.ANY)
    local = pl.BlockSpec(memory_space=pltpu.VMEM)
    block = shape((ranks, slot_rows, features), BF16)
    wide = shape((count, hidden), BF16)
    in_specs = [anywhere] * 4 + [local] * kinds
    operands = [*weights, *outgoing]
    out_shape = [block] * kinds
    out_specs = [local] * kinds
    aliases = {}
    if mode == FORWARD:
        out_shape += [block, wide, wide]
        out_specs += [local, anywhere, anywhere]
    else:
        out_shape += [shape((features, hidden), F32), shape((hidden, features), F32)]
        out_specs += [anywhere, anywhere]
    if mode == BACKWARD:
        aliases = {len(operands) + 3: kinds, len(operands) + 4: kinds + 1}
        operands += [*saved, *grads]
        in_specs += [local, anywhere, anywhere, anywhere, anywhere]
    scratch = [pltpu.VMEM(block.shape, BF16)] * (2 * kinds) + [
        pltpu.VMEM((features, hidden), BF16), pltpu.VMEM((hidden, features), BF16),
        pltpu.VMEM((count, hidden), BF16), pltpu.VMEM((count, hidden), BF16),
        pltpu.VMEM((kinds, BATCH * slot_rows, features), F32),
        pltpu.SemaphoreType.DMA((kinds, ranks)), pltpu.SemaphoreType.DMA((kinds, ranks)),
        pltpu.SemaphoreType.DMA((kinds, ranks)), pltpu.SemaphoreType.DMA((kinds, ranks)),
        pltpu.SemaphoreType.DMA((10,)),
    ]
    if mode != FORWARD:
        pieces = 2 * hidden // tile
        scratch += [
            pltpu.VMEM((pieces, features, tile), BF16), pltpu.VMEM((2, features, tile), F32),
            pltpu.SemaphoreType.DMA((pieces,)), pltpu.SemaphoreType.DMA((pieces,)),
            pltpu.SemaphoreType.DMA((pieces,)),
        ]
    return pl.pallas_call(
        functools.partial(expert_layer, mode, section),
        name="expert_layer_" + mode,
        in_specs=in_specs,
        out_specs=out_specs,
        out_shape=out_shape,
        scratch_shapes=scratch,
        input_output_aliases=aliases,
        compiler_params=pltpu.CompilerParams(
            collective_id={FORWARD: 1, BOTH: 2, BACKWARD: 3}[mode], has_side_effects=True,
            vmem_limit_bytes=VMEM_LIMIT,
        ),
        cost_estimate=pl.CostEstimate(
            flops=8 * kinds * count * features * hidden, bytes_accessed=160 << 20, transcendentals=0
        ),
    )(*operands)


class Sizes:
    def __init__(self, **sizes):
        self.__dict__.update(sizes)
        self.width = self.heads * self.size
        self.length = GROUP * self.span
        self.slots = self.experts * self.capacity
        self.attention = (self.span, self.heads, self.size, self.spacing, self.ranks)
        self.base = 3 * self.width // 128 * 128
        self.offset = 3 * self.width - self.base
        self.table_lane = self.offset + self.experts + 2


def unpack_small(sizes, early, section):
    tail = early[section, :, :, sizes.base :]
    tail = tail.reshape(sizes.features, tail.shape[2])
    tail_t = tail.astype(F32).T
    first = sizes.offset + sizes.experts
    bucket = lax.broadcasted_iota(jnp.int32, (sizes.buckets, sizes.features), 0)
    target = bucket // sizes.table_rows * sizes.shard_rows + bucket % sizes.table_rows
    spot = target == lax.broadcasted_iota(jnp.int32, (sizes.buckets, sizes.features), 1)
    table = mm(spot.astype(BF16), tail).astype(BF16)
    router = tail[:, sizes.offset : first]
    return router, tail_t[first : first + 1, :], tail_t[first + 1 : first + 2, :], table


def qkv_columns(sizes, early, section):
    return early[section, :, :, : 3 * sizes.width].reshape(sizes.features, 3 * sizes.width)


def out_rows(sizes, w_outs, section, group):
    per_group = sizes.ranks // GROUP
    rows = w_outs[section, group * per_group : (group + 1) * per_group]
    return rows.reshape(sizes.width, sizes.features)


def whereabouts():
    core, zhi, zlo = (lax.axis_index(name) for name in (SECTION, ZHI, ZLO))
    return core, zhi, zlo, 2 * zhi + zlo, 2 * zlo + core


def line_peers(core, place):
    peers = []
    for move in range(4):
        spot = across(place, move)
        for turn in range(2):
            if move or turn:
                peers.append(dict(section=1 - core if turn else core, zhi=spot // 2, zlo=spot % 2))
    return peers


class Regroup:
    def __init__(self, block, target, send, recv):
        core, unused, zlo, unused_1, mine = whereabouts()
        self.copies = []
        for index, (turn, move) in enumerate(((0, 1), (1, 1), (1, 0))):
            to_core = 1 - core if turn else core
            to_zlo = 1 - zlo if move else zlo
            copy = remote(block.at[2 * to_zlo + to_core], target.at[mine], send.at[index], recv.at[index],
                          dict(section=to_core, zlo=to_zlo))
            copy.start()
            self.copies.append(copy)
        target[mine] = block[mine]

    def wait(self):
        for copy in self.copies:
            copy.wait()


class WeightGather:
    def __init__(self, blocks, shard, early, w_outs, staged, sems):
        (self.early_send, self.early_recv, self.stage_send, self.stage_recv, self.local_sem,
         self.out_send, self.out_recv) = sems
        self.blocks, self.shard, self.early, self.w_outs, self.staged = blocks, shard, early, w_outs, staged
        self.core, unused, self.zlo, self.place, unused_1 = whereabouts()
        self.other = 1 - self.core
        self.expert = lax.axis_index(EXPERT)
        self.beside_x = across(self.expert, 1)
        self.beside_y = across(self.expert, 2)
        self.places = [across(self.place, move) for move in range(4)]
        self.sections = (self.core, self.other)
        self.started = []
        self.early_count = self.out_count = 0

    def at(self, section, owner, spot):
        return self.early.at[section, owner * 4 + spot]

    def send(self, source, section, owner, spot, peer):
        copy = remote(source, self.at(section, owner, spot), self.early_send.at[self.early_count],
                      self.early_recv.at[section, owner * 4 + spot], peer)
        self.early_count += 1
        copy.start()
        self.started.append(copy)

    def arrived(self, section, owner, spot):
        block = self.at(section, owner, spot)
        remote(block, block, self.early_send.at[0], self.early_recv.at[section, owner * 4 + spot],
               dict(section=self.other)).wait_recv()

    def out_at(self, section, owner, spot):
        return self.w_outs.at[section, owner * 4 + spot]

    def send_out(self, source, owner, spot, peer):
        copy = remote(source, self.out_at(self.core, owner, spot), self.out_send.at[self.out_count],
                      self.out_recv.at[self.core, owner * 4 + spot], peer)
        self.out_count += 1
        copy.start()
        self.started.append(copy)

    def out_arrived(self, section, owner, spot):
        block = self.out_at(section, owner, spot)
        remote(block, block, self.out_send.at[0], self.out_recv.at[section, owner * 4 + spot],
               dict(section=self.other)).wait_recv()

    def trade(self):
        self.trades = []
        for parity in range(2):
            copy = remote(self.blocks.at[2 * parity + self.other], self.staged.at[parity],
                          self.stage_send.at[parity], self.stage_recv.at[parity], dict(section=self.other))
            copy.start()
            self.trades.append(copy)

    def start(self):
        for which, section in enumerate(self.sections):
            if which:
                for copy in self.trades:
                    copy.wait()

            def block_for(parity):
                return self.staged.at[parity] if which else self.blocks.at[2 * parity + self.core]

            for spot in self.places[1:]:
                self.send(block_for(spot % 2), section, self.expert, self.place,
                          dict(zhi=spot // 2, zlo=spot % 2))
            for peer in (self.beside_x, self.beside_y):
                self.send(block_for(self.zlo), section, self.expert, self.place, dict(expert=peer))
            local = pltpu.make_async_copy(
                block_for(self.zlo), self.at(section, self.expert, self.place), self.local_sem
            )
            local.start()
            local.wait()

    def along_z(self):
        for spot in self.places[1:]:
            for section in self.sections:
                self.arrived(section, self.expert, spot)
                for peer in (self.beside_x, self.beside_y):
                    self.send(self.at(section, self.expert, spot), section, self.expert, spot, dict(expert=peer))

    def over_plane(self):
        for section in self.sections:
            for step, spot in enumerate(self.places):
                self.arrived(section, self.beside_x, spot)
                self.arrived(section, self.beside_y, spot)
                source, peer = ((self.beside_x, self.beside_y), (self.beside_y, self.beside_x))[step % 2]
                self.send(self.at(section, source, spot), section, source, spot, dict(expert=peer))

    def finish_early(self):
        diagonal = 3 - self.expert
        for section in self.sections:
            for spot in self.places:
                self.arrived(section, diagonal, spot)

    def out_start(self):
        for spot in self.places[1:]:
            self.send_out(self.shard, self.expert, self.place, dict(zhi=spot // 2, zlo=spot % 2))
        for peer in (self.beside_x, self.beside_y):
            self.send_out(self.shard, self.expert, self.place, dict(expert=peer))
        self.send_out(self.shard, self.expert, self.place, dict(section=self.other))
        local = pltpu.make_async_copy(
            self.shard, self.out_at(self.core, self.expert, self.place), self.local_sem
        )
        local.start()
        local.wait()

    def out_pass(self, owner, spot, peers):
        block = self.out_at(self.core, owner, spot)
        self.out_arrived(self.core, owner, spot)
        for peer in peers + [dict(section=self.other)]:
            self.send_out(block, owner, spot, peer)

    def out_along_z(self):
        for spot in self.places[1:]:
            self.out_pass(self.expert, spot, [dict(expert=self.beside_x), dict(expert=self.beside_y)])

    def out_over_plane(self):
        for step, spot in enumerate(self.places):
            self.out_pass(self.beside_x, spot, [dict(expert=self.beside_y)] if step % 2 == 0 else [])
            self.out_pass(self.beside_y, spot, [dict(expert=self.beside_x)] if step % 2 else [])

    def out_finish(self):
        for spot in self.places:
            self.out_pass(3 - self.expert, spot, [])

    def out_all(self):
        for owner in range(4):
            for spot in range(4):
                self.out_arrived(self.other, owner, spot)

    def close(self):
        for copy in self.started:
            copy.wait_send()


def attend(section, sizes, *refs):
    refs = list(refs)

    def take(count):
        taken = refs[:count]
        del refs[:count]
        return taken

    if section == 0:
        home_rows, home_routes, blocks, shard = take(4)
    else:
        returned, aux_before, middle_before, early, w_outs, routes, given = take(7)
    outcome, mixed, gathered, stats, outgoing, middle, normed_two, aux, attended = take(9)
    if section == 0:
        early, w_outs, routes = take(3)
    else:
        result, difference, spread = take(3)
    vectors, bias, pair_send, pair_recv, group_send, group_recv = take(6)
    span = sizes.span
    core, zhi, zlo, place, group = whereabouts()
    expert = lax.axis_index(EXPERT)

    def rows_of(piece):
        return pl.ds(pl.multiple_of(piece * span, span), span)

    own, flipped = group, 2 * zlo + 1 - core
    side, side_flipped = 2 * (1 - zlo) + core, 2 * (1 - zlo) + 1 - core
    partner, beside_z = dict(section=1 - core), dict(zlo=1 - zlo)
    greet(line_peers(core, place)
          + ([dict(expert=across(expert, 1)), dict(expert=across(expert, 2))] if section == 0 else []))

    pair_copies = []

    def pass_piece(piece, index, peer):
        block = gathered.at[rows_of(piece)]
        copy = remote(block, block, pair_send.at[index], pair_recv.at[index], peer)
        copy.start()
        pair_copies.append(copy)

    def await_piece(piece, index):
        block = gathered.at[rows_of(piece)]
        remote(block, block, pair_send.at[index], pair_recv.at[index], partner).wait_recv()

    if section == 0:
        staged, home_send, home_recv = take(3)
        gather = WeightGather(blocks, shard, early, w_outs, staged, take(7))
        gather.trade()
        aligned = (zlo == zhi) & (zlo == core)

        def to_work(source, target, index, slot, turn):
            peer = dict(section=zlo, zhi=1 - core if turn else core, zlo=zhi)
            return remote(source, target, home_send.at[index], home_recv.at[slot], peer)

        rows_copy = to_work(home_rows, gathered.at[rows_of(place)], 0, 0, 0)
        route_copies = [
            to_work(home_routes.at[1 - core if turn else core], routes.at[core], 1 + turn, 1 + core, turn)
            for turn in range(2)
        ]

        @pl.when(aligned)
        def keep():
            gathered[rows_of(place), :] = home_rows[...]
            routes[core] = home_routes[core]

        @pl.when(jnp.logical_not(aligned))
        def give():
            rows_copy.start()
            route_copies[0].start()

        route_copies[1].start()
        gather.start()

        @pl.when(jnp.logical_not(aligned))
        def landed():
            rows_copy.wait_recv()

        pass_piece(own, 0, beside_z)
        pass_piece(own, 1, partner)
        gather.along_z()
        gather.over_plane()
        gather.out_start()
        await_piece(side, 0)
        pass_piece(side, 2, partner)
        gather.finish_early()
    else:
        total, gap = combined(returned[...], aux_before[...], middle_before[...])
        result[...] = total.astype(BF16)
        gathered[rows_of(own), :] = total.astype(BF16)
        difference[...] = gap
        pass_piece(own, 0, beside_z)
        pass_piece(own, 1, partner)

    router, gain_one, gain_two, table = unpack_small(sizes, early, section)
    fill_bias(group * sizes.heads + sizes.table_lane, sizes.heads, table, vectors, bias, span, sizes.spacing)
    weight = qkv_columns(sizes, early, section)
    project(gathered, rows_of(own), gain_one, weight, mixed)
    await_piece(flipped, 1)
    project(gathered, rows_of(flipped), gain_one, weight, mixed)
    if section:
        await_piece(side, 0)
        pass_piece(side, 2, partner)
    project(gathered, rows_of(side), gain_one, weight, mixed)
    await_piece(side_flipped, 2)
    project(gathered, rows_of(side_flipped), gain_one, weight, mixed)
    for head in range(sizes.heads):
        if section == 0 and head < 3:
            (gather.out_along_z, gather.out_over_plane, gather.out_finish)[head]()
        attend_head(sizes.attention, head, mixed, bias, outcome, stats)
    if section == 0:
        for stage in (gather.out_along_z, gather.out_over_plane, gather.out_finish)[sizes.heads :]:
            stage()
        for which in range(2):
            @pl.when(jnp.logical_not(aligned & (core == which)))
            def routed():
                remote(routes.at[which], routes.at[which], home_send.at[1], home_recv.at[1 + which],
                       partner).wait_recv()
    trade = Regroup(outcome, attended, group_send, group_recv)
    columns_t = routes[section].T
    columns = [columns_t[:, k : k + 1] for k in range(2)]
    masks = route_masks(columns, sizes.experts)
    places = slot_places(columns, masks, sizes.capacity)
    if section == 0:
        gather.out_all()
    total = gathered[rows_of(own), :].astype(F32)
    trade.wait()
    for member in range(GROUP):
        total = total + mm(attended[member], out_rows(sizes, w_outs, section, member), TN)
    middle[...] = total
    packed = dispatch(total, gain_two, router, masks, places, sizes.slots, outgoing, normed_two, aux)
    if section:
        spread[...] = spread_values(given[...].astype(F32), packed, sizes.slots)
    for copy in pair_copies:
        copy.wait_send()
    if section == 0:
        gather.close()

        @pl.when(jnp.logical_not(aligned))
        def given_away():
            rows_copy.wait_send()
            route_copies[0].wait_send()

        route_copies[1].wait_send()


def run_attend(section, sizes, operands, collective):
    dma = pltpu.SemaphoreType.DMA
    span, features, width = sizes.span, sizes.features, sizes.width
    outs = [
        shape((GROUP, width, span), BF16), shape((sizes.length, 3 * width), BF16),
        shape((sizes.length, features), BF16), shape((8, sizes.length), F32),
        shape((sizes.slots, features), BF16), shape((span, features), F32), shape((span, features), BF16),
        shape((span, 128), F32), shape((GROUP, width, span), BF16),
    ]
    scratch = [
        pltpu.VMEM((128, 2 * span * GROUP), F32), pltpu.VMEM((sizes.heads * GROUP, span, span), F32),
        dma((3,)), dma((3,)), dma((3,)), dma((3,)),
    ]
    if section == 0:
        unused, rows, columns = operands[2].shape
        outs += [
            shape((2, sizes.ranks, rows, columns), BF16), shape((2, sizes.ranks, rows, features), BF16),
            shape((2, 8, span), F32),
        ]
        scratch += [
            pltpu.VMEM((2, rows, columns), BF16), dma((3,)), dma((3,)),
            dma((30,)), dma((2, sizes.ranks)), dma((2,)), dma((2,)), dma, dma((34,)), dma((2, sizes.ranks)),
        ]
    else:
        outs += [shape((span, features), BF16), shape((span, features), F32), shape((sizes.slots, features), BF16)]
    return call(
        functools.partial(attend, section, sizes), "attend", outs, operands, scratch=scratch,
        flops=6 << 30, collective=collective,
    )


def unpack(sizes, home, owned, shared, stream_grads, grad_qkv, grad_out, grad_router, grad_gains, grad_table):
    width, features, experts = sizes.width, sizes.features, sizes.experts
    stream_grads[...] = home[...].astype(F32)
    grad_qkv[...] = jnp.concatenate(
        [owned[member, :, part * width : (part + 1) * width] for part in range(3) for member in range(GROUP)],
        axis=1,
    )
    grad_out[...] = shared[:, :features]
    tail = shared[:, features:]
    grad_router[...] = tail[:, :experts]
    ends = [owned[member, :, sizes.base :] for member in range(GROUP)]
    grad_table[...] = jnp.concatenate(
        [end[: sizes.table_rows, sizes.offset : sizes.offset + sizes.heads] for end in ends], axis=1
    )
    spot = sizes.offset + 8
    grad_gains[0:1, :] = (ends[0] + ends[1] + ends[2] + ends[3]).T[spot : spot + 1, :]
    grad_gains[1:2, :] = tail.T[experts : experts + 1, :]


class Homes:
    def __init__(self, home, send, recv):
        self.home, self.send_sem, self.recv_sem = home, send, recv
        self.core, self.zhi, self.zlo, unused, unused_1 = whereabouts()
        self.aligned = (self.zlo == self.zhi) & (self.zlo == self.core)
        self.sent = []

    def copy(self, block, section, index):
        return remote(block, self.home.at[self.zhi], self.send_sem.at[index], self.recv_sem.at[self.zhi],
                      dict(section=section, zhi=self.zlo, zlo=self.core))

    def send(self, block, section):
        index = len(self.sent)
        here = self.aligned & (self.core == section)
        self.sent.append((block, section))

        @pl.when(here)
        def keep():
            self.home[self.zhi] = block[...]

        @pl.when(jnp.logical_not(here))
        def give():
            self.copy(block, section, index).start()

    def close(self):
        for batch in range(2):
            @pl.when(jnp.logical_not(self.aligned & (self.zhi == batch)))
            def landed():
                block = self.home.at[batch]
                remote(block, block, self.send_sem.at[0], self.recv_sem.at[batch],
                       dict(section=1 - self.core)).wait_recv()
        for index, (block, section) in enumerate(self.sent):
            @pl.when(jnp.logical_not(self.aligned & (self.core == section)))
            def left():
                self.copy(block, section, index).wait_send()


class PlaneSum:
    def __init__(self, source, shares, send, recv):
        self.source, self.shares = source, shares
        self.expert = lax.axis_index(EXPERT)
        self.copies = []
        for step in range(1, 4):
            spot = across(self.expert, step)
            copy = remote(source.at[pl.ds(4 * spot, 4)], shares.at[step - 1], send.at[step - 1],
                          recv.at[step - 1], dict(expert=spot))
            copy.start()
            self.copies.append(copy)

    def total(self):
        for copy in self.copies:
            copy.wait()
        total = self.source[pl.ds(4 * self.expert, 4)].astype(F32)
        for step in range(3):
            total = total + self.shares[step].astype(F32)
        return total.astype(BF16)


def attend_back(section, sizes, *refs):
    refs = list(refs)

    def take(count):
        taken = refs[:count]
        del refs[:count]
        return taken

    last = section == 0
    early, mixed, stats, outcome, gathered = take(5)
    if last:
        middle_grad, attended_grad, first_low, *shared, other_qkv = take(6)
        home, owned, owned_shared, = take(3)
    else:
        (returned, returned_grad, aux, middle, given, normed_two, attended, w_outs, routes,
         first_result, next_aux) = take(11)
        shared_grad, low, qkv_grad, home, spread = take(5)
    vectors, bias, *work = take(8)
    (grads, kept, leaving, sent, partner_share, side_share, group_send, group_recv, pair_send, pair_recv,
     home_send, home_recv) = take(12)
    mixed_grad, strips = work[0], work[5]
    span, features, width = sizes.span, sizes.features, sizes.width
    core, zhi, zlo, place, group = whereabouts()
    expert = lax.axis_index(EXPERT)
    if last:
        (low, qkv_grad, other_shares, qkv_shares, shared_in, shared_sum, shared_shares, line_totals, pieces,
         shared_totals, shared_parts, other_send, other_recv, plane_send, plane_recv, in_send, in_recv,
         shared_send, shared_recv, line_send, line_recv, spread_send, spread_recv) = take(23)
    else:
        middle_grad, attended_grad, second_result = take(3)
    greet(line_peers(core, place) + ([dict(expert=across(expert, step)) for step in range(1, 4)] if last else []))
    homes = Homes(home, home_send, home_recv)
    router, gain_one, gain_two, table = unpack_small(sizes, early, 0)
    if not last:
        homes.send(first_result, 0)
        total, difference = combined(returned[...], aux[...], middle[...])
        second_result[...] = total.astype(BF16)
        token_backward(
            returned_grad[...], aux[...], given[...].astype(F32), difference, middle[...], normed_two[...],
            attended, gain_two, router, lambda member: out_rows(sizes, w_outs, 0, member),
            route_columns(routes[section].T), middle_grad, attended_grad, shared_grad,
        )
    trade = Regroup(attended_grad, grads, group_send, group_recv)
    if last:
        partner = dict(section=1 - core)
        for which in range(2):
            @pl.when(core != which)
            def pass_share():
                remote(shared[which], shared_in, in_send, in_recv, partner).start()

        other_sum = PlaneSum(other_qkv, other_shares, other_send, other_recv)
        homes.send(first_low, 1)
    else:
        homes.send(second_result, 1)
    strips[...] = jnp.zeros_like(strips)
    fill_bias(group * sizes.heads + sizes.table_lane, sizes.heads, table, vectors, bias, span, sizes.spacing)
    if last:
        remote(shared[0], shared_in, in_send, in_recv, partner).wait_recv()
        for which in range(2):
            @pl.when(core == which)
            def add_share():
                shared_sum[...] = shared[which][...] + shared_in[...]

        plane_shared = PlaneSum(shared_sum, shared_shares, shared_send, shared_recv)
        line_copies = []

        def to_owners(owner_section, totals):
            line_totals[owner_section] = totals
            turn = (core + owner_section) % 2
            mine = 2 * place + core
            for move in range(4):
                spot = across(place, move)
                copy = remote(line_totals.at[owner_section, spot], pieces.at[mine],
                              line_send.at[owner_section, move], line_recv.at[turn, move],
                              dict(section=owner_section, zhi=spot // 2, zlo=spot % 2))
                line_copies.append((copy, owner_section, move))
                if move:
                    copy.start()
                else:
                    @pl.when(core != owner_section)
                    def give():
                        copy.start()

                    @pl.when(core == owner_section)
                    def keep():
                        pieces[mine] = line_totals[owner_section, place]

    trade.wait()
    for head in range(sizes.heads):
        if last and head == sizes.heads - 1:
            to_owners(1, other_sum.total())
        back_head(sizes.attention, head, mixed, stats, outcome, grads, bias, work)
    weight = qkv_columns(sizes, early, 0)

    def rows_of(piece):
        return pl.ds(pl.multiple_of(piece * span, span), span)

    def piece_back(piece):
        return back_piece(sizes.attention, gathered, rows_of(piece), gain_one, weight, mixed_grad)

    back, gain_total = piece_back(2 * zlo + 1 - core)
    sent[0] = back.astype(BF16)
    back, gain_part = piece_back(2 * (1 - zlo) + 1 - core)
    sent[1] = back.astype(BF16)
    partner_copy = remote(sent, partner_share, pair_send.at[0], pair_recv.at[0], dict(section=1 - core))
    partner_copy.start()
    gain_total = gain_total + gain_part
    leave, gain_part = piece_back(2 * (1 - zlo) + core)
    gain_total = gain_total + gain_part
    partner_copy.wait()
    leaving[...] = (leave + partner_share[1].astype(F32)).astype(BF16)
    stay, gain_part = piece_back(group)
    side_copy = remote(leaving, side_share, pair_send.at[1], pair_recv.at[1], dict(zlo=1 - zlo))
    side_copy.start()
    gain_total = gain_total + gain_part
    kept[...] = stay + partner_share[0].astype(F32)
    columns = qkv_grad.shape[2]
    weights = weight_share(sizes.attention, gathered, gain_one, mixed_grad).astype(BF16)
    extra = extra_columns(sizes.attention, sizes.buckets, features, strips, gain_total)
    by_rank = (sizes.ranks, sizes.shard_rows)
    qkv_grad[:, :, 3 * width :] = jnp.concatenate(
        [extra, jnp.zeros((features, columns - 3 * width - 16), BF16)], axis=1
    ).reshape(*by_rank, columns - 3 * width)
    qkv_grad[:, :, : 3 * width] = weights.reshape(*by_rank, 3 * width)
    if last:
        qkv_sum = PlaneSum(qkv_grad, qkv_shares, plane_send, plane_recv)
        shared_totals[...] = plane_shared.total()
        for move in range(4):
            spot = across(place, move)
            if move:
                copy = remote(shared_totals.at[spot], shared_parts.at[move], spread_send.at[move],
                              spread_recv.at[move], dict(zhi=spot // 2, zlo=spot % 2))
                copy.start()
                line_copies.append((copy, None, move))
            else:
                shared_parts[0] = shared_totals[place]
    side_copy.wait()
    own = gathered[rows_of(group), :].astype(F32)
    back, unused = norm_backward(own, gain_one, kept[...] + side_share[...].astype(F32))
    total = (middle_grad[...] + back).astype(BF16)
    low[...] = total
    if not last:
        spread[...] = spread_values(total.astype(F32), next_aux[...], sizes.slots)
    else:
        homes.send(low, 0)
        to_owners(0, qkv_sum.total())
        for turn in range(2):
            for move in range(4):
                if move or turn:
                    block = pieces.at[2 * across(place, move) + (1 - core if turn else core)]
                    remote(block, block, line_send.at[0, 0], line_recv.at[turn, move], partner).wait_recv()
        for member in range(GROUP):
            owned[member] = pieces[member].astype(F32) + pieces[GROUP + member].astype(F32)
        for copy, owner_section, move in line_copies:
            if owner_section is None:
                copy.wait()
            elif move:
                copy.wait_send()
            else:
                @pl.when(core != owner_section)
                def gone():
                    copy.wait_send()
        owned_shared[...] = sum(shared_parts[move].astype(F32) for move in range(4))
        remote(shared[0], shared_in, in_send, in_recv, partner).wait_send()
    homes.close()


def run_attend_back(section, sizes, operands, picks, collective):
    dma = pltpu.SemaphoreType.DMA
    span, features, width, ranks = sizes.span, sizes.features, sizes.width, sizes.ranks
    rows = sizes.shard_rows
    columns = -(-(3 * width + 16) // 128) * 128
    tail = features + -(-(sizes.experts + 1) // 128) * 128
    block = (span, features)
    last = section == 0
    if last:
        outs = [shape((2, *block), BF16), shape((GROUP, rows, columns), F32), shape((rows, tail), F32)]
    else:
        outs = [shape((features, tail), BF16), shape(block, BF16), shape((ranks, rows, columns), BF16),
                shape((2, *block), BF16), shape((sizes.slots, features), BF16)]
    scratch = [
        pltpu.VMEM((128, 2 * span * GROUP), F32), pltpu.VMEM((sizes.heads * GROUP, span, span), F32),
        pltpu.VMEM((sizes.length, 3 * width), BF16), pltpu.VMEM((GROUP, span, span), F32),
        pltpu.VMEM((sizes.length, sizes.size), F32), pltpu.VMEM((sizes.length, sizes.size), F32),
        pltpu.VMEM((sizes.size, sizes.length), F32), pltpu.VMEM((8, GROUP * 2 * 128), F32),
        pltpu.VMEM((GROUP, width, span), BF16), pltpu.VMEM(block, F32), pltpu.VMEM(block, BF16),
        pltpu.VMEM((2, *block), BF16), pltpu.VMEM((2, *block), BF16), pltpu.VMEM(block, BF16),
        dma((3,)), dma((3,)), dma((2,)), dma((2,)), dma((2,)), dma((2,)),
    ]
    if last:
        scratch += [
            pltpu.VMEM(block, BF16), pltpu.VMEM((ranks, rows, columns), BF16),
            pltpu.VMEM((3, 4, rows, columns), BF16), pltpu.VMEM((3, 4, rows, columns), BF16),
            pltpu.VMEM((ranks, rows, tail), BF16), pltpu.VMEM((ranks, rows, tail), BF16),
            pltpu.VMEM((3, 4, rows, tail), BF16), pltpu.VMEM((2, 4, rows, columns), BF16),
            pltpu.VMEM((2 * GROUP, rows, columns), BF16), pltpu.VMEM((4, rows, tail), BF16),
            pltpu.VMEM((4, rows, tail), BF16),
            dma((3,)), dma((3,)), dma((3,)), dma((3,)), dma, dma, dma((3,)), dma((3,)),
            dma((2, 4)), dma((2, 4)), dma((4,)), dma((4,)),
        ]
    else:
        scratch += [pltpu.VMEM(block, F32), pltpu.VMEM((GROUP, width, span), BF16), pltpu.VMEM(block, BF16)]
    return call(
        functools.partial(attend_back, section, sizes), "attend_back", outs, operands, scratch=scratch,
        flops=10 << 30, collective=collective, picks=picks,
    )


def per_device(inputs, cotangent, qkv_shard, out_shard, router_shard, gain_shard, table_shard,
               w_expert_in, w_expert_out, routes):
    core = lax.axis_index(SECTION)
    zhi = lax.axis_index(ZHI)
    zlo = lax.axis_index(ZLO)
    span, features = inputs.shape[2:]
    ranks = lax.axis_size(RANKS)
    shard_rows = qkv_shard.shape[1]
    experts = router_shard.shape[2]
    table_rows, head_count = table_shard.shape[1:]
    buckets = table_rows * ranks
    heads = head_count // GROUP
    size = features // head_count
    width = heads * size
    spacing = GROUP * span // buckets
    capacity = max(2, 4 * span // experts)
    slots = experts * capacity
    group = 2 * zlo + core
    sizes = (span, heads, size, spacing, ranks)
    ids = jnp.stack([
        group, 2 * zlo + 1 - core, 2 * (1 - zlo) + core, 2 * (1 - zlo) + 1 - core, group,
        group, 2 * (1 - zlo) + core, 2 * zlo + 1 - core, 2 * (1 - zlo) + 1 - core,
    ]).astype(jnp.int32)
    core_id = core.astype(jnp.int32).reshape(1)

    w_in = w_expert_in[0, 0]
    w_down = w_expert_out[0, 0]
    w_in_other = flip(w_in)
    w_down_other = flip(w_down)
    fused = lax.axis_size(EXPERT) == 4 and features == tile_of(w_in.shape[1])
    shared_sizes = Sizes(
        span=span, heads=heads, size=size, spacing=spacing, ranks=ranks, experts=experts, capacity=capacity,
        features=features, buckets=buckets, shard_rows=shard_rows, table_rows=table_rows,
    )

    home_rows = lax.dynamic_index_in_dim(inputs, core, 0, keepdims=False)[0]
    given = to_working(lax.dynamic_index_in_dim(cotangent, core, 0, keepdims=False)[0], 0)
    if not fused:
        own = to_working(home_rows, 0)
        route_parts = [
            to_working(lax.dynamic_index_in_dim(routes[0], core ^ turn, 0, keepdims=False)[0], turn)
            for turn in range(2)
        ]
        section_routes = [
            jnp.where(zhi == section, route_parts[0], route_parts[1]) for section in range(2)
        ]

    small = jnp.concatenate([
        router_shard[0],
        gain_shard[0].T,
        jnp.pad(table_shard[0], ((0, shard_rows - table_rows), (0, 0))),
    ], axis=1)
    by_group = jnp.transpose(
        qkv_shard[0].reshape(shard_rows, 3, GROUP, width), (2, 0, 1, 3)
    ).reshape(GROUP, shard_rows, 3 * width)
    by_group = jnp.concatenate(
        [by_group, jnp.broadcast_to(small[None], (GROUP, *small.shape))], axis=2
    )
    by_group = jnp.pad(by_group, ((0, 0), (0, 0), (0, -by_group.shape[2] % 128)))
    columns = by_group.shape[2]
    if fused:
        home_routes = jnp.pad(
            jnp.swapaxes(routes[0, :, 0], 1, 2).astype(F32), ((0, 0), (0, 6), (0, 0))
        )
        first = run_attend(0, shared_sizes, [home_rows, home_routes, by_group, out_shard[0]], 4)
        early_all, w_out_all, route_all = first[9:]
    else:
        whole_early = lax.all_gather(by_group, RANKS, axis=1, tiled=True)
        kept = lax.dynamic_index_in_dim(whole_early, group, 0, keepdims=False)
        traded = flip(lax.dynamic_index_in_dim(whole_early, 2 * zlo + 1 - core, 0, keepdims=False))
        early = [
            jnp.where(core == section, kept, traded).reshape(features, columns) for section in range(2)
        ]
        w_out_own = lax.all_gather(out_shard[0], RANKS, axis=0, tiled=True)
        w_out_other = flip(w_out_own)
        w_outs = [jnp.where(core == which, w_out_own, w_out_other) for which in range(2)]
    expert_weights = (w_in, w_down, w_in_other, w_down_other)

    def by_rank(block):
        return block.reshape(ranks, capacity, features)

    def by_slot(block):
        return block.reshape(slots, features)

    weights = []
    for section in range(0 if fused else 2):
        is_own = core == section
        others = early[section][:, 3 * width :]
        router = others[:, :experts]
        gains = others[:, experts : experts + 2].T
        table = others[:, experts + 2 : experts + 2 + head_count]
        table = table.reshape(ranks, shard_rows, head_count)[:, :table_rows].reshape(buckets, head_count)
        weights.append((
            early[section], router, gains[0:1], gains[1:2], table,
            jnp.where(is_own, w_in, w_in_other), jnp.where(is_own, w_down, w_down_other),
        ))

    bias_scratch = [
        pltpu.VMEM((-(-head_count // 8) * 8, 2 * span * GROUP), F32),
        pltpu.VMEM((heads * GROUP, span, span), F32),
    ]
    length = GROUP * span
    blocks = span // spacing
    states = []
    results = []
    if fused:
        (outcome, mixed, gathered, stats, outgoing, middle, normed_two, aux, attended) = first[:9]
        returned, arrived, activation, slope = run_expert_layer(FORWARD, 0, expert_weights, [by_rank(outgoing)])
        second = run_attend(
            1, shared_sizes, [by_slot(returned), aux, middle, early_all, w_out_all, route_all, given], 5)
        result, difference, spread = second[9:]
        (outcome, mixed, gathered, stats, outgoing, middle, normed_two, aux, attended) = second[:9]
        returned, returned_grad, grad_in, grad_down = run_expert_layer(
            BOTH, 1, expert_weights, [by_rank(outgoing), by_rank(spread)])
        shared_1, low_1, qkv_1, section_outputs, spread = run_attend_back(
            1, shared_sizes,
            [early_all, mixed, stats, outcome, gathered, by_slot(returned), by_slot(returned_grad), aux, middle,
             given, normed_two, attended, w_out_all, route_all, result, first[7]],
            ((0, 1), (12, 1)), 6)
        returned, grad_in, grad_down = run_expert_layer(
            BACKWARD, 0, expert_weights, [by_rank(spread)], [arrived, activation, slope], [grad_in, grad_down])
        (outcome, mixed, gathered, stats, unused, middle, normed_two, aux, attended) = first[:9]
        pieces = 2 * grad_in.shape[1] // features
        middle_grad, attended_grad, shared_0, grad_in, grad_down = call(
            functools.partial(before_attention_fused, shared_sizes), "before_attention",
            [shape((span, features), F32), shape((GROUP, width, span), BF16), shape(shared_1.shape, BF16),
             shape(grad_in.shape, F32), shape(grad_down.shape, F32)],
            [by_slot(returned), aux, low_1, difference, middle, normed_two, attended, early_all, w_out_all,
             route_all, grad_in, grad_down],
            scratch=[pltpu.VMEM((pieces, features, features), F32),
                     pltpu.SemaphoreType.DMA((pieces,)), pltpu.SemaphoreType.DMA((pieces,))],
            flops=2 << 30, anywhere=(10, 11), out_anywhere=(3, 4), picks=((7, 0), (8, 0)),
        )
        ranked = (ranks, shard_rows, -1)
        home, owned, shared_sum = run_attend_back(
            0, shared_sizes,
            [early_all, mixed, stats, outcome, gathered, middle_grad, attended_grad, low_1,
             shared_0.reshape(ranked), shared_1.reshape(ranked), qkv_1],
            ((0, 0),), 7)
        section_grads, grad_qkv, grad_out, grad_router, grad_gains, grad_table = call(
            functools.partial(unpack, shared_sizes), "unpack",
            [shape(home.shape, F32), shape((shard_rows, 3 * features), F32), shape((shard_rows, features), F32),
             shape((shard_rows, experts), F32), shape((2, shard_rows), F32),
             shape((table_rows, head_count), F32)],
            [home, owned, shared_sum],
        )
    stream = None if fused else own
    for section in range(0 if fused else 2):
        qkv, router, gain_one, gain_two, table, expert_in, expert_down = weights[section]
        route_rows = section_routes[section]
        side = beside(stream)
        pieces = (stream, flip(stream), side, flip(side))
        outcome, mixed, gathered, stats = call(
            functools.partial(attention_forward, sizes), "attention_forward",
            [shape((GROUP, width, span), BF16), shape((length, 3 * width), BF16),
             shape((length, features), BF16), shape((8, length), F32)],
            [*pieces, gain_one, qkv, table], scalars=ids, scratch=bias_scratch, flops=4 << 30,
        )
        attended = regroup(outcome)
        outgoing, middle, normed_two, aux = call(
            functools.partial(after_attention, capacity), "after_attention",
            [shape((slots, features), BF16), shape((span, features), F32),
             shape((span, features), BF16), shape((span, 128), F32)],
            [attended, stream, w_outs[section], gain_two, router, route_rows], flops=1 << 30,
        )
        arrived = exchange(outgoing, experts, capacity)
        activation, slope, produced = run_expert_forward(arrived, expert_in, expert_down)
        returned = exchange(produced, experts, capacity)
        result, difference = call(
            combine, "combine", [shape((span, features), BF16), shape((span, features), F32)],
            [returned, aux, middle], flops=1 << 30,
        )
        states.append((stream, outcome, mixed, gathered, stats, attended, middle, normed_two, aux,
                       arrived, activation, slope, difference))
        results.append(result)
        stream = result

    if not fused:
        section_outputs = home_pair(results, core)

    upstream = given
    shared_grads = [None, None]
    shared_partner = [None, None]
    shared_qkv = [None, None]
    qkv_grads = [None, None]
    expert_states = [None, None]
    partials = [None, None]
    stream_grads = [None, None]
    for section in (() if fused else (1, 0)):
        qkv, router, gain_one, gain_two, table, expert_in, expert_down = weights[section]
        w_out = w_outs[section]
        (stream, outcome, mixed, gathered, stats, attended, middle, normed_two, aux,
         arrived, activation, slope, difference) = states[section]
        route_rows = section_routes[section]
        (spread,) = call(spread_grads, "spread_grads", [shape((slots, features), BF16)],
                         [upstream, aux], flops=1 << 30)
        arrived_grad = exchange(spread, experts, capacity)
        hidden_grad, rows_grad = run_expert_backward(arrived_grad, expert_in, expert_down, slope)
        returned = exchange(rows_grad, experts, capacity)
        expert_states[section] = (arrived, hidden_grad, activation, arrived_grad)
        wanted = (core != section).astype(jnp.int32).reshape(1)
        shares = run_weight_partials(wanted, *expert_states[section])
        partials[section] = [lax.ppermute(part, SECTION, [(1 - section, section)]) for part in shares]
        if section == 0:
            waiting, returned = lax.optimization_barrier((shared_qkv[1], returned))
            qkv_grads[1] = spread_sum(waiting, (EXPERT, ZHI), ranks // 2)
        middle_grad, attended_grad, shared_grads[section] = call(
            before_attention, "before_attention",
            [shape((span, features), F32), shape((GROUP, width, span), BF16),
             shape((features, features + -(-(experts + 1) // 128) * 128), BF16)],
            [returned, aux, upstream, difference, middle, normed_two, attended, gain_two, router, w_out,
             route_rows], flops=2 << 30, after=shares[:1],
        )
        shared_partner[section] = lax.ppermute(shared_grads[section], SECTION, [(1 - section, section)])
        grads = regroup(attended_grad)
        stay, leave, sent, shared_qkv[section] = call(
            functools.partial(attention_backward, sizes), "attention_backward",
            [shape((span, features), BF16), shape((span, features), BF16), shape((2, span, features), BF16),
             shape((features, -(-(3 * width + 16) // 128) * 128), BF16)],
            [mixed, stats, outcome, grads, gathered, gain_one, qkv, table], scalars=ids,
            scratch=[*bias_scratch, pltpu.VMEM((length, 3 * width), BF16),
                     pltpu.VMEM((GROUP, span, span), F32), pltpu.VMEM((length, size), F32),
                     pltpu.VMEM((length, size), F32), pltpu.VMEM((size, length), F32),
                     pltpu.VMEM((8, GROUP * 2 * 128), F32)],
            flops=8 << 30,
        )
        partner = flip(sent)
        leave = leave + partner[1]
        filler = ()
        if section == 0:
            leave, waiting = lax.optimization_barrier((leave, shared_qkv[0]))
            qkv_grads[0] = spread_sum(waiting, (EXPERT, ZHI), ranks // 2)
            grad_in = run_weight_totals(
                core_id, *[(expert_states[which][0], expert_states[which][1], partials[which][0])
                           for which in range(2)], False, sent)
            filler = (grad_in,)
        arrived_share = beside(leave)
        (low,) = call(
            first_norm_grad, "first_norm_grad", [shape((span, features), BF16)],
            [stay, partner, arrived_share, stream, gain_one, middle_grad], after=filler,
        )
        stream_grads[section] = low
        upstream = low

    if not fused:
        shared = jnp.where(
            core == 0,
            shared_grads[0].astype(F32) + shared_partner[0].astype(F32),
            shared_grads[1].astype(F32) + shared_partner[1].astype(F32),
        ).astype(BF16)
        shared = spread_sum(shared, RANKS, ranks)
        grad_out = shared[:, :features]
        grad_router = shared[:, features : features + experts]
        grad_gain_two = shared[:, features + experts]

        columns = qkv_grads[0].shape[1]
        halves = [block.reshape(2, shard_rows, columns) for block in qkv_grads]
        owned = regroup(jnp.stack([halves[0][0], halves[1][0], halves[0][1], halves[1][1]]))
        split = owned[:, :, : 3 * width].reshape(GROUP, shard_rows, 3, width)
        grad_qkv = jnp.transpose(split, (1, 2, 0, 3)).reshape(shard_rows, 3 * features)
        grad_table = jnp.transpose(
            owned[:, :table_rows, 3 * width : 3 * width + heads], (1, 0, 2)
        ).reshape(table_rows, head_count)
        grad_gain_one = jnp.sum(owned[:, :, 3 * width + 8], axis=0)
        grad_gains = jnp.stack([grad_gain_one, grad_gain_two])
        section_grads = home_pair(stream_grads, core).astype(F32)
        grad_down = run_weight_totals(
            core_id, *[(expert_states[which][2], expert_states[which][3], partials[which][1])
                       for which in range(2)], True, stream_grads[0])
    return (
        section_outputs[None, :, None],
        section_grads[None, :, None],
        grad_qkv[None],
        grad_out[None],
        grad_router[None],
        grad_gains[None],
        grad_table[None],
        grad_in[None, None],
        grad_down[None, None],
    )


def solution(mesh):
    sections, ranks, pieces = mesh.devices.shape
    work = Mesh(
        mesh.devices.reshape(sections, ranks, pieces // 2, 2), (SECTION, EXPERT, ZHI, ZLO)
    )
    piece = (ZHI, ZLO)
    in_specs = (
        P(None, EXPERT, piece, None),
        P(None, EXPERT, piece, None),
        P(SECTION, RANKS, None),
        P(SECTION, RANKS, None),
        P(SECTION, RANKS, None),
        P(SECTION, None, RANKS),
        P(SECTION, RANKS, None),
        P(SECTION, RANKS, None, None),
        P(SECTION, RANKS, None, None),
        P(SECTION, None, EXPERT, piece, None),
    )
    out_specs = (
        P(SECTION, None, EXPERT, piece, None),
        P(SECTION, None, EXPERT, piece, None),
        P(SECTION, RANKS, None),
        P(SECTION, RANKS, None),
        P(SECTION, RANKS, None),
        P(SECTION, None, RANKS),
        P(SECTION, RANKS, None),
        P(SECTION, RANKS, None, None),
        P(SECTION, RANKS, None, None),
    )
    return jax.shard_map(per_device, mesh=work, in_specs=in_specs, out_specs=out_specs, check_vma=False)
```

time: 707 us -> 552 us (0.78)
  Pallas kernels: 429 us -> 531 us
  waiting for transfers between devices: 98.7 us -> 0.01 us
  starting transfers between devices: 70.4 us -> 1.46 us
  blocking collectives: 34.7 us -> 0 us
  local copies, waits for them, and re-layouts: 31.5 us -> 7.49 us
  other arithmetic: 17.7 us -> 1.51 us
  between operations: 14.8 us -> 1.01 us
    pallas_call x14 -> x6, Pallas kernels: 94.8 us -> 260 us  [call(): pl.pallas_call(body, name=name, in_specs=specs, out_specs=[pl.BlockSpec(m...]
    ppermute x27 -> x3, waiting for transfers between devices: 65.7 us -> 0.01 us  [the longest x2 0.01 us: flip(): return lax.ppermute(block, SECTION, FLIP)]
    ppermute x27 -> x3, starting transfers between devices: 52.2 us -> 1.46 us  [the longest x1 0.82 us: to_working(): return lax.ppermute(block, (SECTION, ZHI, ZLO), scatter_pairs(turn))]
    pallas_call x3, Pallas kernels: 307 us -> 272 us  [run_expert_layer(): pl.pallas_call(functools.partial(expert_layer, mode, section), name='expe...]
    all_to_all x3 -> x0, blocking collectives: 34.7 us -> none  [regroup(): lax.all_to_all(block, ('zlo', 'section'), split_axis=0, concat_axis=0, ti...]
    all_to_all x5 -> x0, waiting for transfers between devices: 32.9 us -> none  [the longest x3 24.4 us: spread_sum(): lax.all_to_all(block.reshape(parts, rows // parts, columns), axes, split_...]
    pallas_call x1 -> x0, Pallas kernels: 26.8 us -> none  [run_gather_columns(): pl.pallas_call(gather_columns, name='gather_columns', in_specs=[pl.BlockS...]
    all_to_all x5 -> x0, starting transfers between devices: 18.1 us -> none  [the longest x3 11.2 us: spread_sum(): lax.all_to_all(block.reshape(parts, rows // parts, columns), axes, split_...]
  transfers between devices with their start and end apart: 33 -> 3, of which waited for: 13 -> 0; matrix products, arithmetic and copies ran while one was open for 4% -> 1% of each run, Pallas kernels for 9% -> 25%
where the time goes in v5:
time: 552 us; the launch traced here: 543 us
  Pallas kernels  531 us (96%)
  local copies, waits for them, and re-layouts  7.49 us (1%)
    pallas_call x3, Pallas kernels, run_expert_layer(): pl.pallas_call(functools.partial(expert_layer, mode, section), name='expe...  272 us
    pallas_call x6, Pallas kernels, call(): pl.pallas_call(body, name=name, in_specs=specs, out_specs=[pl.BlockSpec(m...  260 us
  transfers between devices with their start and end apart: 3, of which 0 were waited for; matrix products, arithmetic and copies ran while one was open for 1% of the time, Pallas kernels for 25%

profile of v5, /device:TPU:0, one launch (start us, length us, event | category | flops | bytes accessed | tf_op | source)
XLA Modules:
  0.0 542.7 jit_solution(5164016478548346504)
XLA Ops:
  0.6 0.0 copy-start
  0.7 0.0 copy-start.4
  0.7 0.6 collective-permute-start
  1.2 0.1 collective-permute-start.1
  1.3 0.5 copy-done
  1.8 0.8 collective-permute-start.2
  2.6 0.8 copy.35
  3.4 0.7 fusion.4
  4.1 0.1 copy.31
  4.2 1.2 reshape_squeeze.3
  5.5 0.2 copy.37
  5.6 0.3 reshape.55
  6.0 0.6 pad.12.refs_1_
  6.6 0.8 fusion.2.refs_2_
  7.4 0.8 dynamic-slice_bitcast_fusion.1.refs_0_
  8.1 64.8 %attend.2 = (bf16[4,192,256]{2,1,0:T(8,128)(2,1)}, bf16[1024,576]{1,0:T(8,128)(2,1)}, bf16[1024,768]{1,0:T(8,128)(2,1)}, f32[8,1024]{1,0:T(8,128)}, bf16[1024,76...) custom-call(bf16[256,768]{1,0:T(8,128)(2,1)} %dynamic-slice_bitcast_, ...), custom_call_target="tpu_custom_call" | custom-call | flops 6442450944 | bytes 11526144 | tf_op jit(solution)/shard_map/attend/pallas_call | solution.py:103
  72.9 0.0 collective-permute-done.refs_2_
  72.9 0.0 collective-permute-done.1.refs_3_
  72.9 71.1 %expert_layer_forward.1 = (bf16[16,64,768]{2,1,0:T(8,128)(2,1)}, bf16[16,64,768]{2,1,0:T(8,128)(2,1)}, bf16[1024,3072]{1,0:T(8,128)(2,1)}, bf16[1024,3072]{1,0:T(8,128)(2,1)}) custom-call(bf16[768,3072]{1,0:T(8,128)(2,1)} %bitcast.56, bf16[3072,768]{1,0:T(8,128)(2,1)} %bitcast.60, bf16[768,3072]{1,0:T(8,128)(2,1)} %collective-permute-done.refs_2_, ...), custom_call_target="tpu_custom_call" | custom-call | flops 19327352832 | bytes 167772160 | tf_op jit(solution)/shard_map/expert_layer_forward/pallas_call | solution.py:970
  144.0 0.0 collective-permute-done.2.refs_6_.refs_9_
  144.0 0.0 copy-start.5
  144.0 0.7 copy-done.5
  144.7 43.3 %attend.3 = (bf16[4,192,256]{2,1,0:T(8,128)(2,1)}, bf16[1024,576]{1,0:T(8,128)(2,1)}, bf16[1024,768]{1,0:T(8,128)(2,1)}, f32[8,1024]{1,0:T(8,128)}, bf16[1024,76...) custom-call(bf16[1024,768]{1,0:T(8,128)(2,1)} %bitcast.72, ...), custom_call_target="tpu_custom_call" | custom-call | flops 6442450944 | bytes 16433152 | tf_op jit(solution)/shard_map/attend/pallas_call | solution.py:103
  188.1 131.1 %expert_layer_both.1 = (bf16[16,64,768]{2,1,0:T(8,128)(2,1)}, bf16[16,64,768]{2,1,0:T(8,128)(2,1)}, f32[768,3072]{1,0:T(8,128)}, f32[3072,768]{1,0:T(8,128)}) custom-call(bf16[768,3072]{1,0:T(8,128)(2,1)} %bitcast.57, bf16[3072,768]{1,0:T(8,128)(2,1)} %bitcast.61, bf16[768,3072]{1,0:T(8,128)(2,1)} %collective-permute-done.refs_2_, ...), custom_call_target="tpu_custom_call" | custom-call | flops 38654705664 | bytes 167772160 | tf_op jit(solution)/shard_map/expert_layer_both/pallas_call | solution.py:970
  319.2 62.2 %attend_back.2 = (bf16[768,896]{1,0:T(8,128)(2,1)}, bf16[256,768]{1,0:T(8,128)(2,1)}, bf16[16,48,640]{2,1,0:T(8,128)(2,1)}, bf16[2,256,768]{2,1,0:T(8,128)(2,1)}, bf16[1024,768]{1,0:T(8,128)(2,1)}) custom-call(bf16[2,16,48,640]{3,2,1,0:T(8,128)(2,1)} %get-tuple-element.63.refs_3_.refs_0_.refs_7_, bf16[1024,576]{1,0:T(8,128)(2,1)} %get-tuple-element.70.refs_1_, ...), custom_call_target="tpu_custom_call" | custom-call | flops 10737418240 | bytes 18399232 | tf_op jit(solution)/shard_map/attend_back/pallas_call | solution.py:103
  381.4 69.4 %expert_layer_backward.1 = (bf16[16,64,768]{2,1,0:T(8,128)(2,1)}, f32[768,3072]{1,0:T(8,128)}, f32[3072,768]{1,0:T(8,128)}) custom-call(bf16[768,3072]{1,0:T(8,128)(2,1)} %bitcast.58, bf16[3072,768]{1,0:T(8,128)(2,1)} %bitcast.62, bf16[768,3072]{1,0:T(8,128)(2,1)} %collective-permute-done.refs_2_, ...), custom_call_target="tpu_custom_call", output_to_operand_aliasing={{1}: (8, {}), {2}: (9, {})} | custom-call | flops 19327352832 | bytes 167772160 | tf_op jit(solution)/shard_map/expert_layer_backward/pallas_call | solution.py:970
  450.8 18.4 %before_attention.1 = (f32[256,768]{1,0:T(8,128)}, bf16[4,192,256]{2,1,0:T(8,128)(2,1)}, bf16[768,896]{1,0:T(8,128)(2,1)}, f32[768,3072]{1,0:T(8,128)}, f32[3072,768]{1,0:T(8,128)}) custom-call(bf16[1024,768]{1,0:T(8,128)(2,1)} %bitcast.46, f32[256,128]{1,0:T(8,128)} %get-tuple-element.66.refs_1_.refs_15_, ...), custom_call_target="tpu_custom_call" | custom-call | flops 2147483648 | bytes 49102848 | tf_op jit(solution)/shard_map/before_attention/pallas_call | solution.py:103
  469.3 0.0 copy-start.1
  469.3 68.0 %attend_back.3 = (bf16[2,256,768]{2,1,0:T(8,128)(2,1)}, f32[4,48,640]{2,1,0:T(8,128)}, f32[48,896]{1,0:T(8,128)}) custom-call(bf16[2,16,48,640]{3,2,1,0:T(8,128)(2,1)} %get-tuple-element.63.refs_3_.refs_0_.refs_7_, bf16[1024,576]{1,0:T(8,128)(2,1)} %get-tuple-element.84.refs_1_, f32[8,1024]{1,0:T(8,128)} %get-tuple-element.85.refs_2_, ...), custom_call_target="tpu_custom_call" | custom-call | flops 10737418240 | bytes 11902976 | tf_op jit(solution)/shard_map/attend_back/pallas_call | solution.py:103
  537.3 2.9 unpack.1
  540.2 1.4 copy.34
  541.6 0.9 copy.41
  (9 shorter events, 0.0 us)
Async XLA Ops:
  0.6 1.1 copy-start
  0.7 5.3 copy-start.4
  0.7 72.2 %collective-permute-start = (bf16[768,3072]{1,0:T(8,128)(2,1)}, bf16[768,3072]{1,0:T(8,128)(2,1)}, u32[]{:S(2)}, u32[]{:S(2)}) collective-permute-start(bf16[768,3072]{1,0:T(8,128)(2,1)} %bitcast.55), channel_id=1, source_target_pairs={{0,16},{16,0},{1,17},{17,1},{2,18},{18,2},{3,19},{19,3},{4,20},{20... | collective-permute-start | bytes 14155784 | tf_op jit(solution)/shard_map/ppermute | solution.py:679
  1.2 71.7 %collective-permute-start.1 = (bf16[3072,768]{1,0:T(8,128)(2,1)}, bf16[3072,768]{1,0:T(8,128)(2,1)}, u32[]{:S(2)}, u32[]{:S(2)}) collective-permute-start(bf16[3072,768]{1,0:T(8,128)(2,1)} %bitcast.59), channel_id=1, source_target_pairs={{0,16},{16,0},{1,17},{17,1},{2,18},{18,2},{3,19},{19,3},{4,20},{20... | collective-permute-start | bytes 14155784 | tf_op jit(solution)/shard_map/ppermute | solution.py:679
  1.8 5.6 %copy-start.3 = (bf16[2,1,256,768]{3,2,1,0:T(8,128)(2,1)S(1)}, bf16[2,1,256,768]{3,2,1,0:T(8,128)(2,1)}, u32[]{:S(2)}) copy-start(bf16[2,1,256,768]{3,2,1,0:T(8,128)(2,1)} %param.10) | copy-start | bytes 2359300
  1.8 142.2 %collective-permute-start.2 = (bf16[256,768]{1,0:T(8,128)(2,1)S(1)}, bf16[256,768]{1,0:T(8,128)(2,1)S(1)}, u32[]{:S(2)}, u32[]{:S(2)}) collective-permute-start(bf16[256,768]{1,0:T(8,128)(2,1)S(1)} %dynamic-slice_bitcast_fusion), channel_id=1, source_target_pairs={{0,0},{1,16},{2,1},{3,17},{16,2},{17,18},{18,3},{19,19},{4,4},{5,2... | collective-permute-start | bytes 1179656 | tf_op jit(solution)/shard_map/ppermute | solution.py:696
  144.0 0.7 copy-start.5
  469.3 73.2 %copy-start.1 = (bf16[2,1,256,768]{3,2,1,0:T(8,128)(2,1)S(1)}, bf16[2,1,256,768]{3,2,1,0:T(8,128)(2,1)}, u32[]{:S(2)}) copy-start(bf16[2,1,256,768]{3,2,1,0:T(8,128)(2,1)} %param.11) | copy-start | bytes 2359300
  537.3 4.3 copy-start.2

commit v6 on v5

--- a/solution.py
+++ b/solution.py
@@ -467,7 +467,7 @@
     return back, jnp.sum(grad * unit, axis=0, keepdims=True)
 
 
-def publisher(grad_in, grad_down, out_in, out_down, held, in_sem, out_sem):
+def publisher(grad_in, grad_down, out_in, out_down, held, wide, in_sem, out_sem):
     tile = held.shape[2]
     tiles = held.shape[0] // 2
     across_tiles = [(slice(None), pl.ds(index * tile, tile)) for index in range(tiles)]
@@ -478,25 +478,28 @@
         pltpu.make_async_copy(pair[0], held.at[index], in_sem.at[index]) for index, pair in enumerate(places)
     ]
     stores = [
-        pltpu.make_async_copy(held.at[index], pair[1], out_sem.at[index]) for index, pair in enumerate(places)
+        pltpu.make_async_copy(wide.at[index], pair[1], out_sem.at[index]) for index, pair in enumerate(places)
     ]
     for fetch in fetches:
         fetch.start()
-    return fetches, stores
-
-
-def token_backward(returned, packed, flow, difference, middle, normed_two, attended, gain, router, out_block,
-                   columns, middle_grad, attended_grad, shared_grad, fetches=(), stores=()):
-    slots, features = returned.shape
-    experts = router.shape[1]
-    width = attended.shape[1]
 
     def publish(quarter):
         share = len(fetches) // 4
         for index in range(quarter * share, (quarter + 1) * share):
             fetches[index].wait()
+            wide[index] = held[index].astype(F32)
             stores[index].start()
 
+    return publish, stores
+
+
+def token_backward(returned, packed, flow, difference, middle, normed_two, attended, gain, router, out_block,
+                   columns, middle_grad, attended_grad, shared_grad, publish=None, stores=(), hook=None):
+    slots, features = returned.shape
+    experts = router.shape[1]
+    width = attended.shape[1]
+
+    publish = publish or (lambda quarter: None)
     hot = pick_rows(packed[:, 0:1], slots) + pick_rows(packed[:, 1:2], slots)
     token_grad = mm(hot, returned)
     publish(0)
@@ -510,11 +513,13 @@
     branch = total.astype(BF16)
     publish(1)
     for group in range(GROUP):
+        attended_grad[group] = mm(out_block(group), branch, NT).astype(BF16)
+    publish(2)
+    if hook:
+        hook()
+    for group in range(GROUP):
         mine = slice(group * width, (group + 1) * width)
-        attended_grad[group] = mm(out_block(group), branch, NT).astype(BF16)
         shared_grad[mine, :features] = mm(attended[group], branch).astype(BF16)
-        if group == 1:
-            publish(2)
     publish(3)
     tail = shared_grad.shape[1] - features
     gain_column = jnp.broadcast_to(gain_part, (8, features)).T
@@ -537,13 +542,13 @@
 
 def before_attention_fused(sizes, returned, aux, upstream, difference, middle, normed_two, attended,
                            early, w_outs, routes, grad_in, grad_down,
-                           middle_grad, attended_grad, shared_grad, out_in, out_down, held, in_sem, out_sem):
-    fetches, stores = publisher(grad_in, grad_down, out_in, out_down, held, in_sem, out_sem)
+                           middle_grad, attended_grad, shared_grad, out_in, out_down, held, wide, in_sem, out_sem):
+    publish, stores = publisher(grad_in, grad_down, out_in, out_down, held, wide, in_sem, out_sem)
     router, unused, gain_two, unused_1 = unpack_small(sizes, early, 0)
     token_backward(
         returned[...], aux[...], upstream[...].astype(F32), difference[...], middle[...], normed_two[...],
         attended, gain_two, router, lambda group: out_rows(sizes, w_outs, 0, group),
-        route_columns(routes[0].T), middle_grad, attended_grad, shared_grad, fetches, stores,
+        route_columns(routes[0].T), middle_grad, attended_grad, shared_grad, publish, stores,
     )
 
 
@@ -882,30 +887,38 @@
         def share_copy(index):
             return remote(parts.at[index], parts.at[index], part_send.at[index], part_recv.at[index], partner)
 
-        def out_copy(index):
-            spot = pl.ds(index // 2 * tile, tile)
-            target = grad_down.at[spot, :] if index % 2 else grad_in.at[:, spot]
-            return pltpu.make_async_copy(staged.at[index % 2], target, out_sem.at[index])
-
-        for index in range(2 * tiles):
-            spot = pl.ds(index // 2 * tile, tile)
-            if index % 2:
-                value = mm(activation[:, spot], grads[...].reshape(count, features), TN)
-            else:
-                value = mm(inputs[...].reshape(count, features), slope[:, spot], TN)
-
-            @pl.when(core != section)
-            def give():
-                parts[index] = value.astype(BF16)
-                share_copy(index).start()
-
-            @pl.when(core == section)
-            def keep():
-                share_copy(index).wait_recv()
-                if index >= 2:
-                    out_copy(index - 2).wait()
-                staged[index % 2] = value + parts[index].astype(F32)
-                out_copy(index).start()
+        def out_copy(step, kind):
+            spot = pl.ds(pl.multiple_of(step * tile, tile), tile)
+            target = grad_down.at[spot, :] if kind else grad_in.at[:, spot]
+            return pltpu.make_async_copy(staged.at[kind], target, out_sem.at[2 * step + kind])
+
+        def one_step(step, unused):
+            spot = pl.ds(pl.multiple_of(step * tile, tile), tile)
+            for kind in range(2):
+                index = 2 * step + kind
+                if kind:
+                    value = mm(activation[:, spot], grads[...].reshape(count, features), TN)
+                else:
+                    value = mm(inputs[...].reshape(count, features), slope[:, spot], TN)
+
+                @pl.when(core != section)
+                def give():
+                    parts[index] = value.astype(BF16)
+                    share_copy(index).start()
+
+                @pl.when(core == section)
+                def keep():
+                    share_copy(index).wait_recv()
+
+                    @pl.when(step >= 1)
+                    def drained():
+                        out_copy(step - 1, kind).wait()
+
+                    staged[kind] = (value + parts[index].astype(F32)).astype(BF16)
+                    out_copy(step, kind).start()
+            return unused
+
+        lax.fori_loop(0, tiles, one_step, 0)
 
     for slot in range(1, len(OFFSETS)):
         for kind in range(len(outgoing)):
@@ -923,8 +936,8 @@
 
         @pl.when(core == section)
         def stored():
-            for index in range(2 * tiles - 2, 2 * tiles):
-                out_copy(index).wait()
+            for kind in range(2):
+                out_copy(tiles - 1, kind).wait()
 
 
 def run_expert_layer(mode, section, weights, outgoing, saved=(), grads=()):
@@ -946,7 +959,7 @@
         out_shape += [block, wide, wide]
         out_specs += [local, anywhere, anywhere]
     else:
-        out_shape += [shape((features, hidden), F32), shape((hidden, features), F32)]
+        out_shape += [shape((features, hidden), BF16), shape((hidden, features), BF16)]
         out_specs += [anywhere, anywhere]
     if mode == BACKWARD:
         aliases = {len(operands) + 3: kinds, len(operands) + 4: kinds + 1}
@@ -963,7 +976,7 @@
     if mode != FORWARD:
         pieces = 2 * hidden // tile
         scratch += [
-            pltpu.VMEM((pieces, features, tile), BF16), pltpu.VMEM((2, features, tile), F32),
+            pltpu.VMEM((pieces, features, tile), BF16), pltpu.VMEM((2, features, tile), BF16),
             pltpu.SemaphoreType.DMA((pieces,)), pltpu.SemaphoreType.DMA((pieces,)),
             pltpu.SemaphoreType.DMA((pieces,)),
         ]
@@ -1037,16 +1050,20 @@
 
 class Regroup:
     def __init__(self, block, target, send, recv):
-        core, unused, zlo, unused_1, mine = whereabouts()
+        self.block, self.target, self.send, self.recv = block, target, send, recv
+        self.core, unused, self.zlo, unused_1, self.mine = whereabouts()
         self.copies = []
-        for index, (turn, move) in enumerate(((0, 1), (1, 1), (1, 0))):
-            to_core = 1 - core if turn else core
-            to_zlo = 1 - zlo if move else zlo
-            copy = remote(block.at[2 * to_zlo + to_core], target.at[mine], send.at[index], recv.at[index],
-                          dict(section=to_core, zlo=to_zlo))
+
+    def start(self, rows):
+        for turn, move in ((0, 1), (1, 1), (1, 0)):
+            to_core = 1 - self.core if turn else self.core
+            to_zlo = 1 - self.zlo if move else self.zlo
+            index = len(self.copies)
+            copy = remote(self.block.at[2 * to_zlo + to_core, rows], self.target.at[self.mine, rows],
+                          self.send.at[index], self.recv.at[index], dict(section=to_core, zlo=to_zlo))
             copy.start()
             self.copies.append(copy)
-        target[mine] = block[mine]
+        self.target[self.mine, rows] = self.block[self.mine, rows]
 
     def wait(self):
         for copy in self.copies:
@@ -1188,6 +1205,31 @@
             copy.wait_send()
 
 
+def assemble(sizes, route_rows, qkv_shard, router_shard, gain_shard, table_shard, blocks, home_routes):
+    rows, features, width = sizes.shard_rows, sizes.features, sizes.width
+
+    def below(block, count):
+        return jnp.concatenate([block, jnp.zeros((count - block.shape[0], block.shape[1]), F32)], axis=0)
+
+    small = [
+        router_shard[...].astype(F32), below(gain_shard[...].astype(F32), 8).T[:, :2],
+        below(table_shard[...].astype(F32), rows),
+    ]
+    spare = blocks.shape[2] - 3 * width - sum(part.shape[1] for part in small)
+    small.append(jnp.zeros((rows, spare), F32))
+    for member in range(GROUP):
+        parts = [
+            qkv_shard[:, part * features + member * width : part * features + (member + 1) * width].astype(F32)
+            for part in range(3)
+        ]
+        blocks[member] = jnp.concatenate(parts + small, axis=1).astype(BF16)
+    for batch in range(2):
+        wide = jnp.concatenate(
+            [route_rows[batch].astype(F32), jnp.zeros((sizes.span, 126), F32)], axis=1
+        )
+        home_routes[batch] = wide.T[:8, :]
+
+
 def attend(section, sizes, *refs):
     refs = list(refs)
 
@@ -1197,7 +1239,7 @@
         return taken
 
     if section == 0:
-        home_rows, home_routes, blocks, shard = take(4)
+        home_inputs, route_rows, qkv_shard, shard, router_shard, gain_shard, table_shard = take(7)
     else:
         returned, aux_before, middle_before, early, w_outs, routes, given = take(7)
     outcome, mixed, gathered, stats, outgoing, middle, normed_two, aux, attended = take(9)
@@ -1213,6 +1255,9 @@
     def rows_of(piece):
         return pl.ds(pl.multiple_of(piece * span, span), span)
 
+    if section == 0:
+        blocks, home_routes = refs[-2:]
+        assemble(sizes, route_rows, qkv_shard, router_shard, gain_shard, table_shard, blocks, home_routes)
     own, flipped = group, 2 * zlo + 1 - core
     side, side_flipped = 2 * (1 - zlo) + core, 2 * (1 - zlo) + 1 - core
     partner, beside_z = dict(section=1 - core), dict(zlo=1 - zlo)
@@ -1233,6 +1278,7 @@
 
     if section == 0:
         staged, home_send, home_recv = take(3)
+        home_rows = home_inputs.at[core]
         gather = WeightGather(blocks, shard, early, w_outs, staged, take(7))
         gather.trade()
         aligned = (zlo == zhi) & (zlo == core)
@@ -1249,7 +1295,7 @@
 
         @pl.when(aligned)
         def keep():
-            gathered[rows_of(place), :] = home_rows[...]
+            gathered[rows_of(place), :] = home_inputs[core]
             routes[core] = home_routes[core]
 
         @pl.when(jnp.logical_not(aligned))
@@ -1292,10 +1338,12 @@
     project(gathered, rows_of(side), gain_one, weight, mixed)
     await_piece(side_flipped, 2)
     project(gathered, rows_of(side_flipped), gain_one, weight, mixed)
+    trade = Regroup(outcome, attended, group_send, group_recv)
     for head in range(sizes.heads):
         if section == 0 and head < 3:
             (gather.out_along_z, gather.out_over_plane, gather.out_finish)[head]()
         attend_head(sizes.attention, head, mixed, bias, outcome, stats)
+        trade.start(slice(head * sizes.size, (head + 1) * sizes.size))
     if section == 0:
         for stage in (gather.out_along_z, gather.out_over_plane, gather.out_finish)[sizes.heads :]:
             stage()
@@ -1304,7 +1352,6 @@
             def routed():
                 remote(routes.at[which], routes.at[which], home_send.at[1], home_recv.at[1 + which],
                        partner).wait_recv()
-    trade = Regroup(outcome, attended, group_send, group_recv)
     columns_t = routes[section].T
     columns = [columns_t[:, k : k + 1] for k in range(2)]
     masks = route_masks(columns, sizes.experts)
@@ -1343,10 +1390,11 @@
     ]
     scratch = [
         pltpu.VMEM((128, 2 * span * GROUP), F32), pltpu.VMEM((sizes.heads * GROUP, span, span), F32),
-        dma((3,)), dma((3,)), dma((3,)), dma((3,)),
+        dma((3,)), dma((3,)), dma((3 * sizes.heads,)), dma((3 * sizes.heads,)),
     ]
     if section == 0:
-        unused, rows, columns = operands[2].shape
+        rows = sizes.shard_rows
+        columns = -(-(3 * width + sizes.experts + 2 + sizes.heads * GROUP) // 128) * 128
         outs += [
             shape((2, sizes.ranks, rows, columns), BF16), shape((2, sizes.ranks, rows, features), BF16),
             shape((2, 8, span), F32),
@@ -1354,6 +1402,7 @@
         scratch += [
             pltpu.VMEM((2, rows, columns), BF16), dma((3,)), dma((3,)),
             dma((30,)), dma((2, sizes.ranks)), dma((2,)), dma((2,)), dma, dma((34,)), dma((2, sizes.ranks)),
+            pltpu.VMEM((GROUP, rows, columns), BF16), pltpu.VMEM((2, 8, span), F32),
         ]
     else:
         outs += [shape((span, features), BF16), shape((span, features), F32), shape((sizes.slots, features), BF16)]
@@ -1363,8 +1412,9 @@
     )
 
 
-def unpack(sizes, home, owned, shared, stream_grads, grad_qkv, grad_out, grad_router, grad_gains, grad_table):
+def unpack(sizes, home, owned, shared, outputs, section_outputs, stream_grads, grad_qkv, grad_out, grad_router, grad_gains, grad_table):
     width, features, experts = sizes.width, sizes.features, sizes.experts
+    section_outputs[...] = outputs[...]
     stream_grads[...] = home[...].astype(F32)
     grad_qkv[...] = jnp.concatenate(
         [owned[member, :, part * width : (part + 1) * width] for part in range(3) for member in range(GROUP)],
@@ -1473,6 +1523,7 @@
     greet(line_peers(core, place) + ([dict(expert=across(expert, step)) for step in range(1, 4)] if last else []))
     homes = Homes(home, home_send, home_recv)
     router, gain_one, gain_two, table = unpack_small(sizes, early, 0)
+    trade = Regroup(attended_grad, grads, group_send, group_recv)
     if not last:
         homes.send(first_result, 0)
         total, difference = combined(returned[...], aux[...], middle[...])
@@ -1481,8 +1532,10 @@
             returned_grad[...], aux[...], given[...].astype(F32), difference, middle[...], normed_two[...],
             attended, gain_two, router, lambda member: out_rows(sizes, w_outs, 0, member),
             route_columns(routes[section].T), middle_grad, attended_grad, shared_grad,
+            hook=lambda: trade.start(slice(None)),
         )
-    trade = Regroup(attended_grad, grads, group_send, group_recv)
+    else:
+        trade.start(slice(None))
     if last:
         partner = dict(section=1 - core)
         for which in range(2):
@@ -1695,26 +1748,26 @@
             jnp.where(zhi == section, route_parts[0], route_parts[1]) for section in range(2)
         ]
 
-    small = jnp.concatenate([
-        router_shard[0],
-        gain_shard[0].T,
-        jnp.pad(table_shard[0], ((0, shard_rows - table_rows), (0, 0))),
-    ], axis=1)
-    by_group = jnp.transpose(
-        qkv_shard[0].reshape(shard_rows, 3, GROUP, width), (2, 0, 1, 3)
-    ).reshape(GROUP, shard_rows, 3 * width)
-    by_group = jnp.concatenate(
-        [by_group, jnp.broadcast_to(small[None], (GROUP, *small.shape))], axis=2
-    )
-    by_group = jnp.pad(by_group, ((0, 0), (0, 0), (0, -by_group.shape[2] % 128)))
-    columns = by_group.shape[2]
     if fused:
-        home_routes = jnp.pad(
-            jnp.swapaxes(routes[0, :, 0], 1, 2).astype(F32), ((0, 0), (0, 6), (0, 0))
-        )
-        first = run_attend(0, shared_sizes, [home_rows, home_routes, by_group, out_shard[0]], 4)
+        first = run_attend(
+            0, shared_sizes,
+            [inputs[:, 0], routes[0, :, 0], qkv_shard[0], out_shard[0], router_shard[0], gain_shard[0],
+             table_shard[0]], 4)
         early_all, w_out_all, route_all = first[9:]
     else:
+        small = jnp.concatenate([
+            router_shard[0],
+            gain_shard[0].T,
+            jnp.pad(table_shard[0], ((0, shard_rows - table_rows), (0, 0))),
+        ], axis=1)
+        by_group = jnp.transpose(
+            qkv_shard[0].reshape(shard_rows, 3, GROUP, width), (2, 0, 1, 3)
+        ).reshape(GROUP, shard_rows, 3 * width)
+        by_group = jnp.concatenate(
+            [by_group, jnp.broadcast_to(small[None], (GROUP, *small.shape))], axis=2
+        )
+        by_group = jnp.pad(by_group, ((0, 0), (0, 0), (0, -by_group.shape[2] % 128)))
+        columns = by_group.shape[2]
         whole_early = lax.all_gather(by_group, RANKS, axis=1, tiled=True)
         kept = lax.dynamic_index_in_dim(whole_early, group, 0, keepdims=False)
         traded = flip(lax.dynamic_index_in_dim(whole_early, 2 * zlo + 1 - core, 0, keepdims=False))
@@ -1777,7 +1830,7 @@
              shape(grad_in.shape, F32), shape(grad_down.shape, F32)],
             [by_slot(returned), aux, low_1, difference, middle, normed_two, attended, early_all, w_out_all,
              route_all, grad_in, grad_down],
-            scratch=[pltpu.VMEM((pieces, features, features), F32),
+            scratch=[pltpu.VMEM((pieces, features, features), BF16), pltpu.VMEM((pieces, features, features), F32),
                      pltpu.SemaphoreType.DMA((pieces,)), pltpu.SemaphoreType.DMA((pieces,))],
             flops=2 << 30, anywhere=(10, 11), out_anywhere=(3, 4), picks=((7, 0), (8, 0)),
         )
@@ -1787,12 +1840,12 @@
             [early_all, mixed, stats, outcome, gathered, middle_grad, attended_grad, low_1,
              shared_0.reshape(ranked), shared_1.reshape(ranked), qkv_1],
             ((0, 0),), 7)
-        section_grads, grad_qkv, grad_out, grad_router, grad_gains, grad_table = call(
+        section_outputs, section_grads, grad_qkv, grad_out, grad_router, grad_gains, grad_table = call(
             functools.partial(unpack, shared_sizes), "unpack",
-            [shape(home.shape, F32), shape((shard_rows, 3 * features), F32), shape((shard_rows, features), F32),
+            [shape(home.shape, BF16), shape(home.shape, F32), shape((shard_rows, 3 * features), F32), shape((shard_rows, features), F32),
              shape((shard_rows, experts), F32), shape((2, shard_rows), F32),
              shape((table_rows, head_count), F32)],
-            [home, owned, shared_sum],
+            [home, owned, shared_sum, section_outputs],
         )
     stream = None if fused else own
     for section in range(0 if fused else 2):

time: 552 us -> 542 us (0.982)
  Pallas kernels: 531 us -> 524 us
where the time goes in v6:
time: 542 us; the launch traced here: 532 us
  Pallas kernels  524 us (97%)
  local copies, waits for them, and re-layouts  5.58 us (1%)
    pallas_call x3, Pallas kernels, run_expert_layer(): pl.pallas_call(functools.partial(expert_layer, mode, section), name='expe...  270 us
    pallas_call x6, Pallas kernels, call(): pl.pallas_call(body, name=name, in_specs=specs, out_specs=[pl.BlockSpec(m...  254 us
  transfers between devices with their start and end apart: 3, of which 0 were waited for; matrix products, arithmetic and copies ran while one was open for 1% of the time, Pallas kernels for 25%

profile of v6, /device:TPU:0, one launch (start us, length us, event | category | flops | bytes accessed | tf_op | source)
XLA Modules:
  0.0 532.3 jit_solution(13450319367591159873)
XLA Ops:
  0.6 0.0 copy-start
  0.7 0.6 collective-permute-start
  1.2 0.1 collective-permute-start.1
  1.3 0.5 copy-done
  1.8 0.7 collective-permute-start.2
  2.5 1.4 copy.22
  3.9 1.5 copy.21
  5.4 65.5 %attend.2 = (bf16[4,192,256]{2,1,0:T(8,128)(2,1)}, bf16[1024,576]{1,0:T(8,128)(2,1)}, bf16[1024,768]{1,0:T(8,128)(2,1)}, f32[8,1024]{1,0:T(8,128)}, bf16[1024,76...) custom-call(bf16[2,256,768]{2,1,0:T(8,128)(2,1)} %bitcast.50, ...), custom_call_target="tpu_custom_call" | custom-call | flops 6442450944 | bytes 11884320 | tf_op jit(solution)/shard_map/attend/pallas_call | solution.py:103
  71.0 0.0 collective-permute-done.refs_2_
  71.0 0.0 collective-permute-done.1.refs_3_
  71.0 69.1 %expert_layer_forward.1 = (bf16[16,64,768]{2,1,0:T(8,128)(2,1)}, bf16[16,64,768]{2,1,0:T(8,128)(2,1)}, bf16[1024,3072]{1,0:T(8,128)(2,1)}, bf16[1024,3072]{1,0:T(8,128)(2,1)}) custom-call(bf16[768,3072]{1,0:T(8,128)(2,1)} %bitcast.41, bf16[3072,768]{1,0:T(8,128)(2,1)} %bitcast.45, bf16[768,3072]{1,0:T(8,128)(2,1)} %collective-permute-done.refs_2_, ...), custom_call_target="tpu_custom_call" | custom-call | flops 19327352832 | bytes 167772160 | tf_op jit(solution)/shard_map/expert_layer_forward/pallas_call | solution.py:983
  140.1 0.0 collective-permute-done.2.refs_6_.refs_9_
  140.1 0.0 copy-start.2
  140.1 0.7 copy-done.2
  140.8 40.6 %attend.3 = (bf16[4,192,256]{2,1,0:T(8,128)(2,1)}, bf16[1024,576]{1,0:T(8,128)(2,1)}, bf16[1024,768]{1,0:T(8,128)(2,1)}, f32[8,1024]{1,0:T(8,128)}, bf16[1024,76...) custom-call(bf16[1024,768]{1,0:T(8,128)(2,1)} %bitcast.62, ...), custom_call_target="tpu_custom_call" | custom-call | flops 6442450944 | bytes 16433152 | tf_op jit(solution)/shard_map/attend/pallas_call | solution.py:103
  181.4 131.5 %expert_layer_both.1 = (bf16[16,64,768]{2,1,0:T(8,128)(2,1)}, bf16[16,64,768]{2,1,0:T(8,128)(2,1)}, bf16[768,3072]{1,0:T(8,128)(2,1)}, bf16[3072,768]{1,0:T(8,128)(2,1)}) custom-call(bf16[768,3072]{1,0:T(8,128)(2,1)} %bitcast.42, bf16[3072,768]{1,0:T(8,128)(2,1)} %bitcast.46, bf16[768,3072]{1,0:T(8,128)(2,1)} %collective-permute-done.refs_2_, ...), custom_call_target="tpu_custom_call" | custom-call | flops 38654705664 | bytes 167772160 | tf_op jit(solution)/shard_map/expert_layer_both/pallas_call | solution.py:983
  313.0 61.8 %attend_back.2 = (bf16[768,896]{1,0:T(8,128)(2,1)}, bf16[256,768]{1,0:T(8,128)(2,1)}, bf16[16,48,640]{2,1,0:T(8,128)(2,1)}, bf16[2,256,768]{2,1,0:T(8,128)(2,1)}, bf16[1024,768]{1,0:T(8,128)(2,1)}) custom-call(bf16[2,16,48,640]{3,2,1,0:T(8,128)(2,1)} %get-tuple-element.64.refs_3_.refs_0_.refs_7_, bf16[1024,576]{1,0:T(8,128)(2,1)} %get-tuple-element.75.refs_1_, ...), custom_call_target="tpu_custom_call" | custom-call | flops 10737418240 | bytes 18399232 | tf_op jit(solution)/shard_map/attend_back/pallas_call | solution.py:103
  374.8 69.5 %expert_layer_backward.1 = (bf16[16,64,768]{2,1,0:T(8,128)(2,1)}, bf16[768,3072]{1,0:T(8,128)(2,1)}, bf16[3072,768]{1,0:T(8,128)(2,1)}) custom-call(bf16[768,3072]{1,0:T(8,128)(2,1)} %bitcast.43, bf16[3072,768]{1,0:T(8,128)(2,1)} %bitcast.47, bf16[768,3072]{1,0:T(8,128)(2,1)} %collective-permute-done.refs_2_, ...), custom_call_target="tpu_custom_call", output_to_operand_aliasing={{1}: (8, {}), {2}: (9, {})} | custom-call | flops 19327352832 | bytes 167772160 | tf_op jit(solution)/shard_map/expert_layer_backward/pallas_call | solution.py:983
  444.3 14.6 %before_attention.1 = (f32[256,768]{1,0:T(8,128)}, bf16[4,192,256]{2,1,0:T(8,128)(2,1)}, bf16[768,896]{1,0:T(8,128)(2,1)}, f32[768,3072]{1,0:T(8,128)}, f32[3072,768]{1,0:T(8,128)}) custom-call(bf16[1024,768]{1,0:T(8,128)(2,1)} %bitcast.34, f32[256,128]{1,0:T(8,128)} %get-tuple-element.71.refs_1_.refs_15_, ...), custom_call_target="tpu_custom_call" | custom-call | flops 2147483648 | bytes 39665664 | tf_op jit(solution)/shard_map/before_attention/pallas_call | solution.py:103
  458.9 0.0 copy-start.1
  458.9 68.1 %attend_back.3 = (bf16[2,256,768]{2,1,0:T(8,128)(2,1)}, f32[4,48,640]{2,1,0:T(8,128)}, f32[48,896]{1,0:T(8,128)}) custom-call(bf16[2,16,48,640]{3,2,1,0:T(8,128)(2,1)} %get-tuple-element.64.refs_3_.refs_0_.refs_7_, bf16[1024,576]{1,0:T(8,128)(2,1)} %get-tuple-element.65.refs_1_, f32[8,1024]{1,0:T(8,128)} %get-tuple-element.66.refs_2_, ...), custom_call_target="tpu_custom_call" | custom-call | flops 10737418240 | bytes 11902976 | tf_op jit(solution)/shard_map/attend_back/pallas_call | solution.py:103
  527.1 3.4 unpack.1
  530.4 1.4 copy.25
  531.8 0.0 copy-done.1
  (1 shorter events, 0.0 us)
Async XLA Ops:
  0.6 1.1 copy-start
  0.7 70.3 %collective-permute-start = (bf16[768,3072]{1,0:T(8,128)(2,1)}, bf16[768,3072]{1,0:T(8,128)(2,1)}, u32[]{:S(2)}, u32[]{:S(2)}) collective-permute-start(bf16[768,3072]{1,0:T(8,128)(2,1)} %bitcast.40), channel_id=1, source_target_pairs={{0,16},{16,0},{1,17},{17,1},{2,18},{18,2},{3,19},{19,3},{4,20},{20... | collective-permute-start | bytes 14155784 | tf_op jit(solution)/shard_map/ppermute | solution.py:684
  1.2 69.7 %collective-permute-start.1 = (bf16[3072,768]{1,0:T(8,128)(2,1)}, bf16[3072,768]{1,0:T(8,128)(2,1)}, u32[]{:S(2)}, u32[]{:S(2)}) collective-permute-start(bf16[3072,768]{1,0:T(8,128)(2,1)} %bitcast.44), channel_id=1, source_target_pairs={{0,16},{16,0},{1,17},{17,1},{2,18},{18,2},{3,19},{19,3},{4,20},{20... | collective-permute-start | bytes 14155784 | tf_op jit(solution)/shard_map/ppermute | solution.py:684
  1.8 138.3 %collective-permute-start.2 = (bf16[256,768]{1,0:T(8,128)(2,1)S(1)}, bf16[256,768]{1,0:T(8,128)(2,1)S(1)}, u32[]{:S(2)}, u32[]{:S(2)}) collective-permute-start(bf16[256,768]{1,0:T(8,128)(2,1)S(1)} %dynamic-slice_bitcast_fusion), channel_id=1, source_target_pairs={{0,0},{1,16},{2,1},{3,17},{16,2},{17,18},{18,3},{19,19},{4,4},{5,2... | collective-permute-start | bytes 1179656 | tf_op jit(solution)/shard_map/ppermute | solution.py:701
  140.1 0.7 copy-start.2
  458.9 72.9 %copy-start.1 = (bf16[2,1,256,768]{3,2,1,0:T(8,128)(2,1)S(1)}, bf16[2,1,256,768]{3,2,1,0:T(8,128)(2,1)}, u32[]{:S(2)}) copy-start(bf16[2,1,256,768]{3,2,1,0:T(8,128)(2,1)} %param.11) | copy-start | bytes 2359300

commit v7 on v6

--- a/solution.py
+++ b/solution.py
@@ -223,9 +223,9 @@
         packed = jnp.where(lane == index, entry, packed)
     aux[...] = packed
     packed_t = packed.T
-    hot = fill_slots(packed_t, slots, 0) + fill_slots(packed_t, slots, 1)
-    outgoing[...] = mm(hot, normed).astype(BF16)
-    return packed
+    hot = [fill_slots(packed_t, slots, k) for k in range(2)]
+    outgoing[...] = mm(hot[0] + hot[1], normed).astype(BF16)
+    return packed, hot
 
 
 def pick_rows(slot, slots):
@@ -447,11 +447,12 @@
     difference[...] = gap
 
 
-def spread_values(values, packed, slots):
+def spread_values(values, packed, slots, hot=None):
     packed_t = packed.T
     total = jnp.zeros((slots, values.shape[1]), F32)
     for k in range(2):
-        total = total + mm(fill_slots(packed_t, slots, k), (values * packed[:, 2 + k : 3 + k]).astype(BF16))
+        select = hot[k] if hot else fill_slots(packed_t, slots, k)
+        total = total + mm(select, (values * packed[:, 2 + k : 3 + k]).astype(BF16))
     return total.astype(BF16)
 
 
@@ -1212,7 +1213,7 @@
         return jnp.concatenate([block, jnp.zeros((count - block.shape[0], block.shape[1]), F32)], axis=0)
 
     small = [
-        router_shard[...].astype(F32), below(gain_shard[...].astype(F32), 8).T[:, :2],
+        router_shard[...].astype(F32).T, below(gain_shard[...].astype(F32), 8).T[:, :2],
         below(table_shard[...].astype(F32), rows),
     ]
     spare = blocks.shape[2] - 3 * width - sum(part.shape[1] for part in small)
@@ -1224,10 +1225,7 @@
         ]
         blocks[member] = jnp.concatenate(parts + small, axis=1).astype(BF16)
     for batch in range(2):
-        wide = jnp.concatenate(
-            [route_rows[batch].astype(F32), jnp.zeros((sizes.span, 126), F32)], axis=1
-        )
-        home_routes[batch] = wide.T[:8, :]
+        home_routes[batch] = below(route_rows[batch].astype(F32), 8)
 
 
 def attend(section, sizes, *refs):
@@ -1272,6 +1270,24 @@
         copy.start()
         pair_copies.append(copy)
 
+    def half_of(piece, part):
+        return pl.ds(pl.multiple_of(piece * span + part * (span // 2), span // 2), span // 2)
+
+    def pass_half(part, values):
+        gathered[half_of(own, part), :] = values
+        block = gathered.at[half_of(own, part)]
+        copy = remote(block, block, pair_send.at[3 * part], pair_recv.at[3 * part], beside_z)
+        copy.start()
+        pair_copies.append(copy)
+
+    def await_side():
+        if section == 0:
+            await_piece(side, 0)
+            return
+        for part in range(2):
+            block = gathered.at[half_of(side, part)]
+            remote(block, block, pair_send.at[3 * part], pair_recv.at[3 * part], partner).wait_recv()
+
     def await_piece(piece, index):
         block = gathered.at[rows_of(piece)]
         remote(block, block, pair_send.at[index], pair_recv.at[index], partner).wait_recv()
@@ -1315,15 +1331,16 @@
         gather.along_z()
         gather.over_plane()
         gather.out_start()
-        await_piece(side, 0)
+        await_side()
         pass_piece(side, 2, partner)
         gather.finish_early()
     else:
-        total, gap = combined(returned[...], aux_before[...], middle_before[...])
-        result[...] = total.astype(BF16)
-        gathered[rows_of(own), :] = total.astype(BF16)
-        difference[...] = gap
-        pass_piece(own, 0, beside_z)
+        for part in range(2):
+            some = slice(part * span // 2, (part + 1) * span // 2)
+            total, gap = combined(returned[...], aux_before[some, :], middle_before[some, :])
+            result[some, :] = total.astype(BF16)
+            difference[some, :] = gap
+            pass_half(part, total.astype(BF16))
         pass_piece(own, 1, partner)
 
     router, gain_one, gain_two, table = unpack_small(sizes, early, section)
@@ -1333,20 +1350,21 @@
     await_piece(flipped, 1)
     project(gathered, rows_of(flipped), gain_one, weight, mixed)
     if section:
-        await_piece(side, 0)
+        await_side()
         pass_piece(side, 2, partner)
     project(gathered, rows_of(side), gain_one, weight, mixed)
     await_piece(side_flipped, 2)
     project(gathered, rows_of(side_flipped), gain_one, weight, mixed)
     trade = Regroup(outcome, attended, group_send, group_recv)
     for head in range(sizes.heads):
-        if section == 0 and head < 3:
-            (gather.out_along_z, gather.out_over_plane, gather.out_finish)[head]()
+        if section == 0 and 0 < head < 3:
+            (gather.out_along_z, gather.out_over_plane)[head - 1]()
         attend_head(sizes.attention, head, mixed, bias, outcome, stats)
         trade.start(slice(head * sizes.size, (head + 1) * sizes.size))
     if section == 0:
-        for stage in (gather.out_along_z, gather.out_over_plane, gather.out_finish)[sizes.heads :]:
+        for stage in (gather.out_along_z, gather.out_over_plane)[max(sizes.heads - 1, 0) :]:
             stage()
+        gather.out_finish()
         for which in range(2):
             @pl.when(jnp.logical_not(aligned & (core == which)))
             def routed():
@@ -1363,9 +1381,9 @@
     for member in range(GROUP):
         total = total + mm(attended[member], out_rows(sizes, w_outs, section, member), TN)
     middle[...] = total
-    packed = dispatch(total, gain_two, router, masks, places, sizes.slots, outgoing, normed_two, aux)
+    packed, hot = dispatch(total, gain_two, router, masks, places, sizes.slots, outgoing, normed_two, aux)
     if section:
-        spread[...] = spread_values(given[...].astype(F32), packed, sizes.slots)
+        spread[...] = spread_values(given[...].astype(F32), packed, sizes.slots, hot)
     for copy in pair_copies:
         copy.wait_send()
     if section == 0:
@@ -1390,7 +1408,7 @@
     ]
     scratch = [
         pltpu.VMEM((128, 2 * span * GROUP), F32), pltpu.VMEM((sizes.heads * GROUP, span, span), F32),
-        dma((3,)), dma((3,)), dma((3 * sizes.heads,)), dma((3 * sizes.heads,)),
+        dma((4,)), dma((4,)), dma((3 * sizes.heads,)), dma((3 * sizes.heads,)),
     ]
     if section == 0:
         rows = sizes.shard_rows
@@ -1422,7 +1440,7 @@
     )
     grad_out[...] = shared[:, :features]
     tail = shared[:, features:]
-    grad_router[...] = tail[:, :experts]
+    grad_router[...] = tail.T[:experts, :]
     ends = [owned[member, :, sizes.base :] for member in range(GROUP)]
     grad_table[...] = jnp.concatenate(
         [end[: sizes.table_rows, sizes.offset : sizes.offset + sizes.heads] for end in ends], axis=1
@@ -1751,7 +1769,8 @@
     if fused:
         first = run_attend(
             0, shared_sizes,
-            [inputs[:, 0], routes[0, :, 0], qkv_shard[0], out_shard[0], router_shard[0], gain_shard[0],
+            [inputs[:, 0], jnp.swapaxes(routes[0, :, 0], 1, 2), qkv_shard[0], out_shard[0],
+             router_shard[0].T, gain_shard[0],
              table_shard[0]], 4)
         early_all, w_out_all, route_all = first[9:]
     else:
@@ -1843,10 +1862,11 @@
         section_outputs, section_grads, grad_qkv, grad_out, grad_router, grad_gains, grad_table = call(
             functools.partial(unpack, shared_sizes), "unpack",
             [shape(home.shape, BF16), shape(home.shape, F32), shape((shard_rows, 3 * features), F32), shape((shard_rows, features), F32),
-             shape((shard_rows, experts), F32), shape((2, shard_rows), F32),
+             shape((experts, shard_rows), F32), shape((2, shard_rows), F32),
              shape((table_rows, head_count), F32)],
             [home, owned, shared_sum, section_outputs],
         )
+        grad_router = grad_router.T
     stream = None if fused else own
     for section in range(0 if fused else 2):
         qkv, router, gain_one, gain_two, table, expert_in, expert_down = weights[section]

time: 542 us -> 539 us (level)
  transfers between devices with their start and end apart: 3 -> 3, of which waited for: 0 -> 0; matrix products, arithmetic and copies ran while one was open for 1% -> 0% of each run, Pallas kernels for 25% -> 26%
where the time goes in v7:
time: 539 us; the launch traced here: 529 us
  Pallas kernels  526 us (98%)
    pallas_call x3, Pallas kernels, run_expert_layer(): pl.pallas_call(functools.partial(expert_layer, mode, section), name='expe...  271 us
    pallas_call x6, Pallas kernels, call(): pl.pallas_call(body, name=name, in_specs=specs, out_specs=[pl.BlockSpec(m...  255 us
  transfers between devices with their start and end apart: 3, of which 0 were waited for; matrix products, arithmetic and copies ran while one was open for 0% of the time, Pallas kernels for 26%

profile of v7, /device:TPU:0, one launch (start us, length us, event | category | flops | bytes accessed | tf_op | source)
XLA Modules:
  0.0 529.4 jit_solution(17645264424475755645)
XLA Ops:
  0.6 0.0 copy-start
  0.7 0.6 collective-permute-start
  1.2 0.1 collective-permute-start.1
  1.3 0.5 copy-done
  1.8 0.7 collective-permute-start.2
  2.5 66.7 %attend.2 = (bf16[4,192,256]{2,1,0:T(8,128)(2,1)}, bf16[1024,576]{1,0:T(8,128)(2,1)}, bf16[1024,768]{1,0:T(8,128)(2,1)}, f32[8,1024]{1,0:T(8,128)}, bf16[1024,76...) custom-call(bf16[2,256,768]{2,1,0:T(8,128)(2,1)} %bitcast.53, ...), custom_call_target="tpu_custom_call" | custom-call | flops 6442450944 | bytes 11884320 | tf_op jit(solution)/shard_map/attend/pallas_call | solution.py:103
  69.2 0.0 collective-permute-done.refs_2_
  69.2 0.0 collective-permute-done.1.refs_3_
  69.2 69.6 %expert_layer_forward.1 = (bf16[16,64,768]{2,1,0:T(8,128)(2,1)}, bf16[16,64,768]{2,1,0:T(8,128)(2,1)}, bf16[1024,3072]{1,0:T(8,128)(2,1)}, bf16[1024,3072]{1,0:T(8,128)(2,1)}) custom-call(bf16[768,3072]{1,0:T(8,128)(2,1)} %bitcast.44, bf16[3072,768]{1,0:T(8,128)(2,1)} %bitcast.48, bf16[768,3072]{1,0:T(8,128)(2,1)} %collective-permute-done.refs_2_, ...), custom_call_target="tpu_custom_call" | custom-call | flops 19327352832 | bytes 167772160 | tf_op jit(solution)/shard_map/expert_layer_forward/pallas_call | solution.py:984
  138.9 0.0 collective-permute-done.2.refs_6_.refs_9_
  138.9 0.0 copy-start.2
  138.9 0.7 copy-done.2
  139.6 40.3 %attend.3 = (bf16[4,192,256]{2,1,0:T(8,128)(2,1)}, bf16[1024,576]{1,0:T(8,128)(2,1)}, bf16[1024,768]{1,0:T(8,128)(2,1)}, f32[8,1024]{1,0:T(8,128)}, bf16[1024,76...) custom-call(bf16[1024,768]{1,0:T(8,128)(2,1)} %bitcast.68, ...), custom_call_target="tpu_custom_call" | custom-call | flops 6442450944 | bytes 16433152 | tf_op jit(solution)/shard_map/attend/pallas_call | solution.py:103
  179.9 131.4 %expert_layer_both.1 = (bf16[16,64,768]{2,1,0:T(8,128)(2,1)}, bf16[16,64,768]{2,1,0:T(8,128)(2,1)}, bf16[768,3072]{1,0:T(8,128)(2,1)}, bf16[3072,768]{1,0:T(8,128)(2,1)}) custom-call(bf16[768,3072]{1,0:T(8,128)(2,1)} %bitcast.45, bf16[3072,768]{1,0:T(8,128)(2,1)} %bitcast.49, bf16[768,3072]{1,0:T(8,128)(2,1)} %collective-permute-done.refs_2_, ...), custom_call_target="tpu_custom_call" | custom-call | flops 38654705664 | bytes 167772160 | tf_op jit(solution)/shard_map/expert_layer_both/pallas_call | solution.py:984
  311.4 61.9 %attend_back.2 = (bf16[768,896]{1,0:T(8,128)(2,1)}, bf16[256,768]{1,0:T(8,128)(2,1)}, bf16[16,48,640]{2,1,0:T(8,128)(2,1)}, bf16[2,256,768]{2,1,0:T(8,128)(2,1)}, bf16[1024,768]{1,0:T(8,128)(2,1)}) custom-call(bf16[2,16,48,640]{3,2,1,0:T(8,128)(2,1)} %get-tuple-element.64.refs_3_.refs_0_.refs_7_, bf16[1024,576]{1,0:T(8,128)(2,1)} %get-tuple-element.75.refs_1_, ...), custom_call_target="tpu_custom_call" | custom-call | flops 10737418240 | bytes 18399232 | tf_op jit(solution)/shard_map/attend_back/pallas_call | solution.py:103
  373.3 69.5 %expert_layer_backward.1 = (bf16[16,64,768]{2,1,0:T(8,128)(2,1)}, bf16[768,3072]{1,0:T(8,128)(2,1)}, bf16[3072,768]{1,0:T(8,128)(2,1)}) custom-call(bf16[768,3072]{1,0:T(8,128)(2,1)} %bitcast.46, bf16[3072,768]{1,0:T(8,128)(2,1)} %bitcast.50, bf16[768,3072]{1,0:T(8,128)(2,1)} %collective-permute-done.refs_2_, ...), custom_call_target="tpu_custom_call", output_to_operand_aliasing={{1}: (8, {}), {2}: (9, {})} | custom-call | flops 19327352832 | bytes 167772160 | tf_op jit(solution)/shard_map/expert_layer_backward/pallas_call | solution.py:984
  442.8 14.6 %before_attention.1 = (f32[256,768]{1,0:T(8,128)}, bf16[4,192,256]{2,1,0:T(8,128)(2,1)}, bf16[768,896]{1,0:T(8,128)(2,1)}, f32[768,3072]{1,0:T(8,128)}, f32[3072,768]{1,0:T(8,128)}) custom-call(bf16[1024,768]{1,0:T(8,128)(2,1)} %bitcast.40, f32[256,128]{1,0:T(8,128)} %get-tuple-element.71.refs_1_.refs_15_, ...), custom_call_target="tpu_custom_call" | custom-call | flops 2147483648 | bytes 39665664 | tf_op jit(solution)/shard_map/before_attention/pallas_call | solution.py:103
  457.4 0.0 copy-start.1
  457.5 68.1 %attend_back.3 = (bf16[2,256,768]{2,1,0:T(8,128)(2,1)}, f32[4,48,640]{2,1,0:T(8,128)}, f32[48,896]{1,0:T(8,128)}) custom-call(bf16[2,16,48,640]{3,2,1,0:T(8,128)(2,1)} %get-tuple-element.64.refs_3_.refs_0_.refs_7_, bf16[1024,576]{1,0:T(8,128)(2,1)} %get-tuple-element.65.refs_1_, f32[8,1024]{1,0:T(8,128)} %get-tuple-element.66.refs_2_, ...), custom_call_target="tpu_custom_call" | custom-call | flops 10737418240 | bytes 11902976 | tf_op jit(solution)/shard_map/attend_back/pallas_call | solution.py:103
  525.6 3.4 unpack.1
  529.0 0.0 copy-done.1
  (1 shorter events, 0.0 us)
Async XLA Ops:
  0.6 1.1 copy-start
  0.7 68.6 %collective-permute-start = (bf16[768,3072]{1,0:T(8,128)(2,1)}, bf16[768,3072]{1,0:T(8,128)(2,1)}, u32[]{:S(2)}, u32[]{:S(2)}) collective-permute-start(bf16[768,3072]{1,0:T(8,128)(2,1)} %bitcast.43), channel_id=1, source_target_pairs={{0,16},{16,0},{1,17},{17,1},{2,18},{18,2},{3,19},{19,3},{4,20},{20... | collective-permute-start | bytes 14155784 | tf_op jit(solution)/shard_map/ppermute | solution.py:685
  1.2 68.0 %collective-permute-start.1 = (bf16[3072,768]{1,0:T(8,128)(2,1)}, bf16[3072,768]{1,0:T(8,128)(2,1)}, u32[]{:S(2)}, u32[]{:S(2)}) collective-permute-start(bf16[3072,768]{1,0:T(8,128)(2,1)} %bitcast.47), channel_id=1, source_target_pairs={{0,16},{16,0},{1,17},{17,1},{2,18},{18,2},{3,19},{19,3},{4,20},{20... | collective-permute-start | bytes 14155784 | tf_op jit(solution)/shard_map/ppermute | solution.py:685
  1.8 137.1 %collective-permute-start.2 = (bf16[256,768]{1,0:T(8,128)(2,1)S(1)}, bf16[256,768]{1,0:T(8,128)(2,1)S(1)}, u32[]{:S(2)}, u32[]{:S(2)}) collective-permute-start(bf16[256,768]{1,0:T(8,128)(2,1)S(1)} %dynamic-slice_bitcast_fusion), channel_id=1, source_target_pairs={{0,0},{1,16},{2,1},{3,17},{16,2},{17,18},{18,3},{19,19},{4,4},{5,2... | collective-permute-start | bytes 1179656 | tf_op jit(solution)/shard_map/ppermute | solution.py:702
  138.9 0.7 copy-start.2
  457.4 71.5 %copy-start.1 = (bf16[2,1,256,768]{3,2,1,0:T(8,128)(2,1)S(1)}, bf16[2,1,256,768]{3,2,1,0:T(8,128)(2,1)}, u32[]{:S(2)}) copy-start(bf16[2,1,256,768]{3,2,1,0:T(8,128)(2,1)} %param.11) | copy-start | bytes 2359300
